TPU v7x, 32 devices: a whole 2x2x4 slice. The times are simulated.
32 devices in a mesh: groups: 2 (over y), blk: 8 (over z, x), sub: 2 (over core).
Axes of the slice: x: 2, y: 2, z: 4, core: 2. Of those that a mesh axis runs over, the one named last changes fastest.
Arguments:
- embeddings: bfloat16 [16384, 1024], P(('groups', 'blk', 'sub')), parts along dimension 0, may hold values from -0.1875 to 0.1875
- start_panel: bfloat16 [16384, 128], P(('groups', 'blk', 'sub')), parts along dimension 0, may hold values from -6 to 6
- tile_mask: int32 [128, 56], P(('groups', 'blk', 'sub')), parts along dimension 0, may hold values from 0 to 1, as said below
- inv_width: float32 [1], replicated, may hold values from 0.5 to 1.5
Outputs:
- basis: float32 [16384, 128], P(('groups', 'blk', 'sub')), parts along dimension 0
- upper: float32 [256, 128], P('groups'), parts along dimension 0
There are 2 independent parts, one for each index of `groups`. A program takes and returns all parts, laid end to end along the dimension named above; an argument that names none is the same for every part. Nothing has to cross between parts.
Inputs may be any that keep to these rules, and one draw needn't show every extreme that they name: `tile_mask`: 0 or 1; the entry of every tile for its own tile is 1.
All inputs are finite; a program needn't handle non-finite values.
Results may differ from a plain program's by a relative error of at most 0.0088.
Values may be sent and summed in bfloat16 or wider, within the bound.
No kernel may reach another device: no remote copies, remote signals or barrier semaphores. Data moves between devices by JAX's collectives and lax.ppermute only.
A program may use at most 64 MiB of HBM per device.

v0:
```python
import jax
import jax.numpy as jnp
from jax import lax
from jax.sharding import PartitionSpec as P

TILE = 128
REACH = 3


def shifted(block, axis, distance):
    devices = range(lax.axis_size(axis))
    route = [((i - distance) % len(devices), i) for i in devices]
    return lax.ppermute(block, axis, route)


def per_device(embeddings, start_panel, tile_mask, inv_width):
    row_blocks = embeddings.shape[0] // TILE
    feature_count = embeddings.shape[1]
    sub_index = lax.axis_index("sub")
    blk_embed, blk_mask = (
        lax.all_gather(embeddings, "sub", axis=0, tiled=True),
        lax.all_gather(tile_mask, "sub", axis=0, tiled=True),
    )
    blk_blocks = blk_mask.shape[0]
    row_sq = jnp.sum(jnp.square(blk_embed.astype(jnp.float32)), axis=1)
    inverse = inv_width[0]
    own_panel = jnp.concatenate([embeddings, start_panel], axis=1)

    def contribute(accum_rows, offset, source):
        src_embed = source[:, :feature_count]
        src_panel = source[:, feature_count:]
        start = (REACH - offset) * blk_blocks + sub_index * row_blocks
        window = lax.dynamic_slice_in_dim(blk_mask, start, row_blocks, 1)

        def compute(unused):
            gram_tile = lax.dot_general(
                blk_embed, src_embed, (((1,), (1,)), ((), ())), preferred_element_type=jnp.float32
            )
            src_sq = jnp.sum(jnp.square(src_embed.astype(jnp.float32)), axis=1)
            distance = jnp.maximum(row_sq[:, None] + src_sq[None, :] - 2.0 * gram_tile, 0.0)
            kernel = jnp.exp(-inverse * distance).reshape(blk_blocks, TILE, row_blocks, TILE)
            kernel = kernel * window.astype(jnp.float32)[:, None, :, None]
            kernel = kernel.reshape(blk_blocks * TILE, row_blocks * TILE).astype(jnp.bfloat16)
            return jnp.dot(kernel, src_panel, preferred_element_type=jnp.float32)

        def skipped(unused):
            return jnp.zeros_like(accum_rows)

        return accum_rows + lax.cond(jnp.any(window > 0), compute, skipped, jnp.int32(0))

    accum_rows = jnp.zeros((blk_blocks * TILE, start_panel.shape[1]), jnp.float32)
    accum_rows = contribute(accum_rows, 0, own_panel)
    upward_panel = own_panel
    downward_panel = own_panel
    for hop_count in range(1, REACH + 1):
        upward_panel = shifted(upward_panel, "blk", 1)
        accum_rows = contribute(accum_rows, hop_count, upward_panel)
        downward_panel = shifted(downward_panel, "blk", -1)
        accum_rows = contribute(accum_rows, -hop_count, downward_panel)
    own_rows = lax.psum_scatter(accum_rows, "sub", scatter_dimension=0, tiled=True)
    local_gram = jnp.dot(
        own_rows.T, own_rows, precision=lax.Precision.HIGHEST, preferred_element_type=jnp.float32
    )
    lower_factor = jnp.linalg.cholesky(lax.psum(local_gram, ("blk", "sub")))
    basis = lax.linalg.triangular_solve(
        lower_factor, own_rows, left_side=False, lower=True, transpose_a=True
    )
    return (basis, lower_factor.T)


def solution(mesh):
    return jax.shard_map(
        per_device,
        mesh=mesh,
        in_specs=(
            P(("groups", "blk", "sub"), None),
            P(("groups", "blk", "sub"), None),
            P(("groups", "blk", "sub"), None),
            P(),
        ),
        out_specs=(P(("groups", "blk", "sub"), None), P("groups", None)),
        check_vma=False,
    )
```

profile of v0, /device:TPU:0, one launch (start us, length us, event | category | flops | bytes accessed | tf_op | source)
XLA Modules:
  0.0 319.9 jit_solution(6074443228945394355)
XLA Ops:
  8.6 6.0 %collective-permute-start.1 = (bf16[512,1152]{1,0:T(8,128)(2,1)S(1)}, bf16[512,1152]{1,0:T(8,128)(2,1)}, u32[]{:S(2)}, u32[]{:S(2)}) collective-permute-start(bf16[512,1152]{1,0:T(8,128)(2,1)S(1)} %constant_dynamic-update-slice_fusion), channel_id=1, source_target_pairs={{2,0},{4,2},{6,4},{8,6},{10,8},{12,10},{14,12},{0,14},{3,1},{5,3},... | collective-permute-start | bytes 3538952 | tf_op jit(solution)/shard_map/ppermute | solution.py:13
  14.6 48.3 %collective-permute-done.1 = bf16[512,1152]{1,0:T(8,128)(2,1)} collective-permute-done((bf16[512,1152]{1,0:T(8,128)(2,1)S(1)}, bf16[512,1152]{1,0:T(8,128)(2,1)}, u32[]{:S(2)}, u32[]{:S(2)}) %collective-permute-start.1) | collective-permute-done | bytes 1179680 | tf_op jit(solution)/shard_map/ppermute | solution.py:13
  62.9 2.7 collective-permute-start.3
  65.8 49.9 %collective-permute-done.3 = bf16[512,1152]{1,0:T(8,128)(2,1)} collective-permute-done((bf16[512,1152]{1,0:T(8,128)(2,1)}, bf16[512,1152]{1,0:T(8,128)(2,1)}, u32[]{:S(2)}, u32[]{:S(2)}) %collective-permute-start.3) | collective-permute-done | bytes 1179680 | tf_op jit(solution)/shard_map/ppermute | solution.py:13
  115.7 2.5 collective-permute-start.5
  118.2 1.8 all-gather
  125.3 2.2 multiply_reduce_fusion.7
  127.5 6.8 %conditional.7 = (f32[1024,128]{1,0:T(8,128)}) conditional(s32[]{:T(128)} %convert_element_type.87, () %tuple.50, (f32[]{:T(128)}, f32[1024]{0:T(1024)S(1)}, bf16[512,1024]{1,0:T(8,128)(2,1)S(1)}, bf16[1024,1024]{1,0:T(8,128)(2,1)S(1)}, s32[8,4]{1,0:T(8,128)S(1)}, /*index=5*/bf16[512,128]{1,0:T(8,128)(2,1)S(1)}) %tuple.124), branch_computations={%region_2.0_spmd, %region_3.0_spmd} | conditional | flops 1213201920 | bytes 9052564 | solution.py:49
  128.5 1.7 mul.95
  130.2 4.2 %fusion.1 = f32[1024,128]{1,0:T(8,128)} fusion(bf16[512,128]{1,0:T(8,128)(2,1)S(1)} %get-tuple-element.116, f32[128,8,4,128]{3,2,1,0:T(4,128)} %bitcast.82, bf16[1024,1024]{1,0:T(8,128)(2,1)S(1)} %get-tuple-element.114, bf16[512,1024]{1,0:T(8,128)(2,1)S(1)} %get-tuple-element.113, f32[512]{0:T(512)S(1)} %multiply_reduce_fusion, ...), kind=kOutput, calls=%fused_computation.3 | convolution fusion | flops 1211629568 | bytes 5904388 | tf_op jit(solution)/shard_map/cond/branch_1_fun/dot_general | solution.py:44
  134.3 7.5 %conditional.9 = (f32[1024,128]{1,0:T(8,128)S(1)}) conditional(s32[]{:T(128)} %convert_element_type.90, () %tuple.54, (f32[]{:T(128)}, f32[1024]{0:T(1024)S(1)}, bf16[512,1152]{1,0:T(8,128)(2,1)}, bf16[1024,1024]{1,0:T(8,128)(2,1)S(1)}, s32[8,4]{1,0:T(8,128)S(1)}) %tuple.117), branch_computations={%region_10.0_spmd, %region_11.0_spmd} | conditional | flops 1213201920 | bytes 9052564 | solution.py:49
  138.2 3.6 %fusion.22 = f32[1024,128]{1,0:T(8,128)S(1)} fusion(f32[128,8,4,128]{3,2,1,0:T(4,128)} %bitcast.83, bf16[1024,1024]{1,0:T(8,128)(2,1)S(1)} %get-tuple-element.125, f32[512]{0:T(512)S(1)} %multiply_reduce_fusion.2, f32[1024]{0:T(1024)S(1)} %get-tuple-element.123, f32[]{:T(128)S(6)} %neg.16, bf16[512,1152]{1,0:T(8,128)(2,1)} %get-tuple-element.124), kind=kOutput, calls=%fused_computation.27 | convolution fusion | flops 1211629568 | bytes 5904388 | tf_op jit(solution)/shard_map/cond/branch_1_fun/dot_general | solution.py:44
  141.8 7.5 %conditional.8 = (f32[1024,128]{1,0:T(8,128)S(1)}) conditional(s32[]{:T(128)} %convert_element_type.89, () %tuple.52, (f32[]{:T(128)}, f32[1024]{0:T(1024)S(1)}, bf16[512,1152]{1,0:T(8,128)(2,1)}, bf16[1024,1024]{1,0:T(8,128)(2,1)S(1)}, s32[8,4]{1,0:T(8,128)S(1)}) %tuple.123), branch_computations={%region_6.0_spmd, %region_7.0_spmd} | conditional | flops 1213201920 | bytes 9052564 | solution.py:49
  144.0 1.7 mul.115
  145.7 3.6 %fusion.10 = f32[1024,128]{1,0:T(8,128)S(1)} fusion(f32[128,8,4,128]{3,2,1,0:T(4,128)} %bitcast.84, bf16[1024,1024]{1,0:T(8,128)(2,1)S(1)} %get-tuple-element.120, f32[512]{0:T(512)S(1)} %multiply_reduce_fusion.1, f32[1024]{0:T(1024)S(1)} %get-tuple-element.118, f32[]{:T(128)S(6)} %neg.15, bf16[512,1152]{1,0:T(8,128)(2,1)} %get-tuple-element.119), kind=kOutput, calls=%fused_computation.14 | convolution fusion | flops 1211629568 | bytes 5904388 | tf_op jit(solution)/shard_map/cond/branch_1_fun/dot_general | solution.py:44
  149.3 8.3 %conditional.11 = (f32[1024,128]{1,0:T(8,128)}) conditional(s32[]{:T(128)} %convert_element_type.92, () %tuple.58, (f32[]{:T(128)}, f32[1024]{0:T(1024)S(1)}, bf16[512,1152]{1,0:T(8,128)(2,1)}, bf16[1024,1024]{1,0:T(8,128)(2,1)S(1)}, s32[8,4]{1,0:T(8,128)S(1)}) %tuple.119), branch_computations={%region_18.0_spmd, %region_19.0_spmd} | conditional | flops 1213201920 | bytes 9052564 | solution.py:49
  153.2 4.4 %fusion.46 = f32[1024,128]{1,0:T(8,128)} fusion(f32[128,8,4,128]{3,2,1,0:T(4,128)} %bitcast.85, bf16[1024,1024]{1,0:T(8,128)(2,1)S(1)} %get-tuple-element.135, f32[512]{0:T(512)S(1)} %multiply_reduce_fusion.4, f32[1024]{0:T(1024)S(1)} %get-tuple-element.133, f32[]{:T(128)S(6)} %neg.18, bf16[512,1152]{1,0:T(8,128)(2,1)} %get-tuple-element.134), kind=kOutput, calls=%fused_computation.53 | convolution fusion | flops 1211629568 | bytes 5904388 | tf_op jit(solution)/shard_map/cond/branch_1_fun/dot_general | solution.py:44
  157.6 8.3 %conditional.10 = (f32[1024,128]{1,0:T(8,128)}) conditional(s32[]{:T(128)} %convert_element_type.91, () %tuple.56, (f32[]{:T(128)}, f32[1024]{0:T(1024)S(1)}, bf16[512,1152]{1,0:T(8,128)(2,1)}, bf16[1024,1024]{1,0:T(8,128)(2,1)S(1)}, s32[8,4]{1,0:T(8,128)S(1)}) %tuple.120), branch_computations={%region_14.0_spmd, %region_15.0_spmd} | conditional | flops 1213201920 | bytes 9052564 | solution.py:49
  159.7 1.7 mul.127
  161.4 4.4 %fusion.34 = f32[1024,128]{1,0:T(8,128)} fusion(f32[128,8,4,128]{3,2,1,0:T(4,128)} %bitcast.86, bf16[1024,1024]{1,0:T(8,128)(2,1)S(1)} %get-tuple-element.130, f32[512]{0:T(512)S(1)} %multiply_reduce_fusion.3, f32[1024]{0:T(1024)S(1)} %get-tuple-element.128, f32[]{:T(128)S(6)} %neg.17, bf16[512,1152]{1,0:T(8,128)(2,1)} %get-tuple-element.129), kind=kOutput, calls=%fused_computation.40 | convolution fusion | flops 1211629568 | bytes 5904388 | tf_op jit(solution)/shard_map/cond/branch_1_fun/dot_general | solution.py:44
  167.5 8.3 %conditional.13 = (f32[1024,128]{1,0:T(8,128)}) conditional(s32[]{:T(128)} %convert_element_type.94, () %tuple.62, (f32[]{:T(128)}, f32[1024]{0:T(1024)S(1)}, bf16[512,1152]{1,0:T(8,128)(2,1)}, bf16[1024,1024]{1,0:T(8,128)(2,1)S(1)}, s32[8,4]{1,0:T(8,128)S(1)}) %tuple.121), branch_computations={%region_26.0_spmd, %region_27.0_spmd} | conditional | flops 1213201920 | bytes 9052564 | solution.py:49
  169.7 1.7 mul.145
  171.4 4.5 %fusion.70 = f32[1024,128]{1,0:T(8,128)} fusion(f32[128,8,4,128]{3,2,1,0:T(4,128)} %bitcast.87, bf16[1024,1024]{1,0:T(8,128)(2,1)S(1)} %get-tuple-element.145, f32[512]{0:T(512)S(1)} %multiply_reduce_fusion.6, f32[1024]{0:T(1024)S(1)} %get-tuple-element.143, f32[]{:T(128)S(6)} %neg.20, bf16[512,1152]{1,0:T(8,128)(2,1)} %get-tuple-element.144), kind=kOutput, calls=%fused_computation.79 | convolution fusion | flops 1211629568 | bytes 5904388 | tf_op jit(solution)/shard_map/cond/branch_1_fun/dot_general | solution.py:44
  175.8 8.3 %conditional.12 = (f32[1024,128]{1,0:T(8,128)}) conditional(s32[]{:T(128)} %convert_element_type.93, () %tuple.60, (f32[]{:T(128)}, f32[1024]{0:T(1024)S(1)}, bf16[512,1152]{1,0:T(8,128)(2,1)}, bf16[1024,1024]{1,0:T(8,128)(2,1)S(1)}, s32[8,4]{1,0:T(8,128)S(1)}) %tuple.122), branch_computations={%region_22.0_spmd, %region_23.0_spmd} | conditional | flops 1213201920 | bytes 9052564 | solution.py:49
  179.7 4.4 %fusion.58 = f32[1024,128]{1,0:T(8,128)} fusion(f32[128,8,4,128]{3,2,1,0:T(4,128)} %bitcast.88, bf16[1024,1024]{1,0:T(8,128)(2,1)S(1)} %get-tuple-element.140, f32[512]{0:T(512)S(1)} %multiply_reduce_fusion.5, f32[1024]{0:T(1024)S(1)} %get-tuple-element.138, f32[]{:T(128)S(6)} %neg.19, bf16[512,1152]{1,0:T(8,128)(2,1)} %get-tuple-element.139), kind=kOutput, calls=%fused_computation.66 | convolution fusion | flops 1211629568 | bytes 5904388 | tf_op jit(solution)/shard_map/cond/branch_1_fun/dot_general | solution.py:44
  184.1 2.6 add_add_fusion
  187.1 8.9 %reduce-scatter.2.cloned.1.call-done = f32[512,128]{1,0:T(8,128)} async-done(((f32[1024,128]{1,0:T(8,128)}), f32[512,128]{1,0:T(8,128)}) %reduce-scatter.2.cloned.1.call-update) | async-done | bytes 262160 | tf_op jit(solution)/shard_map/reduce_scatter | solution.py:60
  196.0 2.2 fusion.85
  198.3 87.7 %all-reduce.2.cloned.1.call-done = f32[128,128]{0,1:T(8,128)} async-done(((f32[128,128]{0,1:T(8,128)}), f32[128,128]{0,1:T(8,128)}) %all-reduce.2.cloned.1.call-update) | async-done | bytes 65552 | tf_op jit(solution)/shard_map/psum | solution.py:64
  287.7 11.7 %cholesky.16 = f32[128,128]{1,0:T(8,128)S(1)} custom-call(f32[128,128]{1,0:T(8,128)S(1)} %fusion.83), custom_call_target="Cholesky" | custom-call | tf_op jit(solution)/shard_map/jit(cholesky)/cholesky | solution.py:64
  301.5 9.8 %custom-call.6 = f32[1,128,128]{1,2,0:T(8,128)S(1)} custom-call(f32[1,128,128]{2,1,0:T(8,128)S(1)} %get-tuple-element.206), custom_call_target="InvertDiagBlocksLowerTriangular" | custom-call | tf_op jit(solution)/shard_map/triangular_solve | solution.py:65
  311.3 2.0 fusion.81
  (50 shorter events, 22.6 us)
Async XLA Ops:
  7.2 1.4 copy-start.3
  7.2 111.0 %copy-start.4 = (s32[4,56]{1,0:T(4,128)S(1)}, s32[4,56]{1,0:T(4,128)}, u32[]{:S(2)}) copy-start(s32[4,56]{1,0:T(4,128)} %param.20) | copy-start | bytes 2692
  7.2 118.1 %all-gather.3.cloned.1.call-start = ((), (), s32[]{:S(2)}) async-start(), calls=%async_computation.1 | async-start | bytes 3145728 | tf_op jit(solution)/shard_map/all_gather | solution.py:21
  8.5 119.0 %copy-start = (bf16[512,1024]{1,0:T(8,128)(2,1)S(1)}, bf16[512,1024]{1,0:T(8,128)(2,1)}, u32[]{:S(2)}) copy-start(bf16[512,1024]{1,0:T(8,128)(2,1)} %param.18) | copy-start | bytes 3145732
  8.6 54.3 %collective-permute-start.1 = (bf16[512,1152]{1,0:T(8,128)(2,1)S(1)}, bf16[512,1152]{1,0:T(8,128)(2,1)}, u32[]{:S(2)}, u32[]{:S(2)}) collective-permute-start(bf16[512,1152]{1,0:T(8,128)(2,1)S(1)} %constant_dynamic-update-slice_fusion), channel_id=1, source_target_pairs={{2,0},{4,2},{6,4},{8,6},{10,8},{12,10},{14,12},{0,14},{3,1},{5,3},... | collective-permute-start | bytes 3538952 | tf_op jit(solution)/shard_map/ppermute | solution.py:13
  14.6 51.0 %collective-permute-start = (bf16[512,1152]{1,0:T(8,128)(2,1)S(1)}, bf16[512,1152]{1,0:T(8,128)(2,1)S(1)}, u32[]{:S(2)}, u32[]{:S(2)}) collective-permute-start(bf16[512,1152]{1,0:T(8,128)(2,1)S(1)} %constant_dynamic-update-slice_fusion), channel_id=1, source_target_pairs={{14,0},{0,2},{2,4},{4,6},{6,8},{8,10},{10,12},{12,14},{15,1},{1,3}... | collective-permute-start | bytes 3538952 | tf_op jit(solution)/shard_map/ppermute | solution.py:13
  62.9 52.8 %collective-permute-start.3 = (bf16[512,1152]{1,0:T(8,128)(2,1)}, bf16[512,1152]{1,0:T(8,128)(2,1)}, u32[]{:S(2)}, u32[]{:S(2)}) collective-permute-start(bf16[512,1152]{1,0:T(8,128)(2,1)} %collective-permute-done.1), channel_id=1, source_target_pairs={{2,0},{4,2},{6,4},{8,6},{10,8},{12,10},{14,12},{0,14},{3,1},{5,3},... | collective-permute-start | bytes 3538952 | tf_op jit(solution)/shard_map/ppermute | solution.py:13
  65.7 59.6 %copy-start.2 = (bf16[512,1152]{1,0:T(8,128)(2,1)}, bf16[512,1152]{1,0:T(8,128)(2,1)S(1)}, u32[]{:S(2)}) copy-start(bf16[512,1152]{1,0:T(8,128)(2,1)S(1)} %collective-permute-done) | copy-start | bytes 3538948
  65.7 52.5 %collective-permute-start.2 = (bf16[512,1152]{1,0:T(8,128)(2,1)S(1)}, bf16[512,1152]{1,0:T(8,128)(2,1)}, u32[]{:S(2)}, u32[]{:S(2)}) collective-permute-start(bf16[512,1152]{1,0:T(8,128)(2,1)S(1)} %collective-permute-done), channel_id=1, source_target_pairs={{14,0},{0,2},{2,4},{4,6},{6,8},{8,10},{10,12},{12,14},{15,1},{1,3}... | collective-permute-start | bytes 3538952 | tf_op jit(solution)/shard_map/ppermute | solution.py:13
  65.7 130.3 %reduce-scatter.2.cloned.1.call-start = ((), (), s32[]{:S(2)}) async-start(), calls=%async_computation.2 | async-start | bytes 786432 | tf_op jit(solution)/shard_map/reduce_scatter | solution.py:60
  115.7 51.8 %collective-permute-start.5 = (bf16[512,1152]{1,0:T(8,128)(2,1)}, bf16[512,1152]{1,0:T(8,128)(2,1)}, u32[]{:S(2)}, u32[]{:S(2)}) collective-permute-start(bf16[512,1152]{1,0:T(8,128)(2,1)} %collective-permute-done.3), channel_id=1, source_target_pairs={{2,0},{4,2},{6,4},{8,6},{10,8},{12,10},{14,12},{0,14},{3,1},{5,3},... | collective-permute-start | bytes 3538952 | tf_op jit(solution)/shard_map/ppermute | solution.py:13
  118.2 57.6 %collective-permute-start.4 = (bf16[512,1152]{1,0:T(8,128)(2,1)}, bf16[512,1152]{1,0:T(8,128)(2,1)}, u32[]{:S(2)}, u32[]{:S(2)}) collective-permute-start(bf16[512,1152]{1,0:T(8,128)(2,1)} %collective-permute-done.2), channel_id=1, source_target_pairs={{14,0},{0,2},{2,4},{4,6},{6,8},{8,10},{10,12},{12,14},{15,1},{1,3}... | collective-permute-start | bytes 3538952 | tf_op jit(solution)/shard_map/ppermute | solution.py:13
  125.3 2.2 copy-start.1
  186.8 99.2 %all-reduce.2.cloned.1.call-start = ((), (), s32[]{:S(2)}) async-start(), calls=%async_computation.3 | async-start | bytes 131072 | tf_op jit(solution)/shard_map/psum | solution.py:64
Sparse Core Ops, SparseCore 0:
  65.8 12.0 all-gather.2
  186.9 9.0 reduce-scatter.1
  200.4 85.4 all-reduce.1
where the time goes:
time: 322 us; the launch traced here: 320 us
  waiting for transfers between devices  197 us (61%)
  other arithmetic  38.8 us (12%)
  matrix products  33.4 us (10%)
  between operations  18.2 us (6%)
  local copies, waits for them, and re-layouts  14.8 us (5%)
  starting transfers between devices  11.6 us (4%)
  loops' own time  4.67 us (1%)
    ppermute x6, waiting for transfers between devices, shifted(): return lax.ppermute(block, axis, route)  99.9 us
    psum x1, waiting for transfers between devices, per_device(): lower_factor = jnp.linalg.cholesky(lax.psum(local_gram, ('blk', 'sub')))  87.7 us
    dot_general x7, matrix products, compute(): return jnp.dot(kernel, src_panel, preferred_element_type=jnp.float32)  29.1 us
    another operation x3, other arithmetic, per_device(): lower_factor = jnp.linalg.cholesky(lax.psum(local_gram, ('blk', 'sub')))  12.4 us
    mul x7, local copies, waits for them, and re-layouts, compute(): kernel = kernel * window.astype(jnp.float32)[:, None, :, None]  11.8 us
    ppermute x6, starting transfers between devices, shifted(): return lax.ppermute(block, axis, route)  11.3 us
    another operation x1, other arithmetic, per_device(): lax.linalg.triangular_solve(lower_factor, own_rows, left_side=False, lowe...  9.81 us
    reduce_sum x7, other arithmetic, compute(): src_sq = jnp.sum(jnp.square(src_embed.astype(jnp.float32)), axis=1)  9.31 us
  transfers between devices with their start and end apart: 9, of which 5 were waited for; matrix products, arithmetic and copies ran while one was open for 14% of the time, Pallas kernels for 0%

commit v1 on v0

v1 whole, which is shorter than its diff:
```python
import functools

import jax
import jax.numpy as jnp
from jax import lax
from jax.experimental import pallas as pl
from jax.experimental.pallas import tpu as pltpu
from jax.sharding import PartitionSpec as P

TILE = 128
REACH = 3
F32 = jnp.float32
BF16 = jnp.bfloat16
VMEM = pltpu.VMEM


def vmem_call(body, out_shapes, *operands, smem=0):
    spec = lambda space: pl.BlockSpec(memory_space=space)
    return pl.pallas_call(
        body,
        out_shape=out_shapes,
        in_specs=[spec(pltpu.SMEM)] * smem + [spec(VMEM)] * (len(operands) - smem),
        out_specs=jax.tree.map(lambda _: spec(VMEM), out_shapes),
        compiler_params=pltpu.CompilerParams(vmem_limit_bytes=48 << 20),
    )(*operands)


def shape(*dims):
    return jax.ShapeDtypeStruct(dims, F32)


def kernel_tile(inverse, rows2, row_sq, cols, col_sq):
    gram2 = lax.dot_general(rows2, cols, (((1,), (1,)), ((), ())), preferred_element_type=F32)
    return jnp.exp(-inverse * jnp.maximum(row_sq + col_sq - gram2, 0.0))


def masked(kernel, mask, first):
    tiles = kernel.shape[0] // TILE
    return jnp.concatenate(
        [kernel[i * TILE : (i + 1) * TILE] * mask[first + i : first + i + 1] for i in range(tiles)], axis=0
    ).astype(BF16)


def row_squares(rows):
    wide = rows.astype(F32)
    return jnp.sum(wide * wide, axis=1, keepdims=True)


def pair_products(inverse, rows_ref, rows_panel_ref, start, size, others, transposed):
    rows = rows_ref[start : start + size]
    row_sq = row_squares(rows)
    rows2 = rows * 2
    panel_t = None
    if transposed is not None:
        panel_t = rows_panel_ref[start : start + size].astype(F32).T.astype(BF16)
    half = 4
    image = None
    first = start // TILE
    for k, (cols, panel, col_sq, mask_ref) in enumerate(others):
        mask = mask_ref[...]
        kernel = kernel_tile(inverse, rows2, row_sq, cols[...], col_sq[...])
        term = jnp.dot(masked(kernel, mask, first), panel[...], preferred_element_type=F32)
        image = term if image is None else image + term
        if transposed is not None:
            back = jnp.dot(panel_t, masked(kernel, mask, half + first), preferred_element_type=F32)
            transposed[k] = back if transposed[k] is None else transposed[k] + back
    return image


def self_body(inverse_ref, e0, p0, s0, e1, p1, s1, m0, m1, image):
    rows = e0.shape[0]
    step = rows // 2
    for start in range(0, rows, step):
        image[start : start + step] = pair_products(
            inverse_ref[0], e0, p0, start, step, [(e0, p0, s0, m0), (e1, p1, s1, m1)], None
        )


def below_body(inverse_ref, x, xp, e0, p0, s0, m0, e1, p1, s1, m1, image, t0, t1):
    rows = x.shape[0]
    step = rows // 2
    back = [None, None]
    for start in range(0, rows, step):
        image[start : start + step] = pair_products(
            inverse_ref[0], x, xp, start, step, [(e0, p0, s0, m0), (e1, p1, s1, m1)], back
        )
    t0[...] = back[0]
    t1[...] = back[1]


def above_body(part, last, inverse_ref, x, xp, *refs):
    others = [refs[4 * k : 4 * k + 4] for k in range(4)]
    refs = refs[16:]
    sums = refs[: (2 if part == 0 else 4)]
    refs = refs[len(sums) :]
    rows = x.shape[0]
    back = [s[...] for s in sums] + [None] * (4 - len(sums))
    first = part * rows
    inverse = inverse_ref[0]
    if last:
        own_image, below_image = refs[:2]
        refs = refs[2:]
    image = refs[0]
    image[...] = above_products(inverse, x, xp, first, others, back)
    if not last:
        for out, value in zip(refs[1:], back):
            out[...] = value
        return
    own_out, below_out, cross_out = refs[1:]
    half = own_image.shape[0]
    own_out[...] = own_image[...] + back[0].T
    below_out[...] = below_image[...] + back[2].T
    cross_out[:half] = back[3].T
    cross_out[half:] = back[1].T


def above_products(inverse, x, xp, first, others, back):
    rows = x[...]
    row_sq = row_squares(rows)
    rows2 = rows * 2
    panel_t = xp[...].astype(F32).T.astype(BF16)
    image = None
    tile = first // TILE
    for k, (cols, panel, col_sq, mask_ref) in enumerate(others):
        mask = mask_ref[...]
        kernel = kernel_tile(inverse, rows2, row_sq, cols[...], col_sq[...])
        term = jnp.dot(masked(kernel, mask, tile), panel[...], preferred_element_type=F32)
        image = term if image is None else image + term
        term = jnp.dot(panel_t, masked(kernel, mask, 4 + tile), preferred_element_type=F32)
        back[k] = term if back[k] is None else back[k] + term
    return image


def gram_body(own, cross, below, above0, above1, image, gram):
    half = own.shape[0]
    part = above0.shape[0]
    total = own[...] + cross[half:] + below[...]
    total = total + jnp.concatenate([above0[...], above1[...]], axis=0)
    image[...] = total
    gram[...] = lax.dot_general(
        total, total, (((0,), (0,)), ((), ())), precision=lax.Precision.HIGHEST, preferred_element_type=F32
    )


def per_device(embeddings, start_panel, tile_mask, inv_width):
    n_blk, n_sub = lax.axis_size("blk"), lax.axis_size("sub")
    half, width = start_panel.shape
    tiles = half // TILE
    part = half // 2
    sub = lax.axis_index("sub")
    ring = lambda by: [(i, (i + by) % n_blk) for i in range(n_blk)]
    swap = [(0, 1), (1, 0)]
    blk_move = lambda v, by: lax.ppermute(v, "blk", ring(by))
    sub_move = lambda v: lax.ppermute(v, "sub", swap)

    below_e, below_p = blk_move(embeddings, 1), blk_move(start_panel, 1)
    above = [
        (blk_move(embeddings[i * part : (i + 1) * part], -2), blk_move(start_panel[i * part : (i + 1) * part], -2))
        for i in range(2)
    ]
    other_e, other_p = sub_move(embeddings), sub_move(start_panel)
    other_mask = sub_move(tile_mask)
    own_mask = jnp.concatenate([tile_mask, other_mask], axis=0).reshape(2, tiles, 2 * REACH + 1, 2, tiles)
    own_mask = jnp.where(sub == 0, own_mask, own_mask[:, :, :, ::-1]).astype(F32)
    own_mask = own_mask.reshape(2 * tiles, -1)
    below_mask, above_mask = blk_move(own_mask, 1), blk_move(own_mask, -2)
    split = lambda m: m.reshape(2, tiles, 2 * REACH + 1, 2, tiles)
    own_mask, below_mask, above_mask = split(own_mask), split(below_mask), split(above_mask)

    def pair_mask(rows, cols, offset, which):
        forward = rows[0, :, REACH + offset, which, :]
        backward = cols[which, :, REACH - offset, 0, :].T
        return jnp.repeat(jnp.concatenate([forward, backward], axis=0), TILE, axis=1)

    squares = lambda e: jnp.sum(jnp.square(e.astype(F32)), axis=1)[None, :]
    own = (embeddings, start_panel, squares(embeddings))
    other = (other_e, other_p, squares(other_e))
    own_image = vmem_call(
        self_body,
        shape(half, width),
        inv_width,
        *own,
        *other,
        pair_mask(own_mask, own_mask, 0, 0),
        pair_mask(own_mask, own_mask, 0, 1),
        smem=1,
    )
    below_other_e, below_other_p = sub_move(below_e), sub_move(below_p)
    below_image, t_own, t_other = vmem_call(
        below_body,
        (shape(half, width), shape(width, half), shape(width, half)),
        inv_width,
        below_e,
        below_p,
        *own,
        pair_mask(below_mask, own_mask, 1, 0),
        *other,
        pair_mask(below_mask, own_mask, 1, 1),
        smem=1,
    )
    below = (below_e, below_p, squares(below_e))
    below_other = (below_other_e, below_other_p, squares(below_other_e))
    others = [
        *own,
        pair_mask(above_mask, own_mask, -2, 0),
        *other,
        pair_mask(above_mask, own_mask, -2, 1),
        *below,
        pair_mask(above_mask, below_mask, -3, 0),
        *below_other,
        pair_mask(above_mask, below_mask, -3, 1),
    ]
    above_image0, *sums = vmem_call(
        functools.partial(above_body, 0, False),
        (shape(part, width),) + (shape(width, half),) * 4,
        inv_width,
        *above[0],
        *others,
        t_own,
        t_other,
        smem=1,
    )
    above_image1, own_image, below_image, cross = vmem_call(
        functools.partial(above_body, 1, True),
        (shape(part, width), shape(half, width), shape(half, width), shape(2 * half, width)),
        inv_width,
        *above[1],
        *others,
        *sums,
        own_image,
        below_image,
        smem=1,
    )
    cross = sub_move(cross)
    above_image0, above_image1 = blk_move(above_image0, 2), blk_move(above_image1, 2)
    below_image = blk_move(below_image + cross[:half], -1)
    image, gram = vmem_call(
        gram_body, (shape(half, width), shape(width, width)), own_image, cross, below_image, above_image0, above_image1
    )
    if n_blk & (n_blk - 1):
        gram = lax.psum(gram, ("blk", "sub"))
    else:
        gram = gram + sub_move(gram)
        hop = 1
        while hop < n_blk:
            gram = gram + lax.ppermute(gram, "blk", [(i, i ^ hop) for i in range(n_blk)])
            hop *= 2
    lower_factor = jnp.linalg.cholesky(gram)
    basis = lax.linalg.triangular_solve(lower_factor, image, left_side=False, lower=True, transpose_a=True)
    return (basis, lower_factor.T)


def solution(mesh):
    return jax.shard_map(
        per_device,
        mesh=mesh,
        in_specs=(
            P(("groups", "blk", "sub"), None),
            P(("groups", "blk", "sub"), None),
            P(("groups", "blk", "sub"), None),
            P(),
        ),
        out_specs=(P(("groups", "blk", "sub"), None), P("groups", None)),
        check_vma=False,
    )
```

time: 322 us -> 143 us (0.44)
  waiting for transfers between devices: 197 us -> 42.2 us
  matrix products: 33.4 us -> 1.07 us
  between operations: 18.2 us -> 1.58 us
  local copies, waits for them, and re-layouts: 14.8 us -> 27.9 us
  Pallas kernels: 0 us -> 12.8 us
  starting transfers between devices: 11.6 us -> 23.3 us
  other arithmetic: 38.8 us -> 33.6 us
  loops' own time: 4.67 us -> 0 us
    psum x1 -> x0, waiting for transfers between devices: 87.7 us -> none  [per_device(): lower_factor = jnp.linalg.cholesky(lax.psum(local_gram, ('blk', 'sub')))]
    ppermute x6 -> x21, waiting for transfers between devices: 99.9 us -> 42.2 us  [the longest x11 30.1 us: per_device(): blk_move = lambda v, by: lax.ppermute(v, 'blk', ring(by))]
    dot_general x8 -> x0, matrix products: 31.3 us -> none  [the longest x7 29.1 us: compute(): return jnp.dot(kernel, src_panel, preferred_element_type=jnp.float32)]
    pallas_call x0 -> x5, Pallas kernels: none -> 12.8 us  [vmem_call(): pl.pallas_call(body, out_shape=out_shapes, in_specs=[spec(pltpu.SMEM)] *...]
    ppermute x6 -> x21, starting transfers between devices: 11.3 us -> 23.3 us  [the longest x11 17.2 us: per_device(): blk_move = lambda v, by: lax.ppermute(v, 'blk', ring(by))]
    mul x7 -> x0, local copies, waits for them, and re-layouts: 11.8 us -> none  [compute(): kernel = kernel * window.astype(jnp.float32)[:, None, :, None]]
    reduce_scatter x1 -> x0, waiting for transfers between devices: 8.93 us -> none  [per_device(): lax.psum_scatter(accum_rows, 'sub', scatter_dimension=0, tiled=True)]
    reduce_sum x8 -> x4, other arithmetic: 11.5 us -> 2.91 us  [per_device(): squares = lambda e: jnp.sum(jnp.square(e.astype(F32)), axis=1)[None, :]]
  transfers between devices with their start and end apart: 9 -> 21, of which waited for: 5 -> 9; matrix products, arithmetic and copies ran while one was open for 14% -> 26% of each run, Pallas kernels for 0% -> 6%
where the time goes in v1:
time: 143 us
  waiting for transfers between devices  42.2 us (30%)
  other arithmetic  33.6 us (23%)
  local copies, waits for them, and re-layouts  27.9 us (20%)
  starting transfers between devices  23.3 us (16%)
  Pallas kernels  12.8 us (9%)
  between operations  1.58 us (1%)
    ppermute x11, waiting for transfers between devices, per_device(): blk_move = lambda v, by: lax.ppermute(v, 'blk', ring(by))  30.1 us
    ppermute x11, starting transfers between devices, per_device(): blk_move = lambda v, by: lax.ppermute(v, 'blk', ring(by))  17.2 us
    pallas_call x5, Pallas kernels, vmem_call(): pl.pallas_call(body, out_shape=out_shapes, in_specs=[spec(pltpu.SMEM)] *...  12.8 us
    another operation x3, other arithmetic, per_device(): lower_factor = jnp.linalg.cholesky(gram)  12.4 us
    another operation x1, other arithmetic, per_device(): lax.linalg.triangular_solve(lower_factor, image, left_side=False, lower=T...  9.81 us
    ppermute x3, waiting for transfers between devices, per_device(): lax.ppermute(gram, 'blk', [(i, i ^ hop) for i in range(n_blk)])  8.97 us
    concatenate x8, local copies, waits for them, and re-layouts, pair_mask(): jnp.concatenate([forward, backward], axis=0)  8.19 us
    concatenate x8, other arithmetic, pair_mask(): jnp.concatenate([forward, backward], axis=0)  7.67 us
  transfers between devices with their start and end apart: 21, of which 9 were waited for; matrix products, arithmetic and copies ran while one was open for 26% of the time, Pallas kernels for 6%

profile of v1, /device:TPU:0, one launch (start us, length us, event | category | flops | bytes accessed | tf_op | source)
XLA Modules:
  0.0 142.5 jit_solution(16773867073059658589)
XLA Ops:
  0.6 3.0 %collective-permute-start.7 = (bf16[512,128]{1,0:T(8,128)(2,1)}, bf16[512,128]{1,0:T(8,128)(2,1)S(1)}, u32[]{:S(2)}, u32[]{:S(2)}) collective-permute-start(bf16[512,128]{1,0:T(8,128)(2,1)} %refs_1_.3), channel_id=1, source_target_pairs={{0,2},{2,4},{4,6},{6,8},{8,10},{10,12},{12,14},{14,0},{1,3},{3,5},... | collective-permute-start | bytes 393224 | tf_op jit(solution)/shard_map/ppermute | solution.py:153
  4.1 1.5 %collective-permute-start.6 = (bf16[512,1024]{1,0:T(8,128)(2,1)}, bf16[512,1024]{1,0:T(8,128)(2,1)S(1)}, u32[]{:S(2)}, u32[]{:S(2)}) collective-permute-start(bf16[512,1024]{1,0:T(8,128)(2,1)} %refs_0_.3), channel_id=1, source_target_pairs={{0,2},{2,4},{4,6},{6,8},{8,10},{10,12},{12,14},{14,0},{1,3},{3,5},... | collective-permute-start | bytes 3145736 | tf_op jit(solution)/shard_map/ppermute | solution.py:153
  5.7 1.5 %fusion.5 = (bf16[256,128]{1,0:T(8,128)(2,1)}, bf16[256,128]{1,0:T(8,128)(2,1)}) fusion(bf16[512,128]{1,0:T(8,128)(2,1)} %refs_1_.3), kind=kLoop, calls=%fused_computation.35 | loop fusion | bytes 262144 | tf_op jit(solution)/shard_map/slice | solution.py:158
  7.2 2.3 %fusion.4 = (bf16[256,1024]{1,0:T(8,128)(2,1)}, bf16[256,1024]{1,0:T(8,128)(2,1)}) fusion(bf16[512,1024]{1,0:T(8,128)(2,1)} %refs_0_.3), kind=kLoop, calls=%fused_computation.34 | loop fusion | bytes 2097152 | tf_op jit(solution)/shard_map/slice | solution.py:158
  12.1 1.5 %collective-permute-start.8 = (f32[8,56]{1,0:T(8,128)}, f32[8,56]{1,0:T(8,128)}, u32[]{:S(2)}, u32[]{:S(2)}) collective-permute-start(f32[8,56]{1,0:T(8,128)} %reshape.50), channel_id=1, source_target_pairs={{0,2},{2,4},{4,6},{6,8},{8,10},{10,12},{12,14},{14,0},{1,3},{3,5},... | collective-permute-start | bytes 5384 | tf_op jit(solution)/shard_map/ppermute | solution.py:153
  13.7 2.2 %collective-permute-start.3 = (f32[8,56]{1,0:T(8,128)}, f32[8,56]{1,0:T(8,128)}, u32[]{:S(2)}, u32[]{:S(2)}) collective-permute-start(f32[8,56]{1,0:T(8,128)} %reshape.50), channel_id=1, source_target_pairs={{0,12},{2,14},{4,0},{6,2},{8,4},{10,6},{12,8},{14,10},{1,13},{3,15... | collective-permute-start | bytes 5384 | tf_op jit(solution)/shard_map/ppermute | solution.py:153
  19.6 1.4 reshape.51
  21.0 12.1 %collective-permute-done.8 = f32[8,56]{1,0:T(8,128)} collective-permute-done((f32[8,56]{1,0:T(8,128)}, f32[8,56]{1,0:T(8,128)}, u32[]{:S(2)}, u32[]{:S(2)}) %collective-permute-start.8) | collective-permute-done | bytes 1824 | tf_op jit(solution)/shard_map/ppermute | solution.py:153
  33.1 1.7 %collective-permute-start.11 = (bf16[256,1024]{1,0:T(8,128)(2,1)}, bf16[256,1024]{1,0:T(8,128)(2,1)}, u32[]{:S(2)}, u32[]{:S(2)}) collective-permute-start(bf16[256,1024]{1,0:T(8,128)(2,1)} %get-tuple-element.34), channel_id=1, source_target_pairs={{0,12},{2,14},{4,0},{6,2},{8,4},{10,6},{12,8},{14,10},{1,13},{3,15... | collective-permute-start | bytes 1572872 | tf_op jit(solution)/shard_map/ppermute | solution.py:153
  34.8 1.4 reshape.54
  36.2 1.4 fusion.8
  40.1 1.4 fusion.7
  42.7 1.4 copy.34
  50.6 1.3 copy.29
  60.9 2.0 %shard_map.61.refs_20_ = f32[512,128]{1,0:T(8,128)S(1)} custom-call(f32[1]{0:T(128)S(6)} %copy.48.inverse_ref, bf16[512,1024]{1,0:T(8,128)(2,1)S(1)} %copy-done, bf16[512,128]{1,0:T(8,128)(2,1)S(1)} %copy-done.2, f32[1,512]{1,0:T(1,128)S(1)} %bitcast.55, bf16[512,1024]{1,0:T(8,128)(2,1)S(1)} %collective-permute-done.4.e1.refs_4_, ...), custom_call_target="tpu_custom_call" | custom-call | tf_op jit(solution)/shard_map/pallas_call | solution.py:19
  62.9 2.4 %collective-permute-start.1 = (bf16[256,128]{1,0:T(8,128)(2,1)S(1)}, bf16[256,128]{1,0:T(8,128)(2,1)S(1)}, u32[]{:S(2)}, u32[]{:S(2)}) collective-permute-start(bf16[256,128]{1,0:T(8,128)(2,1)S(1)} %copy-done.5), channel_id=1, source_target_pairs={{0,12},{2,14},{4,0},{6,2},{8,4},{10,6},{12,8},{14,10},{1,13},{3,15... | collective-permute-start | bytes 196616 | tf_op jit(solution)/shard_map/ppermute | solution.py:153
  65.3 2.3 %shard_map.59 = (f32[512,128]{1,0:T(8,128)S(1)}, f32[128,512]{1,0:T(8,128)S(1)}, f32[128,512]{1,0:T(8,128)S(1)}) custom-call(f32[1]{0:T(128)S(6)} %copy.48.inverse_ref, bf16[512,1024]{1,0:T(8,128)(2,1)S(1)} %collective-permute-done.6.x.refs_8_, bf16[512,128]{1,0:T(8,128)(2,1)S(1)} %collective-permute-done.7.xp.refs_9_, bf16[512,1024]{1,0:T(8,128)(2,1)S(1)} %copy-done, ...), custom_call_target="tpu_custom_call" | custom-call | tf_op jit(solution)/shard_map/pallas_call | solution.py:19
  68.0 1.5 %multiply_reduce_fusion = f32[512]{0:T(512)S(1)} fusion(bf16[512,1024]{1,0:T(8,128)(2,1)} %collective-permute-done.9.refs_12_), kind=kLoop, calls=%fused_computation | loop fusion | flops 1572352 | bytes 1050624 | tf_op jit(solution)/shard_map/reduce_sum | solution.py:175
  69.5 6.5 %collective-permute-done.12.xp = bf16[256,128]{1,0:T(8,128)(2,1)S(1)} collective-permute-done((bf16[256,128]{1,0:T(8,128)(2,1)S(1)}, bf16[256,128]{1,0:T(8,128)(2,1)S(1)}, u32[]{:S(2)}, u32[]{:S(2)}) %collective-permute-start.12) | collective-permute-done | bytes 65568 | tf_op jit(solution)/shard_map/ppermute | solution.py:153
  76.0 3.9 %shard_map.60 = (f32[256,128]{1,0:T(8,128)S(1)}, f32[128,512]{1,0:T(8,128)S(1)}, f32[128,512]{1,0:T(8,128)S(1)}, f32[128,512]{1,0:T(8,128)S(1)}, f32[128,512]{1,0:T(8,128)S(1)}) custom-call(f32[1]{0:T(128)S(6)} %copy.48.inverse_ref, bf16[256,1024]{1,0:T(8,128)(2,1)} %collective-permute-done.11.x, bf16[256,128]{1,0:T(8,128)(2,1)S(1)} %collective-permute-done.12.xp, ...), custom_call_target="tpu_custom_call" | custom-call | tf_op jit(solution)/shard_map/pallas_call | solution.py:19
  79.9 4.2 %shard_map.62 = (f32[256,128]{1,0:T(8,128)S(1)}, f32[512,128]{1,0:T(8,128)S(1)}, f32[512,128]{1,0:T(8,128)S(1)}, f32[1024,128]{1,0:T(8,128)S(1)}) custom-call(f32[1]{0:T(128)S(6)} %copy.48.inverse_ref, bf16[256,1024]{1,0:T(8,128)(2,1)S(1)} %collective-permute-done.x, bf16[256,128]{1,0:T(8,128)(2,1)S(1)} %collective-permute-done.1.xp, ...), custom_call_target="tpu_custom_call" | custom-call | tf_op jit(solution)/shard_map/pallas_call | solution.py:19
  84.2 1.9 %collective-permute-done.13.cross = f32[1024,128]{1,0:T(8,128)S(1)} collective-permute-done((f32[1024,128]{1,0:T(8,128)S(1)}, f32[1024,128]{1,0:T(8,128)S(1)}, u32[]{:S(2)}, u32[]{:S(2)}) %collective-permute-start.13) | collective-permute-done | bytes 524320 | tf_op jit(solution)/shard_map/ppermute | solution.py:154
  86.1 3.8 %collective-permute-start.14 = (f32[512,128]{1,0:T(8,128)S(1)}, f32[512,128]{1,0:T(8,128)S(1)}, u32[]{:S(2)}, u32[]{:S(2)}) collective-permute-start(f32[512,128]{1,0:T(8,128)S(1)} %slice_add_fusion), channel_id=1, source_target_pairs={{0,14},{2,0},{4,2},{6,4},{8,6},{10,8},{12,10},{14,12},{1,15},{3,1}... | collective-permute-start | bytes 786440 | tf_op jit(solution)/shard_map/ppermute | solution.py:153
  89.9 9.6 %collective-permute-done.16.above1 = f32[256,128]{1,0:T(8,128)S(1)} collective-permute-done((f32[256,128]{1,0:T(8,128)S(1)}, f32[256,128]{1,0:T(8,128)S(1)}, u32[]{:S(2)}, u32[]{:S(2)}) %collective-permute-start.16) | collective-permute-done | bytes 131104 | tf_op jit(solution)/shard_map/ppermute | solution.py:153
  99.5 2.0 %collective-permute-done.15.above0 = f32[256,128]{1,0:T(8,128)S(1)} collective-permute-done((f32[256,128]{1,0:T(8,128)S(1)}, f32[256,128]{1,0:T(8,128)S(1)}, u32[]{:S(2)}, u32[]{:S(2)}) %collective-permute-start.15) | collective-permute-done | bytes 131104 | tf_op jit(solution)/shard_map/ppermute | solution.py:153
  103.4 1.6 %collective-permute-start.18 = (f32[128,128]{0,1:T(8,128)S(1)}, f32[128,128]{0,1:T(8,128)S(1)}, u32[]{:S(2)}, u32[]{:S(2)}) collective-permute-start(f32[128,128]{0,1:T(8,128)S(1)} %add.27), channel_id=1, source_target_pairs={{0,2},{2,0},{4,6},{6,4},{8,10},{10,8},{12,14},{14,12},{1,3},{3,1},... | collective-permute-start | bytes 196616 | tf_op jit(solution)/shard_map/ppermute | solution.py:246
  105.0 2.7 %collective-permute-done.18 = f32[128,128]{0,1:T(8,128)S(1)} collective-permute-done((f32[128,128]{0,1:T(8,128)S(1)}, f32[128,128]{0,1:T(8,128)S(1)}, u32[]{:S(2)}, u32[]{:S(2)}) %collective-permute-start.18) | collective-permute-done | bytes 65568 | tf_op jit(solution)/shard_map/ppermute | solution.py:246
  107.7 2.5 %collective-permute-start.19 = (f32[128,128]{0,1:T(8,128)S(1)}, f32[128,128]{0,1:T(8,128)S(1)}, u32[]{:S(2)}, u32[]{:S(2)}) collective-permute-start(f32[128,128]{0,1:T(8,128)S(1)} %add.28), channel_id=1, source_target_pairs={{0,4},{2,6},{4,0},{6,2},{8,12},{10,14},{12,8},{14,10},{1,5},{3,7},... | collective-permute-start | bytes 196616 | tf_op jit(solution)/shard_map/ppermute | solution.py:246
  110.3 2.2 %collective-permute-done.19 = f32[128,128]{0,1:T(8,128)S(1)} collective-permute-done((f32[128,128]{0,1:T(8,128)S(1)}, f32[128,128]{0,1:T(8,128)S(1)}, u32[]{:S(2)}, u32[]{:S(2)}) %collective-permute-start.19) | collective-permute-done | bytes 65568 | tf_op jit(solution)/shard_map/ppermute | solution.py:246
  113.7 4.0 %collective-permute-done.20 = f32[128,128]{0,1:T(8,128)S(1)} collective-permute-done((f32[128,128]{0,1:T(8,128)S(1)}, f32[128,128]{0,1:T(8,128)S(1)}, u32[]{:S(2)}, u32[]{:S(2)}) %collective-permute-start.20) | collective-permute-done | bytes 65568 | tf_op jit(solution)/shard_map/ppermute | solution.py:246
  117.9 11.7 %cholesky.16 = f32[128,128]{1,0:T(8,128)S(1)} custom-call(f32[128,128]{1,0:T(8,128)S(1)} %fusion.2), custom_call_target="Cholesky" | custom-call | tf_op jit(solution)/shard_map/jit(cholesky)/cholesky | solution.py:248
  131.7 9.8 %custom-call.6 = f32[1,128,128]{1,2,0:T(8,128)S(1)} custom-call(f32[1,128,128]{2,1,0:T(8,128)S(1)} %get-tuple-element.39), custom_call_target="InvertDiagBlocksLowerTriangular" | custom-call | tf_op jit(solution)/shard_map/triangular_solve | solution.py:249
  (90 shorter events, 32.0 us)
Async XLA Ops:
  0.6 62.2 %collective-permute-start.7 = (bf16[512,128]{1,0:T(8,128)(2,1)}, bf16[512,128]{1,0:T(8,128)(2,1)S(1)}, u32[]{:S(2)}, u32[]{:S(2)}) collective-permute-start(bf16[512,128]{1,0:T(8,128)(2,1)} %refs_1_.3), channel_id=1, source_target_pairs={{0,2},{2,4},{4,6},{6,8},{8,10},{10,12},{12,14},{14,0},{1,3},{3,5},... | collective-permute-start | bytes 393224 | tf_op jit(solution)/shard_map/ppermute | solution.py:153
  3.6 56.8 %collective-permute-start.5 = (bf16[512,128]{1,0:T(8,128)(2,1)}, bf16[512,128]{1,0:T(8,128)(2,1)S(1)}, u32[]{:S(2)}, u32[]{:S(2)}) collective-permute-start(bf16[512,128]{1,0:T(8,128)(2,1)} %refs_1_.3), channel_id=1, source_target_pairs={{0,1},{1,0},{2,3},{3,2},{4,5},{5,4},{6,7},{7,6},{8,9},{9,8},{10,11... | collective-permute-start | bytes 393224 | tf_op jit(solution)/shard_map/ppermute | solution.py:154
  3.6 7.5 %collective-permute-start.2 = (s32[4,56]{1,0:T(4,128)}, s32[4,56]{1,0:T(4,128)S(1)}, u32[]{:S(2)}, u32[]{:S(2)}) collective-permute-start(s32[4,56]{1,0:T(4,128)} %param.6), channel_id=1, source_target_pairs={{0,1},{1,0},{2,3},{3,2},{4,5},{5,4},{6,7},{7,6},{8,9},{9,8},{10,11... | collective-permute-start | bytes 2696 | tf_op jit(solution)/shard_map/ppermute | solution.py:154
  4.1 43.9 %collective-permute-start.6 = (bf16[512,1024]{1,0:T(8,128)(2,1)}, bf16[512,1024]{1,0:T(8,128)(2,1)S(1)}, u32[]{:S(2)}, u32[]{:S(2)}) collective-permute-start(bf16[512,1024]{1,0:T(8,128)(2,1)} %refs_0_.3), channel_id=1, source_target_pairs={{0,2},{2,4},{4,6},{6,8},{8,10},{10,12},{12,14},{14,0},{1,3},{3,5},... | collective-permute-start | bytes 3145736 | tf_op jit(solution)/shard_map/ppermute | solution.py:153
  7.2 2.3 %copy-start = (bf16[512,1024]{1,0:T(8,128)(2,1)S(1)}, bf16[512,1024]{1,0:T(8,128)(2,1)}, u32[]{:S(2)}) copy-start(bf16[512,1024]{1,0:T(8,128)(2,1)} %refs_0_.3) | copy-start | bytes 3145732
  9.5 1.6 %copy-start.7 = (s32[4,56]{1,0:T(4,128)S(1)}, s32[4,56]{1,0:T(4,128)}, u32[]{:S(2)}) copy-start(s32[4,56]{1,0:T(4,128)} %param.6) | copy-start | bytes 2692
  10.4 50.5 %copy-start.2 = (bf16[512,128]{1,0:T(8,128)(2,1)S(1)}, bf16[512,128]{1,0:T(8,128)(2,1)}, u32[]{:S(2)}) copy-start(bf16[512,128]{1,0:T(8,128)(2,1)} %refs_1_.3) | copy-start | bytes 393220
  12.1 21.0 %collective-permute-start.8 = (f32[8,56]{1,0:T(8,128)}, f32[8,56]{1,0:T(8,128)}, u32[]{:S(2)}, u32[]{:S(2)}) collective-permute-start(f32[8,56]{1,0:T(8,128)} %reshape.50), channel_id=1, source_target_pairs={{0,2},{2,4},{4,6},{6,8},{8,10},{10,12},{12,14},{14,0},{1,3},{3,5},... | collective-permute-start | bytes 5384 | tf_op jit(solution)/shard_map/ppermute | solution.py:153
  13.7 6.0 %collective-permute-start.3 = (f32[8,56]{1,0:T(8,128)}, f32[8,56]{1,0:T(8,128)}, u32[]{:S(2)}, u32[]{:S(2)}) collective-permute-start(f32[8,56]{1,0:T(8,128)} %reshape.50), channel_id=1, source_target_pairs={{0,12},{2,14},{4,0},{6,2},{8,4},{10,6},{12,8},{14,10},{1,13},{3,15... | collective-permute-start | bytes 5384 | tf_op jit(solution)/shard_map/ppermute | solution.py:153
  19.6 40.0 %collective-permute-start.4 = (bf16[512,1024]{1,0:T(8,128)(2,1)S(1)}, bf16[512,1024]{1,0:T(8,128)(2,1)S(1)}, u32[]{:S(2)}, u32[]{:S(2)}) collective-permute-start(bf16[512,1024]{1,0:T(8,128)(2,1)S(1)} %copy-done), channel_id=1, source_target_pairs={{0,1},{1,0},{2,3},{3,2},{4,5},{5,4},{6,7},{7,6},{8,9},{9,8},{10,11... | collective-permute-start | bytes 3145736 | tf_op jit(solution)/shard_map/ppermute | solution.py:154
  33.1 42.9 %collective-permute-start.11 = (bf16[256,1024]{1,0:T(8,128)(2,1)}, bf16[256,1024]{1,0:T(8,128)(2,1)}, u32[]{:S(2)}, u32[]{:S(2)}) collective-permute-start(bf16[256,1024]{1,0:T(8,128)(2,1)} %get-tuple-element.34), channel_id=1, source_target_pairs={{0,12},{2,14},{4,0},{6,2},{8,4},{10,6},{12,8},{14,10},{1,13},{3,15... | collective-permute-start | bytes 1572872 | tf_op jit(solution)/shard_map/ppermute | solution.py:153
  48.0 28.0 %copy-start.1 = (bf16[512,1024]{1,0:T(8,128)(2,1)}, bf16[512,1024]{1,0:T(8,128)(2,1)S(1)}, u32[]{:S(2)}) copy-start(bf16[512,1024]{1,0:T(8,128)(2,1)S(1)} %collective-permute-done.6.x.refs_8_) | copy-start | bytes 3145732
  48.0 20.0 %collective-permute-start.9 = (bf16[512,1024]{1,0:T(8,128)(2,1)S(1)}, bf16[512,1024]{1,0:T(8,128)(2,1)}, u32[]{:S(2)}, u32[]{:S(2)}) collective-permute-start(bf16[512,1024]{1,0:T(8,128)(2,1)S(1)} %collective-permute-done.6.x.refs_8_), channel_id=1, source_target_pairs={{0,1},{1,0},{2,3},{3,2},{4,5},{5,4},{6,7},{7,6},{8,9},{9,8},{10,11... | collective-permute-start | bytes 3145736 | tf_op jit(solution)/shard_map/ppermute | solution.py:154
  57.3 3.1 %copy-start.6 = (bf16[256,128]{1,0:T(8,128)(2,1)S(1)}, bf16[256,128]{1,0:T(8,128)(2,1)}, u32[]{:S(2)}) copy-start(bf16[256,128]{1,0:T(8,128)(2,1)} %get-tuple-element.36) | copy-start | bytes 196612
  57.3 3.5 %copy-start.3 = (f32[8,512]{1,0:T(8,128)S(1)}, f32[8,512]{1,0:T(8,128)}, u32[]{:S(2)}) copy-start(f32[8,512]{1,0:T(8,128)} %get-tuple-element.62.m0) | copy-start | bytes 49156
  57.3 3.5 %copy-start.4 = (f32[512]{0:T(512)S(1)}, f32[512]{0:T(512)}, u32[]{:S(2)}) copy-start(f32[512]{0:T(512)} %multiply_reduce_fusion.3) | copy-start | bytes 6148
  59.6 20.3 %collective-permute-start = (bf16[256,1024]{1,0:T(8,128)(2,1)}, bf16[256,1024]{1,0:T(8,128)(2,1)S(1)}, u32[]{:S(2)}, u32[]{:S(2)}) collective-permute-start(bf16[256,1024]{1,0:T(8,128)(2,1)} %get-tuple-element.35), channel_id=1, source_target_pairs={{0,12},{2,14},{4,0},{6,2},{8,4},{10,6},{12,8},{14,10},{1,13},{3,15... | collective-permute-start | bytes 1572872 | tf_op jit(solution)/shard_map/ppermute | solution.py:153
  60.4 15.6 %collective-permute-start.12 = (bf16[256,128]{1,0:T(8,128)(2,1)S(1)}, bf16[256,128]{1,0:T(8,128)(2,1)S(1)}, u32[]{:S(2)}, u32[]{:S(2)}) collective-permute-start(bf16[256,128]{1,0:T(8,128)(2,1)S(1)} %copy-done.6), channel_id=1, source_target_pairs={{0,12},{2,14},{4,0},{6,2},{8,4},{10,6},{12,8},{14,10},{1,13},{3,15... | collective-permute-start | bytes 196616 | tf_op jit(solution)/shard_map/ppermute | solution.py:153
  60.9 2.0 %copy-start.5 = (bf16[256,128]{1,0:T(8,128)(2,1)S(1)}, bf16[256,128]{1,0:T(8,128)(2,1)}, u32[]{:S(2)}) copy-start(bf16[256,128]{1,0:T(8,128)(2,1)} %get-tuple-element.37) | copy-start | bytes 196612
  62.9 17.0 %collective-permute-start.1 = (bf16[256,128]{1,0:T(8,128)(2,1)S(1)}, bf16[256,128]{1,0:T(8,128)(2,1)S(1)}, u32[]{:S(2)}, u32[]{:S(2)}) collective-permute-start(bf16[256,128]{1,0:T(8,128)(2,1)S(1)} %copy-done.5), channel_id=1, source_target_pairs={{0,12},{2,14},{4,0},{6,2},{8,4},{10,6},{12,8},{14,10},{1,13},{3,15... | collective-permute-start | bytes 196616 | tf_op jit(solution)/shard_map/ppermute | solution.py:153
  68.0 8.0 %collective-permute-start.10 = (bf16[512,128]{1,0:T(8,128)(2,1)S(1)}, bf16[512,128]{1,0:T(8,128)(2,1)S(1)}, u32[]{:S(2)}, u32[]{:S(2)}) collective-permute-start(bf16[512,128]{1,0:T(8,128)(2,1)S(1)} %collective-permute-done.7.xp.refs_9_), channel_id=1, source_target_pairs={{0,1},{1,0},{2,3},{3,2},{4,5},{5,4},{6,7},{7,6},{8,9},{9,8},{10,11... | collective-permute-start | bytes 393224 | tf_op jit(solution)/shard_map/ppermute | solution.py:154
  84.1 2.0 %collective-permute-start.13 = (f32[1024,128]{1,0:T(8,128)S(1)}, f32[1024,128]{1,0:T(8,128)S(1)}, u32[]{:S(2)}, u32[]{:S(2)}) collective-permute-start(f32[1024,128]{1,0:T(8,128)S(1)} %get-tuple-element.24), channel_id=1, source_target_pairs={{0,1},{1,0},{2,3},{3,2},{4,5},{5,4},{6,7},{7,6},{8,9},{9,8},{10,11... | collective-permute-start | bytes 1572872 | tf_op jit(solution)/shard_map/ppermute | solution.py:154
  86.1 15.4 %collective-permute-start.14 = (f32[512,128]{1,0:T(8,128)S(1)}, f32[512,128]{1,0:T(8,128)S(1)}, u32[]{:S(2)}, u32[]{:S(2)}) collective-permute-start(f32[512,128]{1,0:T(8,128)S(1)} %slice_add_fusion), channel_id=1, source_target_pairs={{0,14},{2,0},{4,2},{6,4},{8,6},{10,8},{12,10},{14,12},{1,15},{3,1}... | collective-permute-start | bytes 786440 | tf_op jit(solution)/shard_map/ppermute | solution.py:153
  89.9 9.6 %collective-permute-start.16 = (f32[256,128]{1,0:T(8,128)S(1)}, f32[256,128]{1,0:T(8,128)S(1)}, u32[]{:S(2)}, u32[]{:S(2)}) collective-permute-start(f32[256,128]{1,0:T(8,128)S(1)} %get-tuple-element.27), channel_id=1, source_target_pairs={{0,4},{2,6},{4,8},{6,10},{8,12},{10,14},{12,0},{14,2},{1,5},{3,7},... | collective-permute-start | bytes 393224 | tf_op jit(solution)/shard_map/ppermute | solution.py:153
  89.9 11.6 %collective-permute-start.15 = (f32[256,128]{1,0:T(8,128)S(1)}, f32[256,128]{1,0:T(8,128)S(1)}, u32[]{:S(2)}, u32[]{:S(2)}) collective-permute-start(f32[256,128]{1,0:T(8,128)S(1)} %get-tuple-element.26), channel_id=1, source_target_pairs={{0,4},{2,6},{4,8},{6,10},{8,12},{10,14},{12,0},{14,2},{1,5},{3,7},... | collective-permute-start | bytes 393224 | tf_op jit(solution)/shard_map/ppermute | solution.py:153
  102.0 1.3 collective-permute-start.17
  103.4 4.3 %collective-permute-start.18 = (f32[128,128]{0,1:T(8,128)S(1)}, f32[128,128]{0,1:T(8,128)S(1)}, u32[]{:S(2)}, u32[]{:S(2)}) collective-permute-start(f32[128,128]{0,1:T(8,128)S(1)} %add.27), channel_id=1, source_target_pairs={{0,2},{2,0},{4,6},{6,4},{8,10},{10,8},{12,14},{14,12},{1,3},{3,1},... | collective-permute-start | bytes 196616 | tf_op jit(solution)/shard_map/ppermute | solution.py:246
  107.7 4.8 %collective-permute-start.19 = (f32[128,128]{0,1:T(8,128)S(1)}, f32[128,128]{0,1:T(8,128)S(1)}, u32[]{:S(2)}, u32[]{:S(2)}) collective-permute-start(f32[128,128]{0,1:T(8,128)S(1)} %add.28), channel_id=1, source_target_pairs={{0,4},{2,6},{4,0},{6,2},{8,12},{10,14},{12,8},{14,10},{1,5},{3,7},... | collective-permute-start | bytes 196616 | tf_op jit(solution)/shard_map/ppermute | solution.py:246
  112.5 5.2 %collective-permute-start.20 = (f32[128,128]{0,1:T(8,128)S(1)}, f32[128,128]{0,1:T(8,128)S(1)}, u32[]{:S(2)}, u32[]{:S(2)}) collective-permute-start(f32[128,128]{0,1:T(8,128)S(1)} %add.29), channel_id=1, source_target_pairs={{0,8},{2,10},{4,12},{6,14},{8,0},{10,2},{12,4},{14,6},{1,9},{3,11}... | collective-permute-start | bytes 196616 | tf_op jit(solution)/shard_map/ppermute | solution.py:246

commit v2 on v0

v2 whole, which is shorter than its diff:
```python
import functools

import jax
import jax.numpy as jnp
from jax import lax
from jax.experimental import pallas as pl
from jax.experimental.pallas import tpu as pltpu
from jax.sharding import PartitionSpec as P

TILE = 128
REACH = 3
F32 = jnp.float32
BF16 = jnp.bfloat16
HIGHEST = lax.Precision.HIGHEST


def vmem_call(body, out_shapes, *operands, scalars=0):
    in_vmem = pl.BlockSpec(memory_space=pltpu.VMEM)
    in_smem = pl.BlockSpec(memory_space=pltpu.SMEM)
    return pl.pallas_call(
        body,
        out_shape=out_shapes,
        in_specs=[in_smem] * scalars + [in_vmem] * (len(operands) - scalars),
        out_specs=jax.tree.map(lambda _: in_vmem, out_shapes),
        compiler_params=pltpu.CompilerParams(vmem_limit_bytes=48 << 20),
    )(*operands)


def shape(*dims):
    return jax.ShapeDtypeStruct(dims, F32)


def contract(a, b, dims, precision=None):
    return lax.dot_general(a, b, (dims, ((), ())), precision=precision, preferred_element_type=F32)


PAIRS = (
    (0, 0, 0, 0),
    (0, 0, 0, 1),
    (1, 0, 1, 0),
    (1, 0, 1, 1),
    (2, 0, -2, 0),
    (2, 0, -2, 1),
    (2, 1, -3, 0),
    (2, 1, -3, 1),
)
SELF, BELOW, ABOVE_OWN, ABOVE_BELOW = 0, 2, 4, 6


def mask_body(sub_ref, own, below, above, out):
    sub = sub_ref[0]
    blocks = [own[...], below[...], above[...]]
    both, window = blocks[0].shape
    tiles = both // 2
    lanes = tiles * TILE
    window_at = lax.broadcasted_iota(jnp.int32, (window, lanes), 0)
    tile_of = lax.broadcasted_iota(jnp.int32, (window, lanes), 1) // TILE
    spread = (lax.broadcasted_iota(jnp.int32, (tiles, lanes), 0) == tile_of[:tiles]).astype(F32)
    row_at = lax.broadcasted_iota(jnp.int32, (tiles, window), 0)
    column_at = lax.broadcasted_iota(jnp.int32, (tiles, window), 1)
    for k, (rows, cols, offset, which) in enumerate(PAIRS):
        actual = sub if which == 0 else 1 - sub
        chosen = (window_at == (REACH + offset) * both + actual * tiles + tile_of).astype(F32)
        out[k, :tiles] = contract(blocks[rows][:tiles], chosen, ((1,), (0,)))
        own_columns = (column_at == (REACH - offset) * both + sub * tiles + row_at).astype(F32)
        back = contract(own_columns, blocks[cols][which * tiles : (which + 1) * tiles], ((1,), (1,)))
        out[k, tiles:] = contract(back, spread, ((1,), (0,)))


def squares(piece, features):
    wide = piece[:, :features].astype(F32)
    return jnp.sum(wide * wide, axis=1, keepdims=True)


def as_row(column):
    return jnp.broadcast_to(column, (column.shape[0], TILE)).T[:1]


def products(inverse, piece, tile, columns, back):
    size, width = piece.shape
    features = width - TILE
    row_sq = squares(piece, features)
    doubled = piece[:, :features] * 2
    panel_t = piece[:, features:].astype(F32).T.astype(BF16)
    image = None
    for k, (other, col_sq, mask_ref, lane) in enumerate(columns):
        count = other.shape[0]
        mask = mask_ref[:, lane : lane + count]
        tiles = mask.shape[0] // 2
        gram2 = contract(doubled, other[:, :features], ((1,), (1,)))
        kernel = jnp.exp(-inverse * jnp.maximum(row_sq + col_sq - gram2, 0.0))

        def masked(first):
            return jnp.concatenate(
                [kernel[i * TILE : (i + 1) * TILE] * mask[first + i : first + i + 1] for i in range(size // TILE)], axis=0
            ).astype(BF16)

        term = contract(masked(tile), other[:, features:], ((1,), (0,)))
        image = term if image is None else image + term
        if back is not None:
            term = contract(panel_t, masked(tiles + tile), ((1,), (0,)))
            back[k] = term if back[k] is None else back[k] + term
    return image


def with_masks(pieces, sq_rows, masks, first):
    per_half = len(pieces) // 2
    return [
        (p[...], sq, masks.at[first + k // per_half], (k % per_half) * p.shape[0])
        for k, (p, sq) in enumerate(zip(pieces, sq_rows))
    ]


def self_body(inverse, masks, o0, o1, x0, x1, image, sq):
    pieces = (o0, o1, x0, x1)
    size, width = o0.shape
    rows = [as_row(squares(p[...], width - TILE)) for p in pieces]
    for k, row in enumerate(rows):
        sq[k : k + 1] = row
    columns = with_masks(pieces, rows, masks, SELF)
    for k, piece in enumerate((o0, o1)):
        image[k * size : (k + 1) * size] = products(inverse[0], piece[...], k * size // TILE, columns, None)


def below_body(part, inverse, masks, sq, x, o0, o1, x0, x1, *refs):
    pieces = (o0, o1, x0, x1)
    back = [r[...] for r in refs[: len(refs) - 5]] or [None] * 4
    outs = refs[-5:]
    columns = with_masks(pieces, [sq[k : k + 1] for k in range(4)], masks, BELOW)
    outs[0][...] = products(inverse[0], x[...], part * x.shape[0] // TILE, columns, back)
    for out, value in zip(outs[1:], back):
        out[...] = value


def above_first_body(inverse, masks, sq, x, o0, o1, x0, x1, b0, b1, y0, y1, t0, t1, t2, t3, image, below_sq, *outs):
    size, width = x.shape
    below = (b0, b1, y0, y1)
    rows = [as_row(squares(p[...], width - TILE)) for p in below]
    for k, row in enumerate(rows):
        below_sq[k : k + 1] = row
    columns = with_masks((o0, o1, x0, x1), [sq[k : k + 1] for k in range(4)], masks, ABOVE_OWN)
    columns += with_masks(below, rows, masks, ABOVE_BELOW)
    back = [t0[...], t1[...], t2[...], t3[...]] + [None] * 4
    image[...] = products(inverse[0], x[...], 0, columns, back)
    for out, value in zip(outs, back):
        out[...] = value


def above_below_body(inverse, masks, below_sq, x, b0, b1, y0, y1, t0, t1, t2, t3, i0, i1, image, own, cross):
    size = x.shape[0]
    columns = with_masks((b0, b1, y0, y1), [below_sq[k : k + 1] for k in range(4)], masks, ABOVE_BELOW)
    back = [t0[...], t1[...], t2[...], t3[...]]
    image[...] = products(inverse[0], x[...], size // TILE, columns, back)
    own[:size] = i0[...] + back[0].T
    own[size:] = i1[...] + back[1].T
    cross[:size] = back[2].T
    cross[size:] = back[3].T


def above_own_body(inverse, masks, sq, x, o0, o1, x0, x1, t0, t1, t2, t3, self_image, above_image, image, own, cross):
    size = x.shape[0]
    columns = with_masks((o0, o1, x0, x1), [sq[k : k + 1] for k in range(4)], masks, ABOVE_OWN)
    back = [t0[...], t1[...], t2[...], t3[...]]
    image[...] = above_image[...] + products(inverse[0], x[...], size // TILE, columns, back)
    own[:size] = self_image[:size] + back[0].T
    own[size:] = self_image[size:] + back[1].T
    cross[:size] = back[2].T
    cross[size:] = back[3].T


def gram_body(own, cross, below, above0, above1, image, gram):
    total = own[...] + cross[...] + below[...] + jnp.concatenate([above0[...], above1[...]], axis=0)
    image[...] = total
    gram[...] = contract(total, total, ((0,), (0,)), HIGHEST)


GROUP = 8


def full(value):
    return jnp.broadcast_to(value, (GROUP, value.shape[1] if value.shape[1] > 1 else TILE))


def factor(gram, block):
    size = gram.shape[0]
    groups = size // GROUP
    upper = [gram[GROUP * r : GROUP * (r + 1)] for r in range(groups)]
    row = lax.broadcasted_iota(jnp.int32, (GROUP, size), 0)
    col = lax.broadcasted_iota(jnp.int32, (GROUP, size), 1)
    inverse = [jnp.where(col == row + GROUP * r, 1.0, 0.0).astype(F32) for r in range(groups)]
    for b in range(0, groups, block):
        if b:
            done_upper, done_inverse = jnp.concatenate(upper[:b], axis=0), jnp.concatenate(inverse[:b], axis=0)
            coefficients = done_upper[:, GROUP * b : GROUP * (b + block)]
            less_upper = contract(coefficients, done_upper, ((0,), (0,)), HIGHEST)
            less_inverse = contract(coefficients, done_inverse, ((0,), (0,)), HIGHEST)
            for k in range(block):
                upper[b + k] = upper[b + k] - less_upper[GROUP * k : GROUP * (k + 1)]
                inverse[b + k] = inverse[b + k] - less_inverse[GROUP * k : GROUP * (k + 1)]
        for r in range(b, b + block):
            lane = GROUP * r
            columns = [full(upper[r][:, lane + k : lane + k + 1]) for k in range(GROUP)]
            diag = [[full(columns[j][i : i + 1]) for j in range(i + 1)] for i in range(GROUP)]
            lower = [[None] * GROUP for _ in range(GROUP)]
            scale = [None] * GROUP
            for i in range(GROUP):
                scale[i] = lax.rsqrt(diag[i][i])
                for k in range(i + 1, GROUP):
                    lower[k][i] = diag[k][i] * scale[i]
                for k in range(i + 1, GROUP):
                    for j in range(i + 1, k + 1):
                        diag[k][j] = diag[k][j] - lower[k][i] * lower[j][i]
            u = [full(upper[r][i : i + 1]) for i in range(GROUP)]
            v = [full(inverse[r][i : i + 1]) for i in range(GROUP)]
            for i in range(GROUP):
                u[i], v[i] = u[i] * scale[i], v[i] * scale[i]
                for k in range(i + 1, GROUP):
                    u[k], v[k] = u[k] - lower[k][i] * u[i], v[k] - lower[k][i] * v[i]
            upper[r], inverse[r] = u[0], v[0]
            for i in range(1, GROUP):
                upper[r] = jnp.where(row == i, u[i], upper[r])
                inverse[r] = jnp.where(row == i, v[i], inverse[r])
            for later in range(r + 1, b + block):
                left = [full(upper[later][:, lane + k : lane + k + 1]) for k in range(GROUP)]
                for i in range(GROUP):
                    left[i] = left[i] * scale[i]
                    for k in range(i + 1, GROUP):
                        left[k] = left[k] - lower[k][i] * left[i]
                    upper[later] = upper[later] - left[i] * u[i]
                    inverse[later] = inverse[later] - left[i] * v[i]
    at_row = lax.broadcasted_iota(jnp.int32, (size, size), 0)
    at_col = lax.broadcasted_iota(jnp.int32, (size, size), 1)
    return jnp.where(at_col >= at_row, jnp.concatenate(upper, axis=0), 0.0), jnp.concatenate(inverse, axis=0)


def basis_body(image, gram, basis, upper):
    upper[...], inverse = factor(gram[...], 4)
    basis[...] = contract(image[...], inverse, ((1,), (1,)), HIGHEST)


def per_device(embeddings, start_panel, tile_mask, inv_width):
    n_blk = lax.axis_size("blk")
    half, width = start_panel.shape
    tiles = half // TILE
    size = half // 2
    sub_move = lambda v: lax.ppermute(v, "sub", [(0, 1), (1, 0)])
    blk_route = lambda v, to: lax.ppermute(v, "blk", [(i, to(i) % n_blk) for i in range(n_blk)])
    blk_move = lambda v, by: blk_route(v, lambda i: i + by)

    own = [jnp.concatenate([embeddings[i : i + size], start_panel[i : i + size]], axis=1) for i in (0, size)]
    mask = tile_mask.astype(F32)
    own_mask = jnp.concatenate([mask, sub_move(mask)], axis=0)
    if n_blk == 8:
        swapped = blk_route(own[1], lambda i: i ^ 1)
        below = [blk_move(own[0], 1), blk_route(swapped, lambda i: i if i & 1 else i + 2)]
    else:
        below = [blk_move(own[0], 1), blk_move(own[1], 1)]
    above = [blk_move(own[0], -2), blk_move(own[1], -2)]
    other = [sub_move(own[0]), sub_move(own[1])]
    below_mask, above_mask = blk_move(own_mask, 1), blk_move(own_mask, -2)
    sub = lax.axis_index("sub").astype(jnp.int32).reshape(1)
    masks = vmem_call(mask_body, shape(len(PAIRS), 2 * tiles, half), sub, own_mask, below_mask, above_mask, scalars=1)

    image = shape(size, width)
    turned = (shape(width, size),) * 4
    sq_rows = shape(4, size)
    block = own + other
    self_image, sq = vmem_call(self_body, (shape(half, width), sq_rows), inv_width, masks, *block, scalars=1)
    below_image, back = [], []
    for part in range(2):
        out, *back = vmem_call(
            functools.partial(below_body, part), (image, *turned), inv_width, masks, sq, below[part], *block, *back, scalars=1
        )
        below_image.append(out)
    below += [sub_move(below[0]), sub_move(below[1])]
    above_image0, below_sq, *back = vmem_call(
        above_first_body, (image, sq_rows, *turned, *turned), inv_width, masks, sq, above[0], *block, *below, *back, scalars=1
    )
    above_image0 = blk_move(above_image0, 2)
    above_image1, below_image, below_cross = vmem_call(
        above_below_body,
        (image, shape(half, width), shape(half, width)),
        inv_width,
        masks,
        below_sq,
        above[1],
        *below,
        *back[4:],
        *below_image,
        scalars=1,
    )
    below_image = blk_move(below_image + sub_move(below_cross), -1)
    above_image1, own_image, own_cross = vmem_call(
        above_own_body,
        (image, shape(half, width), shape(half, width)),
        inv_width,
        masks,
        sq,
        above[1],
        *block,
        *back[:4],
        self_image,
        above_image1,
        scalars=1,
    )
    above_image1 = blk_move(above_image1, 2)
    image, gram = vmem_call(
        gram_body,
        (shape(half, width), shape(width, width)),
        own_image,
        sub_move(own_cross),
        below_image,
        above_image0,
        above_image1,
    )
    if n_blk & (n_blk - 1):
        gram = lax.psum(gram, ("blk", "sub"))
    else:
        gram = gram + sub_move(gram)
        hop = 1
        while hop < n_blk:
            gram = gram + blk_route(gram, lambda i: i ^ hop)
            hop *= 2
    return vmem_call(basis_body, (shape(half, width), shape(width, width)), image, gram)


def solution(mesh):
    return jax.shard_map(
        per_device,
        mesh=mesh,
        in_specs=(
            P(("groups", "blk", "sub"), None),
            P(("groups", "blk", "sub"), None),
            P(("groups", "blk", "sub"), None),
            P(),
        ),
        out_specs=(P(("groups", "blk", "sub"), None), P("groups", None)),
        check_vma=False,
    )
```

time: 322 us -> 119 us (0.37)
  waiting for transfers between devices: 197 us -> 72.6 us
  other arithmetic: 38.8 us -> 0.17 us
  matrix products: 33.4 us -> 0 us
  Pallas kernels: 0 us -> 25.4 us
  between operations: 18.2 us -> 1.49 us
  local copies, waits for them, and re-layouts: 14.8 us -> 1.33 us
  starting transfers between devices: 11.6 us -> 18.1 us
  loops' own time: 4.67 us -> 0 us
    psum x1 -> x0, waiting for transfers between devices: 87.7 us -> none  [per_device(): lower_factor = jnp.linalg.cholesky(lax.psum(local_gram, ('blk', 'sub')))]
    dot_general x8 -> x0, matrix products: 31.3 us -> none  [the longest x7 29.1 us: compute(): return jnp.dot(kernel, src_panel, preferred_element_type=jnp.float32)]
    ppermute x6 -> x21, waiting for transfers between devices: 99.9 us -> 72.6 us  [the longest x13 69.8 us: per_device(): lax.ppermute(v, 'blk', [(i, to(i) % n_blk) for i in range(n_blk)])]
    pallas_call x0 -> x9, Pallas kernels: none -> 25.4 us  [vmem_call(): pl.pallas_call(body, out_shape=out_shapes, in_specs=[in_smem] * scalars +...]
    another operation x4 -> x0, other arithmetic: 22.2 us -> none  [the longest x3 12.4 us: per_device(): lower_factor = jnp.linalg.cholesky(lax.psum(local_gram, ('blk', 'sub')))]
    mul x7 -> x0, local copies, waits for them, and re-layouts: 11.8 us -> none  [compute(): kernel = kernel * window.astype(jnp.float32)[:, None, :, None]]
    reduce_sum x8 -> x0, other arithmetic: 11.5 us -> none  [the longest x7 9.31 us: compute(): src_sq = jnp.sum(jnp.square(src_embed.astype(jnp.float32)), axis=1)]
    reduce_scatter x1 -> x0, waiting for transfers between devices: 8.93 us -> none  [per_device(): lax.psum_scatter(accum_rows, 'sub', scatter_dimension=0, tiled=True)]
  transfers between devices with their start and end apart: 9 -> 21, of which waited for: 5 -> 12; matrix products, arithmetic and copies ran while one was open for 14% -> 0% of each run, Pallas kernels for 0% -> 14%
where the time goes in v2:
time: 119 us
  waiting for transfers between devices  72.6 us (61%)
  Pallas kernels  25.4 us (21%)
  starting transfers between devices  18.1 us (15%)
  between operations  1.49 us (1%)
  local copies, waits for them, and re-layouts  1.33 us (1%)
    ppermute x13, waiting for transfers between devices, per_device(): lax.ppermute(v, 'blk', [(i, to(i) % n_blk) for i in range(n_blk)])  69.8 us
    pallas_call x9, Pallas kernels, vmem_call(): pl.pallas_call(body, out_shape=out_shapes, in_specs=[in_smem] * scalars +...  25.4 us
    ppermute x13, starting transfers between devices, per_device(): lax.ppermute(v, 'blk', [(i, to(i) % n_blk) for i in range(n_blk)])  16.4 us
    ppermute x8, waiting for transfers between devices, per_device(): sub_move = lambda v: lax.ppermute(v, 'sub', [(0, 1), (1, 0)])  2.74 us
  transfers between devices with their start and end apart: 21, of which 12 were waited for; matrix products, arithmetic and copies ran while one was open for 0% of the time, Pallas kernels for 14%

profile of v2, /device:TPU:0, one launch (start us, length us, event | category | flops | bytes accessed | tf_op | source)
XLA Modules:
  0.0 119.1 jit_solution(14034348985211197352)
XLA Ops:
  0.6 1.3 %fusion = (bf16[256,1024]{1,0:T(8,128)(2,1)S(1)}, bf16[256,1024]{1,0:T(8,128)(2,1)S(1)}) fusion(bf16[512,1024]{1,0:T(8,128)(2,1)} %param.4), kind=kLoop, calls=%fused_computation.3 | loop fusion | bytes 2097152 | tf_op jit(solution)/shard_map/slice | solution.py:250
  2.0 3.0 %collective-permute-start.8 = (bf16[256,1152]{1,0:T(8,128)(2,1)S(1)}, bf16[256,1152]{1,0:T(8,128)(2,1)S(1)}, u32[]{:S(2)}, u32[]{:S(2)}) collective-permute-start(bf16[256,1152]{1,0:T(8,128)(2,1)S(1)} %pad_maximum_fusion.1.o1), channel_id=1, source_target_pairs={{0,2},{2,0},{4,6},{6,4},{8,10},{10,8},{12,14},{14,12},{1,3},{3,1},... | collective-permute-start | bytes 1769480 | tf_op jit(solution)/shard_map/ppermute | solution.py:247
  5.2 25.8 %collective-permute-done.8 = bf16[256,1152]{1,0:T(8,128)(2,1)S(1)} collective-permute-done((bf16[256,1152]{1,0:T(8,128)(2,1)S(1)}, bf16[256,1152]{1,0:T(8,128)(2,1)S(1)}, u32[]{:S(2)}, u32[]{:S(2)}) %collective-permute-start.8) | collective-permute-done | bytes 589856 | tf_op jit(solution)/shard_map/ppermute | solution.py:247
  31.0 3.7 %collective-permute-start.9 = (bf16[256,1152]{1,0:T(8,128)(2,1)S(1)}, bf16[256,1152]{1,0:T(8,128)(2,1)S(1)}, u32[]{:S(2)}, u32[]{:S(2)}) collective-permute-start(bf16[256,1152]{1,0:T(8,128)(2,1)S(1)} %collective-permute-done.8), channel_id=1, source_target_pairs={{0,4},{2,2},{4,8},{6,6},{8,12},{10,10},{12,0},{14,14},{1,5},{3,3},... | collective-permute-start | bytes 1769480 | tf_op jit(solution)/shard_map/ppermute | solution.py:247
  34.8 0.5 collective-permute-start
  35.3 1.5 %collective-permute-done = f32[4,56]{1,0:T(4,128)S(1)} collective-permute-done((f32[4,56]{1,0:T(4,128)S(1)}, f32[4,56]{1,0:T(4,128)S(1)}, u32[]{:S(2)}, u32[]{:S(2)}) %collective-permute-start) | collective-permute-done | bytes 928 | tf_op jit(solution)/shard_map/ppermute | solution.py:246
  36.9 2.1 %collective-permute-start.2 = (f32[8,56]{1,0:T(8,128)S(1)}, f32[8,56]{1,0:T(8,128)S(1)}, u32[]{:S(2)}, u32[]{:S(2)}) collective-permute-start(f32[8,56]{1,0:T(8,128)S(1)} %pad_maximum_fusion.2.own), channel_id=1, source_target_pairs={{0,12},{2,14},{4,0},{6,2},{8,4},{10,6},{12,8},{14,10},{1,13},{3,15... | collective-permute-start | bytes 5384 | tf_op jit(solution)/shard_map/ppermute | solution.py:247
  39.0 4.2 %collective-permute-done.1.below = f32[8,56]{1,0:T(8,128)S(1)} collective-permute-done((f32[8,56]{1,0:T(8,128)S(1)}, f32[8,56]{1,0:T(8,128)S(1)}, u32[]{:S(2)}, u32[]{:S(2)}) %collective-permute-start.1) | collective-permute-done | bytes 1824 | tf_op jit(solution)/shard_map/ppermute | solution.py:247
  43.2 3.3 %collective-permute-done.2.above = f32[8,56]{1,0:T(8,128)S(1)} collective-permute-done((f32[8,56]{1,0:T(8,128)S(1)}, f32[8,56]{1,0:T(8,128)S(1)}, u32[]{:S(2)}, u32[]{:S(2)}) %collective-permute-start.2) | collective-permute-done | bytes 1824 | tf_op jit(solution)/shard_map/ppermute | solution.py:247
  46.5 4.4 %collective-permute-start.6 = (bf16[256,1152]{1,0:T(8,128)(2,1)S(1)}, bf16[256,1152]{1,0:T(8,128)(2,1)}, u32[]{:S(2)}, u32[]{:S(2)}) collective-permute-start(bf16[256,1152]{1,0:T(8,128)(2,1)S(1)} %pad_maximum_fusion.o0), channel_id=1, source_target_pairs={{0,12},{2,14},{4,0},{6,2},{8,4},{10,6},{12,8},{14,10},{1,13},{3,15... | collective-permute-start | bytes 1769480 | tf_op jit(solution)/shard_map/ppermute | solution.py:247
  50.9 0.5 collective-permute-start.11
  51.4 0.4 collective-permute-start.5
  52.5 1.1 shard_map.59.masks
  53.6 2.9 %shard_map.60 = (f32[512,128]{1,0:T(8,128)S(1)}, f32[4,256]{1,0:T(4,128)S(1)}) custom-call(f32[1]{0:T(128)S(6)} %copy.6.inverse, f32[8,8,512]{2,1,0:T(8,128)S(1)} %shard_map.59.masks, bf16[256,1152]{1,0:T(8,128)(2,1)S(1)} %pad_maximum_fusion.o0, bf16[256,1152]{1,0:T(8,128)(2,1)S(1)} %pad_maximum_fusion.1.o1, ...), custom_call_target="tpu_custom_call" | custom-call | tf_op jit(solution)/shard_map/pallas_call | solution.py:20
  56.5 2.0 %shard_map.61 = (f32[256,128]{1,0:T(8,128)S(1)}, f32[128,256]{1,0:T(8,128)S(1)}, f32[128,256]{1,0:T(8,128)S(1)}, f32[128,256]{1,0:T(8,128)S(1)}, f32[128,256]{1,0:T(8,128)S(1)}) custom-call(f32[1]{0:T(128)S(6)} %copy.6.inverse, f32[8,8,512]{2,1,0:T(8,128)S(1)} %shard_map.59.masks, f32[4,256]{1,0:T(4,128)S(1)} %get-tuple-element.32.sq, ...), custom_call_target="tpu_custom_call" | custom-call | tf_op jit(solution)/shard_map/pallas_call | solution.py:20
  58.6 2.0 %shard_map.62 = (f32[256,128]{1,0:T(8,128)S(1)}, f32[128,256]{1,0:T(8,128)S(1)}, f32[128,256]{1,0:T(8,128)S(1)}, f32[128,256]{1,0:T(8,128)S(1)}, f32[128,256]{1,0:T(8,128)S(1)}) custom-call(f32[1]{0:T(128)S(6)} %copy.6.inverse, f32[8,8,512]{2,1,0:T(8,128)S(1)} %shard_map.59.masks, f32[4,256]{1,0:T(4,128)S(1)} %get-tuple-element.32.sq, ...), custom_call_target="tpu_custom_call" | custom-call | tf_op jit(solution)/shard_map/pallas_call | solution.py:20
  60.6 4.1 %collective-permute-done.6.x = bf16[256,1152]{1,0:T(8,128)(2,1)} collective-permute-done((bf16[256,1152]{1,0:T(8,128)(2,1)S(1)}, bf16[256,1152]{1,0:T(8,128)(2,1)}, u32[]{:S(2)}, u32[]{:S(2)}) %collective-permute-start.6) | collective-permute-done | bytes 589856 | tf_op jit(solution)/shard_map/ppermute | solution.py:247
  64.7 5.1 %shard_map.63 = (f32[256,128]{1,0:T(8,128)S(1)}, f32[4,256]{1,0:T(4,128)S(1)}, f32[128,256]{1,0:T(8,128)S(1)}, f32[128,256]{1,0:T(8,128)S(1)}, f32[128,256]{1,0:...) custom-call(f32[1]{0:T(128)S(6)} %copy.6.inverse, ...), custom_call_target="tpu_custom_call" | custom-call | tf_op jit(solution)/shard_map/pallas_call | solution.py:20
  69.8 4.9 %collective-permute-done.5.x = bf16[256,1152]{1,0:T(8,128)(2,1)} collective-permute-done((bf16[256,1152]{1,0:T(8,128)(2,1)S(1)}, bf16[256,1152]{1,0:T(8,128)(2,1)}, u32[]{:S(2)}, u32[]{:S(2)}) %collective-permute-start.5) | collective-permute-done | bytes 589856 | tf_op jit(solution)/shard_map/ppermute | solution.py:247
  74.7 3.5 %shard_map.64 = (f32[256,128]{1,0:T(8,128)S(1)}, f32[512,128]{1,0:T(8,128)S(1)}, f32[512,128]{1,0:T(8,128)S(1)}) custom-call(f32[1]{0:T(128)S(6)} %copy.6.inverse, f32[8,8,512]{2,1,0:T(8,128)S(1)} %shard_map.59.masks, f32[4,256]{1,0:T(4,128)S(1)} %get-tuple-element.46.below_sq, bf16[256,1152]{1,0:T(8,128)(2,1)} %collective-permute-done.5.x, ...), custom_call_target="tpu_custom_call" | custom-call | tf_op jit(solution)/shard_map/pallas_call | solution.py:20
  78.3 3.2 %shard_map.65 = (f32[256,128]{1,0:T(8,128)S(1)}, f32[512,128]{1,0:T(8,128)S(1)}, f32[512,128]{1,0:T(8,128)S(1)}) custom-call(f32[1]{0:T(128)S(6)} %copy.6.inverse, f32[8,8,512]{2,1,0:T(8,128)S(1)} %shard_map.59.masks, f32[4,256]{1,0:T(4,128)S(1)} %get-tuple-element.32.sq, bf16[256,1152]{1,0:T(8,128)(2,1)} %collective-permute-done.5.x, ...), custom_call_target="tpu_custom_call" | custom-call | tf_op jit(solution)/shard_map/pallas_call | solution.py:20
  81.5 0.6 collective-permute-start.12
  82.1 1.0 collective-permute-start.14
  83.1 1.4 %collective-permute-start.15 = (f32[256,128]{1,0:T(8,128)S(1)}, f32[256,128]{1,0:T(8,128)S(1)}, u32[]{:S(2)}, u32[]{:S(2)}) collective-permute-start(f32[256,128]{1,0:T(8,128)S(1)} %get-tuple-element.58), channel_id=1, source_target_pairs={{0,4},{2,6},{4,8},{6,10},{8,12},{10,14},{12,0},{14,2},{1,5},{3,7},... | collective-permute-start | bytes 393224 | tf_op jit(solution)/shard_map/ppermute | solution.py:247
  84.5 11.4 %collective-permute-done.16.above1 = f32[256,128]{1,0:T(8,128)S(1)} collective-permute-done((f32[256,128]{1,0:T(8,128)S(1)}, f32[256,128]{1,0:T(8,128)S(1)}, u32[]{:S(2)}, u32[]{:S(2)}) %collective-permute-start.16) | collective-permute-done | bytes 131104 | tf_op jit(solution)/shard_map/ppermute | solution.py:247
  95.9 2.2 %collective-permute-done.15.above0 = f32[256,128]{1,0:T(8,128)S(1)} collective-permute-done((f32[256,128]{1,0:T(8,128)S(1)}, f32[256,128]{1,0:T(8,128)S(1)}, u32[]{:S(2)}, u32[]{:S(2)}) %collective-permute-start.15) | collective-permute-done | bytes 131104 | tf_op jit(solution)/shard_map/ppermute | solution.py:247
  98.1 0.4 shard_map.66
  98.6 1.2 %collective-permute-done.17 = f32[128,128]{1,0:T(8,128)S(1)} collective-permute-done((f32[128,128]{1,0:T(8,128)S(1)}, f32[128,128]{1,0:T(8,128)S(1)}, u32[]{:S(2)}, u32[]{:S(2)}) %collective-permute-start.17) | collective-permute-done | bytes 65568 | tf_op jit(solution)/shard_map/ppermute | solution.py:246
  99.9 4.3 %collective-permute-done.18 = f32[128,128]{1,0:T(8,128)S(1)} collective-permute-done((f32[128,128]{1,0:T(8,128)S(1)}, f32[128,128]{1,0:T(8,128)S(1)}, u32[]{:S(2)}, u32[]{:S(2)}) %collective-permute-start.18) | collective-permute-done | bytes 65568 | tf_op jit(solution)/shard_map/ppermute | solution.py:247
  104.3 4.3 %collective-permute-done.19 = f32[128,128]{1,0:T(8,128)S(1)} collective-permute-done((f32[128,128]{1,0:T(8,128)S(1)}, f32[128,128]{1,0:T(8,128)S(1)}, u32[]{:S(2)}, u32[]{:S(2)}) %collective-permute-start.19) | collective-permute-done | bytes 65568 | tf_op jit(solution)/shard_map/ppermute | solution.py:247
  108.6 5.3 %collective-permute-done.20 = f32[128,128]{1,0:T(8,128)S(1)} collective-permute-done((f32[128,128]{1,0:T(8,128)S(1)}, f32[128,128]{1,0:T(8,128)S(1)}, u32[]{:S(2)}, u32[]{:S(2)}) %collective-permute-start.20) | collective-permute-done | bytes 65568 | tf_op jit(solution)/shard_map/ppermute | solution.py:247
  113.9 5.2 %shard_map.67 = (f32[512,128]{1,0:T(8,128)}, f32[128,128]{1,0:T(8,128)}) custom-call(f32[512,128]{1,0:T(8,128)S(1)} %get-tuple-element.60.image, f32[128,128]{1,0:T(8,128)S(1)} %add.19.gram), custom_call_target="tpu_custom_call" | custom-call | tf_op jit(solution)/shard_map/pallas_call | solution.py:20
  (34 shorter events, 0.8 us)
Async XLA Ops:
  0.6 1.3 %copy-start = (bf16[512,128]{1,0:T(8,128)(2,1)S(1)}, bf16[512,128]{1,0:T(8,128)(2,1)}, u32[]{:S(2)}) copy-start(bf16[512,128]{1,0:T(8,128)(2,1)} %param.5) | copy-start | bytes 393220
  2.0 32.9 %copy-start.1 = (s32[4,56]{1,0:T(4,128)S(1)}, s32[4,56]{1,0:T(4,128)}, u32[]{:S(2)}) copy-start(s32[4,56]{1,0:T(4,128)} %param.6) | copy-start | bytes 2692
  2.0 29.0 %collective-permute-start.8 = (bf16[256,1152]{1,0:T(8,128)(2,1)S(1)}, bf16[256,1152]{1,0:T(8,128)(2,1)S(1)}, u32[]{:S(2)}, u32[]{:S(2)}) collective-permute-start(bf16[256,1152]{1,0:T(8,128)(2,1)S(1)} %pad_maximum_fusion.1.o1), channel_id=1, source_target_pairs={{0,2},{2,0},{4,6},{6,4},{8,10},{10,8},{12,14},{14,12},{1,3},{3,1},... | collective-permute-start | bytes 1769480 | tf_op jit(solution)/shard_map/ppermute | solution.py:247
  5.1 45.8 %collective-permute-start.7 = (bf16[256,1152]{1,0:T(8,128)(2,1)S(1)}, bf16[256,1152]{1,0:T(8,128)(2,1)S(1)}, u32[]{:S(2)}, u32[]{:S(2)}) collective-permute-start(bf16[256,1152]{1,0:T(8,128)(2,1)S(1)} %pad_maximum_fusion.o0), channel_id=1, source_target_pairs={{0,2},{2,4},{4,6},{6,8},{8,10},{10,12},{12,14},{14,0},{1,3},{3,5},... | collective-permute-start | bytes 1769480 | tf_op jit(solution)/shard_map/ppermute | solution.py:247
  31.0 19.9 %collective-permute-start.9 = (bf16[256,1152]{1,0:T(8,128)(2,1)S(1)}, bf16[256,1152]{1,0:T(8,128)(2,1)S(1)}, u32[]{:S(2)}, u32[]{:S(2)}) collective-permute-start(bf16[256,1152]{1,0:T(8,128)(2,1)S(1)} %collective-permute-done.8), channel_id=1, source_target_pairs={{0,4},{2,2},{4,8},{6,6},{8,12},{10,10},{12,0},{14,14},{1,5},{3,3},... | collective-permute-start | bytes 1769480 | tf_op jit(solution)/shard_map/ppermute | solution.py:247
  34.7 16.7 %collective-permute-start.3 = (bf16[256,1152]{1,0:T(8,128)(2,1)S(1)}, bf16[256,1152]{1,0:T(8,128)(2,1)S(1)}, u32[]{:S(2)}, u32[]{:S(2)}) collective-permute-start(bf16[256,1152]{1,0:T(8,128)(2,1)S(1)} %pad_maximum_fusion.o0), channel_id=1, source_target_pairs={{0,1},{1,0},{2,3},{3,2},{4,5},{5,4},{6,7},{7,6},{8,9},{9,8},{10,11... | collective-permute-start | bytes 1769480 | tf_op jit(solution)/shard_map/ppermute | solution.py:246
  34.8 2.0 %collective-permute-start = (f32[4,56]{1,0:T(4,128)S(1)}, f32[4,56]{1,0:T(4,128)S(1)}, u32[]{:S(2)}, u32[]{:S(2)}) collective-permute-start(f32[4,56]{1,0:T(4,128)S(1)} %convert_element_type.3), channel_id=1, source_target_pairs={{0,1},{1,0},{2,3},{3,2},{4,5},{5,4},{6,7},{7,6},{8,9},{9,8},{10,11... | collective-permute-start | bytes 2696 | tf_op jit(solution)/shard_map/ppermute | solution.py:246
  36.8 6.4 %collective-permute-start.1 = (f32[8,56]{1,0:T(8,128)S(1)}, f32[8,56]{1,0:T(8,128)S(1)}, u32[]{:S(2)}, u32[]{:S(2)}) collective-permute-start(f32[8,56]{1,0:T(8,128)S(1)} %pad_maximum_fusion.2.own), channel_id=1, source_target_pairs={{0,2},{2,4},{4,6},{6,8},{8,10},{10,12},{12,14},{14,0},{1,3},{3,5},... | collective-permute-start | bytes 5384 | tf_op jit(solution)/shard_map/ppermute | solution.py:247
  36.9 9.6 %collective-permute-start.2 = (f32[8,56]{1,0:T(8,128)S(1)}, f32[8,56]{1,0:T(8,128)S(1)}, u32[]{:S(2)}, u32[]{:S(2)}) collective-permute-start(f32[8,56]{1,0:T(8,128)S(1)} %pad_maximum_fusion.2.own), channel_id=1, source_target_pairs={{0,12},{2,14},{4,0},{6,2},{8,4},{10,6},{12,8},{14,10},{1,13},{3,15... | collective-permute-start | bytes 5384 | tf_op jit(solution)/shard_map/ppermute | solution.py:247
  43.2 10.5 %collective-permute-start.4 = (bf16[256,1152]{1,0:T(8,128)(2,1)S(1)}, bf16[256,1152]{1,0:T(8,128)(2,1)S(1)}, u32[]{:S(2)}, u32[]{:S(2)}) collective-permute-start(bf16[256,1152]{1,0:T(8,128)(2,1)S(1)} %pad_maximum_fusion.1.o1), channel_id=1, source_target_pairs={{0,1},{1,0},{2,3},{3,2},{4,5},{5,4},{6,7},{7,6},{8,9},{9,8},{10,11... | collective-permute-start | bytes 1769480 | tf_op jit(solution)/shard_map/ppermute | solution.py:246
  46.5 18.2 %collective-permute-start.6 = (bf16[256,1152]{1,0:T(8,128)(2,1)S(1)}, bf16[256,1152]{1,0:T(8,128)(2,1)}, u32[]{:S(2)}, u32[]{:S(2)}) collective-permute-start(bf16[256,1152]{1,0:T(8,128)(2,1)S(1)} %pad_maximum_fusion.o0), channel_id=1, source_target_pairs={{0,12},{2,14},{4,0},{6,2},{8,4},{10,6},{12,8},{14,10},{1,13},{3,15... | collective-permute-start | bytes 1769480 | tf_op jit(solution)/shard_map/ppermute | solution.py:247
  50.9 13.8 %collective-permute-start.10 = (bf16[256,1152]{1,0:T(8,128)(2,1)S(1)}, bf16[256,1152]{1,0:T(8,128)(2,1)}, u32[]{:S(2)}, u32[]{:S(2)}) collective-permute-start(bf16[256,1152]{1,0:T(8,128)(2,1)S(1)} %collective-permute-done.7.x.b0), channel_id=1, source_target_pairs={{0,1},{1,0},{2,3},{3,2},{4,5},{5,4},{6,7},{7,6},{8,9},{9,8},{10,11... | collective-permute-start | bytes 1769480 | tf_op jit(solution)/shard_map/ppermute | solution.py:246
  50.9 13.8 %collective-permute-start.11 = (bf16[256,1152]{1,0:T(8,128)(2,1)S(1)}, bf16[256,1152]{1,0:T(8,128)(2,1)}, u32[]{:S(2)}, u32[]{:S(2)}) collective-permute-start(bf16[256,1152]{1,0:T(8,128)(2,1)S(1)} %collective-permute-done.9.x.b1), channel_id=1, source_target_pairs={{0,1},{1,0},{2,3},{3,2},{4,5},{5,4},{6,7},{7,6},{8,9},{9,8},{10,11... | collective-permute-start | bytes 1769480 | tf_op jit(solution)/shard_map/ppermute | solution.py:246
  51.4 23.2 %collective-permute-start.5 = (bf16[256,1152]{1,0:T(8,128)(2,1)S(1)}, bf16[256,1152]{1,0:T(8,128)(2,1)}, u32[]{:S(2)}, u32[]{:S(2)}) collective-permute-start(bf16[256,1152]{1,0:T(8,128)(2,1)S(1)} %pad_maximum_fusion.1.o1), channel_id=1, source_target_pairs={{0,12},{2,14},{4,0},{6,2},{8,4},{10,6},{12,8},{14,10},{1,13},{3,15... | collective-permute-start | bytes 1769480 | tf_op jit(solution)/shard_map/ppermute | solution.py:247
  78.2 3.8 %collective-permute-start.13 = (f32[512,128]{1,0:T(8,128)S(1)}, f32[512,128]{1,0:T(8,128)S(1)}, u32[]{:S(2)}, u32[]{:S(2)}) collective-permute-start(f32[512,128]{1,0:T(8,128)S(1)} %get-tuple-element.57), channel_id=1, source_target_pairs={{0,1},{1,0},{2,3},{3,2},{4,5},{5,4},{6,7},{7,6},{8,9},{9,8},{10,11... | collective-permute-start | bytes 786440 | tf_op jit(solution)/shard_map/ppermute | solution.py:246
  81.5 16.6 %collective-permute-start.12 = (f32[512,128]{1,0:T(8,128)S(1)}, f32[512,128]{1,0:T(8,128)S(1)}, u32[]{:S(2)}, u32[]{:S(2)}) collective-permute-start(f32[512,128]{1,0:T(8,128)S(1)} %get-tuple-element.55), channel_id=1, source_target_pairs={{0,1},{1,0},{2,3},{3,2},{4,5},{5,4},{6,7},{7,6},{8,9},{9,8},{10,11... | collective-permute-start | bytes 786440 | tf_op jit(solution)/shard_map/ppermute | solution.py:246
  82.1 16.0 %collective-permute-start.14 = (f32[512,128]{1,0:T(8,128)S(1)}, f32[512,128]{1,0:T(8,128)S(1)}, u32[]{:S(2)}, u32[]{:S(2)}) collective-permute-start(f32[512,128]{1,0:T(8,128)S(1)} %add.15), channel_id=1, source_target_pairs={{0,14},{2,0},{4,2},{6,4},{8,6},{10,8},{12,10},{14,12},{1,15},{3,1}... | collective-permute-start | bytes 786440 | tf_op jit(solution)/shard_map/ppermute | solution.py:247
  83.1 12.8 %collective-permute-start.16 = (f32[256,128]{1,0:T(8,128)S(1)}, f32[256,128]{1,0:T(8,128)S(1)}, u32[]{:S(2)}, u32[]{:S(2)}) collective-permute-start(f32[256,128]{1,0:T(8,128)S(1)} %get-tuple-element.59), channel_id=1, source_target_pairs={{0,4},{2,6},{4,8},{6,10},{8,12},{10,14},{12,0},{14,2},{1,5},{3,7},... | collective-permute-start | bytes 393224 | tf_op jit(solution)/shard_map/ppermute | solution.py:247
  83.1 15.0 %collective-permute-start.15 = (f32[256,128]{1,0:T(8,128)S(1)}, f32[256,128]{1,0:T(8,128)S(1)}, u32[]{:S(2)}, u32[]{:S(2)}) collective-permute-start(f32[256,128]{1,0:T(8,128)S(1)} %get-tuple-element.58), channel_id=1, source_target_pairs={{0,4},{2,6},{4,8},{6,10},{8,12},{10,14},{12,0},{14,2},{1,5},{3,7},... | collective-permute-start | bytes 393224 | tf_op jit(solution)/shard_map/ppermute | solution.py:247
  98.5 1.3 %collective-permute-start.17 = (f32[128,128]{1,0:T(8,128)S(1)}, f32[128,128]{1,0:T(8,128)S(1)}, u32[]{:S(2)}, u32[]{:S(2)}) collective-permute-start(f32[128,128]{1,0:T(8,128)S(1)} %get-tuple-element.61), channel_id=1, source_target_pairs={{0,1},{1,0},{2,3},{3,2},{4,5},{5,4},{6,7},{7,6},{8,9},{9,8},{10,11... | collective-permute-start | bytes 196616 | tf_op jit(solution)/shard_map/ppermute | solution.py:246
  99.9 4.3 %collective-permute-start.18 = (f32[128,128]{1,0:T(8,128)S(1)}, f32[128,128]{1,0:T(8,128)S(1)}, u32[]{:S(2)}, u32[]{:S(2)}) collective-permute-start(f32[128,128]{1,0:T(8,128)S(1)} %add.16), channel_id=1, source_target_pairs={{0,2},{2,0},{4,6},{6,4},{8,10},{10,8},{12,14},{14,12},{1,3},{3,1},... | collective-permute-start | bytes 196616 | tf_op jit(solution)/shard_map/ppermute | solution.py:247
  104.2 4.3 %collective-permute-start.19 = (f32[128,128]{1,0:T(8,128)S(1)}, f32[128,128]{1,0:T(8,128)S(1)}, u32[]{:S(2)}, u32[]{:S(2)}) collective-permute-start(f32[128,128]{1,0:T(8,128)S(1)} %add.17), channel_id=1, source_target_pairs={{0,4},{2,6},{4,0},{6,2},{8,12},{10,14},{12,8},{14,10},{1,5},{3,7},... | collective-permute-start | bytes 196616 | tf_op jit(solution)/shard_map/ppermute | solution.py:247
  108.5 5.4 %collective-permute-start.20 = (f32[128,128]{1,0:T(8,128)S(1)}, f32[128,128]{1,0:T(8,128)S(1)}, u32[]{:S(2)}, u32[]{:S(2)}) collective-permute-start(f32[128,128]{1,0:T(8,128)S(1)} %add.18), channel_id=1, source_target_pairs={{0,8},{2,10},{4,12},{6,14},{8,0},{10,2},{12,4},{14,6},{1,9},{3,11}... | collective-permute-start | bytes 196616 | tf_op jit(solution)/shard_map/ppermute | solution.py:247

commit v3 on v2

--- a/solution.py
+++ b/solution.py
@@ -34,37 +34,32 @@
     return lax.dot_general(a, b, (dims, ((), ())), precision=precision, preferred_element_type=F32)
 
 
-PAIRS = (
-    (0, 0, 0, 0),
-    (0, 0, 0, 1),
-    (1, 0, 1, 0),
-    (1, 0, 1, 1),
-    (2, 0, -2, 0),
-    (2, 0, -2, 1),
-    (2, 1, -3, 0),
-    (2, 1, -3, 1),
-)
-SELF, BELOW, ABOVE_OWN, ABOVE_BELOW = 0, 2, 4, 6
-
-
-def mask_body(sub_ref, own, below, above, out):
-    sub = sub_ref[0]
-    blocks = [own[...], below[...], above[...]]
-    both, window = blocks[0].shape
-    tiles = both // 2
-    lanes = tiles * TILE
-    window_at = lax.broadcasted_iota(jnp.int32, (window, lanes), 0)
-    tile_of = lax.broadcasted_iota(jnp.int32, (window, lanes), 1) // TILE
+MARK = 8
+OWN, BELOW, ABOVE = 0, 1, -2
+
+
+def pair_mask(sub, rows, cols, offset, which):
+    tiles = rows.shape[0]
+    padded, lanes = rows.shape[1], tiles * TILE
+    tile_of = lax.broadcasted_iota(jnp.int32, (padded, lanes), 1) // TILE
+    first = (REACH + offset) * 2 * tiles + (sub if which == 0 else 1 - sub) * tiles
+    chosen = (lax.broadcasted_iota(jnp.int32, (padded, lanes), 0) == first + tile_of).astype(F32)
+    ahead = contract(rows, chosen, ((1,), (0,)))
+    first = (REACH - offset) * 2 * tiles + sub * tiles
+    row_at = lax.broadcasted_iota(jnp.int32, (tiles, padded), 0)
+    chosen = (lax.broadcasted_iota(jnp.int32, (tiles, padded), 1) == first + row_at).astype(F32)
     spread = (lax.broadcasted_iota(jnp.int32, (tiles, lanes), 0) == tile_of[:tiles]).astype(F32)
-    row_at = lax.broadcasted_iota(jnp.int32, (tiles, window), 0)
-    column_at = lax.broadcasted_iota(jnp.int32, (tiles, window), 1)
-    for k, (rows, cols, offset, which) in enumerate(PAIRS):
-        actual = sub if which == 0 else 1 - sub
-        chosen = (window_at == (REACH + offset) * both + actual * tiles + tile_of).astype(F32)
-        out[k, :tiles] = contract(blocks[rows][:tiles], chosen, ((1,), (0,)))
-        own_columns = (column_at == (REACH - offset) * both + sub * tiles + row_at).astype(F32)
-        back = contract(own_columns, blocks[cols][which * tiles : (which + 1) * tiles], ((1,), (1,)))
-        out[k, tiles:] = contract(back, spread, ((1,), (0,)))
+    back = contract(contract(chosen, cols, ((1,), (1,))), spread, ((1,), (0,)))
+    return jnp.concatenate([ahead, back], axis=0)
+
+
+def marks(ref, size):
+    return ref[size : size + MARK, :TILE].astype(F32)[: 2 * size // TILE]
+
+
+def pieces(ref):
+    size = (ref.shape[0] - MARK) // 2
+    return [ref[:size], ref[size + MARK :]]
 
 
 def squares(piece, features):
@@ -74,6 +69,26 @@
 
 def as_row(column):
     return jnp.broadcast_to(column, (column.shape[0], TILE)).T[:1]
+
+
+def square_rows(blocks, out):
+    rows = [as_row(squares(p, p.shape[1] - TILE)) for block in blocks for p in pieces(block)]
+    for k, row in enumerate(rows):
+        out[k : k + 1] = row
+    return rows
+
+
+def read_rows(ref):
+    return [ref[k : k + 1] for k in range(ref.shape[0])]
+
+
+def columns_of(blocks, sq_rows, masks):
+    out = []
+    for h, block in enumerate(blocks):
+        for k, piece in enumerate(pieces(block)):
+            size = piece.shape[0]
+            out.append((piece, sq_rows[2 * h + k], masks[h][:, k * size : (k + 1) * size]))
+    return out
 
 
 def products(inverse, piece, tile, columns, back):
@@ -83,9 +98,7 @@
     doubled = piece[:, :features] * 2
     panel_t = piece[:, features:].astype(F32).T.astype(BF16)
     image = None
-    for k, (other, col_sq, mask_ref, lane) in enumerate(columns):
-        count = other.shape[0]
-        mask = mask_ref[:, lane : lane + count]
+    for k, (other, col_sq, mask) in enumerate(columns):
         tiles = mask.shape[0] // 2
         gram2 = contract(doubled, other[:, :features], ((1,), (1,)))
         kernel = jnp.exp(-inverse * jnp.maximum(row_sq + col_sq - gram2, 0.0))
@@ -103,69 +116,77 @@
     return image
 
 
-def with_masks(pieces, sq_rows, masks, first):
-    per_half = len(pieces) // 2
-    return [
-        (p[...], sq, masks.at[first + k // per_half], (k % per_half) * p.shape[0])
-        for k, (p, sq) in enumerate(zip(pieces, sq_rows))
-    ]
-
-
-def self_body(inverse, masks, o0, o1, x0, x1, image, sq):
-    pieces = (o0, o1, x0, x1)
-    size, width = o0.shape
-    rows = [as_row(squares(p[...], width - TILE)) for p in pieces]
-    for k, row in enumerate(rows):
-        sq[k : k + 1] = row
-    columns = with_masks(pieces, rows, masks, SELF)
-    for k, piece in enumerate((o0, o1)):
-        image[k * size : (k + 1) * size] = products(inverse[0], piece[...], k * size // TILE, columns, None)
-
-
-def below_body(part, inverse, masks, sq, x, o0, o1, x0, x1, *refs):
-    pieces = (o0, o1, x0, x1)
-    back = [r[...] for r in refs[: len(refs) - 5]] or [None] * 4
-    outs = refs[-5:]
-    columns = with_masks(pieces, [sq[k : k + 1] for k in range(4)], masks, BELOW)
-    outs[0][...] = products(inverse[0], x[...], part * x.shape[0] // TILE, columns, back)
-    for out, value in zip(outs[1:], back):
+def store_all(outs, values):
+    for out, value in zip(outs, values):
         out[...] = value
 
 
-def above_first_body(inverse, masks, sq, x, o0, o1, x0, x1, b0, b1, y0, y1, t0, t1, t2, t3, image, below_sq, *outs):
-    size, width = x.shape
-    below = (b0, b1, y0, y1)
-    rows = [as_row(squares(p[...], width - TILE)) for p in below]
-    for k, row in enumerate(rows):
-        below_sq[k : k + 1] = row
-    columns = with_masks((o0, o1, x0, x1), [sq[k : k + 1] for k in range(4)], masks, ABOVE_OWN)
-    columns += with_masks(below, rows, masks, ABOVE_BELOW)
+def self_body(inverse, sub, own, other, image, sq):
+    rows = square_rows((own, other), sq)
+    size = rows[0].shape[1]
+    masks = [pair_mask(sub[0], marks(own, size), marks(r, size), OWN, h) for h, r in enumerate((own, other))]
+    columns = columns_of((own, other), rows, masks)
+    for k, piece in enumerate(pieces(own)):
+        image[k * size : (k + 1) * size] = products(inverse[0], piece, k * size // TILE, columns, None)
+
+
+def below_first_body(inverse, sub, sq, x, own, other, image, masks_out, *outs):
+    size = x.shape[0] - MARK
+    masks = [pair_mask(sub[0], marks(x, size), marks(r, size), BELOW, h) for h, r in enumerate((own, other))]
+    back = [None] * 4
+    image[...] = products(inverse[0], x[:size], 0, columns_of((own, other), read_rows(sq), masks), back)
+    store_all_at(masks_out, masks)
+    store_all(outs, back)
+
+
+def store_all_at(ref, values):
+    for k, value in enumerate(values):
+        ref[k] = value
+
+
+def below_last_body(inverse, masks, sq, x, own, other, t0, t1, t2, t3, image, *outs):
+    back = [t0[...], t1[...], t2[...], t3[...]]
+    columns = columns_of((own, other), read_rows(sq), [masks[0], masks[1]])
+    image[...] = products(inverse[0], x[...], x.shape[0] // TILE, columns, back)
+    store_all(outs, back)
+
+
+def above_first_body(inverse, sub, sq, x, own, other, below, below_other, t0, t1, t2, t3, image, below_sq, masks_out, *outs):
+    rows = square_rows((below, below_other), below_sq)
+    size = x.shape[0] - MARK
+    mine = marks(x, size)
+    masks = [pair_mask(sub[0], mine, marks(r, size), ABOVE, h) for h, r in enumerate((own, other))]
+    masks += [pair_mask(sub[0], mine, marks(r, size), ABOVE - BELOW, h) for h, r in enumerate((below, below_other))]
+    columns = columns_of((own, other), read_rows(sq), masks[:2]) + columns_of((below, below_other), rows, masks[2:])
     back = [t0[...], t1[...], t2[...], t3[...]] + [None] * 4
-    image[...] = products(inverse[0], x[...], 0, columns, back)
-    for out, value in zip(outs, back):
-        out[...] = value
-
-
-def above_below_body(inverse, masks, below_sq, x, b0, b1, y0, y1, t0, t1, t2, t3, i0, i1, image, own, cross):
+    image[...] = products(inverse[0], x[:size], 0, columns, back)
+    store_all_at(masks_out, masks)
+    store_all(outs, back)
+
+
+def above_last(inverse, sq, x, blocks, masks, sums, own, cross, images):
     size = x.shape[0]
-    columns = with_masks((b0, b1, y0, y1), [below_sq[k : k + 1] for k in range(4)], masks, ABOVE_BELOW)
-    back = [t0[...], t1[...], t2[...], t3[...]]
-    image[...] = products(inverse[0], x[...], size // TILE, columns, back)
-    own[:size] = i0[...] + back[0].T
-    own[size:] = i1[...] + back[1].T
+    back = [t[...] for t in sums]
+    image = products(inverse, x[...], size // TILE, columns_of(blocks, read_rows(sq), masks), back)
+    own[:size] = images[0] + back[0].T
+    own[size:] = images[1] + back[1].T
     cross[:size] = back[2].T
     cross[size:] = back[3].T
-
-
-def above_own_body(inverse, masks, sq, x, o0, o1, x0, x1, t0, t1, t2, t3, self_image, above_image, image, own, cross):
+    return image
+
+
+def above_below_body(inverse, masks, below_sq, x, below, below_other, t0, t1, t2, t3, i0, i1, image, own, cross):
+    image[...] = above_last(
+        inverse[0], below_sq, x, (below, below_other), [masks[2], masks[3]], (t0, t1, t2, t3), own, cross, (i0[...], i1[...])
+    )
+
+
+def above_own_body(inverse, masks, sq, x, own_block, other, t0, t1, t2, t3, self_image, above_image, image, own, cross):
     size = x.shape[0]
-    columns = with_masks((o0, o1, x0, x1), [sq[k : k + 1] for k in range(4)], masks, ABOVE_OWN)
-    back = [t0[...], t1[...], t2[...], t3[...]]
-    image[...] = above_image[...] + products(inverse[0], x[...], size // TILE, columns, back)
-    own[:size] = self_image[:size] + back[0].T
-    own[size:] = self_image[size:] + back[1].T
-    cross[:size] = back[2].T
-    cross[size:] = back[3].T
+    image[...] = above_image[...] + above_last(
+        inverse[0], sq, x, (own_block, other), [masks[0], masks[1]], (t0, t1, t2, t3), own, cross,
+        (self_image[:size], self_image[size:]),
+    )
 
 
 def gram_body(own, cross, below, above0, above1, image, gram):
@@ -247,34 +268,54 @@
     blk_route = lambda v, to: lax.ppermute(v, "blk", [(i, to(i) % n_blk) for i in range(n_blk)])
     blk_move = lambda v, by: blk_route(v, lambda i: i + by)
 
-    own = [jnp.concatenate([embeddings[i : i + size], start_panel[i : i + size]], axis=1) for i in (0, size)]
-    mask = tile_mask.astype(F32)
-    own_mask = jnp.concatenate([mask, sub_move(mask)], axis=0)
-    if n_blk == 8:
-        swapped = blk_route(own[1], lambda i: i ^ 1)
-        below = [blk_move(own[0], 1), blk_route(swapped, lambda i: i if i & 1 else i + 2)]
-    else:
-        below = [blk_move(own[0], 1), blk_move(own[1], 1)]
-    above = [blk_move(own[0], -2), blk_move(own[1], -2)]
-    other = [sub_move(own[0]), sub_move(own[1])]
-    below_mask, above_mask = blk_move(own_mask, 1), blk_move(own_mask, -2)
+    mark = jnp.pad(tile_mask.astype(BF16), ((0, MARK - tiles), (0, embeddings.shape[1] + width - tile_mask.shape[1])))
+    pack = lambda rows: jnp.concatenate([embeddings[rows], start_panel[rows]], axis=1)
+    first, last = jnp.concatenate([pack(slice(0, size)), mark], axis=0), pack(slice(size, half))
+    own = jnp.concatenate([first, last], axis=0)
+    after = lambda v, *earlier: lax.optimization_barrier((v, *earlier))[0]
     sub = lax.axis_index("sub").astype(jnp.int32).reshape(1)
-    masks = vmem_call(mask_body, shape(len(PAIRS), 2 * tiles, half), sub, own_mask, below_mask, above_mask, scalars=1)
-
+    relayed = n_blk == 8
+    swapped = blk_route(last, lambda i: i ^ 1) if relayed else last
+    above0 = blk_move(first, -2)
+    other = sub_move(own)
     image = shape(size, width)
     turned = (shape(width, size),) * 4
     sq_rows = shape(4, size)
-    block = own + other
-    self_image, sq = vmem_call(self_body, (shape(half, width), sq_rows), inv_width, masks, *block, scalars=1)
-    below_image, back = [], []
-    for part in range(2):
-        out, *back = vmem_call(
-            functools.partial(below_body, part), (image, *turned), inv_width, masks, sq, below[part], *block, *back, scalars=1
-        )
-        below_image.append(out)
-    below += [sub_move(below[0]), sub_move(below[1])]
-    above_image0, below_sq, *back = vmem_call(
-        above_first_body, (image, sq_rows, *turned, *turned), inv_width, masks, sq, above[0], *block, *below, *back, scalars=1
+    mask_of = lambda count: shape(count, 2 * tiles, half)
+    self_image, sq = vmem_call(self_body, (shape(half, width), sq_rows), inv_width, sub, own, other, scalars=2)
+    below0 = blk_move(after(first, swapped, above0, self_image), 1)
+    swapped = after(swapped, above0, self_image)
+    below1 = blk_route(swapped, lambda i: i if i & 1 else i + 2) if relayed else blk_move(swapped, 1)
+    below = jnp.concatenate([below0, below1], axis=0)
+    below_other = sub_move(below)
+    above1 = blk_move(after(last, below0, below1), -2)
+    below_image0, masks, *back = vmem_call(
+        below_first_body,
+        (image, mask_of(2), *turned),
+        inv_width,
+        sub,
+        sq,
+        after(below0, below_other),
+        own,
+        other,
+        scalars=2,
+    )
+    below_image1, *back = vmem_call(
+        below_last_body, (image, *turned), inv_width, masks, sq, below1, own, other, *back, scalars=1
+    )
+    above_image0, below_sq, masks, *back = vmem_call(
+        above_first_body,
+        (image, sq_rows, mask_of(4), *turned, *turned),
+        inv_width,
+        sub,
+        sq,
+        above0,
+        own,
+        other,
+        below,
+        below_other,
+        *back,
+        scalars=2,
     )
     above_image0 = blk_move(above_image0, 2)
     above_image1, below_image, below_cross = vmem_call(
@@ -283,10 +324,12 @@
         inv_width,
         masks,
         below_sq,
-        above[1],
-        *below,
+        after(above1, above_image0),
+        below,
+        below_other,
         *back[4:],
-        *below_image,
+        below_image0,
+        below_image1,
         scalars=1,
     )
     below_image = blk_move(below_image + sub_move(below_cross), -1)
@@ -296,8 +339,9 @@
         inv_width,
         masks,
         sq,
-        above[1],
-        *block,
+        above1,
+        own,
+        other,
         *back[:4],
         self_image,
         above_image1,

time: 119 us -> 103 us (0.87)
  waiting for transfers between devices: 72.6 us -> 60.6 us
  starting transfers between devices: 18.1 us -> 13.5 us
  Pallas kernels: 25.4 us -> 22.5 us
  other arithmetic: 0.17 us -> 2.61 us
    ppermute x13 -> x11, waiting for transfers between devices: 69.8 us -> 56.6 us  [per_device(): lax.ppermute(v, 'blk', [(i, to(i) % n_blk) for i in range(n_blk)])]
    ppermute x13 -> x11, starting transfers between devices: 16.4 us -> 12.2 us  [per_device(): lax.ppermute(v, 'blk', [(i, to(i) % n_blk) for i in range(n_blk)])]
    pallas_call x9 -> x8, Pallas kernels: 25.4 us -> 22.5 us  [vmem_call(): pl.pallas_call(body, out_shape=out_shapes, in_specs=[in_smem] * scalars +...]
    concatenate x3, other arithmetic: 0.1 us -> 1.85 us  [the longest x1 0.9 us: per_device(): jnp.concatenate([pack(slice(0, size)), mark], axis=0)]
    ppermute x8 -> x5, waiting for transfers between devices: 2.74 us -> 4.03 us  [per_device(): sub_move = lambda v: lax.ppermute(v, 'sub', [(0, 1), (1, 0)])]
  transfers between devices with their start and end apart: 21 -> 16, of which waited for: 12 -> 11; matrix products, arithmetic and copies ran while one was open for 0% -> 2% of each run, Pallas kernels for 14% -> 14%
where the time goes in v3:
time: 103 us
  waiting for transfers between devices  60.6 us (59%)
  Pallas kernels  22.5 us (22%)
  starting transfers between devices  13.5 us (13%)
  other arithmetic  2.61 us (3%)
  local copies, waits for them, and re-layouts  2.28 us (2%)
  between operations  1.47 us (1%)
    ppermute x11, waiting for transfers between devices, per_device(): lax.ppermute(v, 'blk', [(i, to(i) % n_blk) for i in range(n_blk)])  56.6 us
    pallas_call x8, Pallas kernels, vmem_call(): pl.pallas_call(body, out_shape=out_shapes, in_specs=[in_smem] * scalars +...  22.5 us
    ppermute x11, starting transfers between devices, per_device(): lax.ppermute(v, 'blk', [(i, to(i) % n_blk) for i in range(n_blk)])  12.2 us
    ppermute x5, waiting for transfers between devices, per_device(): sub_move = lambda v: lax.ppermute(v, 'sub', [(0, 1), (1, 0)])  4.03 us
  transfers between devices with their start and end apart: 16, of which 11 were waited for; matrix products, arithmetic and copies ran while one was open for 2% of the time, Pallas kernels for 14%

profile of v3, /device:TPU:0, one launch (start us, length us, event | category | flops | bytes accessed | tf_op | source)
XLA Modules:
  0.0 103.0 jit_solution(11461641079496414990)
XLA Ops:
  0.6 0.7 convert_element_type.5
  1.3 0.9 fusion.1
  2.2 1.3 %fusion = (bf16[256,1024]{1,0:T(8,128)(2,1)S(1)}, bf16[256,1024]{1,0:T(8,128)(2,1)S(1)}) fusion(bf16[512,1024]{1,0:T(8,128)(2,1)} %param.4), kind=kLoop, calls=%fused_computation.5 | loop fusion | bytes 2097152 | tf_op jit(solution)/shard_map/slice | solution.py:272
  3.6 0.5 collective-permute-start
  4.1 0.9 pad_maximum_fusion
  5.0 4.6 %collective-permute-start.1 = (bf16[264,1152]{1,0:T(8,128)(2,1)}, bf16[264,1152]{1,0:T(8,128)(2,1)S(1)}, u32[]{:S(2)}, u32[]{:S(2)}) collective-permute-start(bf16[264,1152]{1,0:T(8,128)(2,1)} %pad_maximum_fusion), channel_id=1, source_target_pairs={{0,12},{2,14},{4,0},{6,2},{8,4},{10,6},{12,8},{14,10},{1,13},{3,15... | collective-permute-start | bytes 1824776 | tf_op jit(solution)/shard_map/ppermute | solution.py:268
  9.6 0.9 pad_maximum_fusion.1
  10.5 1.5 %collective-permute-start.2 = (bf16[256,1152]{1,0:T(8,128)(2,1)}, bf16[256,1152]{1,0:T(8,128)(2,1)}, u32[]{:S(2)}, u32[]{:S(2)}) collective-permute-start(bf16[256,1152]{1,0:T(8,128)(2,1)} %pad_maximum_fusion.1), channel_id=1, source_target_pairs={{0,2},{2,0},{4,6},{6,4},{8,10},{10,8},{12,14},{14,12},{1,3},{3,1},... | collective-permute-start | bytes 1769480 | tf_op jit(solution)/shard_map/ppermute | solution.py:268
  12.6 3.0 %shard_map.59 = (f32[512,128]{1,0:T(8,128)S(1)}, f32[4,256]{1,0:T(4,128)S(1)}) custom-call(f32[1]{0:T(128)S(6)} %copy.7.inverse, s32[1]{0:T(128)} %bitcast.sub, bf16[520,1152]{1,0:T(8,128)(2,1)S(1)} %maximum_maximum_fusion.own.own_block, bf16[520,1152]{1,0:T(8,128)(2,1)S(1)} %collective-permute-done.other), custom_call_target="tpu_custom_call" | custom-call | tf_op jit(solution)/shard_map/pallas_call | solution.py:20
  15.7 10.6 %collective-permute-done.2 = bf16[256,1152]{1,0:T(8,128)(2,1)} collective-permute-done((bf16[256,1152]{1,0:T(8,128)(2,1)}, bf16[256,1152]{1,0:T(8,128)(2,1)}, u32[]{:S(2)}, u32[]{:S(2)}) %collective-permute-start.2) | collective-permute-done | bytes 589856 | tf_op jit(solution)/shard_map/ppermute | solution.py:268
  26.2 1.5 %collective-permute-start.3 = (bf16[264,1152]{1,0:T(8,128)(2,1)}, bf16[264,1152]{1,0:T(8,128)(2,1)S(1)}, u32[]{:S(2)}, u32[]{:S(2)}) collective-permute-start(bf16[264,1152]{1,0:T(8,128)(2,1)} %pad_maximum_fusion), channel_id=1, source_target_pairs={{0,2},{2,4},{4,6},{6,8},{8,10},{10,12},{12,14},{14,0},{1,3},{3,5},... | collective-permute-start | bytes 1824776 | tf_op jit(solution)/shard_map/ppermute | solution.py:268
  27.7 1.9 %collective-permute-start.4 = (bf16[256,1152]{1,0:T(8,128)(2,1)}, bf16[256,1152]{1,0:T(8,128)(2,1)S(1)}, u32[]{:S(2)}, u32[]{:S(2)}) collective-permute-start(bf16[256,1152]{1,0:T(8,128)(2,1)} %collective-permute-done.2), channel_id=1, source_target_pairs={{0,4},{2,2},{4,8},{6,6},{8,12},{10,10},{12,0},{14,14},{1,5},{3,3},... | collective-permute-start | bytes 1769480 | tf_op jit(solution)/shard_map/ppermute | solution.py:268
  29.7 14.5 %collective-permute-done.3.x = bf16[264,1152]{1,0:T(8,128)(2,1)S(1)} collective-permute-done((bf16[264,1152]{1,0:T(8,128)(2,1)}, bf16[264,1152]{1,0:T(8,128)(2,1)S(1)}, u32[]{:S(2)}, u32[]{:S(2)}) %collective-permute-start.3) | collective-permute-done | bytes 608288 | tf_op jit(solution)/shard_map/ppermute | solution.py:268
  44.2 1.7 %collective-permute-done.4.x = bf16[256,1152]{1,0:T(8,128)(2,1)S(1)} collective-permute-done((bf16[256,1152]{1,0:T(8,128)(2,1)}, bf16[256,1152]{1,0:T(8,128)(2,1)S(1)}, u32[]{:S(2)}, u32[]{:S(2)}) %collective-permute-start.4) | collective-permute-done | bytes 589856 | tf_op jit(solution)/shard_map/ppermute | solution.py:268
  46.2 2.8 %collective-permute-done.5.below_other = bf16[520,1152]{1,0:T(8,128)(2,1)S(1)} collective-permute-done((bf16[520,1152]{1,0:T(8,128)(2,1)S(1)}, bf16[520,1152]{1,0:T(8,128)(2,1)S(1)}, u32[]{:S(2)}, u32[]{:S(2)}) %collective-permute-start.5) | collective-permute-done | bytes 1198112 | tf_op jit(solution)/shard_map/ppermute | solution.py:267
  49.0 2.2 %shard_map.60 = (f32[256,128]{1,0:T(8,128)S(1)}, f32[2,8,512]{2,1,0:T(8,128)S(1)}, f32[128,256]{1,0:T(8,128)S(1)}, f32[128,256]{1,0:T(8,128)S(1)}, f32[128,256]{1,0:T(8,128)S(1)}, /*index=5*/f32[128,256]{1,0:T(8,128)S(1)}) custom-call(f32[1]{0:T(128)S(6)} %copy.7.inverse, s32[1]{0:T(128)} %bitcast.sub, f32[4,256]{1,0:T(4,128)S(1)} %get-tuple-element.39.sq, ...), custom_call_target="tpu_custom_call" | custom-call | tf_op jit(solution)/shard_map/pallas_call | solution.py:20
  51.2 2.1 %shard_map.61 = (f32[256,128]{1,0:T(8,128)S(1)}, f32[128,256]{1,0:T(8,128)S(1)}, f32[128,256]{1,0:T(8,128)S(1)}, f32[128,256]{1,0:T(8,128)S(1)}, f32[128,256]{1,0:T(8,128)S(1)}) custom-call(f32[1]{0:T(128)S(6)} %copy.7.inverse, f32[2,8,512]{2,1,0:T(8,128)S(1)} %get-tuple-element.44.masks, f32[4,256]{1,0:T(4,128)S(1)} %get-tuple-element.39.sq, ...), custom_call_target="tpu_custom_call" | custom-call | tf_op jit(solution)/shard_map/pallas_call | solution.py:20
  53.3 5.4 %shard_map.62 = (f32[256,128]{1,0:T(8,128)S(1)}, f32[4,256]{1,0:T(4,128)S(1)}, f32[4,8,512]{2,1,0:T(8,128)S(1)}, f32[128,256]{1,0:T(8,128)S(1)}, f32[128,256]{1,...) custom-call(f32[1]{0:T(128)S(6)} %copy.7.inverse, ...), custom_call_target="tpu_custom_call" | custom-call | tf_op jit(solution)/shard_map/pallas_call | solution.py:20
  58.7 3.4 %collective-permute-done.6.x = bf16[256,1152]{1,0:T(8,128)(2,1)S(1)} collective-permute-done((bf16[256,1152]{1,0:T(8,128)(2,1)}, bf16[256,1152]{1,0:T(8,128)(2,1)S(1)}, u32[]{:S(2)}, u32[]{:S(2)}) %collective-permute-start.6) | collective-permute-done | bytes 589856 | tf_op jit(solution)/shard_map/ppermute | solution.py:268
  62.1 4.0 %collective-permute-done.7.above0 = f32[256,128]{1,0:T(8,128)S(1)} collective-permute-done((f32[256,128]{1,0:T(8,128)S(1)}, f32[256,128]{1,0:T(8,128)S(1)}, u32[]{:S(2)}, u32[]{:S(2)}) %collective-permute-start.7) | collective-permute-done | bytes 131104 | tf_op jit(solution)/shard_map/ppermute | solution.py:268
  66.0 2.1 %shard_map.63 = (f32[256,128]{1,0:T(8,128)S(1)}, f32[512,128]{1,0:T(8,128)S(1)}, f32[512,128]{1,0:T(8,128)S(1)}) custom-call(f32[1]{0:T(128)S(6)} %copy.7.inverse, f32[4,8,512]{2,1,0:T(8,128)S(1)} %get-tuple-element.53.masks, f32[4,256]{1,0:T(4,128)S(1)} %get-tuple-element.59.below_sq, bf16[256,1152]{1,0:T(8,128)(2,1)S(1)} %collective-permute-done.6.x, ...), custom_call_target="tpu_custom_call" | custom-call | tf_op jit(solution)/shard_map/pallas_call | solution.py:20
  68.2 2.1 %shard_map.64 = (f32[256,128]{1,0:T(8,128)S(1)}, f32[512,128]{1,0:T(8,128)S(1)}, f32[512,128]{1,0:T(8,128)S(1)}) custom-call(f32[1]{0:T(128)S(6)} %copy.7.inverse, f32[4,8,512]{2,1,0:T(8,128)S(1)} %get-tuple-element.53.masks, f32[4,256]{1,0:T(4,128)S(1)} %get-tuple-element.39.sq, bf16[256,1152]{1,0:T(8,128)(2,1)S(1)} %collective-permute-done.6.x, ...), custom_call_target="tpu_custom_call" | custom-call | tf_op jit(solution)/shard_map/pallas_call | solution.py:20
  70.4 0.6 collective-permute-start.8
  71.3 10.1 %collective-permute-done.11.above1 = f32[256,128]{1,0:T(8,128)S(1)} collective-permute-done((f32[256,128]{1,0:T(8,128)S(1)}, f32[256,128]{1,0:T(8,128)S(1)}, u32[]{:S(2)}, u32[]{:S(2)}) %collective-permute-start.11) | collective-permute-done | bytes 131104 | tf_op jit(solution)/shard_map/ppermute | solution.py:268
  81.4 0.4 shard_map.65
  82.0 1.2 %collective-permute-done.12 = f32[128,128]{1,0:T(8,128)S(1)} collective-permute-done((f32[128,128]{1,0:T(8,128)S(1)}, f32[128,128]{1,0:T(8,128)S(1)}, u32[]{:S(2)}, u32[]{:S(2)}) %collective-permute-start.12) | collective-permute-done | bytes 65568 | tf_op jit(solution)/shard_map/ppermute | solution.py:267
  83.3 4.3 %collective-permute-done.13 = f32[128,128]{1,0:T(8,128)S(1)} collective-permute-done((f32[128,128]{1,0:T(8,128)S(1)}, f32[128,128]{1,0:T(8,128)S(1)}, u32[]{:S(2)}, u32[]{:S(2)}) %collective-permute-start.13) | collective-permute-done | bytes 65568 | tf_op jit(solution)/shard_map/ppermute | solution.py:268
  87.5 1.2 %collective-permute-start.14 = (f32[128,128]{1,0:T(8,128)S(1)}, f32[128,128]{1,0:T(8,128)S(1)}, u32[]{:S(2)}, u32[]{:S(2)}) collective-permute-start(f32[128,128]{1,0:T(8,128)S(1)} %add.19), channel_id=1, source_target_pairs={{0,4},{2,6},{4,0},{6,2},{8,12},{10,14},{12,8},{14,10},{1,5},{3,7},... | collective-permute-start | bytes 196616 | tf_op jit(solution)/shard_map/ppermute | solution.py:268
  88.8 3.1 %collective-permute-done.14 = f32[128,128]{1,0:T(8,128)S(1)} collective-permute-done((f32[128,128]{1,0:T(8,128)S(1)}, f32[128,128]{1,0:T(8,128)S(1)}, u32[]{:S(2)}, u32[]{:S(2)}) %collective-permute-start.14) | collective-permute-done | bytes 65568 | tf_op jit(solution)/shard_map/ppermute | solution.py:268
  91.9 1.0 collective-permute-start.15
  92.9 4.9 %collective-permute-done.15 = f32[128,128]{1,0:T(8,128)S(1)} collective-permute-done((f32[128,128]{1,0:T(8,128)S(1)}, f32[128,128]{1,0:T(8,128)S(1)}, u32[]{:S(2)}, u32[]{:S(2)}) %collective-permute-start.15) | collective-permute-done | bytes 65568 | tf_op jit(solution)/shard_map/ppermute | solution.py:268
  97.8 5.2 %shard_map.66 = (f32[512,128]{1,0:T(8,128)}, f32[128,128]{1,0:T(8,128)}) custom-call(f32[512,128]{1,0:T(8,128)S(1)} %get-tuple-element.74.image, f32[128,128]{1,0:T(8,128)S(1)} %add.21.gram), custom_call_target="tpu_custom_call" | custom-call | tf_op jit(solution)/shard_map/pallas_call | solution.py:20
  (26 shorter events, 1.0 us)
Async XLA Ops:
  3.6 9.0 %collective-permute-start = (bf16[520,1152]{1,0:T(8,128)(2,1)S(1)}, bf16[520,1152]{1,0:T(8,128)(2,1)S(1)}, u32[]{:S(2)}, u32[]{:S(2)}) collective-permute-start(bf16[520,1152]{1,0:T(8,128)(2,1)S(1)} %maximum_maximum_fusion.own.own_block), channel_id=1, source_target_pairs={{0,1},{1,0},{2,3},{3,2},{4,5},{5,4},{6,7},{7,6},{8,9},{9,8},{10,11... | collective-permute-start | bytes 3594248 | tf_op jit(solution)/shard_map/ppermute | solution.py:267
  5.0 21.2 %collective-permute-start.1 = (bf16[264,1152]{1,0:T(8,128)(2,1)}, bf16[264,1152]{1,0:T(8,128)(2,1)S(1)}, u32[]{:S(2)}, u32[]{:S(2)}) collective-permute-start(bf16[264,1152]{1,0:T(8,128)(2,1)} %pad_maximum_fusion), channel_id=1, source_target_pairs={{0,12},{2,14},{4,0},{6,2},{8,4},{10,6},{12,8},{14,10},{1,13},{3,15... | collective-permute-start | bytes 1824776 | tf_op jit(solution)/shard_map/ppermute | solution.py:268
  10.5 15.8 %collective-permute-start.2 = (bf16[256,1152]{1,0:T(8,128)(2,1)}, bf16[256,1152]{1,0:T(8,128)(2,1)}, u32[]{:S(2)}, u32[]{:S(2)}) collective-permute-start(bf16[256,1152]{1,0:T(8,128)(2,1)} %pad_maximum_fusion.1), channel_id=1, source_target_pairs={{0,2},{2,0},{4,6},{6,4},{8,10},{10,8},{12,14},{14,12},{1,3},{3,1},... | collective-permute-start | bytes 1769480 | tf_op jit(solution)/shard_map/ppermute | solution.py:268
  26.2 17.9 %collective-permute-start.3 = (bf16[264,1152]{1,0:T(8,128)(2,1)}, bf16[264,1152]{1,0:T(8,128)(2,1)S(1)}, u32[]{:S(2)}, u32[]{:S(2)}) collective-permute-start(bf16[264,1152]{1,0:T(8,128)(2,1)} %pad_maximum_fusion), channel_id=1, source_target_pairs={{0,2},{2,4},{4,6},{6,8},{8,10},{10,12},{12,14},{14,0},{1,3},{3,5},... | collective-permute-start | bytes 1824776 | tf_op jit(solution)/shard_map/ppermute | solution.py:268
  27.7 18.2 %collective-permute-start.4 = (bf16[256,1152]{1,0:T(8,128)(2,1)}, bf16[256,1152]{1,0:T(8,128)(2,1)S(1)}, u32[]{:S(2)}, u32[]{:S(2)}) collective-permute-start(bf16[256,1152]{1,0:T(8,128)(2,1)} %collective-permute-done.2), channel_id=1, source_target_pairs={{0,4},{2,2},{4,8},{6,6},{8,12},{10,10},{12,0},{14,14},{1,5},{3,3},... | collective-permute-start | bytes 1769480 | tf_op jit(solution)/shard_map/ppermute | solution.py:268
  46.0 2.9 %collective-permute-start.5 = (bf16[520,1152]{1,0:T(8,128)(2,1)S(1)}, bf16[520,1152]{1,0:T(8,128)(2,1)S(1)}, u32[]{:S(2)}, u32[]{:S(2)}) collective-permute-start(bf16[520,1152]{1,0:T(8,128)(2,1)S(1)} %constant_dynamic-update-slice_fusion.below), channel_id=1, source_target_pairs={{0,1},{1,0},{2,3},{3,2},{4,5},{5,4},{6,7},{7,6},{8,9},{9,8},{10,11... | collective-permute-start | bytes 3594248 | tf_op jit(solution)/shard_map/ppermute | solution.py:267
  46.1 15.9 %collective-permute-start.6 = (bf16[256,1152]{1,0:T(8,128)(2,1)}, bf16[256,1152]{1,0:T(8,128)(2,1)S(1)}, u32[]{:S(2)}, u32[]{:S(2)}) collective-permute-start(bf16[256,1152]{1,0:T(8,128)(2,1)} %pad_maximum_fusion.1), channel_id=1, source_target_pairs={{0,12},{2,14},{4,0},{6,2},{8,4},{10,6},{12,8},{14,10},{1,13},{3,15... | collective-permute-start | bytes 1769480 | tf_op jit(solution)/shard_map/ppermute | solution.py:268
  49.0 2.2 %copy-start = (bf16[520,1152]{1,0:T(8,128)(2,1)}, bf16[520,1152]{1,0:T(8,128)(2,1)S(1)}, u32[]{:S(2)}) copy-start(bf16[520,1152]{1,0:T(8,128)(2,1)S(1)} %collective-permute-done.5.below_other) | copy-start | bytes 3594244
  53.2 12.8 %copy-start.1 = (bf16[520,1152]{1,0:T(8,128)(2,1)S(1)}, bf16[520,1152]{1,0:T(8,128)(2,1)}, u32[]{:S(2)}) copy-start(bf16[520,1152]{1,0:T(8,128)(2,1)} %copy-done) | copy-start | bytes 3594244
  58.7 7.4 %collective-permute-start.7 = (f32[256,128]{1,0:T(8,128)S(1)}, f32[256,128]{1,0:T(8,128)S(1)}, u32[]{:S(2)}, u32[]{:S(2)}) collective-permute-start(f32[256,128]{1,0:T(8,128)S(1)} %get-tuple-element.60), channel_id=1, source_target_pairs={{0,4},{2,6},{4,8},{6,10},{8,12},{10,14},{12,0},{14,2},{1,5},{3,7},... | collective-permute-start | bytes 393224 | tf_op jit(solution)/shard_map/ppermute | solution.py:268
  68.2 2.8 %collective-permute-start.9 = (f32[512,128]{1,0:T(8,128)S(1)}, f32[512,128]{1,0:T(8,128)S(1)}, u32[]{:S(2)}, u32[]{:S(2)}) collective-permute-start(f32[512,128]{1,0:T(8,128)S(1)} %get-tuple-element.72), channel_id=1, source_target_pairs={{0,1},{1,0},{2,3},{3,2},{4,5},{5,4},{6,7},{7,6},{8,9},{9,8},{10,11... | collective-permute-start | bytes 786440 | tf_op jit(solution)/shard_map/ppermute | solution.py:267
  70.4 11.1 %collective-permute-start.8 = (f32[512,128]{1,0:T(8,128)S(1)}, f32[512,128]{1,0:T(8,128)S(1)}, u32[]{:S(2)}, u32[]{:S(2)}) collective-permute-start(f32[512,128]{1,0:T(8,128)S(1)} %get-tuple-element.70), channel_id=1, source_target_pairs={{0,1},{1,0},{2,3},{3,2},{4,5},{5,4},{6,7},{7,6},{8,9},{9,8},{10,11... | collective-permute-start | bytes 786440 | tf_op jit(solution)/shard_map/ppermute | solution.py:267
  71.0 10.5 %collective-permute-start.10 = (f32[512,128]{1,0:T(8,128)S(1)}, f32[512,128]{1,0:T(8,128)S(1)}, u32[]{:S(2)}, u32[]{:S(2)}) collective-permute-start(f32[512,128]{1,0:T(8,128)S(1)} %add.17), channel_id=1, source_target_pairs={{0,14},{2,0},{4,2},{6,4},{8,6},{10,8},{12,10},{14,12},{1,15},{3,1}... | collective-permute-start | bytes 786440 | tf_op jit(solution)/shard_map/ppermute | solution.py:268
  71.2 10.2 %collective-permute-start.11 = (f32[256,128]{1,0:T(8,128)S(1)}, f32[256,128]{1,0:T(8,128)S(1)}, u32[]{:S(2)}, u32[]{:S(2)}) collective-permute-start(f32[256,128]{1,0:T(8,128)S(1)} %get-tuple-element.73), channel_id=1, source_target_pairs={{0,4},{2,6},{4,8},{6,10},{8,12},{10,14},{12,0},{14,2},{1,5},{3,7},... | collective-permute-start | bytes 393224 | tf_op jit(solution)/shard_map/ppermute | solution.py:268
  81.9 1.3 %collective-permute-start.12 = (f32[128,128]{1,0:T(8,128)S(1)}, f32[128,128]{1,0:T(8,128)S(1)}, u32[]{:S(2)}, u32[]{:S(2)}) collective-permute-start(f32[128,128]{1,0:T(8,128)S(1)} %get-tuple-element.75), channel_id=1, source_target_pairs={{0,1},{1,0},{2,3},{3,2},{4,5},{5,4},{6,7},{7,6},{8,9},{9,8},{10,11... | collective-permute-start | bytes 196616 | tf_op jit(solution)/shard_map/ppermute | solution.py:267
  83.2 4.3 %collective-permute-start.13 = (f32[128,128]{1,0:T(8,128)S(1)}, f32[128,128]{1,0:T(8,128)S(1)}, u32[]{:S(2)}, u32[]{:S(2)}) collective-permute-start(f32[128,128]{1,0:T(8,128)S(1)} %add.18), channel_id=1, source_target_pairs={{0,2},{2,0},{4,6},{6,4},{8,10},{10,8},{12,14},{14,12},{1,3},{3,1},... | collective-permute-start | bytes 196616 | tf_op jit(solution)/shard_map/ppermute | solution.py:268
  87.5 4.3 %collective-permute-start.14 = (f32[128,128]{1,0:T(8,128)S(1)}, f32[128,128]{1,0:T(8,128)S(1)}, u32[]{:S(2)}, u32[]{:S(2)}) collective-permute-start(f32[128,128]{1,0:T(8,128)S(1)} %add.19), channel_id=1, source_target_pairs={{0,4},{2,6},{4,0},{6,2},{8,12},{10,14},{12,8},{14,10},{1,5},{3,7},... | collective-permute-start | bytes 196616 | tf_op jit(solution)/shard_map/ppermute | solution.py:268
  91.9 5.9 %collective-permute-start.15 = (f32[128,128]{1,0:T(8,128)S(1)}, f32[128,128]{1,0:T(8,128)S(1)}, u32[]{:S(2)}, u32[]{:S(2)}) collective-permute-start(f32[128,128]{1,0:T(8,128)S(1)} %add.20), channel_id=1, source_target_pairs={{0,8},{2,10},{4,12},{6,14},{8,0},{10,2},{12,4},{14,6},{1,9},{3,11}... | collective-permute-start | bytes 196616 | tf_op jit(solution)/shard_map/ppermute | solution.py:268

commit v4 on v3

--- a/solution.py
+++ b/solution.py
@@ -1,5 +1,3 @@
-import functools
-
 import jax
 import jax.numpy as jnp
 from jax import lax
@@ -121,76 +119,75 @@
         out[...] = value
 
 
+def pack_body(embeddings, panel, tile_mask, own, first, last):
+    half, features = embeddings.shape
+    size = half // 2
+    tiles, window = tile_mask.shape
+    at = lax.broadcasted_iota(jnp.int32, (window, TILE), 0) == lax.broadcasted_iota(jnp.int32, (window, TILE), 1)
+    mask = contract(tile_mask[...].astype(F32), at.astype(F32), ((1,), (0,)))
+    mask = jnp.concatenate([mask, jnp.zeros((MARK - tiles, TILE), F32)], axis=0).astype(BF16)
+    for ref in (own, first):
+        ref[:size, :features] = embeddings[:size]
+        ref[:size, features:] = panel[:size]
+        ref[size : size + MARK, :TILE] = mask
+        ref[size : size + MARK, TILE:] = jnp.zeros((MARK, features), BF16)
+    for ref, start in ((own, size + MARK), (last, 0)):
+        ref[start : start + size, :features] = embeddings[size:]
+        ref[start : start + size, features:] = panel[size:]
+
+
+def masks_of(sub, ref, others, offset):
+    size = (ref.shape[0] - MARK) // 2
+    mine = marks(ref, size)
+    return [pair_mask(sub, mine, marks(r, size), offset, h) for h, r in enumerate(others)]
+
+
+def block_products(inverse, block, columns, back):
+    out = []
+    for piece in pieces(block):
+        out.append(products(inverse, piece, len(out) * piece.shape[0] // TILE, columns, back))
+    return out
+
+
 def self_body(inverse, sub, own, other, image, sq):
     rows = square_rows((own, other), sq)
-    size = rows[0].shape[1]
-    masks = [pair_mask(sub[0], marks(own, size), marks(r, size), OWN, h) for h, r in enumerate((own, other))]
-    columns = columns_of((own, other), rows, masks)
-    for k, piece in enumerate(pieces(own)):
-        image[k * size : (k + 1) * size] = products(inverse[0], piece, k * size // TILE, columns, None)
-
-
-def below_first_body(inverse, sub, sq, x, own, other, image, masks_out, *outs):
-    size = x.shape[0] - MARK
-    masks = [pair_mask(sub[0], marks(x, size), marks(r, size), BELOW, h) for h, r in enumerate((own, other))]
+    columns = columns_of((own, other), rows, masks_of(sub[0], own, (own, other), OWN))
+    image[...] = jnp.concatenate(block_products(inverse[0], own, columns, None), axis=0)
+
+
+def above_own_body(inverse, sub, sq, above, own, other, image, *sums):
+    columns = columns_of((own, other), read_rows(sq), masks_of(sub[0], above, (own, other), ABOVE))
     back = [None] * 4
-    image[...] = products(inverse[0], x[:size], 0, columns_of((own, other), read_rows(sq), masks), back)
-    store_all_at(masks_out, masks)
-    store_all(outs, back)
-
-
-def store_all_at(ref, values):
-    for k, value in enumerate(values):
-        ref[k] = value
-
-
-def below_last_body(inverse, masks, sq, x, own, other, t0, t1, t2, t3, image, *outs):
+    image[...] = jnp.concatenate(block_products(inverse[0], above, columns, back), axis=0)
+    store_all(sums, back)
+
+
+def split_back(back, own_rows, own, cross):
+    size = back[0].shape[1]
+    for k in range(2):
+        own[k * size : (k + 1) * size] = own_rows[k] + back[k].T
+        cross[k * size : (k + 1) * size] = back[2 + k].T
+
+
+def below_own_body(inverse, sub, sq, below, own, other, self_image, t0, t1, t2, t3, image, own_image, cross):
+    columns = columns_of((own, other), read_rows(sq), masks_of(sub[0], below, (own, other), BELOW))
     back = [t0[...], t1[...], t2[...], t3[...]]
-    columns = columns_of((own, other), read_rows(sq), [masks[0], masks[1]])
-    image[...] = products(inverse[0], x[...], x.shape[0] // TILE, columns, back)
-    store_all(outs, back)
-
-
-def above_first_body(inverse, sub, sq, x, own, other, below, below_other, t0, t1, t2, t3, image, below_sq, masks_out, *outs):
-    rows = square_rows((below, below_other), below_sq)
-    size = x.shape[0] - MARK
-    mine = marks(x, size)
-    masks = [pair_mask(sub[0], mine, marks(r, size), ABOVE, h) for h, r in enumerate((own, other))]
-    masks += [pair_mask(sub[0], mine, marks(r, size), ABOVE - BELOW, h) for h, r in enumerate((below, below_other))]
-    columns = columns_of((own, other), read_rows(sq), masks[:2]) + columns_of((below, below_other), rows, masks[2:])
-    back = [t0[...], t1[...], t2[...], t3[...]] + [None] * 4
-    image[...] = products(inverse[0], x[:size], 0, columns, back)
-    store_all_at(masks_out, masks)
-    store_all(outs, back)
-
-
-def above_last(inverse, sq, x, blocks, masks, sums, own, cross, images):
-    size = x.shape[0]
-    back = [t[...] for t in sums]
-    image = products(inverse, x[...], size // TILE, columns_of(blocks, read_rows(sq), masks), back)
-    own[:size] = images[0] + back[0].T
-    own[size:] = images[1] + back[1].T
-    cross[:size] = back[2].T
-    cross[size:] = back[3].T
-    return image
-
-
-def above_below_body(inverse, masks, below_sq, x, below, below_other, t0, t1, t2, t3, i0, i1, image, own, cross):
-    image[...] = above_last(
-        inverse[0], below_sq, x, (below, below_other), [masks[2], masks[3]], (t0, t1, t2, t3), own, cross, (i0[...], i1[...])
-    )
-
-
-def above_own_body(inverse, masks, sq, x, own_block, other, t0, t1, t2, t3, self_image, above_image, image, own, cross):
-    size = x.shape[0]
-    image[...] = above_image[...] + above_last(
-        inverse[0], sq, x, (own_block, other), [masks[0], masks[1]], (t0, t1, t2, t3), own, cross,
-        (self_image[:size], self_image[size:]),
-    )
-
-
-def gram_body(own, cross, below, above0, above1, image, gram):
-    total = own[...] + cross[...] + below[...] + jnp.concatenate([above0[...], above1[...]], axis=0)
+    image[...] = jnp.concatenate(block_products(inverse[0], below, columns, back), axis=0)
+    size = back[0].shape[1]
+    split_back(back, (self_image[:size], self_image[size:]), own_image, cross)
+
+
+def above_below_body(inverse, sub, above, below, other, above_image, below_image, image, below_out, cross):
+    rows = [as_row(squares(p, p.shape[1] - TILE)) for block in (below, other) for p in pieces(block)]
+    columns = columns_of((below, other), rows, masks_of(sub[0], above, (below, other), ABOVE - BELOW))
+    back = [None] * 4
+    image[...] = above_image[...] + jnp.concatenate(block_products(inverse[0], above, columns, back), axis=0)
+    size = back[0].shape[1]
+    split_back(back, (below_image[:size], below_image[size:]), below_out, cross)
+
+
+def gram_body(own, cross, below, above, image, gram):
+    total = own[...] + cross[...] + below[...] + above[...]
     image[...] = total
     gram[...] = contract(total, total, ((0,), (0,)), HIGHEST)
 
@@ -262,100 +259,42 @@
 def per_device(embeddings, start_panel, tile_mask, inv_width):
     n_blk = lax.axis_size("blk")
     half, width = start_panel.shape
-    tiles = half // TILE
     size = half // 2
     sub_move = lambda v: lax.ppermute(v, "sub", [(0, 1), (1, 0)])
     blk_route = lambda v, to: lax.ppermute(v, "blk", [(i, to(i) % n_blk) for i in range(n_blk)])
     blk_move = lambda v, by: blk_route(v, lambda i: i + by)
 
-    mark = jnp.pad(tile_mask.astype(BF16), ((0, MARK - tiles), (0, embeddings.shape[1] + width - tile_mask.shape[1])))
-    pack = lambda rows: jnp.concatenate([embeddings[rows], start_panel[rows]], axis=1)
-    first, last = jnp.concatenate([pack(slice(0, size)), mark], axis=0), pack(slice(size, half))
-    own = jnp.concatenate([first, last], axis=0)
     after = lambda v, *earlier: lax.optimization_barrier((v, *earlier))[0]
     sub = lax.axis_index("sub").astype(jnp.int32).reshape(1)
+    wide = embeddings.shape[1] + width
+    packed = lambda rows: jax.ShapeDtypeStruct((rows, wide), BF16)
+    own, first, last = vmem_call(
+        pack_body, (packed(half + MARK), packed(size + MARK), packed(size)), embeddings, start_panel, tile_mask
+    )
     relayed = n_blk == 8
     swapped = blk_route(last, lambda i: i ^ 1) if relayed else last
-    above0 = blk_move(first, -2)
+    above = blk_move(own, -2)
     other = sub_move(own)
-    image = shape(size, width)
-    turned = (shape(width, size),) * 4
+    image = shape(half, width)
     sq_rows = shape(4, size)
-    mask_of = lambda count: shape(count, 2 * tiles, half)
-    self_image, sq = vmem_call(self_body, (shape(half, width), sq_rows), inv_width, sub, own, other, scalars=2)
-    below0 = blk_move(after(first, swapped, above0, self_image), 1)
-    swapped = after(swapped, above0, self_image)
-    below1 = blk_route(swapped, lambda i: i if i & 1 else i + 2) if relayed else blk_move(swapped, 1)
-    below = jnp.concatenate([below0, below1], axis=0)
+    self_image, sq = vmem_call(self_body, (image, sq_rows), inv_width, sub, own, other, scalars=2)
+    first, swapped = after(first, swapped, above, self_image), after(swapped, above, self_image)
+    below = [blk_move(first, 1), blk_route(swapped, lambda i: i if i & 1 else i + 2) if relayed else blk_move(swapped, 1)]
+    above_image, *back = vmem_call(
+        above_own_body, (image, *(shape(width, size),) * 4), inv_width, sub, sq, above, own, other, scalars=2
+    )
+    below = after(jnp.concatenate(below, axis=0), above_image)
     below_other = sub_move(below)
-    above1 = blk_move(after(last, below0, below1), -2)
-    below_image0, masks, *back = vmem_call(
-        below_first_body,
-        (image, mask_of(2), *turned),
-        inv_width,
-        sub,
-        sq,
-        after(below0, below_other),
-        own,
-        other,
-        scalars=2,
-    )
-    below_image1, *back = vmem_call(
-        below_last_body, (image, *turned), inv_width, masks, sq, below1, own, other, *back, scalars=1
-    )
-    above_image0, below_sq, masks, *back = vmem_call(
-        above_first_body,
-        (image, sq_rows, mask_of(4), *turned, *turned),
-        inv_width,
-        sub,
-        sq,
-        above0,
-        own,
-        other,
-        below,
-        below_other,
-        *back,
-        scalars=2,
-    )
-    above_image0 = blk_move(above_image0, 2)
-    above_image1, below_image, below_cross = vmem_call(
-        above_below_body,
-        (image, shape(half, width), shape(half, width)),
-        inv_width,
-        masks,
-        below_sq,
-        after(above1, above_image0),
-        below,
-        below_other,
-        *back[4:],
-        below_image0,
-        below_image1,
-        scalars=1,
-    )
+    below_image, own_image, own_cross = vmem_call(
+        below_own_body, (image,) * 3, inv_width, sub, sq, below, own, other, self_image, *back, scalars=2
+    )
+    above_image, below_image, below_cross = vmem_call(
+        above_below_body, (image,) * 3, inv_width, sub, above, below, below_other, above_image, below_image, scalars=2
+    )
+    above_image = blk_move(above_image, 2)
     below_image = blk_move(below_image + sub_move(below_cross), -1)
-    above_image1, own_image, own_cross = vmem_call(
-        above_own_body,
-        (image, shape(half, width), shape(half, width)),
-        inv_width,
-        masks,
-        sq,
-        above1,
-        own,
-        other,
-        *back[:4],
-        self_image,
-        above_image1,
-        scalars=1,
-    )
-    above_image1 = blk_move(above_image1, 2)
     image, gram = vmem_call(
-        gram_body,
-        (shape(half, width), shape(width, width)),
-        own_image,
-        sub_move(own_cross),
-        below_image,
-        above_image0,
-        above_image1,
+        gram_body, (image, shape(width, width)), own_image, sub_move(own_cross), below_image, above_image
     )
     if n_blk & (n_blk - 1):
         gram = lax.psum(gram, ("blk", "sub"))

time: 103 us -> 101 us (0.981)
  waiting for transfers between devices: 60.6 us -> 53 us
  starting transfers between devices: 13.5 us -> 19.8 us
  other arithmetic: 2.61 us -> 0.16 us
  Pallas kernels: 22.5 us -> 23.7 us
    ppermute x11 -> x9, starting transfers between devices: 12.2 us -> 18.6 us  [per_device(): lax.ppermute(v, 'blk', [(i, to(i) % n_blk) for i in range(n_blk)])]
    ppermute x11 -> x9, waiting for transfers between devices: 56.6 us -> 50.5 us  [per_device(): lax.ppermute(v, 'blk', [(i, to(i) % n_blk) for i in range(n_blk)])]
    unnamed x5 -> x6, local copies, waits for them, and re-layouts: 0.06 us -> 2.8 us
    slice x2 -> x0, local copies, waits for them, and re-layouts: 2.15 us -> none  [the longest x1 1.27 us: per_device(): embeddings[rows]]
    concatenate x3 -> x1, other arithmetic: 1.85 us -> 0.09 us  [per_device(): below = after(jnp.concatenate(below, axis=0), above_image)]
    ppermute x5, waiting for transfers between devices: 4.03 us -> 2.42 us  [per_device(): sub_move = lambda v: lax.ppermute(v, 'sub', [(0, 1), (1, 0)])]
    pallas_call x8 -> x7, Pallas kernels: 22.5 us -> 23.7 us  [vmem_call(): pl.pallas_call(body, out_shape=out_shapes, in_specs=[in_smem] * scalars +...]
  transfers between devices with their start and end apart: 16 -> 14, of which waited for: 11 -> 11; matrix products, arithmetic and copies ran while one was open for 2% -> 0% of each run, Pallas kernels for 14% -> 12%
where the time goes in v4:
time: 101 us
  waiting for transfers between devices  53 us (52%)
  Pallas kernels  23.7 us (23%)
  starting transfers between devices  19.8 us (20%)
  local copies, waits for them, and re-layouts  2.8 us (3%)
  between operations  1.41 us (1%)
    ppermute x9, waiting for transfers between devices, per_device(): lax.ppermute(v, 'blk', [(i, to(i) % n_blk) for i in range(n_blk)])  50.5 us
    pallas_call x7, Pallas kernels, vmem_call(): pl.pallas_call(body, out_shape=out_shapes, in_specs=[in_smem] * scalars +...  23.7 us
    ppermute x9, starting transfers between devices, per_device(): lax.ppermute(v, 'blk', [(i, to(i) % n_blk) for i in range(n_blk)])  18.6 us
    unnamed x6, local copies, waits for them, and re-layouts  2.8 us
    ppermute x5, waiting for transfers between devices, per_device(): sub_move = lambda v: lax.ppermute(v, 'sub', [(0, 1), (1, 0)])  2.42 us
  transfers between devices with their start and end apart: 14, of which 11 were waited for; matrix products, arithmetic and copies ran while one was open for 0% of the time, Pallas kernels for 12%

profile of v4, /device:TPU:0, one launch (start us, length us, event | category | flops | bytes accessed | tf_op | source)
XLA Modules:
  0.0 100.8 jit_solution(4643690336020036637)
XLA Ops:
  0.6 1.2 %copy-done = bf16[512,1024]{1,0:T(8,128)(2,1)S(1)} copy-done((bf16[512,1024]{1,0:T(8,128)(2,1)S(1)}, bf16[512,1024]{1,0:T(8,128)(2,1)}, u32[]{:S(2)}) %copy-start) | copy-done | bytes 1048600
  1.9 0.9 copy-done.1
  2.8 0.7 copy-done.2
  3.4 1.0 shard_map.59
  4.4 0.5 collective-permute-start
  4.9 4.6 %collective-permute-start.2 = (bf16[520,1152]{1,0:T(8,128)(2,1)S(1)}, bf16[520,1152]{1,0:T(8,128)(2,1)}, u32[]{:S(2)}, u32[]{:S(2)}) collective-permute-start(bf16[520,1152]{1,0:T(8,128)(2,1)S(1)} %get-tuple-element.23.own), channel_id=1, source_target_pairs={{0,12},{2,14},{4,0},{6,2},{8,4},{10,6},{12,8},{14,10},{1,13},{3,15... | collective-permute-start | bytes 3594248 | tf_op jit(solution)/shard_map/ppermute | solution.py:264
  9.5 1.5 %collective-permute-start.1 = (bf16[256,1152]{1,0:T(8,128)(2,1)}, bf16[256,1152]{1,0:T(8,128)(2,1)}, u32[]{:S(2)}, u32[]{:S(2)}) collective-permute-start(bf16[256,1152]{1,0:T(8,128)(2,1)} %get-tuple-element.26), channel_id=1, source_target_pairs={{0,2},{2,0},{4,6},{6,4},{8,10},{10,8},{12,14},{14,12},{1,3},{3,1},... | collective-permute-start | bytes 1769480 | tf_op jit(solution)/shard_map/ppermute | solution.py:264
  11.6 3.0 %shard_map.60 = (f32[512,128]{1,0:T(8,128)S(1)}, f32[4,256]{1,0:T(4,128)S(1)}) custom-call(f32[1]{0:T(128)S(6)} %copy.6.inverse, s32[1]{0:T(128)} %bitcast.sub, bf16[520,1152]{1,0:T(8,128)(2,1)S(1)} %get-tuple-element.23.own, bf16[520,1152]{1,0:T(8,128)(2,1)S(1)} %collective-permute-done.other), custom_call_target="tpu_custom_call" | custom-call | tf_op jit(solution)/shard_map/pallas_call | solution.py:18
  14.7 10.6 %collective-permute-done.1 = bf16[256,1152]{1,0:T(8,128)(2,1)} collective-permute-done((bf16[256,1152]{1,0:T(8,128)(2,1)}, bf16[256,1152]{1,0:T(8,128)(2,1)}, u32[]{:S(2)}, u32[]{:S(2)}) %collective-permute-start.1) | collective-permute-done | bytes 589856 | tf_op jit(solution)/shard_map/ppermute | solution.py:264
  25.3 10.5 %collective-permute-done.2.above = bf16[520,1152]{1,0:T(8,128)(2,1)} collective-permute-done((bf16[520,1152]{1,0:T(8,128)(2,1)S(1)}, bf16[520,1152]{1,0:T(8,128)(2,1)}, u32[]{:S(2)}, u32[]{:S(2)}) %collective-permute-start.2) | collective-permute-done | bytes 1198112 | tf_op jit(solution)/shard_map/ppermute | solution.py:264
  35.8 1.5 %collective-permute-start.3 = (bf16[264,1152]{1,0:T(8,128)(2,1)S(1)}, bf16[264,1152]{1,0:T(8,128)(2,1)S(1)}, u32[]{:S(2)}, u32[]{:S(2)}) collective-permute-start(bf16[264,1152]{1,0:T(8,128)(2,1)S(1)} %get-tuple-element.28), channel_id=1, source_target_pairs={{0,2},{2,4},{4,6},{6,8},{8,10},{10,12},{12,14},{14,0},{1,3},{3,5},... | collective-permute-start | bytes 1824776 | tf_op jit(solution)/shard_map/ppermute | solution.py:264
  37.3 2.5 %collective-permute-start.4 = (bf16[256,1152]{1,0:T(8,128)(2,1)}, bf16[256,1152]{1,0:T(8,128)(2,1)S(1)}, u32[]{:S(2)}, u32[]{:S(2)}) collective-permute-start(bf16[256,1152]{1,0:T(8,128)(2,1)} %collective-permute-done.1), channel_id=1, source_target_pairs={{0,4},{2,2},{4,8},{6,6},{8,12},{10,10},{12,0},{14,14},{1,5},{3,3},... | collective-permute-start | bytes 1769480 | tf_op jit(solution)/shard_map/ppermute | solution.py:264
  39.7 5.0 %shard_map.61 = (f32[512,128]{1,0:T(8,128)S(1)}, f32[128,256]{1,0:T(8,128)S(1)}, f32[128,256]{1,0:T(8,128)S(1)}, f32[128,256]{1,0:T(8,128)S(1)}, f32[128,256]{1,0:T(8,128)S(1)}) custom-call(f32[1]{0:T(128)S(6)} %copy.6.inverse, s32[1]{0:T(128)} %bitcast.sub, f32[4,256]{1,0:T(4,128)S(1)} %get-tuple-element.24.sq, ...), custom_call_target="tpu_custom_call" | custom-call | tf_op jit(solution)/shard_map/pallas_call | solution.py:18
  44.7 11.9 %collective-permute-done.4 = bf16[256,1152]{1,0:T(8,128)(2,1)S(1)} collective-permute-done((bf16[256,1152]{1,0:T(8,128)(2,1)}, bf16[256,1152]{1,0:T(8,128)(2,1)S(1)}, u32[]{:S(2)}, u32[]{:S(2)}) %collective-permute-start.4) | collective-permute-done | bytes 589856 | tf_op jit(solution)/shard_map/ppermute | solution.py:264
  56.7 0.1 pad_maximum_fusion.below
  56.9 3.9 %shard_map.62 = (f32[512,128]{1,0:T(8,128)S(1)}, f32[512,128]{1,0:T(8,128)S(1)}, f32[512,128]{1,0:T(8,128)S(1)}) custom-call(f32[1]{0:T(128)S(6)} %copy.6.inverse, s32[1]{0:T(128)} %bitcast.sub, f32[4,256]{1,0:T(4,128)S(1)} %get-tuple-element.24.sq, bf16[520,1152]{1,0:T(8,128)(2,1)S(1)} %pad_maximum_fusion.below, ...), custom_call_target="tpu_custom_call" | custom-call | tf_op jit(solution)/shard_map/pallas_call | solution.py:18
  60.7 5.2 %shard_map.63 = (f32[512,128]{1,0:T(8,128)S(1)}, f32[512,128]{1,0:T(8,128)S(1)}, f32[512,128]{1,0:T(8,128)S(1)}) custom-call(f32[1]{0:T(128)S(6)} %copy.6.inverse, s32[1]{0:T(128)} %bitcast.sub, bf16[520,1152]{1,0:T(8,128)(2,1)} %collective-permute-done.2.above, bf16[520,1152]{1,0:T(8,128)(2,1)S(1)} %pad_maximum_fusion.below, ...), custom_call_target="tpu_custom_call" | custom-call | tf_op jit(solution)/shard_map/pallas_call | solution.py:18
  65.9 0.6 collective-permute-start.7
  66.6 1.1 %collective-permute-done.7 = f32[512,128]{1,0:T(8,128)S(1)} collective-permute-done((f32[512,128]{1,0:T(8,128)S(1)}, f32[512,128]{1,0:T(8,128)S(1)}, u32[]{:S(2)}, u32[]{:S(2)}) %collective-permute-start.7) | collective-permute-done | bytes 262176 | tf_op jit(solution)/shard_map/ppermute | solution.py:263
  67.7 0.2 collective-permute-start.8
  67.9 0.1 collective-permute-done.5.cross
  68.0 9.5 %collective-permute-done.9.above = f32[512,128]{1,0:T(8,128)S(1)} collective-permute-done((f32[512,128]{1,0:T(8,128)S(1)}, f32[512,128]{1,0:T(8,128)S(1)}, u32[]{:S(2)}, u32[]{:S(2)}) %collective-permute-start.9) | collective-permute-done | bytes 262176 | tf_op jit(solution)/shard_map/ppermute | solution.py:264
  77.5 1.1 %collective-permute-done.8.below = f32[512,128]{1,0:T(8,128)S(1)} collective-permute-done((f32[512,128]{1,0:T(8,128)S(1)}, f32[512,128]{1,0:T(8,128)S(1)}, u32[]{:S(2)}, u32[]{:S(2)}) %collective-permute-start.8) | collective-permute-done | bytes 262176 | tf_op jit(solution)/shard_map/ppermute | solution.py:264
  78.6 0.4 shard_map.64
  79.2 1.2 %collective-permute-done.10 = f32[128,128]{1,0:T(8,128)S(1)} collective-permute-done((f32[128,128]{1,0:T(8,128)S(1)}, f32[128,128]{1,0:T(8,128)S(1)}, u32[]{:S(2)}, u32[]{:S(2)}) %collective-permute-start.10) | collective-permute-done | bytes 65568 | tf_op jit(solution)/shard_map/ppermute | solution.py:263
  80.4 2.5 %collective-permute-start.11 = (f32[128,128]{1,0:T(8,128)S(1)}, f32[128,128]{1,0:T(8,128)S(1)}, u32[]{:S(2)}, u32[]{:S(2)}) collective-permute-start(f32[128,128]{1,0:T(8,128)S(1)} %add.16), channel_id=1, source_target_pairs={{0,2},{2,0},{4,6},{6,4},{8,10},{10,8},{12,14},{14,12},{1,3},{3,1},... | collective-permute-start | bytes 196616 | tf_op jit(solution)/shard_map/ppermute | solution.py:264
  82.9 2.4 %collective-permute-done.11 = f32[128,128]{1,0:T(8,128)S(1)} collective-permute-done((f32[128,128]{1,0:T(8,128)S(1)}, f32[128,128]{1,0:T(8,128)S(1)}, u32[]{:S(2)}, u32[]{:S(2)}) %collective-permute-start.11) | collective-permute-done | bytes 65568 | tf_op jit(solution)/shard_map/ppermute | solution.py:264
  85.3 2.4 %collective-permute-start.12 = (f32[128,128]{1,0:T(8,128)S(1)}, f32[128,128]{1,0:T(8,128)S(1)}, u32[]{:S(2)}, u32[]{:S(2)}) collective-permute-start(f32[128,128]{1,0:T(8,128)S(1)} %add.17), channel_id=1, source_target_pairs={{0,4},{2,6},{4,0},{6,2},{8,12},{10,14},{12,8},{14,10},{1,5},{3,7},... | collective-permute-start | bytes 196616 | tf_op jit(solution)/shard_map/ppermute | solution.py:264
  87.7 2.2 %collective-permute-done.12 = f32[128,128]{1,0:T(8,128)S(1)} collective-permute-done((f32[128,128]{1,0:T(8,128)S(1)}, f32[128,128]{1,0:T(8,128)S(1)}, u32[]{:S(2)}, u32[]{:S(2)}) %collective-permute-start.12) | collective-permute-done | bytes 65568 | tf_op jit(solution)/shard_map/ppermute | solution.py:264
  90.0 3.4 %collective-permute-start.13 = (f32[128,128]{1,0:T(8,128)S(1)}, f32[128,128]{1,0:T(8,128)S(1)}, u32[]{:S(2)}, u32[]{:S(2)}) collective-permute-start(f32[128,128]{1,0:T(8,128)S(1)} %add.18), channel_id=1, source_target_pairs={{0,8},{2,10},{4,12},{6,14},{8,0},{10,2},{12,4},{14,6},{1,9},{3,11}... | collective-permute-start | bytes 196616 | tf_op jit(solution)/shard_map/ppermute | solution.py:264
  93.4 2.2 %collective-permute-done.13 = f32[128,128]{1,0:T(8,128)S(1)} collective-permute-done((f32[128,128]{1,0:T(8,128)S(1)}, f32[128,128]{1,0:T(8,128)S(1)}, u32[]{:S(2)}, u32[]{:S(2)}) %collective-permute-start.13) | collective-permute-done | bytes 65568 | tf_op jit(solution)/shard_map/ppermute | solution.py:264
  95.7 5.2 %shard_map.65 = (f32[512,128]{1,0:T(8,128)}, f32[128,128]{1,0:T(8,128)}) custom-call(f32[512,128]{1,0:T(8,128)S(1)} %get-tuple-element.42.image, f32[128,128]{1,0:T(8,128)S(1)} %add.19.gram), custom_call_target="tpu_custom_call" | custom-call | tf_op jit(solution)/shard_map/pallas_call | solution.py:18
  (15 shorter events, 0.3 us)
Async XLA Ops:
  0.6 1.2 %copy-start = (bf16[512,1024]{1,0:T(8,128)(2,1)S(1)}, bf16[512,1024]{1,0:T(8,128)(2,1)}, u32[]{:S(2)}) copy-start(bf16[512,1024]{1,0:T(8,128)(2,1)} %embeddings.1) | copy-start | bytes 3145732
  1.9 0.9 copy-start.1
  2.8 0.7 copy-start.2
  4.4 7.2 %collective-permute-start = (bf16[520,1152]{1,0:T(8,128)(2,1)S(1)}, bf16[520,1152]{1,0:T(8,128)(2,1)S(1)}, u32[]{:S(2)}, u32[]{:S(2)}) collective-permute-start(bf16[520,1152]{1,0:T(8,128)(2,1)S(1)} %get-tuple-element.23.own), channel_id=1, source_target_pairs={{0,1},{1,0},{2,3},{3,2},{4,5},{5,4},{6,7},{7,6},{8,9},{9,8},{10,11... | collective-permute-start | bytes 3594248 | tf_op jit(solution)/shard_map/ppermute | solution.py:263
  4.9 30.9 %collective-permute-start.2 = (bf16[520,1152]{1,0:T(8,128)(2,1)S(1)}, bf16[520,1152]{1,0:T(8,128)(2,1)}, u32[]{:S(2)}, u32[]{:S(2)}) collective-permute-start(bf16[520,1152]{1,0:T(8,128)(2,1)S(1)} %get-tuple-element.23.own), channel_id=1, source_target_pairs={{0,12},{2,14},{4,0},{6,2},{8,4},{10,6},{12,8},{14,10},{1,13},{3,15... | collective-permute-start | bytes 3594248 | tf_op jit(solution)/shard_map/ppermute | solution.py:264
  9.5 15.8 %collective-permute-start.1 = (bf16[256,1152]{1,0:T(8,128)(2,1)}, bf16[256,1152]{1,0:T(8,128)(2,1)}, u32[]{:S(2)}, u32[]{:S(2)}) collective-permute-start(bf16[256,1152]{1,0:T(8,128)(2,1)} %get-tuple-element.26), channel_id=1, source_target_pairs={{0,2},{2,0},{4,6},{6,4},{8,10},{10,8},{12,14},{14,12},{1,3},{3,1},... | collective-permute-start | bytes 1769480 | tf_op jit(solution)/shard_map/ppermute | solution.py:264
  35.8 20.9 %collective-permute-start.3 = (bf16[264,1152]{1,0:T(8,128)(2,1)S(1)}, bf16[264,1152]{1,0:T(8,128)(2,1)S(1)}, u32[]{:S(2)}, u32[]{:S(2)}) collective-permute-start(bf16[264,1152]{1,0:T(8,128)(2,1)S(1)} %get-tuple-element.28), channel_id=1, source_target_pairs={{0,2},{2,4},{4,6},{6,8},{8,10},{10,12},{12,14},{14,0},{1,3},{3,5},... | collective-permute-start | bytes 1824776 | tf_op jit(solution)/shard_map/ppermute | solution.py:264
  37.3 19.4 %collective-permute-start.4 = (bf16[256,1152]{1,0:T(8,128)(2,1)}, bf16[256,1152]{1,0:T(8,128)(2,1)S(1)}, u32[]{:S(2)}, u32[]{:S(2)}) collective-permute-start(bf16[256,1152]{1,0:T(8,128)(2,1)} %collective-permute-done.1), channel_id=1, source_target_pairs={{0,4},{2,2},{4,8},{6,6},{8,12},{10,10},{12,0},{14,14},{1,5},{3,3},... | collective-permute-start | bytes 1769480 | tf_op jit(solution)/shard_map/ppermute | solution.py:264
  56.8 3.9 %collective-permute-start.6 = (bf16[520,1152]{1,0:T(8,128)(2,1)S(1)}, bf16[520,1152]{1,0:T(8,128)(2,1)S(1)}, u32[]{:S(2)}, u32[]{:S(2)}) collective-permute-start(bf16[520,1152]{1,0:T(8,128)(2,1)S(1)} %pad_maximum_fusion.below), channel_id=1, source_target_pairs={{0,1},{1,0},{2,3},{3,2},{4,5},{5,4},{6,7},{7,6},{8,9},{9,8},{10,11... | collective-permute-start | bytes 3594248 | tf_op jit(solution)/shard_map/ppermute | solution.py:263
  65.9 1.7 %collective-permute-start.7 = (f32[512,128]{1,0:T(8,128)S(1)}, f32[512,128]{1,0:T(8,128)S(1)}, u32[]{:S(2)}, u32[]{:S(2)}) collective-permute-start(f32[512,128]{1,0:T(8,128)S(1)} %get-tuple-element.40), channel_id=1, source_target_pairs={{0,1},{1,0},{2,3},{3,2},{4,5},{5,4},{6,7},{7,6},{8,9},{9,8},{10,11... | collective-permute-start | bytes 786440 | tf_op jit(solution)/shard_map/ppermute | solution.py:263
  66.5 1.5 %collective-permute-start.5 = (f32[512,128]{1,0:T(8,128)S(1)}, f32[512,128]{1,0:T(8,128)S(1)}, u32[]{:S(2)}, u32[]{:S(2)}) collective-permute-start(f32[512,128]{1,0:T(8,128)S(1)} %get-tuple-element.37), channel_id=1, source_target_pairs={{0,1},{1,0},{2,3},{3,2},{4,5},{5,4},{6,7},{7,6},{8,9},{9,8},{10,11... | collective-permute-start | bytes 786440 | tf_op jit(solution)/shard_map/ppermute | solution.py:263
  66.6 11.0 %collective-permute-start.9 = (f32[512,128]{1,0:T(8,128)S(1)}, f32[512,128]{1,0:T(8,128)S(1)}, u32[]{:S(2)}, u32[]{:S(2)}) collective-permute-start(f32[512,128]{1,0:T(8,128)S(1)} %get-tuple-element.41), channel_id=1, source_target_pairs={{0,4},{2,6},{4,8},{6,10},{8,12},{10,14},{12,0},{14,2},{1,5},{3,7},... | collective-permute-start | bytes 786440 | tf_op jit(solution)/shard_map/ppermute | solution.py:264
  67.7 10.9 %collective-permute-start.8 = (f32[512,128]{1,0:T(8,128)S(1)}, f32[512,128]{1,0:T(8,128)S(1)}, u32[]{:S(2)}, u32[]{:S(2)}) collective-permute-start(f32[512,128]{1,0:T(8,128)S(1)} %add.15), channel_id=1, source_target_pairs={{0,14},{2,0},{4,2},{6,4},{8,6},{10,8},{12,10},{14,12},{1,15},{3,1}... | collective-permute-start | bytes 786440 | tf_op jit(solution)/shard_map/ppermute | solution.py:264
  79.1 1.3 %collective-permute-start.10 = (f32[128,128]{1,0:T(8,128)S(1)}, f32[128,128]{1,0:T(8,128)S(1)}, u32[]{:S(2)}, u32[]{:S(2)}) collective-permute-start(f32[128,128]{1,0:T(8,128)S(1)} %get-tuple-element.43), channel_id=1, source_target_pairs={{0,1},{1,0},{2,3},{3,2},{4,5},{5,4},{6,7},{7,6},{8,9},{9,8},{10,11... | collective-permute-start | bytes 196616 | tf_op jit(solution)/shard_map/ppermute | solution.py:263
  80.4 4.9 %collective-permute-start.11 = (f32[128,128]{1,0:T(8,128)S(1)}, f32[128,128]{1,0:T(8,128)S(1)}, u32[]{:S(2)}, u32[]{:S(2)}) collective-permute-start(f32[128,128]{1,0:T(8,128)S(1)} %add.16), channel_id=1, source_target_pairs={{0,2},{2,0},{4,6},{6,4},{8,10},{10,8},{12,14},{14,12},{1,3},{3,1},... | collective-permute-start | bytes 196616 | tf_op jit(solution)/shard_map/ppermute | solution.py:264
  85.3 4.7 %collective-permute-start.12 = (f32[128,128]{1,0:T(8,128)S(1)}, f32[128,128]{1,0:T(8,128)S(1)}, u32[]{:S(2)}, u32[]{:S(2)}) collective-permute-start(f32[128,128]{1,0:T(8,128)S(1)} %add.17), channel_id=1, source_target_pairs={{0,4},{2,6},{4,0},{6,2},{8,12},{10,14},{12,8},{14,10},{1,5},{3,7},... | collective-permute-start | bytes 196616 | tf_op jit(solution)/shard_map/ppermute | solution.py:264
  90.0 5.6 %collective-permute-start.13 = (f32[128,128]{1,0:T(8,128)S(1)}, f32[128,128]{1,0:T(8,128)S(1)}, u32[]{:S(2)}, u32[]{:S(2)}) collective-permute-start(f32[128,128]{1,0:T(8,128)S(1)} %add.18), channel_id=1, source_target_pairs={{0,8},{2,10},{4,12},{6,14},{8,0},{10,2},{12,4},{14,6},{1,9},{3,11}... | collective-permute-start | bytes 196616 | tf_op jit(solution)/shard_map/ppermute | solution.py:264

commit v5 on v4

v5 whole, which is shorter than its diff:
```python
import jax
import jax.numpy as jnp
from jax import lax
from jax.experimental import pallas as pl
from jax.experimental.pallas import tpu as pltpu
from jax.sharding import PartitionSpec as P

TILE = 128
REACH = 3
F32 = jnp.float32
BF16 = jnp.bfloat16
HIGHEST = lax.Precision.HIGHEST


def vmem_call(body, out_shapes, *operands, scalars=0, in_hbm=0, scratch=()):
    in_vmem = pl.BlockSpec(memory_space=pltpu.VMEM)
    lead = [pl.BlockSpec(memory_space=pltpu.SMEM)] * scalars + [pl.BlockSpec(memory_space=pltpu.HBM)] * in_hbm
    return pl.pallas_call(
        body,
        out_shape=out_shapes,
        in_specs=lead + [in_vmem] * (len(operands) - len(lead)),
        out_specs=jax.tree.map(lambda _: in_vmem, out_shapes),
        scratch_shapes=scratch,
        compiler_params=pltpu.CompilerParams(vmem_limit_bytes=48 << 20),
        cost_estimate=pl.CostEstimate(flops=10**11, transcendentals=0, bytes_accessed=0),
    )(*operands)


def shape(*dims):
    return jax.ShapeDtypeStruct(dims, F32)


def contract(a, b, dims, precision=None):
    return lax.dot_general(a, b, (dims, ((), ())), precision=precision, preferred_element_type=F32)


MARK = 8
OWN, BELOW, ABOVE = 0, 1, -2


def pair_mask(sub, rows, cols, offset, which):
    tiles = rows.shape[0]
    padded, lanes = rows.shape[1], tiles * TILE
    tile_of = lax.broadcasted_iota(jnp.int32, (padded, lanes), 1) // TILE
    first = (REACH + offset) * 2 * tiles + (sub if which == 0 else 1 - sub) * tiles
    chosen = (lax.broadcasted_iota(jnp.int32, (padded, lanes), 0) == first + tile_of).astype(F32)
    ahead = contract(rows, chosen, ((1,), (0,)))
    first = (REACH - offset) * 2 * tiles + sub * tiles
    row_at = lax.broadcasted_iota(jnp.int32, (tiles, padded), 0)
    chosen = (lax.broadcasted_iota(jnp.int32, (tiles, padded), 1) == first + row_at).astype(F32)
    spread = (lax.broadcasted_iota(jnp.int32, (tiles, lanes), 0) == tile_of[:tiles]).astype(F32)
    back = contract(contract(chosen, cols, ((1,), (1,))), spread, ((1,), (0,)))
    return jnp.concatenate([ahead, back], axis=0)


def marks(ref, at, half):
    return ref[at : at + MARK, :TILE].astype(F32)[: half // TILE]


def pieces(*refs, count, size):
    out = []
    for k in range(count):
        rows = slice(k * size, (k + 1) * size)
        if len(refs) == 2:
            out.append((refs[0][rows], refs[1][rows]))
        else:
            features = refs[0].shape[1] - TILE
            out.append((refs[0][rows, :features], refs[0][rows, features:]))
    return out


def squares(features):
    wide = features.astype(F32)
    return jnp.sum(wide * wide, axis=1, keepdims=True)


def as_row(column):
    return jnp.broadcast_to(column, (column.shape[0], TILE)).T[:1]


def read_rows(ref):
    return [ref[k : k + 1] for k in range(ref.shape[0])]


def columns_of(all_pieces, sq_rows, masks, first=0):
    count = len(all_pieces) // 2
    out = []
    for k, (features, panel) in enumerate(all_pieces):
        size = features.shape[0]
        at = (first + k % count) * size
        out.append((features, panel, sq_rows[k], masks[k // count][:, at : at + size]))
    return out


def products(inverse, piece, tile, columns, back):
    features, panel = piece
    size = features.shape[0]
    row_sq = squares(features)
    doubled = features * 2
    panel_t = panel.astype(F32).T.astype(BF16)
    image = None
    for k, (other, other_panel, col_sq, mask) in enumerate(columns):
        tiles = mask.shape[0] // 2
        gram2 = contract(doubled, other, ((1,), (1,)))
        kernel = jnp.exp(-inverse * jnp.maximum(row_sq + col_sq - gram2, 0.0))

        def masked(first):
            return jnp.concatenate(
                [kernel[i * TILE : (i + 1) * TILE] * mask[first + i : first + i + 1] for i in range(size // TILE)], axis=0
            ).astype(BF16)

        term = contract(masked(tile), other_panel, ((1,), (0,)))
        image = term if image is None else image + term
        if back is not None:
            term = contract(panel_t, masked(tiles + tile), ((1,), (0,)))
            back[k] = term if back[k] is None else back[k] + term
    return image


def piece_images(inverse, rows, columns, back):
    images = [products(inverse, piece, k * piece[0].shape[0] // TILE, columns, back) for k, piece in enumerate(rows)]
    return jnp.concatenate(images, axis=0)


def store_all(outs, values):
    for out, value in zip(outs, values):
        out[...] = value


def pack_body(embeddings, panel, tile_mask, own, first, last, panel_mark, mask_here, done):
    half, features = embeddings.shape
    size = half // 2
    tiles, window = tile_mask.shape
    moves = [(tile_mask, mask_here), (panel, panel_mark.at[:half])]
    for ref, start, stop in ((own, 0, half), (first, 0, size), (last, size, half)):
        rows = ref.at[: stop - start]
        moves.append((embeddings.at[start:stop], rows.at[:, :features]))
        moves.append((panel.at[start:stop], rows.at[:, features:]))
    copies = [pltpu.make_async_copy(a, b, done.at[k]) for k, (a, b) in enumerate(moves)]
    for copy in copies:
        copy.start()
    for copy in copies:
        copy.wait()
    at = lax.broadcasted_iota(jnp.int32, (window, TILE), 0) == lax.broadcasted_iota(jnp.int32, (window, TILE), 1)
    mask = contract(mask_here[...].astype(F32), at.astype(F32), ((1,), (0,)))
    mask = jnp.concatenate([mask, jnp.zeros((MARK - tiles, TILE), F32)], axis=0).astype(BF16)
    for ref in (own, first):
        ref[ref.shape[0] - MARK :, :TILE] = mask
        ref[ref.shape[0] - MARK :, TILE:] = jnp.zeros((MARK, features), BF16)
    panel_mark[half:] = mask


def masks_of(sub, rows, others, offset):
    return [pair_mask(sub, rows, r, offset, h) for h, r in enumerate(others)]


def own_pieces(own, other):
    size = own.shape[0] // 2 - MARK // 2
    return [p for ref in (own, other) for p in pieces(ref, count=2, size=size)]


def own_marks(own, other):
    half = own.shape[0] - MARK
    return [marks(ref, half, half) for ref in (own, other)]


def self_body(inverse, sub, own, other, image, sq):
    blocks = own_pieces(own, other)
    rows = [as_row(squares(features)) for features, _ in blocks]
    for k, row in enumerate(rows):
        sq[k : k + 1] = row
    both = own_marks(own, other)
    columns = columns_of(blocks, rows, masks_of(sub[0], both[0], both, OWN))
    image[...] = piece_images(inverse[0], blocks[:2], columns, None)


def above_own_body(inverse, sub, sq, above, above_panel, own, other, image, *sums):
    half = above.shape[0]
    masks = masks_of(sub[0], marks(above_panel, half, half), own_marks(own, other), ABOVE)
    back = [None] * 4
    columns = columns_of(own_pieces(own, other), read_rows(sq), masks)
    image[...] = piece_images(inverse[0], pieces(above, above_panel, count=2, size=half // 2), columns, back)
    store_all(sums, back)


def below_first_body(inverse, sub, sq, below, own, other, t0, t1, t2, t3, image, *sums):
    size = below.shape[0] - MARK
    masks = masks_of(sub[0], marks(below, size, 2 * size), own_marks(own, other), BELOW)
    back = [t0[...], t1[...], t2[...], t3[...]]
    columns = columns_of(own_pieces(own, other), read_rows(sq), masks)
    image[...] = products(inverse[0], pieces(below, count=1, size=size)[0], 0, columns, back)
    store_all(sums, back)


def below_last_body(inverse, sub, sq, marked, below, own, other, self_image, t0, t1, t2, t3, image, own_image, cross):
    size = below.shape[0]
    masks = masks_of(sub[0], marks(marked, 0, 2 * size), own_marks(own, other), BELOW)
    back = [t0[...], t1[...], t2[...], t3[...]]
    columns = columns_of(own_pieces(own, other), read_rows(sq), masks)
    image[...] = products(inverse[0], pieces(below, count=1, size=size)[0], size // TILE, columns, back)
    for k in range(2):
        rows = slice(k * size, (k + 1) * size)
        own_image[rows] = self_image[rows] + back[k].T
        cross[rows] = back[2 + k].T


def above_below(part, inverse, sub, above, above_panel, pair, pair_marks, above_image, image):
    half = above.shape[0]
    size = half // 2
    masks = masks_of(sub[0], marks(above_panel, half, half), pair_marks, ABOVE - BELOW)
    back = [None] * 2
    rows = [as_row(squares(features)) for features, _ in pair]
    columns = columns_of(pair, rows, masks, part)
    image[...] = above_image[...] + piece_images(inverse[0], pieces(above, above_panel, count=2, size=size), columns, back)
    return back[0].T, back[1].T


def above_below_first_body(inverse, sub, above, above_panel, below, other, above_image, below_image, image, below_out, cross, marked):
    size = above.shape[0] // 2
    pair = [pieces(r, count=1, size=size)[0] for r in (below, other)]
    both = [marks(r, size, 2 * size) for r in (below, other)]
    mine, cross[...] = above_below(0, inverse, sub, above, above_panel, pair, both, above_image, image)
    below_out[...] = below_image[...] + mine
    marked[:MARK] = below[size:, :TILE]
    marked[MARK:] = other[size:, :TILE]


def above_below_last_body(inverse, sub, above, above_panel, below, other, marked, above_image, image, below_out, cross):
    size = above.shape[0] // 2
    pair = [pieces(r, count=1, size=size)[0] for r in (below, other)]
    both = [marks(marked, at, 2 * size) for at in (0, MARK)]
    below_out[...], cross[...] = above_below(1, inverse, sub, above, above_panel, pair, both, above_image, image)


def gram_body(own, cross, below0, below1, above, image, gram):
    below = jnp.concatenate([below0[...], below1[...]], axis=0)
    total = own[...] + cross[...] + below + above[...]
    image[...] = total
    gram[...] = contract(total, total, ((0,), (0,)), HIGHEST)


GROUP = 8


def full(value):
    return jnp.broadcast_to(value, (GROUP, value.shape[1] if value.shape[1] > 1 else TILE))


def factor(gram, block):
    size = gram.shape[0]
    groups = size // GROUP
    upper = [gram[GROUP * r : GROUP * (r + 1)] for r in range(groups)]
    row = lax.broadcasted_iota(jnp.int32, (GROUP, size), 0)
    col = lax.broadcasted_iota(jnp.int32, (GROUP, size), 1)
    inverse = [jnp.where(col == row + GROUP * r, 1.0, 0.0).astype(F32) for r in range(groups)]
    for b in range(0, groups, block):
        if b:
            done_upper, done_inverse = jnp.concatenate(upper[:b], axis=0), jnp.concatenate(inverse[:b], axis=0)
            coefficients = done_upper[:, GROUP * b : GROUP * (b + block)]
            less_upper = contract(coefficients, done_upper, ((0,), (0,)), HIGHEST)
            less_inverse = contract(coefficients, done_inverse, ((0,), (0,)), HIGHEST)
            for k in range(block):
                upper[b + k] = upper[b + k] - less_upper[GROUP * k : GROUP * (k + 1)]
                inverse[b + k] = inverse[b + k] - less_inverse[GROUP * k : GROUP * (k + 1)]
        for r in range(b, b + block):
            lane = GROUP * r
            columns = [full(upper[r][:, lane + k : lane + k + 1]) for k in range(GROUP)]
            diag = [[full(columns[j][i : i + 1]) for j in range(i + 1)] for i in range(GROUP)]
            lower = [[None] * GROUP for _ in range(GROUP)]
            scale = [None] * GROUP
            for i in range(GROUP):
                scale[i] = lax.rsqrt(diag[i][i])
                for k in range(i + 1, GROUP):
                    lower[k][i] = diag[k][i] * scale[i]
                for k in range(i + 1, GROUP):
                    for j in range(i + 1, k + 1):
                        diag[k][j] = diag[k][j] - lower[k][i] * lower[j][i]
            u = [full(upper[r][i : i + 1]) for i in range(GROUP)]
            v = [full(inverse[r][i : i + 1]) for i in range(GROUP)]
            for i in range(GROUP):
                u[i], v[i] = u[i] * scale[i], v[i] * scale[i]
                for k in range(i + 1, GROUP):
                    u[k], v[k] = u[k] - lower[k][i] * u[i], v[k] - lower[k][i] * v[i]
            upper[r], inverse[r] = u[0], v[0]
            for i in range(1, GROUP):
                upper[r] = jnp.where(row == i, u[i], upper[r])
                inverse[r] = jnp.where(row == i, v[i], inverse[r])
            for later in range(r + 1, b + block):
                left = [full(upper[later][:, lane + k : lane + k + 1]) for k in range(GROUP)]
                for i in range(GROUP):
                    left[i] = left[i] * scale[i]
                    for k in range(i + 1, GROUP):
                        left[k] = left[k] - lower[k][i] * left[i]
                    upper[later] = upper[later] - left[i] * u[i]
                    inverse[later] = inverse[later] - left[i] * v[i]
    at_row = lax.broadcasted_iota(jnp.int32, (size, size), 0)
    at_col = lax.broadcasted_iota(jnp.int32, (size, size), 1)
    return jnp.where(at_col >= at_row, jnp.concatenate(upper, axis=0), 0.0), jnp.concatenate(inverse, axis=0)


def basis_body(image, gram, basis, upper):
    upper[...], inverse = factor(gram[...], 4)
    basis[...] = contract(image[...], inverse, ((1,), (1,)), HIGHEST)


def per_device(embeddings, start_panel, tile_mask, inv_width):
    n_blk = lax.axis_size("blk")
    half, width = start_panel.shape
    size = half // 2
    sub_move = lambda v: lax.ppermute(v, "sub", [(0, 1), (1, 0)])
    blk_route = lambda v, to: lax.ppermute(v, "blk", [(i, to(i) % n_blk) for i in range(n_blk)])
    blk_move = lambda v, by: blk_route(v, lambda i: i + by)

    after = lambda v, *earlier: lax.optimization_barrier((v, *earlier))[0]
    sub = lax.axis_index("sub").astype(jnp.int32).reshape(1)
    wide = embeddings.shape[1] + width
    packed = lambda rows, lanes: jax.ShapeDtypeStruct((rows, lanes), BF16)
    above = blk_move(embeddings, -2)
    own, first, last, panel_mark = vmem_call(
        pack_body,
        (packed(half + MARK, wide), packed(size + MARK, wide), packed(size, wide), packed(half + MARK, width)),
        embeddings,
        start_panel,
        tile_mask,
        in_hbm=3,
        scratch=[pltpu.VMEM(tile_mask.shape, tile_mask.dtype), pltpu.SemaphoreType.DMA((8,))],
    )
    relayed = n_blk == 8
    swapped = blk_route(last, lambda i: i ^ 1) if relayed else last
    above_panel = blk_move(panel_mark, -2)
    other = sub_move(own)
    image, piece_image = shape(half, width), shape(size, width)
    turned = (shape(width, size),) * 4
    self_image, sq = vmem_call(self_body, (image, shape(4, size)), inv_width, sub, own, other, scalars=2)
    first = after(first, swapped, above, above_panel, self_image)
    swapped = after(swapped, above, above_panel, self_image)
    below0 = blk_move(first, 1)
    below1 = blk_route(swapped, lambda i: i if i & 1 else i + 2) if relayed else blk_move(swapped, 1)
    above_image, *back = vmem_call(
        above_own_body, (image, *turned), inv_width, sub, sq, above, above_panel, own, other, scalars=2
    )
    below_other0 = sub_move(after(below0, above_image))
    below_image0, *back = vmem_call(
        below_first_body, (piece_image, *turned), inv_width, sub, sq, below0, own, other, *back, scalars=2
    )
    above_image, below_image0, below_cross0, marked = vmem_call(
        above_below_first_body,
        (image, piece_image, piece_image, packed(2 * MARK, TILE)),
        inv_width,
        sub,
        above,
        above_panel,
        below0,
        below_other0,
        above_image,
        below_image0,
        scalars=2,
    )
    below1 = after(below1, above_image)
    below_other1 = sub_move(below1)
    above_image, below_sum1, below_cross1 = vmem_call(
        above_below_last_body,
        (image, piece_image, piece_image),
        inv_width,
        sub,
        above,
        above_panel,
        below1,
        below_other1,
        marked,
        above_image,
        scalars=2,
    )
    below_image1, own_image, own_cross = vmem_call(
        below_last_body, (piece_image, image, image), inv_width, sub, sq, marked, below1, own, other, self_image, *back, scalars=2
    )
    above_image = blk_move(above_image, 2)
    below_image0 = blk_move(below_image0 + sub_move(below_cross0), -1)
    below_image1 = blk_move(below_image1 + below_sum1 + sub_move(below_cross1), -1)
    image, gram = vmem_call(
        gram_body, (image, shape(width, width)), own_image, sub_move(own_cross), below_image0, below_image1, above_image
    )
    if n_blk & (n_blk - 1):
        gram = lax.psum(gram, ("blk", "sub"))
    else:
        gram = gram + sub_move(gram)
        hop = 1
        while hop < n_blk:
            gram = gram + blk_route(gram, lambda i: i ^ hop)
            hop *= 2
    return vmem_call(basis_body, (shape(half, width), shape(width, width)), image, gram)


def solution(mesh):
    return jax.shard_map(
        per_device,
        mesh=mesh,
        in_specs=(
            P(("groups", "blk", "sub"), None),
            P(("groups", "blk", "sub"), None),
            P(("groups", "blk", "sub"), None),
            P(),
        ),
        out_specs=(P(("groups", "blk", "sub"), None), P("groups", None)),
        check_vma=False,
    )
```

time: 101 us -> 113 us (1.12)
  starting transfers between devices: 19.8 us -> 24.9 us
  Pallas kernels: 23.7 us -> 27.8 us
  waiting for transfers between devices: 53 us -> 54.8 us
    ppermute x9 -> x11, starting transfers between devices: 18.6 us -> 23.2 us  [per_device(): lax.ppermute(v, 'blk', [(i, to(i) % n_blk) for i in range(n_blk)])]
    pallas_call x7 -> x9, Pallas kernels: 23.7 us -> 27.8 us  [vmem_call(): pl.pallas_call(body, out_shape=out_shapes, in_specs=lead + [in_vmem] * (l...]
    ppermute x9 -> x11, waiting for transfers between devices: 50.5 us -> 51.5 us  [per_device(): lax.ppermute(v, 'blk', [(i, to(i) % n_blk) for i in range(n_blk)])]
    ppermute x5 -> x7, waiting for transfers between devices: 2.42 us -> 3.28 us  [per_device(): sub_move = lambda v: lax.ppermute(v, 'sub', [(0, 1), (1, 0)])]
    unnamed x6 -> x12, local copies, waits for them, and re-layouts: 2.8 us -> 2.41 us
  transfers between devices with their start and end apart: 14 -> 18, of which waited for: 11 -> 9; matrix products, arithmetic and copies ran while one was open for 0% -> 1% of each run, Pallas kernels for 12% -> 18%
where the time goes in v5:
time: 113 us; the launch traced here: 112 us
  waiting for transfers between devices  54.8 us (48%)
  Pallas kernels  27.8 us (25%)
  starting transfers between devices  24.9 us (22%)
  local copies, waits for them, and re-layouts  2.41 us (2%)
  between operations  1.44 us (1%)
    ppermute x11, waiting for transfers between devices, per_device(): lax.ppermute(v, 'blk', [(i, to(i) % n_blk) for i in range(n_blk)])  51.5 us
    pallas_call x9, Pallas kernels, vmem_call(): pl.pallas_call(body, out_shape=out_shapes, in_specs=lead + [in_vmem] * (l...  27.8 us
    ppermute x11, starting transfers between devices, per_device(): lax.ppermute(v, 'blk', [(i, to(i) % n_blk) for i in range(n_blk)])  23.2 us
    ppermute x7, waiting for transfers between devices, per_device(): sub_move = lambda v: lax.ppermute(v, 'sub', [(0, 1), (1, 0)])  3.28 us
    unnamed x12, local copies, waits for them, and re-layouts  2.41 us
  transfers between devices with their start and end apart: 18, of which 9 were waited for; matrix products, arithmetic and copies ran while one was open for 1% of the time, Pallas kernels for 18%

profile of v5, /device:TPU:0, one launch (start us, length us, event | category | flops | bytes accessed | tf_op | source)
XLA Modules:
  0.0 112.3 jit_solution(15170392285196243171)
XLA Ops:
  0.6 0.9 copy-done.2
  1.5 0.7 copy-done.3
  2.2 2.6 %shard_map.59 = (bf16[520,1152]{1,0:T(8,128)(2,1)S(1)}, bf16[264,1152]{1,0:T(8,128)(2,1)S(1)}, bf16[256,1152]{1,0:T(8,128)(2,1)}, bf16[520,128]{1,0:T(8,128)(2,1)}) custom-call(bf16[512,1024]{1,0:T(8,128)(2,1)} %embeddings.1, bf16[512,128]{1,0:T(8,128)(2,1)S(1)} %copy-done.2, s32[4,56]{1,0:T(4,128)S(1)} %copy-done.3), custom_call_target="tpu_custom_call" | custom-call | flops 99999997952 | tf_op jit(solution)/shard_map/pallas_call | solution.py:18
  4.8 0.8 copy-done
  5.6 0.5 collective-permute-start
  6.1 4.6 %collective-permute-start.1 = (bf16[512,1024]{1,0:T(8,128)(2,1)}, bf16[512,1024]{1,0:T(8,128)(2,1)S(1)}, u32[]{:S(2)}, u32[]{:S(2)}) collective-permute-start(bf16[512,1024]{1,0:T(8,128)(2,1)} %embeddings.1), channel_id=1, source_target_pairs={{0,12},{2,14},{4,0},{6,2},{8,4},{10,6},{12,8},{14,10},{1,13},{3,15... | collective-permute-start | bytes 3145736 | tf_op jit(solution)/shard_map/ppermute | solution.py:311
  10.7 0.4 collective-permute-start.2
  11.1 1.5 %collective-permute-start.3 = (bf16[256,1152]{1,0:T(8,128)(2,1)}, bf16[256,1152]{1,0:T(8,128)(2,1)}, u32[]{:S(2)}, u32[]{:S(2)}) collective-permute-start(bf16[256,1152]{1,0:T(8,128)(2,1)} %get-tuple-element.38), channel_id=1, source_target_pairs={{0,2},{2,0},{4,6},{6,4},{8,10},{10,8},{12,14},{14,12},{1,3},{3,1},... | collective-permute-start | bytes 1769480 | tf_op jit(solution)/shard_map/ppermute | solution.py:311
  13.3 3.0 %shard_map.60 = (f32[512,128]{1,0:T(8,128)S(1)}, f32[4,256]{1,0:T(4,128)S(1)}) custom-call(f32[1]{0:T(128)S(6)} %copy.6.inverse, s32[1]{0:T(128)} %bitcast.sub, bf16[520,1152]{1,0:T(8,128)(2,1)S(1)} %get-tuple-element.34.own, bf16[520,1152]{1,0:T(8,128)(2,1)S(1)} %collective-permute-done.other), custom_call_target="tpu_custom_call" | custom-call | flops 99999997952 | tf_op jit(solution)/shard_map/pallas_call | solution.py:18
  16.3 20.6 %collective-permute-done.2.above_panel = bf16[520,128]{1,0:T(8,128)(2,1)} collective-permute-done((bf16[520,128]{1,0:T(8,128)(2,1)}, bf16[520,128]{1,0:T(8,128)(2,1)}, u32[]{:S(2)}, u32[]{:S(2)}) %collective-permute-start.2) | collective-permute-done | bytes 133152 | tf_op jit(solution)/shard_map/ppermute | solution.py:311
  37.0 2.4 %collective-permute-start.6 = (bf16[256,1152]{1,0:T(8,128)(2,1)}, bf16[256,1152]{1,0:T(8,128)(2,1)}, u32[]{:S(2)}, u32[]{:S(2)}) collective-permute-start(bf16[256,1152]{1,0:T(8,128)(2,1)} %collective-permute-done.3), channel_id=1, source_target_pairs={{0,4},{2,2},{4,8},{6,6},{8,12},{10,10},{12,0},{14,14},{1,5},{3,3},... | collective-permute-start | bytes 1769480 | tf_op jit(solution)/shard_map/ppermute | solution.py:311
  39.3 5.1 %collective-permute-start.4 = (bf16[264,1152]{1,0:T(8,128)(2,1)S(1)}, bf16[264,1152]{1,0:T(8,128)(2,1)S(1)}, u32[]{:S(2)}, u32[]{:S(2)}) collective-permute-start(bf16[264,1152]{1,0:T(8,128)(2,1)S(1)} %copy-done.1), channel_id=1, source_target_pairs={{0,2},{2,4},{4,6},{6,8},{8,10},{10,12},{12,14},{14,0},{1,3},{3,5},... | collective-permute-start | bytes 1824776 | tf_op jit(solution)/shard_map/ppermute | solution.py:311
  44.4 4.7 %shard_map.61 = (f32[512,128]{1,0:T(8,128)S(1)}, f32[128,256]{1,0:T(8,128)S(1)}, f32[128,256]{1,0:T(8,128)S(1)}, f32[128,256]{1,0:T(8,128)S(1)}, f32[128,256]{1,0:T(8,128)S(1)}) custom-call(f32[1]{0:T(128)S(6)} %copy.6.inverse, s32[1]{0:T(128)} %bitcast.sub, f32[4,256]{1,0:T(4,128)S(1)} %get-tuple-element.35.sq, ...), custom_call_target="tpu_custom_call" | custom-call | flops 99999997952 | tf_op jit(solution)/shard_map/pallas_call | solution.py:18
  49.1 12.7 %collective-permute-done.4.below = bf16[264,1152]{1,0:T(8,128)(2,1)S(1)} collective-permute-done((bf16[264,1152]{1,0:T(8,128)(2,1)S(1)}, bf16[264,1152]{1,0:T(8,128)(2,1)S(1)}, u32[]{:S(2)}, u32[]{:S(2)}) %collective-permute-start.4) | collective-permute-done | bytes 608288 | tf_op jit(solution)/shard_map/ppermute | solution.py:311
  61.7 2.2 %shard_map.62 = (f32[256,128]{1,0:T(8,128)S(1)}, f32[128,256]{1,0:T(8,128)S(1)}, f32[128,256]{1,0:T(8,128)S(1)}, f32[128,256]{1,0:T(8,128)S(1)}, f32[128,256]{1,0:T(8,128)S(1)}) custom-call(f32[1]{0:T(128)S(6)} %copy.6.inverse, s32[1]{0:T(128)} %bitcast.sub, f32[4,256]{1,0:T(4,128)S(1)} %get-tuple-element.35.sq, ...), custom_call_target="tpu_custom_call" | custom-call | flops 99999997952 | tf_op jit(solution)/shard_map/pallas_call | solution.py:18
  63.9 3.5 %shard_map.63 = (f32[512,128]{1,0:T(8,128)S(1)}, f32[256,128]{1,0:T(8,128)S(1)}, f32[256,128]{1,0:T(8,128)}, bf16[16,128]{1,0:T(8,128)(2,1)S(1)}) custom-call(f32[1]{0:T(128)S(6)} %copy.6.inverse, s32[1]{0:T(128)} %bitcast.sub, bf16[512,1024]{1,0:T(8,128)(2,1)S(1)} %collective-permute-done.1.above, bf16[520,128]{1,0:T(8,128)(2,1)} %collective-permute-done.2.above_panel, ...), custom_call_target="tpu_custom_call" | custom-call | flops 99999997952 | tf_op jit(solution)/shard_map/pallas_call | solution.py:18
  67.4 0.5 collective-permute-start.10
  67.9 2.0 %collective-permute-done.10.other = bf16[256,1152]{1,0:T(8,128)(2,1)S(1)} collective-permute-done((bf16[256,1152]{1,0:T(8,128)(2,1)}, bf16[256,1152]{1,0:T(8,128)(2,1)S(1)}, u32[]{:S(2)}, u32[]{:S(2)}) %collective-permute-start.10) | collective-permute-done | bytes 589856 | tf_op jit(solution)/shard_map/ppermute | solution.py:310
  69.9 3.1 %shard_map.65 = (f32[512,128]{1,0:T(8,128)S(1)}, f32[256,128]{1,0:T(8,128)S(1)}, f32[256,128]{1,0:T(8,128)S(1)}) custom-call(f32[1]{0:T(128)S(6)} %copy.6.inverse, s32[1]{0:T(128)} %bitcast.sub, bf16[512,1024]{1,0:T(8,128)(2,1)S(1)} %collective-permute-done.1.above, bf16[520,128]{1,0:T(8,128)(2,1)} %collective-permute-done.2.above_panel, ...), custom_call_target="tpu_custom_call" | custom-call | flops 99999997952 | tf_op jit(solution)/shard_map/pallas_call | solution.py:18
  73.4 3.3 %shard_map.64 = (f32[256,128]{1,0:T(8,128)S(1)}, f32[512,128]{1,0:T(8,128)S(1)}, f32[512,128]{1,0:T(8,128)S(1)}) custom-call(f32[1]{0:T(128)S(6)} %copy.6.inverse, s32[1]{0:T(128)} %bitcast.sub, f32[4,256]{1,0:T(4,128)S(1)} %copy-done.5, bf16[16,128]{1,0:T(8,128)(2,1)S(1)} %get-tuple-element.48.marked, bf16[256,1152]{1,0:T(8,128)(2,1)} %collective-permute-done.6.below, ...), custom_call_target="tpu_custom_call" | custom-call | flops 99999997952 | tf_op jit(solution)/shard_map/pallas_call | solution.py:18
  77.0 0.9 add.21
  77.9 1.8 %collective-permute-start.9 = (f32[256,128]{1,0:T(8,128)S(1)}, f32[256,128]{1,0:T(8,128)S(1)}, u32[]{:S(2)}, u32[]{:S(2)}) collective-permute-start(f32[256,128]{1,0:T(8,128)S(1)} %add.21), channel_id=1, source_target_pairs={{0,14},{2,0},{4,2},{6,4},{8,6},{10,8},{12,10},{14,12},{1,15},{3,1}... | collective-permute-start | bytes 393224 | tf_op jit(solution)/shard_map/ppermute | solution.py:311
  79.7 3.8 %collective-permute-start.12 = (f32[256,128]{1,0:T(8,128)S(1)}, f32[256,128]{1,0:T(8,128)S(1)}, u32[]{:S(2)}, u32[]{:S(2)}) collective-permute-start(f32[256,128]{1,0:T(8,128)S(1)} %add_add_fusion), channel_id=1, source_target_pairs={{0,14},{2,0},{4,2},{6,4},{8,6},{10,8},{12,10},{14,12},{1,15},{3,1}... | collective-permute-start | bytes 393224 | tf_op jit(solution)/shard_map/ppermute | solution.py:311
  83.5 0.8 collective-permute-done.9.below0
  84.3 7.2 %collective-permute-done.12.below1 = f32[256,128]{1,0:T(8,128)S(1)} collective-permute-done((f32[256,128]{1,0:T(8,128)S(1)}, f32[256,128]{1,0:T(8,128)S(1)}, u32[]{:S(2)}, u32[]{:S(2)}) %collective-permute-start.12) | collective-permute-done | bytes 131104 | tf_op jit(solution)/shard_map/ppermute | solution.py:311
  92.0 1.2 %collective-permute-done.14 = f32[128,128]{1,0:T(8,128)S(1)} collective-permute-done((f32[128,128]{1,0:T(8,128)S(1)}, f32[128,128]{1,0:T(8,128)S(1)}, u32[]{:S(2)}, u32[]{:S(2)}) %collective-permute-start.14) | collective-permute-done | bytes 65568 | tf_op jit(solution)/shard_map/ppermute | solution.py:310
  93.2 0.9 collective-permute-start.15
  94.1 3.5 %collective-permute-done.15 = f32[128,128]{1,0:T(8,128)S(1)} collective-permute-done((f32[128,128]{1,0:T(8,128)S(1)}, f32[128,128]{1,0:T(8,128)S(1)}, u32[]{:S(2)}, u32[]{:S(2)}) %collective-permute-start.15) | collective-permute-done | bytes 65568 | tf_op jit(solution)/shard_map/ppermute | solution.py:311
  97.8 4.0 %collective-permute-done.16 = f32[128,128]{1,0:T(8,128)S(1)} collective-permute-done((f32[128,128]{1,0:T(8,128)S(1)}, f32[128,128]{1,0:T(8,128)S(1)}, u32[]{:S(2)}, u32[]{:S(2)}) %collective-permute-start.16) | collective-permute-done | bytes 65568 | tf_op jit(solution)/shard_map/ppermute | solution.py:311
  101.9 2.5 %collective-permute-start.17 = (f32[128,128]{1,0:T(8,128)S(1)}, f32[128,128]{1,0:T(8,128)S(1)}, u32[]{:S(2)}, u32[]{:S(2)}) collective-permute-start(f32[128,128]{1,0:T(8,128)S(1)} %add.26), channel_id=1, source_target_pairs={{0,8},{2,10},{4,12},{6,14},{8,0},{10,2},{12,4},{14,6},{1,9},{3,11}... | collective-permute-start | bytes 196616 | tf_op jit(solution)/shard_map/ppermute | solution.py:311
  104.4 2.7 %collective-permute-done.17 = f32[128,128]{1,0:T(8,128)S(1)} collective-permute-done((f32[128,128]{1,0:T(8,128)S(1)}, f32[128,128]{1,0:T(8,128)S(1)}, u32[]{:S(2)}, u32[]{:S(2)}) %collective-permute-start.17) | collective-permute-done | bytes 65568 | tf_op jit(solution)/shard_map/ppermute | solution.py:311
  107.1 5.2 %shard_map.67 = (f32[512,128]{1,0:T(8,128)}, f32[128,128]{1,0:T(8,128)}) custom-call(f32[512,128]{1,0:T(8,128)S(1)} %get-tuple-element.64.image, f32[128,128]{1,0:T(8,128)S(1)} %add.27.gram), custom_call_target="tpu_custom_call" | custom-call | flops 99999997952 | tf_op jit(solution)/shard_map/pallas_call | solution.py:18
  (31 shorter events, 1.5 us)
Async XLA Ops:
  0.6 0.9 copy-start.2
  1.5 0.7 copy-start.3
  4.8 0.8 copy-start
  5.6 7.6 %collective-permute-start = (bf16[520,1152]{1,0:T(8,128)(2,1)S(1)}, bf16[520,1152]{1,0:T(8,128)(2,1)S(1)}, u32[]{:S(2)}, u32[]{:S(2)}) collective-permute-start(bf16[520,1152]{1,0:T(8,128)(2,1)S(1)} %get-tuple-element.34.own), channel_id=1, source_target_pairs={{0,1},{1,0},{2,3},{3,2},{4,5},{5,4},{6,7},{7,6},{8,9},{9,8},{10,11... | collective-permute-start | bytes 3594248 | tf_op jit(solution)/shard_map/ppermute | solution.py:310
  6.1 30.9 %collective-permute-start.1 = (bf16[512,1024]{1,0:T(8,128)(2,1)}, bf16[512,1024]{1,0:T(8,128)(2,1)S(1)}, u32[]{:S(2)}, u32[]{:S(2)}) collective-permute-start(bf16[512,1024]{1,0:T(8,128)(2,1)} %embeddings.1), channel_id=1, source_target_pairs={{0,12},{2,14},{4,0},{6,2},{8,4},{10,6},{12,8},{14,10},{1,13},{3,15... | collective-permute-start | bytes 3145736 | tf_op jit(solution)/shard_map/ppermute | solution.py:311
  10.7 26.3 %collective-permute-start.2 = (bf16[520,128]{1,0:T(8,128)(2,1)}, bf16[520,128]{1,0:T(8,128)(2,1)}, u32[]{:S(2)}, u32[]{:S(2)}) collective-permute-start(bf16[520,128]{1,0:T(8,128)(2,1)} %get-tuple-element.36), channel_id=1, source_target_pairs={{0,12},{2,14},{4,0},{6,2},{8,4},{10,6},{12,8},{14,10},{1,13},{3,15... | collective-permute-start | bytes 399368 | tf_op jit(solution)/shard_map/ppermute | solution.py:311
  11.1 25.8 %collective-permute-start.3 = (bf16[256,1152]{1,0:T(8,128)(2,1)}, bf16[256,1152]{1,0:T(8,128)(2,1)}, u32[]{:S(2)}, u32[]{:S(2)}) collective-permute-start(bf16[256,1152]{1,0:T(8,128)(2,1)} %get-tuple-element.38), channel_id=1, source_target_pairs={{0,2},{2,0},{4,6},{6,4},{8,10},{10,8},{12,14},{14,12},{1,3},{3,1},... | collective-permute-start | bytes 1769480 | tf_op jit(solution)/shard_map/ppermute | solution.py:311
  13.3 26.0 %copy-start.1 = (bf16[264,1152]{1,0:T(8,128)(2,1)S(1)}, bf16[264,1152]{1,0:T(8,128)(2,1)}, u32[]{:S(2)}) copy-start(bf16[264,1152]{1,0:T(8,128)(2,1)} %copy-done) | copy-start | bytes 1824772
  16.3 45.4 %copy-start.4 = (f32[4,256]{1,0:T(4,128)}, f32[4,256]{1,0:T(4,128)S(1)}, u32[]{:S(2)}) copy-start(f32[4,256]{1,0:T(4,128)S(1)} %get-tuple-element.35.sq) | copy-start | bytes 12292
  37.0 30.4 %collective-permute-start.6 = (bf16[256,1152]{1,0:T(8,128)(2,1)}, bf16[256,1152]{1,0:T(8,128)(2,1)}, u32[]{:S(2)}, u32[]{:S(2)}) collective-permute-start(bf16[256,1152]{1,0:T(8,128)(2,1)} %collective-permute-done.3), channel_id=1, source_target_pairs={{0,4},{2,2},{4,8},{6,6},{8,12},{10,10},{12,0},{14,14},{1,5},{3,3},... | collective-permute-start | bytes 1769480 | tf_op jit(solution)/shard_map/ppermute | solution.py:311
  39.3 22.4 %collective-permute-start.4 = (bf16[264,1152]{1,0:T(8,128)(2,1)S(1)}, bf16[264,1152]{1,0:T(8,128)(2,1)S(1)}, u32[]{:S(2)}, u32[]{:S(2)}) collective-permute-start(bf16[264,1152]{1,0:T(8,128)(2,1)S(1)} %copy-done.1), channel_id=1, source_target_pairs={{0,2},{2,4},{4,6},{6,8},{8,10},{10,12},{12,14},{14,0},{1,3},{3,5},... | collective-permute-start | bytes 1824776 | tf_op jit(solution)/shard_map/ppermute | solution.py:311
  61.7 2.2 %collective-permute-start.5 = (bf16[264,1152]{1,0:T(8,128)(2,1)S(1)}, bf16[264,1152]{1,0:T(8,128)(2,1)S(1)}, u32[]{:S(2)}, u32[]{:S(2)}) collective-permute-start(bf16[264,1152]{1,0:T(8,128)(2,1)S(1)} %collective-permute-done.4.below), channel_id=1, source_target_pairs={{0,1},{1,0},{2,3},{3,2},{4,5},{5,4},{6,7},{7,6},{8,9},{9,8},{10,11... | collective-permute-start | bytes 1824776 | tf_op jit(solution)/shard_map/ppermute | solution.py:310
  67.4 2.5 %collective-permute-start.10 = (bf16[256,1152]{1,0:T(8,128)(2,1)}, bf16[256,1152]{1,0:T(8,128)(2,1)S(1)}, u32[]{:S(2)}, u32[]{:S(2)}) collective-permute-start(bf16[256,1152]{1,0:T(8,128)(2,1)} %collective-permute-done.6.below), channel_id=1, source_target_pairs={{0,1},{1,0},{2,3},{3,2},{4,5},{5,4},{6,7},{7,6},{8,9},{9,8},{10,11... | collective-permute-start | bytes 1769480 | tf_op jit(solution)/shard_map/ppermute | solution.py:310
  67.9 9.1 %collective-permute-start.8 = (f32[256,128]{1,0:T(8,128)}, f32[256,128]{1,0:T(8,128)}, u32[]{:S(2)}, u32[]{:S(2)}) collective-permute-start(f32[256,128]{1,0:T(8,128)} %get-tuple-element.59), channel_id=1, source_target_pairs={{0,1},{1,0},{2,3},{3,2},{4,5},{5,4},{6,7},{7,6},{8,9},{9,8},{10,11... | collective-permute-start | bytes 393224 | tf_op jit(solution)/shard_map/ppermute | solution.py:310
  69.9 3.5 %copy-start.5 = (f32[4,256]{1,0:T(4,128)S(1)}, f32[4,256]{1,0:T(4,128)}, u32[]{:S(2)}) copy-start(f32[4,256]{1,0:T(4,128)} %copy-done.4) | copy-start | bytes 12292
  73.0 6.7 %collective-permute-start.11 = (f32[256,128]{1,0:T(8,128)S(1)}, f32[256,128]{1,0:T(8,128)S(1)}, u32[]{:S(2)}, u32[]{:S(2)}) collective-permute-start(f32[256,128]{1,0:T(8,128)S(1)} %get-tuple-element.62), channel_id=1, source_target_pairs={{0,1},{1,0},{2,3},{3,2},{4,5},{5,4},{6,7},{7,6},{8,9},{9,8},{10,11... | collective-permute-start | bytes 393224 | tf_op jit(solution)/shard_map/ppermute | solution.py:310
  76.7 6.7 %collective-permute-start.7 = (f32[512,128]{1,0:T(8,128)S(1)}, f32[512,128]{1,0:T(8,128)S(1)}, u32[]{:S(2)}, u32[]{:S(2)}) collective-permute-start(f32[512,128]{1,0:T(8,128)S(1)} %get-tuple-element.57), channel_id=1, source_target_pairs={{0,1},{1,0},{2,3},{3,2},{4,5},{5,4},{6,7},{7,6},{8,9},{9,8},{10,11... | collective-permute-start | bytes 786440 | tf_op jit(solution)/shard_map/ppermute | solution.py:310
  77.9 6.4 %collective-permute-start.9 = (f32[256,128]{1,0:T(8,128)S(1)}, f32[256,128]{1,0:T(8,128)S(1)}, u32[]{:S(2)}, u32[]{:S(2)}) collective-permute-start(f32[256,128]{1,0:T(8,128)S(1)} %add.21), channel_id=1, source_target_pairs={{0,14},{2,0},{4,2},{6,4},{8,6},{10,8},{12,10},{14,12},{1,15},{3,1}... | collective-permute-start | bytes 393224 | tf_op jit(solution)/shard_map/ppermute | solution.py:311
  79.7 11.8 %collective-permute-start.13 = (f32[512,128]{1,0:T(8,128)S(1)}, f32[512,128]{1,0:T(8,128)S(1)}, u32[]{:S(2)}, u32[]{:S(2)}) collective-permute-start(f32[512,128]{1,0:T(8,128)S(1)} %get-tuple-element.63), channel_id=1, source_target_pairs={{0,4},{2,6},{4,8},{6,10},{8,12},{10,14},{12,0},{14,2},{1,5},{3,7},... | collective-permute-start | bytes 786440 | tf_op jit(solution)/shard_map/ppermute | solution.py:311
  79.7 11.7 %collective-permute-start.12 = (f32[256,128]{1,0:T(8,128)S(1)}, f32[256,128]{1,0:T(8,128)S(1)}, u32[]{:S(2)}, u32[]{:S(2)}) collective-permute-start(f32[256,128]{1,0:T(8,128)S(1)} %add_add_fusion), channel_id=1, source_target_pairs={{0,14},{2,0},{4,2},{6,4},{8,6},{10,8},{12,10},{14,12},{1,15},{3,1}... | collective-permute-start | bytes 393224 | tf_op jit(solution)/shard_map/ppermute | solution.py:311
  91.9 1.3 %collective-permute-start.14 = (f32[128,128]{1,0:T(8,128)S(1)}, f32[128,128]{1,0:T(8,128)S(1)}, u32[]{:S(2)}, u32[]{:S(2)}) collective-permute-start(f32[128,128]{1,0:T(8,128)S(1)} %get-tuple-element.65), channel_id=1, source_target_pairs={{0,1},{1,0},{2,3},{3,2},{4,5},{5,4},{6,7},{7,6},{8,9},{9,8},{10,11... | collective-permute-start | bytes 196616 | tf_op jit(solution)/shard_map/ppermute | solution.py:310
  93.2 4.3 %collective-permute-start.15 = (f32[128,128]{1,0:T(8,128)S(1)}, f32[128,128]{1,0:T(8,128)S(1)}, u32[]{:S(2)}, u32[]{:S(2)}) collective-permute-start(f32[128,128]{1,0:T(8,128)S(1)} %add.24), channel_id=1, source_target_pairs={{0,2},{2,0},{4,6},{6,4},{8,10},{10,8},{12,14},{14,12},{1,3},{3,1},... | collective-permute-start | bytes 196616 | tf_op jit(solution)/shard_map/ppermute | solution.py:311
  97.6 4.3 %collective-permute-start.16 = (f32[128,128]{1,0:T(8,128)S(1)}, f32[128,128]{1,0:T(8,128)S(1)}, u32[]{:S(2)}, u32[]{:S(2)}) collective-permute-start(f32[128,128]{1,0:T(8,128)S(1)} %add.25), channel_id=1, source_target_pairs={{0,4},{2,6},{4,0},{6,2},{8,12},{10,14},{12,8},{14,10},{1,5},{3,7},... | collective-permute-start | bytes 196616 | tf_op jit(solution)/shard_map/ppermute | solution.py:311
  101.9 5.2 %collective-permute-start.17 = (f32[128,128]{1,0:T(8,128)S(1)}, f32[128,128]{1,0:T(8,128)S(1)}, u32[]{:S(2)}, u32[]{:S(2)}) collective-permute-start(f32[128,128]{1,0:T(8,128)S(1)} %add.26), channel_id=1, source_target_pairs={{0,8},{2,10},{4,12},{6,14},{8,0},{10,2},{12,4},{14,6},{1,9},{3,11}... | collective-permute-start | bytes 196616 | tf_op jit(solution)/shard_map/ppermute | solution.py:311

commit v6 on v4

--- a/solution.py
+++ b/solution.py
@@ -21,6 +21,7 @@
         in_specs=[in_smem] * scalars + [in_vmem] * (len(operands) - scalars),
         out_specs=jax.tree.map(lambda _: in_vmem, out_shapes),
         compiler_params=pltpu.CompilerParams(vmem_limit_bytes=48 << 20),
+        cost_estimate=pl.CostEstimate(flops=10**11, transcendentals=0, bytes_accessed=0),
     )(*operands)
 
 
@@ -278,7 +279,7 @@
     image = shape(half, width)
     sq_rows = shape(4, size)
     self_image, sq = vmem_call(self_body, (image, sq_rows), inv_width, sub, own, other, scalars=2)
-    first, swapped = after(first, swapped, above, self_image), after(swapped, above, self_image)
+    first, swapped = after(first, swapped, self_image), after(swapped, self_image)
     below = [blk_move(first, 1), blk_route(swapped, lambda i: i if i & 1 else i + 2) if relayed else blk_move(swapped, 1)]
     above_image, *back = vmem_call(
         above_own_body, (image, *(shape(width, size),) * 4), inv_width, sub, sq, above, own, other, scalars=2

time: 101 us -> 97.6 us (0.966)
  waiting for transfers between devices: 53 us -> 48.3 us
  Pallas kernels: 23.7 us -> 24.9 us
    ppermute x9, waiting for transfers between devices: 50.5 us -> 47 us  [per_device(): lax.ppermute(v, 'blk', [(i, to(i) % n_blk) for i in range(n_blk)])]
    pallas_call x7, Pallas kernels: 23.7 us -> 24.9 us  [vmem_call(): pl.pallas_call(body, out_shape=out_shapes, in_specs=[in_smem] * scalars +...]
    ppermute x5, waiting for transfers between devices: 2.42 us -> 1.25 us  [per_device(): sub_move = lambda v: lax.ppermute(v, 'sub', [(0, 1), (1, 0)])]
  transfers between devices with their start and end apart: 14 -> 14, of which waited for: 11 -> 10; matrix products, arithmetic and copies ran while one was open for 0% -> 0% of each run, Pallas kernels for 12% -> 15%
where the time goes in v6:
time: 97.6 us; the launch traced here: 97.3 us
  waiting for transfers between devices  48.3 us (49%)
  Pallas kernels  24.9 us (26%)
  starting transfers between devices  19.7 us (20%)
  local copies, waits for them, and re-layouts  2.8 us (3%)
  between operations  1.4 us (1%)
    ppermute x9, waiting for transfers between devices, per_device(): lax.ppermute(v, 'blk', [(i, to(i) % n_blk) for i in range(n_blk)])  47 us
    pallas_call x7, Pallas kernels, vmem_call(): pl.pallas_call(body, out_shape=out_shapes, in_specs=[in_smem] * scalars +...  24.9 us
    ppermute x9, starting transfers between devices, per_device(): lax.ppermute(v, 'blk', [(i, to(i) % n_blk) for i in range(n_blk)])  18.4 us
    unnamed x6, local copies, waits for them, and re-layouts  2.8 us
  transfers between devices with their start and end apart: 14, of which 10 were waited for; matrix products, arithmetic and copies ran while one was open for 0% of the time, Pallas kernels for 15%

profile of v6, /device:TPU:0, one launch (start us, length us, event | category | flops | bytes accessed | tf_op | source)
XLA Modules:
  0.0 97.3 jit_solution(354009481171298376)
XLA Ops:
  0.6 1.2 %copy-done = bf16[512,1024]{1,0:T(8,128)(2,1)S(1)} copy-done((bf16[512,1024]{1,0:T(8,128)(2,1)S(1)}, bf16[512,1024]{1,0:T(8,128)(2,1)}, u32[]{:S(2)}) %copy-start) | copy-done | bytes 1048600
  1.9 0.9 copy-done.1
  2.8 0.7 copy-done.2
  3.4 1.0 %shard_map.59 = (bf16[520,1152]{1,0:T(8,128)(2,1)S(1)}, bf16[264,1152]{1,0:T(8,128)(2,1)S(1)}, bf16[256,1152]{1,0:T(8,128)(2,1)}) custom-call(bf16[512,1024]{1,0:T(8,128)(2,1)S(1)} %copy-done, bf16[512,128]{1,0:T(8,128)(2,1)S(1)} %copy-done.1, s32[4,56]{1,0:T(4,128)S(1)} %copy-done.2), custom_call_target="tpu_custom_call" | custom-call | flops 99999997952 | tf_op jit(solution)/shard_map/pallas_call | solution.py:18
  4.4 0.5 collective-permute-start
  4.9 4.6 %collective-permute-start.4 = (bf16[520,1152]{1,0:T(8,128)(2,1)S(1)}, bf16[520,1152]{1,0:T(8,128)(2,1)S(1)}, u32[]{:S(2)}, u32[]{:S(2)}) collective-permute-start(bf16[520,1152]{1,0:T(8,128)(2,1)S(1)} %get-tuple-element.23.own), channel_id=1, source_target_pairs={{0,12},{2,14},{4,0},{6,2},{8,4},{10,6},{12,8},{14,10},{1,13},{3,15... | collective-permute-start | bytes 3594248 | tf_op jit(solution)/shard_map/ppermute | solution.py:265
  9.5 1.5 %collective-permute-start.1 = (bf16[256,1152]{1,0:T(8,128)(2,1)}, bf16[256,1152]{1,0:T(8,128)(2,1)}, u32[]{:S(2)}, u32[]{:S(2)}) collective-permute-start(bf16[256,1152]{1,0:T(8,128)(2,1)} %get-tuple-element.26), channel_id=1, source_target_pairs={{0,2},{2,0},{4,6},{6,4},{8,10},{10,8},{12,14},{14,12},{1,3},{3,1},... | collective-permute-start | bytes 1769480 | tf_op jit(solution)/shard_map/ppermute | solution.py:265
  11.6 4.3 %shard_map.60 = (f32[512,128]{1,0:T(8,128)S(1)}, f32[4,256]{1,0:T(4,128)S(1)}) custom-call(f32[1]{0:T(128)S(6)} %copy.6.inverse, s32[1]{0:T(128)} %bitcast.sub, bf16[520,1152]{1,0:T(8,128)(2,1)S(1)} %get-tuple-element.23.own, bf16[520,1152]{1,0:T(8,128)(2,1)} %collective-permute-done.other), custom_call_target="tpu_custom_call" | custom-call | flops 99999997952 | tf_op jit(solution)/shard_map/pallas_call | solution.py:18
  16.0 9.3 %collective-permute-done.1 = bf16[256,1152]{1,0:T(8,128)(2,1)} collective-permute-done((bf16[256,1152]{1,0:T(8,128)(2,1)}, bf16[256,1152]{1,0:T(8,128)(2,1)}, u32[]{:S(2)}, u32[]{:S(2)}) %collective-permute-start.1) | collective-permute-done | bytes 589856 | tf_op jit(solution)/shard_map/ppermute | solution.py:265
  25.3 1.9 %collective-permute-start.3 = (bf16[256,1152]{1,0:T(8,128)(2,1)}, bf16[256,1152]{1,0:T(8,128)(2,1)S(1)}, u32[]{:S(2)}, u32[]{:S(2)}) collective-permute-start(bf16[256,1152]{1,0:T(8,128)(2,1)} %collective-permute-done.1), channel_id=1, source_target_pairs={{0,4},{2,2},{4,8},{6,6},{8,12},{10,10},{12,0},{14,14},{1,5},{3,3},... | collective-permute-start | bytes 1769480 | tf_op jit(solution)/shard_map/ppermute | solution.py:265
  27.2 1.3 %collective-permute-start.2 = (bf16[264,1152]{1,0:T(8,128)(2,1)S(1)}, bf16[264,1152]{1,0:T(8,128)(2,1)S(1)}, u32[]{:S(2)}, u32[]{:S(2)}) collective-permute-start(bf16[264,1152]{1,0:T(8,128)(2,1)S(1)} %get-tuple-element.28), channel_id=1, source_target_pairs={{0,2},{2,4},{4,6},{6,8},{8,10},{10,12},{12,14},{14,0},{1,3},{3,5},... | collective-permute-start | bytes 1824776 | tf_op jit(solution)/shard_map/ppermute | solution.py:265
  28.5 7.7 %collective-permute-done.4.above = bf16[520,1152]{1,0:T(8,128)(2,1)S(1)} collective-permute-done((bf16[520,1152]{1,0:T(8,128)(2,1)S(1)}, bf16[520,1152]{1,0:T(8,128)(2,1)S(1)}, u32[]{:S(2)}, u32[]{:S(2)}) %collective-permute-start.4) | collective-permute-done | bytes 1198112 | tf_op jit(solution)/shard_map/ppermute | solution.py:265
  36.2 5.0 %shard_map.61 = (f32[512,128]{1,0:T(8,128)S(1)}, f32[128,256]{1,0:T(8,128)S(1)}, f32[128,256]{1,0:T(8,128)S(1)}, f32[128,256]{1,0:T(8,128)S(1)}, f32[128,256]{1,0:T(8,128)S(1)}) custom-call(f32[1]{0:T(128)S(6)} %copy.6.inverse, s32[1]{0:T(128)} %bitcast.sub, f32[4,256]{1,0:T(4,128)S(1)} %get-tuple-element.24.sq, ...), custom_call_target="tpu_custom_call" | custom-call | flops 99999997952 | tf_op jit(solution)/shard_map/pallas_call | solution.py:18
  41.2 8.1 %collective-permute-done.3 = bf16[256,1152]{1,0:T(8,128)(2,1)S(1)} collective-permute-done((bf16[256,1152]{1,0:T(8,128)(2,1)}, bf16[256,1152]{1,0:T(8,128)(2,1)S(1)}, u32[]{:S(2)}, u32[]{:S(2)}) %collective-permute-start.3) | collective-permute-done | bytes 589856 | tf_op jit(solution)/shard_map/ppermute | solution.py:265
  49.3 1.3 %collective-permute-done.2 = bf16[264,1152]{1,0:T(8,128)(2,1)S(1)} collective-permute-done((bf16[264,1152]{1,0:T(8,128)(2,1)S(1)}, bf16[264,1152]{1,0:T(8,128)(2,1)S(1)}, u32[]{:S(2)}, u32[]{:S(2)}) %collective-permute-start.2) | collective-permute-done | bytes 608288 | tf_op jit(solution)/shard_map/ppermute | solution.py:265
  50.6 0.1 pad_maximum_fusion.below
  50.8 5.1 %shard_map.62 = (f32[512,128]{1,0:T(8,128)S(1)}, f32[512,128]{1,0:T(8,128)S(1)}, f32[512,128]{1,0:T(8,128)S(1)}) custom-call(f32[1]{0:T(128)S(6)} %copy.6.inverse, s32[1]{0:T(128)} %bitcast.sub, f32[4,256]{1,0:T(4,128)S(1)} %get-tuple-element.24.sq, bf16[520,1152]{1,0:T(8,128)(2,1)S(1)} %pad_maximum_fusion.below, ...), custom_call_target="tpu_custom_call" | custom-call | flops 99999997952 | tf_op jit(solution)/shard_map/pallas_call | solution.py:18
  55.9 3.9 %shard_map.63 = (f32[512,128]{1,0:T(8,128)S(1)}, f32[512,128]{1,0:T(8,128)S(1)}, f32[512,128]{1,0:T(8,128)S(1)}) custom-call(f32[1]{0:T(128)S(6)} %copy.6.inverse, s32[1]{0:T(128)} %bitcast.sub, bf16[520,1152]{1,0:T(8,128)(2,1)S(1)} %collective-permute-done.4.above, bf16[520,1152]{1,0:T(8,128)(2,1)S(1)} %pad_maximum_fusion.below, ...), custom_call_target="tpu_custom_call" | custom-call | flops 99999997952 | tf_op jit(solution)/shard_map/pallas_call | solution.py:18
  59.9 0.6 collective-permute-start.7
  60.5 1.7 %collective-permute-start.9 = (f32[512,128]{1,0:T(8,128)S(1)}, f32[512,128]{1,0:T(8,128)S(1)}, u32[]{:S(2)}, u32[]{:S(2)}) collective-permute-start(f32[512,128]{1,0:T(8,128)S(1)} %get-tuple-element.41), channel_id=1, source_target_pairs={{0,4},{2,6},{4,8},{6,10},{8,12},{10,14},{12,0},{14,2},{1,5},{3,7},... | collective-permute-start | bytes 786440 | tf_op jit(solution)/shard_map/ppermute | solution.py:265
  62.2 1.6 %collective-permute-start.8 = (f32[512,128]{1,0:T(8,128)S(1)}, f32[512,128]{1,0:T(8,128)S(1)}, u32[]{:S(2)}, u32[]{:S(2)}) collective-permute-start(f32[512,128]{1,0:T(8,128)S(1)} %add.15), channel_id=1, source_target_pairs={{0,14},{2,0},{4,2},{6,4},{8,6},{10,8},{12,10},{14,12},{1,15},{3,1}... | collective-permute-start | bytes 786440 | tf_op jit(solution)/shard_map/ppermute | solution.py:265
  63.8 7.7 %collective-permute-done.9.above = f32[512,128]{1,0:T(8,128)S(1)} collective-permute-done((f32[512,128]{1,0:T(8,128)S(1)}, f32[512,128]{1,0:T(8,128)S(1)}, u32[]{:S(2)}, u32[]{:S(2)}) %collective-permute-start.9) | collective-permute-done | bytes 262176 | tf_op jit(solution)/shard_map/ppermute | solution.py:265
  71.5 2.5 %collective-permute-done.8.below = f32[512,128]{1,0:T(8,128)S(1)} collective-permute-done((f32[512,128]{1,0:T(8,128)S(1)}, f32[512,128]{1,0:T(8,128)S(1)}, u32[]{:S(2)}, u32[]{:S(2)}) %collective-permute-start.8) | collective-permute-done | bytes 262176 | tf_op jit(solution)/shard_map/ppermute | solution.py:265
  74.0 0.4 shard_map.64
  74.5 1.2 %collective-permute-done.10 = f32[128,128]{1,0:T(8,128)S(1)} collective-permute-done((f32[128,128]{1,0:T(8,128)S(1)}, f32[128,128]{1,0:T(8,128)S(1)}, u32[]{:S(2)}, u32[]{:S(2)}) %collective-permute-start.10) | collective-permute-done | bytes 65568 | tf_op jit(solution)/shard_map/ppermute | solution.py:264
  75.8 3.6 %collective-permute-start.11 = (f32[128,128]{1,0:T(8,128)S(1)}, f32[128,128]{1,0:T(8,128)S(1)}, u32[]{:S(2)}, u32[]{:S(2)}) collective-permute-start(f32[128,128]{1,0:T(8,128)S(1)} %add.16), channel_id=1, source_target_pairs={{0,2},{2,0},{4,6},{6,4},{8,10},{10,8},{12,14},{14,12},{1,3},{3,1},... | collective-permute-start | bytes 196616 | tf_op jit(solution)/shard_map/ppermute | solution.py:265
  79.4 2.4 %collective-permute-done.11 = f32[128,128]{1,0:T(8,128)S(1)} collective-permute-done((f32[128,128]{1,0:T(8,128)S(1)}, f32[128,128]{1,0:T(8,128)S(1)}, u32[]{:S(2)}, u32[]{:S(2)}) %collective-permute-start.11) | collective-permute-done | bytes 65568 | tf_op jit(solution)/shard_map/ppermute | solution.py:265
  81.8 1.1 %collective-permute-start.12 = (f32[128,128]{1,0:T(8,128)S(1)}, f32[128,128]{1,0:T(8,128)S(1)}, u32[]{:S(2)}, u32[]{:S(2)}) collective-permute-start(f32[128,128]{1,0:T(8,128)S(1)} %add.17), channel_id=1, source_target_pairs={{0,4},{2,6},{4,0},{6,2},{8,12},{10,14},{12,8},{14,10},{1,5},{3,7},... | collective-permute-start | bytes 196616 | tf_op jit(solution)/shard_map/ppermute | solution.py:265
  82.9 3.2 %collective-permute-done.12 = f32[128,128]{1,0:T(8,128)S(1)} collective-permute-done((f32[128,128]{1,0:T(8,128)S(1)}, f32[128,128]{1,0:T(8,128)S(1)}, u32[]{:S(2)}, u32[]{:S(2)}) %collective-permute-start.12) | collective-permute-done | bytes 65568 | tf_op jit(solution)/shard_map/ppermute | solution.py:265
  86.2 1.2 %collective-permute-start.13 = (f32[128,128]{1,0:T(8,128)S(1)}, f32[128,128]{1,0:T(8,128)S(1)}, u32[]{:S(2)}, u32[]{:S(2)}) collective-permute-start(f32[128,128]{1,0:T(8,128)S(1)} %add.18), channel_id=1, source_target_pairs={{0,8},{2,10},{4,12},{6,14},{8,0},{10,2},{12,4},{14,6},{1,9},{3,11}... | collective-permute-start | bytes 196616 | tf_op jit(solution)/shard_map/ppermute | solution.py:265
  87.3 4.8 %collective-permute-done.13 = f32[128,128]{1,0:T(8,128)S(1)} collective-permute-done((f32[128,128]{1,0:T(8,128)S(1)}, f32[128,128]{1,0:T(8,128)S(1)}, u32[]{:S(2)}, u32[]{:S(2)}) %collective-permute-start.13) | collective-permute-done | bytes 65568 | tf_op jit(solution)/shard_map/ppermute | solution.py:265
  92.1 5.1 %shard_map.65 = (f32[512,128]{1,0:T(8,128)}, f32[128,128]{1,0:T(8,128)}) custom-call(f32[512,128]{1,0:T(8,128)S(1)} %get-tuple-element.42.image, f32[128,128]{1,0:T(8,128)S(1)} %add.19.gram), custom_call_target="tpu_custom_call" | custom-call | flops 99999997952 | tf_op jit(solution)/shard_map/pallas_call | solution.py:18
  (15 shorter events, 0.3 us)
Async XLA Ops:
  0.6 1.2 %copy-start = (bf16[512,1024]{1,0:T(8,128)(2,1)S(1)}, bf16[512,1024]{1,0:T(8,128)(2,1)}, u32[]{:S(2)}) copy-start(bf16[512,1024]{1,0:T(8,128)(2,1)} %embeddings.1) | copy-start | bytes 3145732
  1.9 0.9 copy-start.1
  2.8 0.7 copy-start.2
  4.4 7.2 %collective-permute-start = (bf16[520,1152]{1,0:T(8,128)(2,1)S(1)}, bf16[520,1152]{1,0:T(8,128)(2,1)}, u32[]{:S(2)}, u32[]{:S(2)}) collective-permute-start(bf16[520,1152]{1,0:T(8,128)(2,1)S(1)} %get-tuple-element.23.own), channel_id=1, source_target_pairs={{0,1},{1,0},{2,3},{3,2},{4,5},{5,4},{6,7},{7,6},{8,9},{9,8},{10,11... | collective-permute-start | bytes 3594248 | tf_op jit(solution)/shard_map/ppermute | solution.py:264
  4.9 31.3 %collective-permute-start.4 = (bf16[520,1152]{1,0:T(8,128)(2,1)S(1)}, bf16[520,1152]{1,0:T(8,128)(2,1)S(1)}, u32[]{:S(2)}, u32[]{:S(2)}) collective-permute-start(bf16[520,1152]{1,0:T(8,128)(2,1)S(1)} %get-tuple-element.23.own), channel_id=1, source_target_pairs={{0,12},{2,14},{4,0},{6,2},{8,4},{10,6},{12,8},{14,10},{1,13},{3,15... | collective-permute-start | bytes 3594248 | tf_op jit(solution)/shard_map/ppermute | solution.py:265
  9.5 15.8 %collective-permute-start.1 = (bf16[256,1152]{1,0:T(8,128)(2,1)}, bf16[256,1152]{1,0:T(8,128)(2,1)}, u32[]{:S(2)}, u32[]{:S(2)}) collective-permute-start(bf16[256,1152]{1,0:T(8,128)(2,1)} %get-tuple-element.26), channel_id=1, source_target_pairs={{0,2},{2,0},{4,6},{6,4},{8,10},{10,8},{12,14},{14,12},{1,3},{3,1},... | collective-permute-start | bytes 1769480 | tf_op jit(solution)/shard_map/ppermute | solution.py:265
  25.3 24.1 %collective-permute-start.3 = (bf16[256,1152]{1,0:T(8,128)(2,1)}, bf16[256,1152]{1,0:T(8,128)(2,1)S(1)}, u32[]{:S(2)}, u32[]{:S(2)}) collective-permute-start(bf16[256,1152]{1,0:T(8,128)(2,1)} %collective-permute-done.1), channel_id=1, source_target_pairs={{0,4},{2,2},{4,8},{6,6},{8,12},{10,10},{12,0},{14,14},{1,5},{3,3},... | collective-permute-start | bytes 1769480 | tf_op jit(solution)/shard_map/ppermute | solution.py:265
  27.2 23.5 %collective-permute-start.2 = (bf16[264,1152]{1,0:T(8,128)(2,1)S(1)}, bf16[264,1152]{1,0:T(8,128)(2,1)S(1)}, u32[]{:S(2)}, u32[]{:S(2)}) collective-permute-start(bf16[264,1152]{1,0:T(8,128)(2,1)S(1)} %get-tuple-element.28), channel_id=1, source_target_pairs={{0,2},{2,4},{4,6},{6,8},{8,10},{10,12},{12,14},{14,0},{1,3},{3,5},... | collective-permute-start | bytes 1824776 | tf_op jit(solution)/shard_map/ppermute | solution.py:265
  50.7 5.2 %collective-permute-start.6 = (bf16[520,1152]{1,0:T(8,128)(2,1)S(1)}, bf16[520,1152]{1,0:T(8,128)(2,1)S(1)}, u32[]{:S(2)}, u32[]{:S(2)}) collective-permute-start(bf16[520,1152]{1,0:T(8,128)(2,1)S(1)} %pad_maximum_fusion.below), channel_id=1, source_target_pairs={{0,1},{1,0},{2,3},{3,2},{4,5},{5,4},{6,7},{7,6},{8,9},{9,8},{10,11... | collective-permute-start | bytes 3594248 | tf_op jit(solution)/shard_map/ppermute | solution.py:264
  59.9 2.3 %collective-permute-start.7 = (f32[512,128]{1,0:T(8,128)S(1)}, f32[512,128]{1,0:T(8,128)S(1)}, u32[]{:S(2)}, u32[]{:S(2)}) collective-permute-start(f32[512,128]{1,0:T(8,128)S(1)} %get-tuple-element.40), channel_id=1, source_target_pairs={{0,1},{1,0},{2,3},{3,2},{4,5},{5,4},{6,7},{7,6},{8,9},{9,8},{10,11... | collective-permute-start | bytes 786440 | tf_op jit(solution)/shard_map/ppermute | solution.py:264
  60.4 3.4 %collective-permute-start.5 = (f32[512,128]{1,0:T(8,128)S(1)}, f32[512,128]{1,0:T(8,128)S(1)}, u32[]{:S(2)}, u32[]{:S(2)}) collective-permute-start(f32[512,128]{1,0:T(8,128)S(1)} %get-tuple-element.37), channel_id=1, source_target_pairs={{0,1},{1,0},{2,3},{3,2},{4,5},{5,4},{6,7},{7,6},{8,9},{9,8},{10,11... | collective-permute-start | bytes 786440 | tf_op jit(solution)/shard_map/ppermute | solution.py:264
  60.5 11.0 %collective-permute-start.9 = (f32[512,128]{1,0:T(8,128)S(1)}, f32[512,128]{1,0:T(8,128)S(1)}, u32[]{:S(2)}, u32[]{:S(2)}) collective-permute-start(f32[512,128]{1,0:T(8,128)S(1)} %get-tuple-element.41), channel_id=1, source_target_pairs={{0,4},{2,6},{4,8},{6,10},{8,12},{10,14},{12,0},{14,2},{1,5},{3,7},... | collective-permute-start | bytes 786440 | tf_op jit(solution)/shard_map/ppermute | solution.py:265
  62.2 11.8 %collective-permute-start.8 = (f32[512,128]{1,0:T(8,128)S(1)}, f32[512,128]{1,0:T(8,128)S(1)}, u32[]{:S(2)}, u32[]{:S(2)}) collective-permute-start(f32[512,128]{1,0:T(8,128)S(1)} %add.15), channel_id=1, source_target_pairs={{0,14},{2,0},{4,2},{6,4},{8,6},{10,8},{12,10},{14,12},{1,15},{3,1}... | collective-permute-start | bytes 786440 | tf_op jit(solution)/shard_map/ppermute | solution.py:265
  74.4 1.3 %collective-permute-start.10 = (f32[128,128]{1,0:T(8,128)S(1)}, f32[128,128]{1,0:T(8,128)S(1)}, u32[]{:S(2)}, u32[]{:S(2)}) collective-permute-start(f32[128,128]{1,0:T(8,128)S(1)} %get-tuple-element.43), channel_id=1, source_target_pairs={{0,1},{1,0},{2,3},{3,2},{4,5},{5,4},{6,7},{7,6},{8,9},{9,8},{10,11... | collective-permute-start | bytes 196616 | tf_op jit(solution)/shard_map/ppermute | solution.py:264
  75.8 6.1 %collective-permute-start.11 = (f32[128,128]{1,0:T(8,128)S(1)}, f32[128,128]{1,0:T(8,128)S(1)}, u32[]{:S(2)}, u32[]{:S(2)}) collective-permute-start(f32[128,128]{1,0:T(8,128)S(1)} %add.16), channel_id=1, source_target_pairs={{0,2},{2,0},{4,6},{6,4},{8,10},{10,8},{12,14},{14,12},{1,3},{3,1},... | collective-permute-start | bytes 196616 | tf_op jit(solution)/shard_map/ppermute | solution.py:265
  81.8 4.3 %collective-permute-start.12 = (f32[128,128]{1,0:T(8,128)S(1)}, f32[128,128]{1,0:T(8,128)S(1)}, u32[]{:S(2)}, u32[]{:S(2)}) collective-permute-start(f32[128,128]{1,0:T(8,128)S(1)} %add.17), channel_id=1, source_target_pairs={{0,4},{2,6},{4,0},{6,2},{8,12},{10,14},{12,8},{14,10},{1,5},{3,7},... | collective-permute-start | bytes 196616 | tf_op jit(solution)/shard_map/ppermute | solution.py:265
  86.2 5.9 %collective-permute-start.13 = (f32[128,128]{1,0:T(8,128)S(1)}, f32[128,128]{1,0:T(8,128)S(1)}, u32[]{:S(2)}, u32[]{:S(2)}) collective-permute-start(f32[128,128]{1,0:T(8,128)S(1)} %add.18), channel_id=1, source_target_pairs={{0,8},{2,10},{4,12},{6,14},{8,0},{10,2},{12,4},{14,6},{1,9},{3,11}... | collective-permute-start | bytes 196616 | tf_op jit(solution)/shard_map/ppermute | solution.py:265

commit v7 on v6

--- a/solution.py
+++ b/solution.py
@@ -20,7 +20,7 @@
         out_shape=out_shapes,
         in_specs=[in_smem] * scalars + [in_vmem] * (len(operands) - scalars),
         out_specs=jax.tree.map(lambda _: in_vmem, out_shapes),
-        compiler_params=pltpu.CompilerParams(vmem_limit_bytes=48 << 20),
+        compiler_params=pltpu.CompilerParams(vmem_limit_bytes=24 << 20),
         cost_estimate=pl.CostEstimate(flops=10**11, transcendentals=0, bytes_accessed=0),
     )(*operands)
 
@@ -52,17 +52,22 @@
     return jnp.concatenate([ahead, back], axis=0)
 
 
-def marks(ref, size):
-    return ref[size : size + MARK, :TILE].astype(F32)[: 2 * size // TILE]
-
-
-def pieces(ref):
-    size = (ref.shape[0] - MARK) // 2
-    return [ref[:size], ref[size + MARK :]]
-
-
-def squares(piece, features):
-    wide = piece[:, :features].astype(F32)
+def marks(ref, half):
+    return ref[ref.shape[0] - MARK :, ref.shape[1] - TILE :].astype(F32)[: half // TILE]
+
+
+def pieces(*refs):
+    size = min(r.shape[0] for r in refs)
+    return [(r[:size, : r.shape[1] - TILE], r[:size, r.shape[1] - TILE :]) for r in refs]
+
+
+def apart(features, panel):
+    size = features.shape[0] // 2
+    return [(features[rows], panel[rows]) for rows in (slice(0, size), slice(size, 2 * size))]
+
+
+def squares(features):
+    wide = features.astype(F32)
     return jnp.sum(wide * wide, axis=1, keepdims=True)
 
 
@@ -70,121 +75,104 @@
     return jnp.broadcast_to(column, (column.shape[0], TILE)).T[:1]
 
 
-def square_rows(blocks, out):
-    rows = [as_row(squares(p, p.shape[1] - TILE)) for block in blocks for p in pieces(block)]
-    for k, row in enumerate(rows):
-        out[k : k + 1] = row
-    return rows
-
-
 def read_rows(ref):
     return [ref[k : k + 1] for k in range(ref.shape[0])]
 
 
-def columns_of(blocks, sq_rows, masks):
+def columns_of(own, other, sq_rows, masks):
     out = []
-    for h, block in enumerate(blocks):
-        for k, piece in enumerate(pieces(block)):
-            size = piece.shape[0]
-            out.append((piece, sq_rows[2 * h + k], masks[h][:, k * size : (k + 1) * size]))
+    for half, mask in zip((own, other), masks):
+        for k, (features, panel) in enumerate(half):
+            size = features.shape[0]
+            out.append((features, panel, sq_rows[len(out)], mask[:, k * size : (k + 1) * size]))
     return out
 
 
-def products(inverse, piece, tile, columns, back):
-    size, width = piece.shape
-    features = width - TILE
-    row_sq = squares(piece, features)
-    doubled = piece[:, :features] * 2
-    panel_t = piece[:, features:].astype(F32).T.astype(BF16)
-    image = None
-    for k, (other, col_sq, mask) in enumerate(columns):
-        tiles = mask.shape[0] // 2
-        gram2 = contract(doubled, other[:, :features], ((1,), (1,)))
-        kernel = jnp.exp(-inverse * jnp.maximum(row_sq + col_sq - gram2, 0.0))
-
-        def masked(first):
-            return jnp.concatenate(
-                [kernel[i * TILE : (i + 1) * TILE] * mask[first + i : first + i + 1] for i in range(size // TILE)], axis=0
-            ).astype(BF16)
-
-        term = contract(masked(tile), other[:, features:], ((1,), (0,)))
-        image = term if image is None else image + term
+def products(inverse, rows, columns, back):
+    panels = jnp.concatenate([panel for _, panel, _, _ in columns], axis=0)
+    images = []
+    for r, (features, panel) in enumerate(rows):
+        size = features.shape[0]
+        row_sq = squares(features)
+        doubled = features * 2
+        tile = r * size // TILE
+        ahead, behind = [], []
+        for other, _, col_sq, mask in columns:
+            tiles = mask.shape[0] // 2
+            gram2 = contract(doubled, other, ((1,), (1,)))
+            kernel = jnp.exp(-inverse * jnp.maximum(row_sq + col_sq - gram2, 0.0))
+
+            def masked(first):
+                parts = [kernel[i * TILE : (i + 1) * TILE] * mask[first + i : first + i + 1] for i in range(size // TILE)]
+                return jnp.concatenate(parts, axis=0).astype(BF16)
+
+            ahead.append(masked(tile))
+            if back is not None:
+                behind.append(masked(tiles + tile))
+        images.append(contract(jnp.concatenate(ahead, axis=1), panels, ((1,), (0,))))
         if back is not None:
-            term = contract(panel_t, masked(tiles + tile), ((1,), (0,)))
-            back[k] = term if back[k] is None else back[k] + term
-    return image
-
-
-def store_all(outs, values):
-    for out, value in zip(outs, values):
-        out[...] = value
-
-
-def pack_body(embeddings, panel, tile_mask, own, first, last):
+            panel_t = panel.astype(F32).T.astype(BF16)
+            back = back + contract(panel_t, jnp.concatenate(behind, axis=1), ((1,), (0,)))
+    return jnp.concatenate(images, axis=0), back
+
+
+def pack_body(embeddings, panel, tile_mask, first, last, panel_mark):
     half, features = embeddings.shape
     size = half // 2
     tiles, window = tile_mask.shape
     at = lax.broadcasted_iota(jnp.int32, (window, TILE), 0) == lax.broadcasted_iota(jnp.int32, (window, TILE), 1)
     mask = contract(tile_mask[...].astype(F32), at.astype(F32), ((1,), (0,)))
     mask = jnp.concatenate([mask, jnp.zeros((MARK - tiles, TILE), F32)], axis=0).astype(BF16)
-    for ref in (own, first):
-        ref[:size, :features] = embeddings[:size]
-        ref[:size, features:] = panel[:size]
-        ref[size : size + MARK, :TILE] = mask
-        ref[size : size + MARK, TILE:] = jnp.zeros((MARK, features), BF16)
-    for ref, start in ((own, size + MARK), (last, 0)):
-        ref[start : start + size, :features] = embeddings[size:]
-        ref[start : start + size, features:] = panel[size:]
-
-
-def masks_of(sub, ref, others, offset):
-    size = (ref.shape[0] - MARK) // 2
-    mine = marks(ref, size)
-    return [pair_mask(sub, mine, marks(r, size), offset, h) for h, r in enumerate(others)]
-
-
-def block_products(inverse, block, columns, back):
-    out = []
-    for piece in pieces(block):
-        out.append(products(inverse, piece, len(out) * piece.shape[0] // TILE, columns, back))
-    return out
-
-
-def self_body(inverse, sub, own, other, image, sq):
-    rows = square_rows((own, other), sq)
-    columns = columns_of((own, other), rows, masks_of(sub[0], own, (own, other), OWN))
-    image[...] = jnp.concatenate(block_products(inverse[0], own, columns, None), axis=0)
-
-
-def above_own_body(inverse, sub, sq, above, own, other, image, *sums):
-    columns = columns_of((own, other), read_rows(sq), masks_of(sub[0], above, (own, other), ABOVE))
-    back = [None] * 4
-    image[...] = jnp.concatenate(block_products(inverse[0], above, columns, back), axis=0)
-    store_all(sums, back)
-
-
-def split_back(back, own_rows, own, cross):
-    size = back[0].shape[1]
-    for k in range(2):
-        own[k * size : (k + 1) * size] = own_rows[k] + back[k].T
-        cross[k * size : (k + 1) * size] = back[2 + k].T
-
-
-def below_own_body(inverse, sub, sq, below, own, other, self_image, t0, t1, t2, t3, image, own_image, cross):
-    columns = columns_of((own, other), read_rows(sq), masks_of(sub[0], below, (own, other), BELOW))
-    back = [t0[...], t1[...], t2[...], t3[...]]
-    image[...] = jnp.concatenate(block_products(inverse[0], below, columns, back), axis=0)
-    size = back[0].shape[1]
-    split_back(back, (self_image[:size], self_image[size:]), own_image, cross)
-
-
-def above_below_body(inverse, sub, above, below, other, above_image, below_image, image, below_out, cross):
-    rows = [as_row(squares(p, p.shape[1] - TILE)) for block in (below, other) for p in pieces(block)]
-    columns = columns_of((below, other), rows, masks_of(sub[0], above, (below, other), ABOVE - BELOW))
-    back = [None] * 4
-    image[...] = above_image[...] + jnp.concatenate(block_products(inverse[0], above, columns, back), axis=0)
-    size = back[0].shape[1]
-    split_back(back, (below_image[:size], below_image[size:]), below_out, cross)
+    for ref, start in ((first, 0), (last, size)):
+        ref[:size, :features] = embeddings[start : start + size]
+        ref[:size, features:] = panel[start : start + size]
+    first[size:, : features] = jnp.zeros((MARK, features), BF16)
+    first[size:, features:] = mask
+    panel_mark[:half] = panel[...]
+    panel_mark[half:] = mask
+
+
+def masks_of(sub, rows, others, offset):
+    return [pair_mask(sub, rows, r, offset, h) for h, r in enumerate(others)]
+
+
+def self_body(inverse, sub, first, last, other_first, other_last, image, sq):
+    half = 2 * last.shape[0]
+    own, other = pieces(first, last), pieces(other_first, other_last)
+    rows = [as_row(squares(features)) for features, _ in own + other]
+    for k, row in enumerate(rows):
+        sq[k : k + 1] = row
+    both = [marks(r, half) for r in (first, other_first)]
+    image[...], _ = products(inverse[0], own, columns_of(own, other, rows, masks_of(sub[0], both[0], both, OWN)), None)
+
+
+def above_own_body(inverse, sub, sq, above, panel, first, last, other_first, other_last, image, back):
+    half = above.shape[0]
+    masks = masks_of(sub[0], marks(panel, half), [marks(r, half) for r in (first, other_first)], ABOVE)
+    columns = columns_of(pieces(first, last), pieces(other_first, other_last), read_rows(sq), masks)
+    image[...], back[...] = products(inverse[0], apart(above, panel), columns, jnp.zeros(back.shape, F32))
+
+
+def below_own_body(inverse, sub, sq, below0, below1, first, last, other_first, other_last, self_image, back, image, own_image, cross):
+    half = image.shape[0]
+    masks = masks_of(sub[0], marks(below0, half), [marks(r, half) for r in (first, other_first)], BELOW)
+    columns = columns_of(pieces(first, last), pieces(other_first, other_last), read_rows(sq), masks)
+    image[...], total = products(inverse[0], pieces(below0, below1), columns, back[...])
+    own_image[...] = self_image[...] + total[:, :half].T
+    cross[...] = total[:, half:].T
+
+
+def above_below_body(
+    inverse, sub, above, panel, below0, below1, other0, other1, above_image, below_image, image, below_out, cross
+):
+    half = image.shape[0]
+    masks = masks_of(sub[0], marks(panel, half), [marks(r, half) for r in (below0, other0)], ABOVE - BELOW)
+    own, other = pieces(below0, below1), pieces(other0, other1)
+    columns = columns_of(own, other, [as_row(squares(features)) for features, _ in own + other], masks)
+    products_image, total = products(inverse[0], apart(above, panel), columns, jnp.zeros((TILE, 2 * half), F32))
+    image[...] = above_image[...] + products_image
+    below_out[...] = below_image[...] + total[:, :half].T
+    cross[...] = total[:, half:].T
 
 
 def gram_body(own, cross, below, above, image, gram):
@@ -268,29 +256,43 @@
     after = lambda v, *earlier: lax.optimization_barrier((v, *earlier))[0]
     sub = lax.axis_index("sub").astype(jnp.int32).reshape(1)
     wide = embeddings.shape[1] + width
-    packed = lambda rows: jax.ShapeDtypeStruct((rows, wide), BF16)
-    own, first, last = vmem_call(
-        pack_body, (packed(half + MARK), packed(size + MARK), packed(size)), embeddings, start_panel, tile_mask
+    packed = lambda rows, lanes: jax.ShapeDtypeStruct((rows, lanes), BF16)
+    above = blk_move(embeddings, -2)
+    first, last, panel_mark = vmem_call(
+        pack_body,
+        (packed(size + MARK, wide), packed(size, wide), packed(half + MARK, width)),
+        embeddings,
+        start_panel,
+        tile_mask,
     )
     relayed = n_blk == 8
     swapped = blk_route(last, lambda i: i ^ 1) if relayed else last
-    above = blk_move(own, -2)
-    other = sub_move(own)
-    image = shape(half, width)
-    sq_rows = shape(4, size)
-    self_image, sq = vmem_call(self_body, (image, sq_rows), inv_width, sub, own, other, scalars=2)
-    first, swapped = after(first, swapped, self_image), after(swapped, self_image)
-    below = [blk_move(first, 1), blk_route(swapped, lambda i: i if i & 1 else i + 2) if relayed else blk_move(swapped, 1)]
-    above_image, *back = vmem_call(
-        above_own_body, (image, *(shape(width, size),) * 4), inv_width, sub, sq, above, own, other, scalars=2
-    )
-    below = after(jnp.concatenate(below, axis=0), above_image)
-    below_other = sub_move(below)
+    above_panel = blk_move(panel_mark, -2)
+    own = (first, last, sub_move(first), sub_move(last))
+    image, turned = shape(half, width), shape(width, 2 * half)
+    self_image, sq = vmem_call(self_body, (image, shape(4, size)), inv_width, sub, *own, scalars=2)
+    below0 = blk_move(after(first, swapped, self_image), 1)
+    swapped = after(swapped, self_image)
+    below1 = blk_route(swapped, lambda i: i if i & 1 else i + 2) if relayed else blk_move(swapped, 1)
+    above_image, back = vmem_call(above_own_body, (image, turned), inv_width, sub, sq, above, above_panel, *own, scalars=2)
+    below0, below1 = after(below0, above_image, below1), after(below1, above_image, below0)
+    below_other = (sub_move(below0), sub_move(below1))
     below_image, own_image, own_cross = vmem_call(
-        below_own_body, (image,) * 3, inv_width, sub, sq, below, own, other, self_image, *back, scalars=2
+        below_own_body, (image,) * 3, inv_width, sub, sq, below0, below1, *own, self_image, back, scalars=2
     )
     above_image, below_image, below_cross = vmem_call(
-        above_below_body, (image,) * 3, inv_width, sub, above, below, below_other, above_image, below_image, scalars=2
+        above_below_body,
+        (image,) * 3,
+        inv_width,
+        sub,
+        above,
+        above_panel,
+        below0,
+        below1,
+        *below_other,
+        above_image,
+        below_image,
+        scalars=2,
     )
     above_image = blk_move(above_image, 2)
     below_image = blk_move(below_image + sub_move(below_cross), -1)

time: 97.6 us -> 94.3 us (0.966)
  Pallas kernels: 24.9 us -> 19.3 us
  waiting for transfers between devices: 48.3 us -> 50.6 us
  starting transfers between devices: 19.7 us -> 21 us
  local copies, waits for them, and re-layouts: 2.8 us -> 1.58 us
    pallas_call x7, Pallas kernels: 24.9 us -> 19.3 us  [vmem_call(): pl.pallas_call(body, out_shape=out_shapes, in_specs=[in_smem] * scalars +...]
    ppermute x9 -> x10, waiting for transfers between devices: 47 us -> 49.3 us  [per_device(): lax.ppermute(v, 'blk', [(i, to(i) % n_blk) for i in range(n_blk)])]
    unnamed x6 -> x4, local copies, waits for them, and re-layouts: 2.8 us -> 1.58 us
    ppermute x9 -> x10, starting transfers between devices: 18.4 us -> 19.4 us  [per_device(): lax.ppermute(v, 'blk', [(i, to(i) % n_blk) for i in range(n_blk)])]
  transfers between devices with their start and end apart: 14 -> 17, of which waited for: 10 -> 10; matrix products, arithmetic and copies ran while one was open for 0% -> 0% of each run, Pallas kernels for 15% -> 8%
where the time goes in v7:
time: 94.3 us; the launch traced here: 94 us
  waiting for transfers between devices  50.6 us (54%)
  starting transfers between devices  21 us (22%)
  Pallas kernels  19.3 us (20%)
  local copies, waits for them, and re-layouts  1.58 us (2%)
  between operations  1.4 us (1%)
    ppermute x10, waiting for transfers between devices, per_device(): lax.ppermute(v, 'blk', [(i, to(i) % n_blk) for i in range(n_blk)])  49.3 us
    ppermute x10, starting transfers between devices, per_device(): lax.ppermute(v, 'blk', [(i, to(i) % n_blk) for i in range(n_blk)])  19.4 us
    pallas_call x7, Pallas kernels, vmem_call(): pl.pallas_call(body, out_shape=out_shapes, in_specs=[in_smem] * scalars +...  19.3 us
  transfers between devices with their start and end apart: 17, of which 10 were waited for; matrix products, arithmetic and copies ran while one was open for 0% of the time, Pallas kernels for 8%

profile of v7, /device:TPU:0, one launch (start us, length us, event | category | flops | bytes accessed | tf_op | source)
XLA Modules:
  0.0 94.0 jit_solution(16222804837515066734)
XLA Ops:
  0.6 0.9 copy-done
  1.5 0.7 copy-done.1
  2.2 2.1 %shard_map.59 = (bf16[264,1152]{1,0:T(8,128)(2,1)S(1)}, bf16[256,1152]{1,0:T(8,128)(2,1)S(1)}, bf16[520,128]{1,0:T(8,128)(2,1)}) custom-call(bf16[512,1024]{1,0:T(8,128)(2,1)} %embeddings.1, bf16[512,128]{1,0:T(8,128)(2,1)S(1)} %copy-done, s32[4,56]{1,0:T(4,128)S(1)} %copy-done.1), custom_call_target="tpu_custom_call" | custom-call | flops 99999997952 | tf_op jit(solution)/shard_map/pallas_call | solution.py:18
  4.3 0.5 collective-permute-start
  4.8 5.0 %collective-permute-start.4 = (bf16[512,1024]{1,0:T(8,128)(2,1)}, bf16[512,1024]{1,0:T(8,128)(2,1)S(1)}, u32[]{:S(2)}, u32[]{:S(2)}) collective-permute-start(bf16[512,1024]{1,0:T(8,128)(2,1)} %embeddings.1), channel_id=1, source_target_pairs={{0,12},{2,14},{4,0},{6,2},{8,4},{10,6},{12,8},{14,10},{1,13},{3,15... | collective-permute-start | bytes 3145736 | tf_op jit(solution)/shard_map/ppermute | solution.py:253
  9.9 1.5 %collective-permute-start.2 = (bf16[256,1152]{1,0:T(8,128)(2,1)S(1)}, bf16[256,1152]{1,0:T(8,128)(2,1)}, u32[]{:S(2)}, u32[]{:S(2)}) collective-permute-start(bf16[256,1152]{1,0:T(8,128)(2,1)S(1)} %get-tuple-element.22.last), channel_id=1, source_target_pairs={{0,2},{2,0},{4,6},{6,4},{8,10},{10,8},{12,14},{14,12},{1,3},{3,1},... | collective-permute-start | bytes 1769480 | tf_op jit(solution)/shard_map/ppermute | solution.py:253
  11.4 0.4 collective-permute-start.5
  12.5 2.4 %shard_map.60 = (f32[512,128]{1,0:T(8,128)S(1)}, f32[4,256]{1,0:T(4,128)S(1)}) custom-call(f32[1]{0:T(128)S(6)} %copy.6.inverse, s32[1]{0:T(128)} %bitcast.sub, bf16[264,1152]{1,0:T(8,128)(2,1)S(1)} %get-tuple-element.25.first, bf16[256,1152]{1,0:T(8,128)(2,1)S(1)} %get-tuple-element.22.last, bf16[264,1152]{1,0:T(8,128)(2,1)S(1)} %collective-permute-done.other_first, ...), custom_call_target="tpu_custom_call" | custom-call | flops 99999997952 | tf_op jit(solution)/shard_map/pallas_call | solution.py:18
  14.9 10.1 %collective-permute-done.2 = bf16[256,1152]{1,0:T(8,128)(2,1)} collective-permute-done((bf16[256,1152]{1,0:T(8,128)(2,1)S(1)}, bf16[256,1152]{1,0:T(8,128)(2,1)}, u32[]{:S(2)}, u32[]{:S(2)}) %collective-permute-start.2) | collective-permute-done | bytes 589856 | tf_op jit(solution)/shard_map/ppermute | solution.py:253
  24.9 1.9 %collective-permute-start.6 = (bf16[256,1152]{1,0:T(8,128)(2,1)}, bf16[256,1152]{1,0:T(8,128)(2,1)S(1)}, u32[]{:S(2)}, u32[]{:S(2)}) collective-permute-start(bf16[256,1152]{1,0:T(8,128)(2,1)} %collective-permute-done.2), channel_id=1, source_target_pairs={{0,4},{2,2},{4,8},{6,6},{8,12},{10,10},{12,0},{14,14},{1,5},{3,3},... | collective-permute-start | bytes 1769480 | tf_op jit(solution)/shard_map/ppermute | solution.py:253
  26.9 1.3 %collective-permute-start.3 = (bf16[264,1152]{1,0:T(8,128)(2,1)S(1)}, bf16[264,1152]{1,0:T(8,128)(2,1)S(1)}, u32[]{:S(2)}, u32[]{:S(2)}) collective-permute-start(bf16[264,1152]{1,0:T(8,128)(2,1)S(1)} %get-tuple-element.25.first), channel_id=1, source_target_pairs={{0,2},{2,4},{4,6},{6,8},{8,10},{10,12},{12,14},{14,0},{1,3},{3,5},... | collective-permute-start | bytes 1824776 | tf_op jit(solution)/shard_map/ppermute | solution.py:253
  28.1 8.5 %collective-permute-done.5.panel = bf16[520,128]{1,0:T(8,128)(2,1)} collective-permute-done((bf16[520,128]{1,0:T(8,128)(2,1)}, bf16[520,128]{1,0:T(8,128)(2,1)}, u32[]{:S(2)}, u32[]{:S(2)}) %collective-permute-start.5) | collective-permute-done | bytes 133152 | tf_op jit(solution)/shard_map/ppermute | solution.py:253
  36.6 3.1 %shard_map.61 = (f32[512,128]{1,0:T(8,128)S(1)}, f32[128,1024]{1,0:T(8,128)S(1)}) custom-call(f32[1]{0:T(128)S(6)} %copy.6.inverse, s32[1]{0:T(128)} %bitcast.sub, f32[4,256]{1,0:T(4,128)S(1)} %get-tuple-element.23.sq, bf16[512,1024]{1,0:T(8,128)(2,1)S(1)} %collective-permute-done.4.above, bf16[520,128]{1,0:T(8,128)(2,1)} %collective-permute-done.5.panel, ...), custom_call_target="tpu_custom_call" | custom-call | flops 99999997952 | tf_op jit(solution)/shard_map/pallas_call | solution.py:18
  39.8 9.3 %collective-permute-done.6.below1 = bf16[256,1152]{1,0:T(8,128)(2,1)S(1)} collective-permute-done((bf16[256,1152]{1,0:T(8,128)(2,1)}, bf16[256,1152]{1,0:T(8,128)(2,1)S(1)}, u32[]{:S(2)}, u32[]{:S(2)}) %collective-permute-start.6) | collective-permute-done | bytes 589856 | tf_op jit(solution)/shard_map/ppermute | solution.py:253
  49.1 1.3 %collective-permute-done.3.below0 = bf16[264,1152]{1,0:T(8,128)(2,1)S(1)} collective-permute-done((bf16[264,1152]{1,0:T(8,128)(2,1)S(1)}, bf16[264,1152]{1,0:T(8,128)(2,1)S(1)}, u32[]{:S(2)}, u32[]{:S(2)}) %collective-permute-start.3) | collective-permute-done | bytes 608288 | tf_op jit(solution)/shard_map/ppermute | solution.py:253
  50.4 0.5 collective-permute-start.8
  50.9 2.4 %shard_map.62 = (f32[512,128]{1,0:T(8,128)S(1)}, f32[512,128]{1,0:T(8,128)S(1)}, f32[512,128]{1,0:T(8,128)S(1)}) custom-call(f32[1]{0:T(128)S(6)} %copy.6.inverse, s32[1]{0:T(128)} %bitcast.sub, f32[4,256]{1,0:T(4,128)S(1)} %get-tuple-element.23.sq, bf16[264,1152]{1,0:T(8,128)(2,1)S(1)} %collective-permute-done.3.below0, ...), custom_call_target="tpu_custom_call" | custom-call | flops 99999997952 | tf_op jit(solution)/shard_map/pallas_call | solution.py:18
  53.4 3.7 %shard_map.63 = (f32[512,128]{1,0:T(8,128)S(1)}, f32[512,128]{1,0:T(8,128)S(1)}, f32[512,128]{1,0:T(8,128)S(1)}) custom-call(f32[1]{0:T(128)S(6)} %copy.6.inverse, s32[1]{0:T(128)} %bitcast.sub, bf16[512,1024]{1,0:T(8,128)(2,1)S(1)} %collective-permute-done.4.above, bf16[520,128]{1,0:T(8,128)(2,1)} %collective-permute-done.5.panel, ...), custom_call_target="tpu_custom_call" | custom-call | flops 99999997952 | tf_op jit(solution)/shard_map/pallas_call | solution.py:18
  57.2 0.5 collective-permute-start.7
  57.6 1.7 %collective-permute-start.12 = (f32[512,128]{1,0:T(8,128)S(1)}, f32[512,128]{1,0:T(8,128)S(1)}, u32[]{:S(2)}, u32[]{:S(2)}) collective-permute-start(f32[512,128]{1,0:T(8,128)S(1)} %get-tuple-element.37), channel_id=1, source_target_pairs={{0,4},{2,6},{4,8},{6,10},{8,12},{10,14},{12,0},{14,2},{1,5},{3,7},... | collective-permute-start | bytes 786440 | tf_op jit(solution)/shard_map/ppermute | solution.py:253
  59.3 1.6 %collective-permute-start.11 = (f32[512,128]{1,0:T(8,128)S(1)}, f32[512,128]{1,0:T(8,128)S(1)}, u32[]{:S(2)}, u32[]{:S(2)}) collective-permute-start(f32[512,128]{1,0:T(8,128)S(1)} %add.15), channel_id=1, source_target_pairs={{0,14},{2,0},{4,2},{6,4},{8,6},{10,8},{12,10},{14,12},{1,15},{3,1}... | collective-permute-start | bytes 786440 | tf_op jit(solution)/shard_map/ppermute | solution.py:253
  60.9 7.7 %collective-permute-done.12.above = f32[512,128]{1,0:T(8,128)S(1)} collective-permute-done((f32[512,128]{1,0:T(8,128)S(1)}, f32[512,128]{1,0:T(8,128)S(1)}, u32[]{:S(2)}, u32[]{:S(2)}) %collective-permute-start.12) | collective-permute-done | bytes 262176 | tf_op jit(solution)/shard_map/ppermute | solution.py:253
  68.6 2.1 %collective-permute-done.11.below = f32[512,128]{1,0:T(8,128)S(1)} collective-permute-done((f32[512,128]{1,0:T(8,128)S(1)}, f32[512,128]{1,0:T(8,128)S(1)}, u32[]{:S(2)}, u32[]{:S(2)}) %collective-permute-start.11) | collective-permute-done | bytes 262176 | tf_op jit(solution)/shard_map/ppermute | solution.py:253
  70.7 0.5 shard_map.64
  71.3 1.2 %collective-permute-done.13 = f32[128,128]{1,0:T(8,128)S(1)} collective-permute-done((f32[128,128]{1,0:T(8,128)S(1)}, f32[128,128]{1,0:T(8,128)S(1)}, u32[]{:S(2)}, u32[]{:S(2)}) %collective-permute-start.13) | collective-permute-done | bytes 65568 | tf_op jit(solution)/shard_map/ppermute | solution.py:252
  72.5 3.6 %collective-permute-start.14 = (f32[128,128]{1,0:T(8,128)S(1)}, f32[128,128]{1,0:T(8,128)S(1)}, u32[]{:S(2)}, u32[]{:S(2)}) collective-permute-start(f32[128,128]{1,0:T(8,128)S(1)} %add.16), channel_id=1, source_target_pairs={{0,2},{2,0},{4,6},{6,4},{8,10},{10,8},{12,14},{14,12},{1,3},{3,1},... | collective-permute-start | bytes 196616 | tf_op jit(solution)/shard_map/ppermute | solution.py:253
  76.1 2.4 %collective-permute-done.14 = f32[128,128]{1,0:T(8,128)S(1)} collective-permute-done((f32[128,128]{1,0:T(8,128)S(1)}, f32[128,128]{1,0:T(8,128)S(1)}, u32[]{:S(2)}, u32[]{:S(2)}) %collective-permute-start.14) | collective-permute-done | bytes 65568 | tf_op jit(solution)/shard_map/ppermute | solution.py:253
  78.6 1.1 %collective-permute-start.15 = (f32[128,128]{1,0:T(8,128)S(1)}, f32[128,128]{1,0:T(8,128)S(1)}, u32[]{:S(2)}, u32[]{:S(2)}) collective-permute-start(f32[128,128]{1,0:T(8,128)S(1)} %add.17), channel_id=1, source_target_pairs={{0,4},{2,6},{4,0},{6,2},{8,12},{10,14},{12,8},{14,10},{1,5},{3,7},... | collective-permute-start | bytes 196616 | tf_op jit(solution)/shard_map/ppermute | solution.py:253
  79.7 3.2 %collective-permute-done.15 = f32[128,128]{1,0:T(8,128)S(1)} collective-permute-done((f32[128,128]{1,0:T(8,128)S(1)}, f32[128,128]{1,0:T(8,128)S(1)}, u32[]{:S(2)}, u32[]{:S(2)}) %collective-permute-start.15) | collective-permute-done | bytes 65568 | tf_op jit(solution)/shard_map/ppermute | solution.py:253
  82.9 1.2 %collective-permute-start.16 = (f32[128,128]{1,0:T(8,128)S(1)}, f32[128,128]{1,0:T(8,128)S(1)}, u32[]{:S(2)}, u32[]{:S(2)}) collective-permute-start(f32[128,128]{1,0:T(8,128)S(1)} %add.18), channel_id=1, source_target_pairs={{0,8},{2,10},{4,12},{6,14},{8,0},{10,2},{12,4},{14,6},{1,9},{3,11}... | collective-permute-start | bytes 196616 | tf_op jit(solution)/shard_map/ppermute | solution.py:253
  84.1 4.8 %collective-permute-done.16 = f32[128,128]{1,0:T(8,128)S(1)} collective-permute-done((f32[128,128]{1,0:T(8,128)S(1)}, f32[128,128]{1,0:T(8,128)S(1)}, u32[]{:S(2)}, u32[]{:S(2)}) %collective-permute-start.16) | collective-permute-done | bytes 65568 | tf_op jit(solution)/shard_map/ppermute | solution.py:253
  88.9 5.2 %shard_map.65 = (f32[512,128]{1,0:T(8,128)}, f32[128,128]{1,0:T(8,128)}) custom-call(f32[512,128]{1,0:T(8,128)S(1)} %get-tuple-element.38.image, f32[128,128]{1,0:T(8,128)S(1)} %add.19.gram), custom_call_target="tpu_custom_call" | custom-call | flops 99999997952 | tf_op jit(solution)/shard_map/pallas_call | solution.py:18
  (18 shorter events, 0.3 us)
Async XLA Ops:
  0.6 0.9 copy-start
  1.5 0.7 copy-start.1
  4.3 8.2 %collective-permute-start = (bf16[264,1152]{1,0:T(8,128)(2,1)S(1)}, bf16[264,1152]{1,0:T(8,128)(2,1)S(1)}, u32[]{:S(2)}, u32[]{:S(2)}) collective-permute-start(bf16[264,1152]{1,0:T(8,128)(2,1)S(1)} %get-tuple-element.25.first), channel_id=1, source_target_pairs={{0,1},{1,0},{2,3},{3,2},{4,5},{5,4},{6,7},{7,6},{8,9},{9,8},{10,11... | collective-permute-start | bytes 1824776 | tf_op jit(solution)/shard_map/ppermute | solution.py:252
  4.8 7.7 %collective-permute-start.1 = (bf16[256,1152]{1,0:T(8,128)(2,1)S(1)}, bf16[256,1152]{1,0:T(8,128)(2,1)S(1)}, u32[]{:S(2)}, u32[]{:S(2)}) collective-permute-start(bf16[256,1152]{1,0:T(8,128)(2,1)S(1)} %get-tuple-element.22.last), channel_id=1, source_target_pairs={{0,1},{1,0},{2,3},{3,2},{4,5},{5,4},{6,7},{7,6},{8,9},{9,8},{10,11... | collective-permute-start | bytes 1769480 | tf_op jit(solution)/shard_map/ppermute | solution.py:252
  4.8 31.8 %collective-permute-start.4 = (bf16[512,1024]{1,0:T(8,128)(2,1)}, bf16[512,1024]{1,0:T(8,128)(2,1)S(1)}, u32[]{:S(2)}, u32[]{:S(2)}) collective-permute-start(bf16[512,1024]{1,0:T(8,128)(2,1)} %embeddings.1), channel_id=1, source_target_pairs={{0,12},{2,14},{4,0},{6,2},{8,4},{10,6},{12,8},{14,10},{1,13},{3,15... | collective-permute-start | bytes 3145736 | tf_op jit(solution)/shard_map/ppermute | solution.py:253
  9.9 15.1 %collective-permute-start.2 = (bf16[256,1152]{1,0:T(8,128)(2,1)S(1)}, bf16[256,1152]{1,0:T(8,128)(2,1)}, u32[]{:S(2)}, u32[]{:S(2)}) collective-permute-start(bf16[256,1152]{1,0:T(8,128)(2,1)S(1)} %get-tuple-element.22.last), channel_id=1, source_target_pairs={{0,2},{2,0},{4,6},{6,4},{8,10},{10,8},{12,14},{14,12},{1,3},{3,1},... | collective-permute-start | bytes 1769480 | tf_op jit(solution)/shard_map/ppermute | solution.py:253
  11.4 25.3 %collective-permute-start.5 = (bf16[520,128]{1,0:T(8,128)(2,1)}, bf16[520,128]{1,0:T(8,128)(2,1)}, u32[]{:S(2)}, u32[]{:S(2)}) collective-permute-start(bf16[520,128]{1,0:T(8,128)(2,1)} %get-tuple-element.26), channel_id=1, source_target_pairs={{0,12},{2,14},{4,0},{6,2},{8,4},{10,6},{12,8},{14,10},{1,13},{3,15... | collective-permute-start | bytes 399368 | tf_op jit(solution)/shard_map/ppermute | solution.py:253
  24.9 24.1 %collective-permute-start.6 = (bf16[256,1152]{1,0:T(8,128)(2,1)}, bf16[256,1152]{1,0:T(8,128)(2,1)S(1)}, u32[]{:S(2)}, u32[]{:S(2)}) collective-permute-start(bf16[256,1152]{1,0:T(8,128)(2,1)} %collective-permute-done.2), channel_id=1, source_target_pairs={{0,4},{2,2},{4,8},{6,6},{8,12},{10,10},{12,0},{14,14},{1,5},{3,3},... | collective-permute-start | bytes 1769480 | tf_op jit(solution)/shard_map/ppermute | solution.py:253
  26.9 23.5 %collective-permute-start.3 = (bf16[264,1152]{1,0:T(8,128)(2,1)S(1)}, bf16[264,1152]{1,0:T(8,128)(2,1)S(1)}, u32[]{:S(2)}, u32[]{:S(2)}) collective-permute-start(bf16[264,1152]{1,0:T(8,128)(2,1)S(1)} %get-tuple-element.25.first), channel_id=1, source_target_pairs={{0,2},{2,4},{4,6},{6,8},{8,10},{10,12},{12,14},{14,0},{1,3},{3,5},... | collective-permute-start | bytes 1824776 | tf_op jit(solution)/shard_map/ppermute | solution.py:253
  50.4 3.0 %collective-permute-start.9 = (bf16[256,1152]{1,0:T(8,128)(2,1)S(1)}, bf16[256,1152]{1,0:T(8,128)(2,1)S(1)}, u32[]{:S(2)}, u32[]{:S(2)}) collective-permute-start(bf16[256,1152]{1,0:T(8,128)(2,1)S(1)} %collective-permute-done.6.below1), channel_id=1, source_target_pairs={{0,1},{1,0},{2,3},{3,2},{4,5},{5,4},{6,7},{7,6},{8,9},{9,8},{10,11... | collective-permute-start | bytes 1769480 | tf_op jit(solution)/shard_map/ppermute | solution.py:252
  50.4 3.0 %collective-permute-start.8 = (bf16[264,1152]{1,0:T(8,128)(2,1)S(1)}, bf16[264,1152]{1,0:T(8,128)(2,1)S(1)}, u32[]{:S(2)}, u32[]{:S(2)}) collective-permute-start(bf16[264,1152]{1,0:T(8,128)(2,1)S(1)} %collective-permute-done.3.below0), channel_id=1, source_target_pairs={{0,1},{1,0},{2,3},{3,2},{4,5},{5,4},{6,7},{7,6},{8,9},{9,8},{10,11... | collective-permute-start | bytes 1824776 | tf_op jit(solution)/shard_map/ppermute | solution.py:252
  57.1 2.2 %collective-permute-start.10 = (f32[512,128]{1,0:T(8,128)S(1)}, f32[512,128]{1,0:T(8,128)S(1)}, u32[]{:S(2)}, u32[]{:S(2)}) collective-permute-start(f32[512,128]{1,0:T(8,128)S(1)} %get-tuple-element.36), channel_id=1, source_target_pairs={{0,1},{1,0},{2,3},{3,2},{4,5},{5,4},{6,7},{7,6},{8,9},{9,8},{10,11... | collective-permute-start | bytes 786440 | tf_op jit(solution)/shard_map/ppermute | solution.py:252
  57.2 3.8 %collective-permute-start.7 = (f32[512,128]{1,0:T(8,128)S(1)}, f32[512,128]{1,0:T(8,128)S(1)}, u32[]{:S(2)}, u32[]{:S(2)}) collective-permute-start(f32[512,128]{1,0:T(8,128)S(1)} %get-tuple-element.33), channel_id=1, source_target_pairs={{0,1},{1,0},{2,3},{3,2},{4,5},{5,4},{6,7},{7,6},{8,9},{9,8},{10,11... | collective-permute-start | bytes 786440 | tf_op jit(solution)/shard_map/ppermute | solution.py:252
  57.6 11.0 %collective-permute-start.12 = (f32[512,128]{1,0:T(8,128)S(1)}, f32[512,128]{1,0:T(8,128)S(1)}, u32[]{:S(2)}, u32[]{:S(2)}) collective-permute-start(f32[512,128]{1,0:T(8,128)S(1)} %get-tuple-element.37), channel_id=1, source_target_pairs={{0,4},{2,6},{4,8},{6,10},{8,12},{10,14},{12,0},{14,2},{1,5},{3,7},... | collective-permute-start | bytes 786440 | tf_op jit(solution)/shard_map/ppermute | solution.py:253
  59.3 11.4 %collective-permute-start.11 = (f32[512,128]{1,0:T(8,128)S(1)}, f32[512,128]{1,0:T(8,128)S(1)}, u32[]{:S(2)}, u32[]{:S(2)}) collective-permute-start(f32[512,128]{1,0:T(8,128)S(1)} %add.15), channel_id=1, source_target_pairs={{0,14},{2,0},{4,2},{6,4},{8,6},{10,8},{12,10},{14,12},{1,15},{3,1}... | collective-permute-start | bytes 786440 | tf_op jit(solution)/shard_map/ppermute | solution.py:253
  71.2 1.3 %collective-permute-start.13 = (f32[128,128]{1,0:T(8,128)S(1)}, f32[128,128]{1,0:T(8,128)S(1)}, u32[]{:S(2)}, u32[]{:S(2)}) collective-permute-start(f32[128,128]{1,0:T(8,128)S(1)} %get-tuple-element.39), channel_id=1, source_target_pairs={{0,1},{1,0},{2,3},{3,2},{4,5},{5,4},{6,7},{7,6},{8,9},{9,8},{10,11... | collective-permute-start | bytes 196616 | tf_op jit(solution)/shard_map/ppermute | solution.py:252
  72.5 6.0 %collective-permute-start.14 = (f32[128,128]{1,0:T(8,128)S(1)}, f32[128,128]{1,0:T(8,128)S(1)}, u32[]{:S(2)}, u32[]{:S(2)}) collective-permute-start(f32[128,128]{1,0:T(8,128)S(1)} %add.16), channel_id=1, source_target_pairs={{0,2},{2,0},{4,6},{6,4},{8,10},{10,8},{12,14},{14,12},{1,3},{3,1},... | collective-permute-start | bytes 196616 | tf_op jit(solution)/shard_map/ppermute | solution.py:253
  78.6 4.3 %collective-permute-start.15 = (f32[128,128]{1,0:T(8,128)S(1)}, f32[128,128]{1,0:T(8,128)S(1)}, u32[]{:S(2)}, u32[]{:S(2)}) collective-permute-start(f32[128,128]{1,0:T(8,128)S(1)} %add.17), channel_id=1, source_target_pairs={{0,4},{2,6},{4,0},{6,2},{8,12},{10,14},{12,8},{14,10},{1,5},{3,7},... | collective-permute-start | bytes 196616 | tf_op jit(solution)/shard_map/ppermute | solution.py:253
  82.9 5.9 %collective-permute-start.16 = (f32[128,128]{1,0:T(8,128)S(1)}, f32[128,128]{1,0:T(8,128)S(1)}, u32[]{:S(2)}, u32[]{:S(2)}) collective-permute-start(f32[128,128]{1,0:T(8,128)S(1)} %add.18), channel_id=1, source_target_pairs={{0,8},{2,10},{4,12},{6,14},{8,0},{10,2},{12,4},{14,6},{1,9},{3,11}... | collective-permute-start | bytes 196616 | tf_op jit(solution)/shard_map/ppermute | solution.py:253

commit v8 on v7

--- a/solution.py
+++ b/solution.py
@@ -12,7 +12,7 @@
 HIGHEST = lax.Precision.HIGHEST
 
 
-def vmem_call(body, out_shapes, *operands, scalars=0):
+def vmem_call(body, out_shapes, *operands, scalars=0, long=True):
     in_vmem = pl.BlockSpec(memory_space=pltpu.VMEM)
     in_smem = pl.BlockSpec(memory_space=pltpu.SMEM)
     return pl.pallas_call(
@@ -21,7 +21,7 @@
         in_specs=[in_smem] * scalars + [in_vmem] * (len(operands) - scalars),
         out_specs=jax.tree.map(lambda _: in_vmem, out_shapes),
         compiler_params=pltpu.CompilerParams(vmem_limit_bytes=24 << 20),
-        cost_estimate=pl.CostEstimate(flops=10**11, transcendentals=0, bytes_accessed=0),
+        cost_estimate=pl.CostEstimate(flops=10**11 if long else 1, transcendentals=0, bytes_accessed=1),
     )(*operands)
 
 
@@ -264,13 +264,14 @@
         embeddings,
         start_panel,
         tile_mask,
+        long=False,
     )
     relayed = n_blk == 8
     swapped = blk_route(last, lambda i: i ^ 1) if relayed else last
     above_panel = blk_move(panel_mark, -2)
     own = (first, last, sub_move(first), sub_move(last))
     image, turned = shape(half, width), shape(width, 2 * half)
-    self_image, sq = vmem_call(self_body, (image, shape(4, size)), inv_width, sub, *own, scalars=2)
+    self_image, sq = vmem_call(self_body, (image, shape(4, size)), inv_width, sub, *own, scalars=2, long=False)
     below0 = blk_move(after(first, swapped, self_image), 1)
     swapped = after(swapped, self_image)
     below1 = blk_route(swapped, lambda i: i if i & 1 else i + 2) if relayed else blk_move(swapped, 1)

time: 94.3 us -> 90 us (0.954)
  waiting for transfers between devices: 50.6 us -> 46.3 us
  local copies, waits for them, and re-layouts: 1.58 us -> 2.84 us
  Pallas kernels: 19.3 us -> 18.1 us
    ppermute x10, waiting for transfers between devices: 49.3 us -> 45 us  [per_device(): lax.ppermute(v, 'blk', [(i, to(i) % n_blk) for i in range(n_blk)])]
    pallas_call x7, Pallas kernels: 19.3 us -> 18.1 us  [vmem_call(): pl.pallas_call(body, out_shape=out_shapes, in_specs=[in_smem] * scalars +...]
    unnamed x4 -> x6, local copies, waits for them, and re-layouts: 1.58 us -> 2.84 us
  transfers between devices with their start and end apart: 17 -> 17, of which waited for: 10 -> 10; matrix products, arithmetic and copies ran while one was open for 0% -> 0% of each run, Pallas kernels for 8% -> 10%
where the time goes in v8:
time: 90 us; the launch traced here: 89.7 us
  waiting for transfers between devices  46.3 us (51%)
  starting transfers between devices  21.1 us (23%)
  Pallas kernels  18.1 us (20%)
  local copies, waits for them, and re-layouts  2.84 us (3%)
  between operations  1.39 us (2%)
    ppermute x10, waiting for transfers between devices, per_device(): lax.ppermute(v, 'blk', [(i, to(i) % n_blk) for i in range(n_blk)])  45 us
    ppermute x10, starting transfers between devices, per_device(): lax.ppermute(v, 'blk', [(i, to(i) % n_blk) for i in range(n_blk)])  19.4 us
    pallas_call x7, Pallas kernels, vmem_call(): pl.pallas_call(body, out_shape=out_shapes, in_specs=[in_smem] * scalars +...  18.1 us
    unnamed x6, local copies, waits for them, and re-layouts  2.84 us
  transfers between devices with their start and end apart: 17, of which 10 were waited for; matrix products, arithmetic and copies ran while one was open for 0% of the time, Pallas kernels for 10%

profile of v8, /device:TPU:0, one launch (start us, length us, event | category | flops | bytes accessed | tf_op | source)
XLA Modules:
  0.0 89.7 jit_solution(687922652377280336)
XLA Ops:
  0.6 5.1 %collective-permute-start.4 = (bf16[512,1024]{1,0:T(8,128)(2,1)}, bf16[512,1024]{1,0:T(8,128)(2,1)S(1)}, u32[]{:S(2)}, u32[]{:S(2)}) collective-permute-start(bf16[512,1024]{1,0:T(8,128)(2,1)} %embeddings.1), channel_id=1, source_target_pairs={{0,12},{2,14},{4,0},{6,2},{8,4},{10,6},{12,8},{14,10},{1,13},{3,15... | collective-permute-start | bytes 3145736 | tf_op jit(solution)/shard_map/ppermute | solution.py:253
  5.7 1.3 %copy-done = bf16[512,1024]{1,0:T(8,128)(2,1)S(1)} copy-done((bf16[512,1024]{1,0:T(8,128)(2,1)S(1)}, bf16[512,1024]{1,0:T(8,128)(2,1)}, u32[]{:S(2)}) %copy-start) | copy-done | bytes 1048600
  7.0 0.9 %copy-done.1 = bf16[512,128]{1,0:T(8,128)(2,1)S(1)} copy-done((bf16[512,128]{1,0:T(8,128)(2,1)S(1)}, bf16[512,128]{1,0:T(8,128)(2,1)}, u32[]{:S(2)}) %copy-start.1) | copy-done | bytes 131096
  7.9 0.7 copy-done.2
  8.6 0.8 shard_map.59
  9.4 0.5 collective-permute-start.1
  9.9 1.5 %collective-permute-start.2 = (bf16[256,1152]{1,0:T(8,128)(2,1)S(1)}, bf16[256,1152]{1,0:T(8,128)(2,1)}, u32[]{:S(2)}, u32[]{:S(2)}) collective-permute-start(bf16[256,1152]{1,0:T(8,128)(2,1)S(1)} %get-tuple-element.22.last), channel_id=1, source_target_pairs={{0,2},{2,0},{4,6},{6,4},{8,10},{10,8},{12,14},{14,12},{1,3},{3,1},... | collective-permute-start | bytes 1769480 | tf_op jit(solution)/shard_map/ppermute | solution.py:253
  12.5 2.4 %shard_map.60 = (f32[512,128]{1,0:T(8,128)S(1)}, f32[4,256]{1,0:T(4,128)S(1)}) custom-call(f32[1]{0:T(128)S(6)} %copy.6.inverse, s32[1]{0:T(128)} %bitcast.sub, bf16[264,1152]{1,0:T(8,128)(2,1)S(1)} %get-tuple-element.25.first, bf16[256,1152]{1,0:T(8,128)(2,1)S(1)} %get-tuple-element.22.last, bf16[264,1152]{1,0:T(8,128)(2,1)S(1)} %collective-permute-done.other_first, ...), custom_call_target="tpu_custom_call" | custom-call | flops 1 | bytes 1 | tf_op jit(solution)/shard_map/pallas_call | solution.py:18
  14.9 10.3 %collective-permute-done.2 = bf16[256,1152]{1,0:T(8,128)(2,1)} collective-permute-done((bf16[256,1152]{1,0:T(8,128)(2,1)S(1)}, bf16[256,1152]{1,0:T(8,128)(2,1)}, u32[]{:S(2)}, u32[]{:S(2)}) %collective-permute-start.2) | collective-permute-done | bytes 589856 | tf_op jit(solution)/shard_map/ppermute | solution.py:253
  25.2 1.9 %collective-permute-start.6 = (bf16[256,1152]{1,0:T(8,128)(2,1)}, bf16[256,1152]{1,0:T(8,128)(2,1)S(1)}, u32[]{:S(2)}, u32[]{:S(2)}) collective-permute-start(bf16[256,1152]{1,0:T(8,128)(2,1)} %collective-permute-done.2), channel_id=1, source_target_pairs={{0,4},{2,2},{4,8},{6,6},{8,12},{10,10},{12,0},{14,14},{1,5},{3,3},... | collective-permute-start | bytes 1769480 | tf_op jit(solution)/shard_map/ppermute | solution.py:253
  27.1 1.3 %collective-permute-start.3 = (bf16[264,1152]{1,0:T(8,128)(2,1)S(1)}, bf16[264,1152]{1,0:T(8,128)(2,1)S(1)}, u32[]{:S(2)}, u32[]{:S(2)}) collective-permute-start(bf16[264,1152]{1,0:T(8,128)(2,1)S(1)} %get-tuple-element.25.first), channel_id=1, source_target_pairs={{0,2},{2,4},{4,6},{6,8},{8,10},{10,12},{12,14},{14,0},{1,3},{3,5},... | collective-permute-start | bytes 1824776 | tf_op jit(solution)/shard_map/ppermute | solution.py:253
  28.4 4.1 %collective-permute-done.5.panel = bf16[520,128]{1,0:T(8,128)(2,1)} collective-permute-done((bf16[520,128]{1,0:T(8,128)(2,1)}, bf16[520,128]{1,0:T(8,128)(2,1)}, u32[]{:S(2)}, u32[]{:S(2)}) %collective-permute-start.5) | collective-permute-done | bytes 133152 | tf_op jit(solution)/shard_map/ppermute | solution.py:253
  32.5 3.1 %shard_map.61 = (f32[512,128]{1,0:T(8,128)S(1)}, f32[128,1024]{1,0:T(8,128)S(1)}) custom-call(f32[1]{0:T(128)S(6)} %copy.6.inverse, s32[1]{0:T(128)} %bitcast.sub, f32[4,256]{1,0:T(4,128)S(1)} %get-tuple-element.23.sq, bf16[512,1024]{1,0:T(8,128)(2,1)S(1)} %collective-permute-done.4.above, bf16[520,128]{1,0:T(8,128)(2,1)} %collective-permute-done.5.panel, ...), custom_call_target="tpu_custom_call" | custom-call | flops 99999997952 | bytes 1 | tf_op jit(solution)/shard_map/pallas_call | solution.py:18
  35.7 9.1 %collective-permute-done.6.below1 = bf16[256,1152]{1,0:T(8,128)(2,1)S(1)} collective-permute-done((bf16[256,1152]{1,0:T(8,128)(2,1)}, bf16[256,1152]{1,0:T(8,128)(2,1)S(1)}, u32[]{:S(2)}, u32[]{:S(2)}) %collective-permute-start.6) | collective-permute-done | bytes 589856 | tf_op jit(solution)/shard_map/ppermute | solution.py:253
  44.8 1.3 %collective-permute-done.3.below0 = bf16[264,1152]{1,0:T(8,128)(2,1)S(1)} collective-permute-done((bf16[264,1152]{1,0:T(8,128)(2,1)S(1)}, bf16[264,1152]{1,0:T(8,128)(2,1)S(1)}, u32[]{:S(2)}, u32[]{:S(2)}) %collective-permute-start.3) | collective-permute-done | bytes 608288 | tf_op jit(solution)/shard_map/ppermute | solution.py:253
  46.1 0.5 collective-permute-start.8
  46.6 2.5 %shard_map.62 = (f32[512,128]{1,0:T(8,128)S(1)}, f32[512,128]{1,0:T(8,128)S(1)}, f32[512,128]{1,0:T(8,128)S(1)}) custom-call(f32[1]{0:T(128)S(6)} %copy.6.inverse, s32[1]{0:T(128)} %bitcast.sub, f32[4,256]{1,0:T(4,128)S(1)} %get-tuple-element.23.sq, bf16[264,1152]{1,0:T(8,128)(2,1)S(1)} %collective-permute-done.3.below0, ...), custom_call_target="tpu_custom_call" | custom-call | flops 99999997952 | bytes 1 | tf_op jit(solution)/shard_map/pallas_call | solution.py:18
  49.1 3.7 %shard_map.63 = (f32[512,128]{1,0:T(8,128)S(1)}, f32[512,128]{1,0:T(8,128)S(1)}, f32[512,128]{1,0:T(8,128)S(1)}) custom-call(f32[1]{0:T(128)S(6)} %copy.6.inverse, s32[1]{0:T(128)} %bitcast.sub, bf16[512,1024]{1,0:T(8,128)(2,1)S(1)} %collective-permute-done.4.above, bf16[520,128]{1,0:T(8,128)(2,1)} %collective-permute-done.5.panel, ...), custom_call_target="tpu_custom_call" | custom-call | flops 99999997952 | bytes 1 | tf_op jit(solution)/shard_map/pallas_call | solution.py:18
  52.9 0.5 collective-permute-start.7
  53.3 1.6 %collective-permute-start.12 = (f32[512,128]{1,0:T(8,128)S(1)}, f32[512,128]{1,0:T(8,128)S(1)}, u32[]{:S(2)}, u32[]{:S(2)}) collective-permute-start(f32[512,128]{1,0:T(8,128)S(1)} %get-tuple-element.37), channel_id=1, source_target_pairs={{0,4},{2,6},{4,8},{6,10},{8,12},{10,14},{12,0},{14,2},{1,5},{3,7},... | collective-permute-start | bytes 786440 | tf_op jit(solution)/shard_map/ppermute | solution.py:253
  55.0 1.6 %collective-permute-start.11 = (f32[512,128]{1,0:T(8,128)S(1)}, f32[512,128]{1,0:T(8,128)S(1)}, u32[]{:S(2)}, u32[]{:S(2)}) collective-permute-start(f32[512,128]{1,0:T(8,128)S(1)} %add.15), channel_id=1, source_target_pairs={{0,14},{2,0},{4,2},{6,4},{8,6},{10,8},{12,10},{14,12},{1,15},{3,1}... | collective-permute-start | bytes 786440 | tf_op jit(solution)/shard_map/ppermute | solution.py:253
  56.6 7.8 %collective-permute-done.12.above = f32[512,128]{1,0:T(8,128)S(1)} collective-permute-done((f32[512,128]{1,0:T(8,128)S(1)}, f32[512,128]{1,0:T(8,128)S(1)}, u32[]{:S(2)}, u32[]{:S(2)}) %collective-permute-start.12) | collective-permute-done | bytes 262176 | tf_op jit(solution)/shard_map/ppermute | solution.py:253
  64.4 2.0 %collective-permute-done.11.below = f32[512,128]{1,0:T(8,128)S(1)} collective-permute-done((f32[512,128]{1,0:T(8,128)S(1)}, f32[512,128]{1,0:T(8,128)S(1)}, u32[]{:S(2)}, u32[]{:S(2)}) %collective-permute-start.11) | collective-permute-done | bytes 262176 | tf_op jit(solution)/shard_map/ppermute | solution.py:253
  66.4 0.5 shard_map.64
  66.9 1.2 %collective-permute-done.13 = f32[128,128]{1,0:T(8,128)S(1)} collective-permute-done((f32[128,128]{1,0:T(8,128)S(1)}, f32[128,128]{1,0:T(8,128)S(1)}, u32[]{:S(2)}, u32[]{:S(2)}) %collective-permute-start.13) | collective-permute-done | bytes 65568 | tf_op jit(solution)/shard_map/ppermute | solution.py:252
  68.2 3.7 %collective-permute-start.14 = (f32[128,128]{1,0:T(8,128)S(1)}, f32[128,128]{1,0:T(8,128)S(1)}, u32[]{:S(2)}, u32[]{:S(2)}) collective-permute-start(f32[128,128]{1,0:T(8,128)S(1)} %add.16), channel_id=1, source_target_pairs={{0,2},{2,0},{4,6},{6,4},{8,10},{10,8},{12,14},{14,12},{1,3},{3,1},... | collective-permute-start | bytes 196616 | tf_op jit(solution)/shard_map/ppermute | solution.py:253
  71.9 2.4 %collective-permute-done.14 = f32[128,128]{1,0:T(8,128)S(1)} collective-permute-done((f32[128,128]{1,0:T(8,128)S(1)}, f32[128,128]{1,0:T(8,128)S(1)}, u32[]{:S(2)}, u32[]{:S(2)}) %collective-permute-start.14) | collective-permute-done | bytes 65568 | tf_op jit(solution)/shard_map/ppermute | solution.py:253
  74.3 1.1 %collective-permute-start.15 = (f32[128,128]{1,0:T(8,128)S(1)}, f32[128,128]{1,0:T(8,128)S(1)}, u32[]{:S(2)}, u32[]{:S(2)}) collective-permute-start(f32[128,128]{1,0:T(8,128)S(1)} %add.17), channel_id=1, source_target_pairs={{0,4},{2,6},{4,0},{6,2},{8,12},{10,14},{12,8},{14,10},{1,5},{3,7},... | collective-permute-start | bytes 196616 | tf_op jit(solution)/shard_map/ppermute | solution.py:253
  75.4 3.2 %collective-permute-done.15 = f32[128,128]{1,0:T(8,128)S(1)} collective-permute-done((f32[128,128]{1,0:T(8,128)S(1)}, f32[128,128]{1,0:T(8,128)S(1)}, u32[]{:S(2)}, u32[]{:S(2)}) %collective-permute-start.15) | collective-permute-done | bytes 65568 | tf_op jit(solution)/shard_map/ppermute | solution.py:253
  78.6 1.2 %collective-permute-start.16 = (f32[128,128]{1,0:T(8,128)S(1)}, f32[128,128]{1,0:T(8,128)S(1)}, u32[]{:S(2)}, u32[]{:S(2)}) collective-permute-start(f32[128,128]{1,0:T(8,128)S(1)} %add.18), channel_id=1, source_target_pairs={{0,8},{2,10},{4,12},{6,14},{8,0},{10,2},{12,4},{14,6},{1,9},{3,11}... | collective-permute-start | bytes 196616 | tf_op jit(solution)/shard_map/ppermute | solution.py:253
  79.8 4.8 %collective-permute-done.16 = f32[128,128]{1,0:T(8,128)S(1)} collective-permute-done((f32[128,128]{1,0:T(8,128)S(1)}, f32[128,128]{1,0:T(8,128)S(1)}, u32[]{:S(2)}, u32[]{:S(2)}) %collective-permute-start.16) | collective-permute-done | bytes 65568 | tf_op jit(solution)/shard_map/ppermute | solution.py:253
  84.6 5.2 %shard_map.65 = (f32[512,128]{1,0:T(8,128)}, f32[128,128]{1,0:T(8,128)}) custom-call(f32[512,128]{1,0:T(8,128)S(1)} %get-tuple-element.38.image, f32[128,128]{1,0:T(8,128)S(1)} %add.19.gram), custom_call_target="tpu_custom_call" | custom-call | flops 99999997952 | bytes 1 | tf_op jit(solution)/shard_map/pallas_call | solution.py:18
  (20 shorter events, 0.7 us)
Async XLA Ops:
  0.6 31.9 %collective-permute-start.4 = (bf16[512,1024]{1,0:T(8,128)(2,1)}, bf16[512,1024]{1,0:T(8,128)(2,1)S(1)}, u32[]{:S(2)}, u32[]{:S(2)}) collective-permute-start(bf16[512,1024]{1,0:T(8,128)(2,1)} %embeddings.1), channel_id=1, source_target_pairs={{0,12},{2,14},{4,0},{6,2},{8,4},{10,6},{12,8},{14,10},{1,13},{3,15... | collective-permute-start | bytes 3145736 | tf_op jit(solution)/shard_map/ppermute | solution.py:253
  5.7 1.3 %copy-start = (bf16[512,1024]{1,0:T(8,128)(2,1)S(1)}, bf16[512,1024]{1,0:T(8,128)(2,1)}, u32[]{:S(2)}) copy-start(bf16[512,1024]{1,0:T(8,128)(2,1)} %embeddings.1) | copy-start | bytes 3145732
  7.0 0.9 %copy-start.1 = (bf16[512,128]{1,0:T(8,128)(2,1)S(1)}, bf16[512,128]{1,0:T(8,128)(2,1)}, u32[]{:S(2)}) copy-start(bf16[512,128]{1,0:T(8,128)(2,1)} %panel.1) | copy-start | bytes 393220
  7.9 0.7 copy-start.2
  9.4 3.1 %collective-permute-start = (bf16[264,1152]{1,0:T(8,128)(2,1)S(1)}, bf16[264,1152]{1,0:T(8,128)(2,1)S(1)}, u32[]{:S(2)}, u32[]{:S(2)}) collective-permute-start(bf16[264,1152]{1,0:T(8,128)(2,1)S(1)} %get-tuple-element.25.first), channel_id=1, source_target_pairs={{0,1},{1,0},{2,3},{3,2},{4,5},{5,4},{6,7},{7,6},{8,9},{9,8},{10,11... | collective-permute-start | bytes 1824776 | tf_op jit(solution)/shard_map/ppermute | solution.py:252
  9.4 3.1 %collective-permute-start.1 = (bf16[256,1152]{1,0:T(8,128)(2,1)S(1)}, bf16[256,1152]{1,0:T(8,128)(2,1)S(1)}, u32[]{:S(2)}, u32[]{:S(2)}) collective-permute-start(bf16[256,1152]{1,0:T(8,128)(2,1)S(1)} %get-tuple-element.22.last), channel_id=1, source_target_pairs={{0,1},{1,0},{2,3},{3,2},{4,5},{5,4},{6,7},{7,6},{8,9},{9,8},{10,11... | collective-permute-start | bytes 1769480 | tf_op jit(solution)/shard_map/ppermute | solution.py:252
  9.9 15.3 %collective-permute-start.2 = (bf16[256,1152]{1,0:T(8,128)(2,1)S(1)}, bf16[256,1152]{1,0:T(8,128)(2,1)}, u32[]{:S(2)}, u32[]{:S(2)}) collective-permute-start(bf16[256,1152]{1,0:T(8,128)(2,1)S(1)} %get-tuple-element.22.last), channel_id=1, source_target_pairs={{0,2},{2,0},{4,6},{6,4},{8,10},{10,8},{12,14},{14,12},{1,3},{3,1},... | collective-permute-start | bytes 1769480 | tf_op jit(solution)/shard_map/ppermute | solution.py:253
  11.4 21.1 %collective-permute-start.5 = (bf16[520,128]{1,0:T(8,128)(2,1)}, bf16[520,128]{1,0:T(8,128)(2,1)}, u32[]{:S(2)}, u32[]{:S(2)}) collective-permute-start(bf16[520,128]{1,0:T(8,128)(2,1)} %get-tuple-element.26), channel_id=1, source_target_pairs={{0,12},{2,14},{4,0},{6,2},{8,4},{10,6},{12,8},{14,10},{1,13},{3,15... | collective-permute-start | bytes 399368 | tf_op jit(solution)/shard_map/ppermute | solution.py:253
  25.2 19.5 %collective-permute-start.6 = (bf16[256,1152]{1,0:T(8,128)(2,1)}, bf16[256,1152]{1,0:T(8,128)(2,1)S(1)}, u32[]{:S(2)}, u32[]{:S(2)}) collective-permute-start(bf16[256,1152]{1,0:T(8,128)(2,1)} %collective-permute-done.2), channel_id=1, source_target_pairs={{0,4},{2,2},{4,8},{6,6},{8,12},{10,10},{12,0},{14,14},{1,5},{3,3},... | collective-permute-start | bytes 1769480 | tf_op jit(solution)/shard_map/ppermute | solution.py:253
  27.1 19.0 %collective-permute-start.3 = (bf16[264,1152]{1,0:T(8,128)(2,1)S(1)}, bf16[264,1152]{1,0:T(8,128)(2,1)S(1)}, u32[]{:S(2)}, u32[]{:S(2)}) collective-permute-start(bf16[264,1152]{1,0:T(8,128)(2,1)S(1)} %get-tuple-element.25.first), channel_id=1, source_target_pairs={{0,2},{2,4},{4,6},{6,8},{8,10},{10,12},{12,14},{14,0},{1,3},{3,5},... | collective-permute-start | bytes 1824776 | tf_op jit(solution)/shard_map/ppermute | solution.py:253
  46.1 3.0 %collective-permute-start.9 = (bf16[256,1152]{1,0:T(8,128)(2,1)S(1)}, bf16[256,1152]{1,0:T(8,128)(2,1)S(1)}, u32[]{:S(2)}, u32[]{:S(2)}) collective-permute-start(bf16[256,1152]{1,0:T(8,128)(2,1)S(1)} %collective-permute-done.6.below1), channel_id=1, source_target_pairs={{0,1},{1,0},{2,3},{3,2},{4,5},{5,4},{6,7},{7,6},{8,9},{9,8},{10,11... | collective-permute-start | bytes 1769480 | tf_op jit(solution)/shard_map/ppermute | solution.py:252
  46.1 3.0 %collective-permute-start.8 = (bf16[264,1152]{1,0:T(8,128)(2,1)S(1)}, bf16[264,1152]{1,0:T(8,128)(2,1)S(1)}, u32[]{:S(2)}, u32[]{:S(2)}) collective-permute-start(bf16[264,1152]{1,0:T(8,128)(2,1)S(1)} %collective-permute-done.3.below0), channel_id=1, source_target_pairs={{0,1},{1,0},{2,3},{3,2},{4,5},{5,4},{6,7},{7,6},{8,9},{9,8},{10,11... | collective-permute-start | bytes 1824776 | tf_op jit(solution)/shard_map/ppermute | solution.py:252
  52.8 2.2 %collective-permute-start.10 = (f32[512,128]{1,0:T(8,128)S(1)}, f32[512,128]{1,0:T(8,128)S(1)}, u32[]{:S(2)}, u32[]{:S(2)}) collective-permute-start(f32[512,128]{1,0:T(8,128)S(1)} %get-tuple-element.36), channel_id=1, source_target_pairs={{0,1},{1,0},{2,3},{3,2},{4,5},{5,4},{6,7},{7,6},{8,9},{9,8},{10,11... | collective-permute-start | bytes 786440 | tf_op jit(solution)/shard_map/ppermute | solution.py:252
  52.9 3.7 %collective-permute-start.7 = (f32[512,128]{1,0:T(8,128)S(1)}, f32[512,128]{1,0:T(8,128)S(1)}, u32[]{:S(2)}, u32[]{:S(2)}) collective-permute-start(f32[512,128]{1,0:T(8,128)S(1)} %get-tuple-element.33), channel_id=1, source_target_pairs={{0,1},{1,0},{2,3},{3,2},{4,5},{5,4},{6,7},{7,6},{8,9},{9,8},{10,11... | collective-permute-start | bytes 786440 | tf_op jit(solution)/shard_map/ppermute | solution.py:252
  53.3 11.0 %collective-permute-start.12 = (f32[512,128]{1,0:T(8,128)S(1)}, f32[512,128]{1,0:T(8,128)S(1)}, u32[]{:S(2)}, u32[]{:S(2)}) collective-permute-start(f32[512,128]{1,0:T(8,128)S(1)} %get-tuple-element.37), channel_id=1, source_target_pairs={{0,4},{2,6},{4,8},{6,10},{8,12},{10,14},{12,0},{14,2},{1,5},{3,7},... | collective-permute-start | bytes 786440 | tf_op jit(solution)/shard_map/ppermute | solution.py:253
  55.0 11.4 %collective-permute-start.11 = (f32[512,128]{1,0:T(8,128)S(1)}, f32[512,128]{1,0:T(8,128)S(1)}, u32[]{:S(2)}, u32[]{:S(2)}) collective-permute-start(f32[512,128]{1,0:T(8,128)S(1)} %add.15), channel_id=1, source_target_pairs={{0,14},{2,0},{4,2},{6,4},{8,6},{10,8},{12,10},{14,12},{1,15},{3,1}... | collective-permute-start | bytes 786440 | tf_op jit(solution)/shard_map/ppermute | solution.py:253
  66.8 1.3 %collective-permute-start.13 = (f32[128,128]{1,0:T(8,128)S(1)}, f32[128,128]{1,0:T(8,128)S(1)}, u32[]{:S(2)}, u32[]{:S(2)}) collective-permute-start(f32[128,128]{1,0:T(8,128)S(1)} %get-tuple-element.39), channel_id=1, source_target_pairs={{0,1},{1,0},{2,3},{3,2},{4,5},{5,4},{6,7},{7,6},{8,9},{9,8},{10,11... | collective-permute-start | bytes 196616 | tf_op jit(solution)/shard_map/ppermute | solution.py:252
  68.2 6.1 %collective-permute-start.14 = (f32[128,128]{1,0:T(8,128)S(1)}, f32[128,128]{1,0:T(8,128)S(1)}, u32[]{:S(2)}, u32[]{:S(2)}) collective-permute-start(f32[128,128]{1,0:T(8,128)S(1)} %add.16), channel_id=1, source_target_pairs={{0,2},{2,0},{4,6},{6,4},{8,10},{10,8},{12,14},{14,12},{1,3},{3,1},... | collective-permute-start | bytes 196616 | tf_op jit(solution)/shard_map/ppermute | solution.py:253
  74.3 4.3 %collective-permute-start.15 = (f32[128,128]{1,0:T(8,128)S(1)}, f32[128,128]{1,0:T(8,128)S(1)}, u32[]{:S(2)}, u32[]{:S(2)}) collective-permute-start(f32[128,128]{1,0:T(8,128)S(1)} %add.17), channel_id=1, source_target_pairs={{0,4},{2,6},{4,0},{6,2},{8,12},{10,14},{12,8},{14,10},{1,5},{3,7},... | collective-permute-start | bytes 196616 | tf_op jit(solution)/shard_map/ppermute | solution.py:253
  78.6 5.9 %collective-permute-start.16 = (f32[128,128]{1,0:T(8,128)S(1)}, f32[128,128]{1,0:T(8,128)S(1)}, u32[]{:S(2)}, u32[]{:S(2)}) collective-permute-start(f32[128,128]{1,0:T(8,128)S(1)} %add.18), channel_id=1, source_target_pairs={{0,8},{2,10},{4,12},{6,14},{8,0},{10,2},{12,4},{14,6},{1,9},{3,11}... | collective-permute-start | bytes 196616 | tf_op jit(solution)/shard_map/ppermute | solution.py:253

commit v9 on v8

--- a/solution.py
+++ b/solution.py
@@ -75,8 +75,18 @@
     return jnp.broadcast_to(column, (column.shape[0], TILE)).T[:1]
 
 
-def read_rows(ref):
-    return [ref[k : k + 1] for k in range(ref.shape[0])]
+def as_column(row):
+    return jnp.broadcast_to(row, (TILE, row.shape[1])).T[:, :1]
+
+
+SPLIT = 3
+
+
+def square_rows(ref):
+    size = ref.shape[0] - MARK
+    parts = ref[size:, : 2 * size].astype(F32)
+    row = (parts[0:1] + parts[1:2]) + parts[2:3]
+    return [row[:, :size], row[:, size:]]
 
 
 def columns_of(own, other, sq_rows, masks):
@@ -88,12 +98,12 @@
     return out
 
 
-def products(inverse, rows, columns, back):
+def products(inverse, rows, squares_of, columns, back):
     panels = jnp.concatenate([panel for _, panel, _, _ in columns], axis=0)
     images = []
     for r, (features, panel) in enumerate(rows):
         size = features.shape[0]
-        row_sq = squares(features)
+        row_sq = squares_of[r]
         doubled = features * 2
         tile = r * size // TILE
         ahead, behind = [], []
@@ -126,7 +136,13 @@
     for ref, start in ((first, 0), (last, size)):
         ref[:size, :features] = embeddings[start : start + size]
         ref[:size, features:] = panel[start : start + size]
-    first[size:, : features] = jnp.zeros((MARK, features), BF16)
+    row = as_row(jnp.concatenate([squares(r[:size, :features]) for r in (first, last)], axis=0))
+    carried = []
+    for _ in range(SPLIT):
+        carried.append(row.astype(BF16).astype(F32))
+        row = row - carried[-1]
+    carried = jnp.concatenate(carried + [jnp.zeros((MARK - SPLIT, half), F32)], axis=0).astype(BF16)
+    first[size:, :features] = jnp.concatenate([carried, jnp.zeros((MARK, features - half), BF16)], axis=1)
     first[size:, features:] = mask
     panel_mark[:half] = panel[...]
     panel_mark[half:] = mask
@@ -136,40 +152,50 @@
     return [pair_mask(sub, rows, r, offset, h) for h, r in enumerate(others)]
 
 
-def self_body(inverse, sub, first, last, other_first, other_last, image, sq):
+def self_body(inverse, sub, first, last, other_first, other_last, image):
     half = 2 * last.shape[0]
     own, other = pieces(first, last), pieces(other_first, other_last)
-    rows = [as_row(squares(features)) for features, _ in own + other]
-    for k, row in enumerate(rows):
-        sq[k : k + 1] = row
+    rows = square_rows(first)
     both = [marks(r, half) for r in (first, other_first)]
-    image[...], _ = products(inverse[0], own, columns_of(own, other, rows, masks_of(sub[0], both[0], both, OWN)), None)
-
-
-def above_own_body(inverse, sub, sq, above, panel, first, last, other_first, other_last, image, back):
+    columns = columns_of(own, other, rows + square_rows(other_first), masks_of(sub[0], both[0], both, OWN))
+    image[...], _ = products(inverse[0], own, [as_column(r) for r in rows], columns, None)
+
+
+def own_columns(sub, mark, first, last, other_first, other_last, offset):
+    half = 2 * last.shape[0]
+    masks = masks_of(sub, mark, [marks(r, half) for r in (first, other_first)], offset)
+    rows = square_rows(first) + square_rows(other_first)
+    return columns_of(pieces(first, last), pieces(other_first, other_last), rows, masks)
+
+
+def above_own_body(inverse, sub, above, panel, first, last, other_first, other_last, image, back, above_sq):
     half = above.shape[0]
-    masks = masks_of(sub[0], marks(panel, half), [marks(r, half) for r in (first, other_first)], ABOVE)
-    columns = columns_of(pieces(first, last), pieces(other_first, other_last), read_rows(sq), masks)
-    image[...], back[...] = products(inverse[0], apart(above, panel), columns, jnp.zeros(back.shape, F32))
-
-
-def below_own_body(inverse, sub, sq, below0, below1, first, last, other_first, other_last, self_image, back, image, own_image, cross):
+    size = half // 2
+    columns = own_columns(sub[0], marks(panel, half), first, last, other_first, other_last, ABOVE)
+    rows = apart(above, panel)
+    columns_sq = [squares(features) for features, _ in rows]
+    for k, column in enumerate(columns_sq):
+        above_sq[k * size : (k + 1) * size] = jnp.broadcast_to(column, (size, TILE))
+    image[...], back[...] = products(inverse[0], rows, columns_sq, columns, jnp.zeros(back.shape, F32))
+
+
+def below_own_body(inverse, sub, below0, below1, first, last, other_first, other_last, self_image, back, image, own_image, cross):
     half = image.shape[0]
-    masks = masks_of(sub[0], marks(below0, half), [marks(r, half) for r in (first, other_first)], BELOW)
-    columns = columns_of(pieces(first, last), pieces(other_first, other_last), read_rows(sq), masks)
-    image[...], total = products(inverse[0], pieces(below0, below1), columns, back[...])
+    columns = own_columns(sub[0], marks(below0, half), first, last, other_first, other_last, BELOW)
+    rows_sq = [as_column(r) for r in square_rows(below0)]
+    image[...], total = products(inverse[0], pieces(below0, below1), rows_sq, columns, back[...])
     own_image[...] = self_image[...] + total[:, :half].T
     cross[...] = total[:, half:].T
 
 
 def above_below_body(
-    inverse, sub, above, panel, below0, below1, other0, other1, above_image, below_image, image, below_out, cross
+    inverse, sub, above, panel, above_sq, below0, below1, other0, other1, above_image, below_image, image, below_out, cross
 ):
     half = image.shape[0]
-    masks = masks_of(sub[0], marks(panel, half), [marks(r, half) for r in (below0, other0)], ABOVE - BELOW)
-    own, other = pieces(below0, below1), pieces(other0, other1)
-    columns = columns_of(own, other, [as_row(squares(features)) for features, _ in own + other], masks)
-    products_image, total = products(inverse[0], apart(above, panel), columns, jnp.zeros((TILE, 2 * half), F32))
+    size = half // 2
+    columns = own_columns(sub[0], marks(panel, half), below0, below1, other0, other1, ABOVE - BELOW)
+    rows_sq = [above_sq[k * size : (k + 1) * size, :1] for k in range(2)]
+    products_image, total = products(inverse[0], apart(above, panel), rows_sq, columns, jnp.zeros((TILE, 2 * half), F32))
     image[...] = above_image[...] + products_image
     below_out[...] = below_image[...] + total[:, :half].T
     cross[...] = total[:, half:].T
@@ -240,8 +266,9 @@
     return jnp.where(at_col >= at_row, jnp.concatenate(upper, axis=0), 0.0), jnp.concatenate(inverse, axis=0)
 
 
-def basis_body(image, gram, basis, upper):
-    upper[...], inverse = factor(gram[...], 4)
+def basis_body(image, *refs):
+    *grams, basis, upper = refs
+    upper[...], inverse = factor(jnp.concatenate([g[...] for g in grams], axis=0), 4)
     basis[...] = contract(image[...], inverse, ((1,), (1,)), HIGHEST)
 
 
@@ -271,15 +298,17 @@
     above_panel = blk_move(panel_mark, -2)
     own = (first, last, sub_move(first), sub_move(last))
     image, turned = shape(half, width), shape(width, 2 * half)
-    self_image, sq = vmem_call(self_body, (image, shape(4, size)), inv_width, sub, *own, scalars=2, long=False)
+    self_image = vmem_call(self_body, image, inv_width, sub, *own, scalars=2, long=False)
     below0 = blk_move(after(first, swapped, self_image), 1)
     swapped = after(swapped, self_image)
     below1 = blk_route(swapped, lambda i: i if i & 1 else i + 2) if relayed else blk_move(swapped, 1)
-    above_image, back = vmem_call(above_own_body, (image, turned), inv_width, sub, sq, above, above_panel, *own, scalars=2)
+    above_image, back, above_sq = vmem_call(
+        above_own_body, (image, turned, image), inv_width, sub, above, above_panel, *own, scalars=2
+    )
     below0, below1 = after(below0, above_image, below1), after(below1, above_image, below0)
     below_other = (sub_move(below0), sub_move(below1))
     below_image, own_image, own_cross = vmem_call(
-        below_own_body, (image,) * 3, inv_width, sub, sq, below0, below1, *own, self_image, back, scalars=2
+        below_own_body, (image,) * 3, inv_width, sub, below0, below1, *own, self_image, back, scalars=2
     )
     above_image, below_image, below_cross = vmem_call(
         above_below_body,
@@ -288,6 +317,7 @@
         sub,
         above,
         above_panel,
+        above_sq,
         below0,
         below1,
         *below_other,
@@ -297,18 +327,27 @@
     )
     above_image = blk_move(above_image, 2)
     below_image = blk_move(below_image + sub_move(below_cross), -1)
-    image, gram = vmem_call(
+    image_rows, gram = vmem_call(
         gram_body, (image, shape(width, width)), own_image, sub_move(own_cross), below_image, above_image
     )
     if n_blk & (n_blk - 1):
-        gram = lax.psum(gram, ("blk", "sub"))
+        gram_parts = [lax.psum(gram, ("blk", "sub"))]
     else:
-        gram = gram + sub_move(gram)
-        hop = 1
-        while hop < n_blk:
-            gram = gram + blk_route(gram, lambda i: i ^ hop)
-            hop *= 2
-    return vmem_call(basis_body, (shape(half, width), shape(width, width)), image, gram)
+        rows = width // 2
+        top, bottom = gram[:rows], gram[rows:]
+        mine = lax.axis_index("sub") == 0
+        part = jnp.where(mine, top, bottom) + sub_move(jnp.where(mine, bottom, top))
+        hops = [1 << k for k in range(n_blk.bit_length() - 1)]
+        part = part + blk_route(part, lambda i: i ^ hops[0])
+        for k in range(1, len(hops), 2):
+            a, *b = hops[k : k + 2]
+            near = part + blk_route(part, lambda i: i ^ a)
+            if b:
+                near = near + (blk_route(part, lambda i: i ^ b[0]) + blk_route(part, lambda i: i ^ a ^ b[0]))
+            part = near
+        moved = sub_move(part)
+        gram_parts = [jnp.where(mine, part, moved), jnp.where(mine, moved, part)]
+    return vmem_call(basis_body, (image, shape(width, width)), image_rows, *gram_parts)
 
 
 def solution(mesh):

time: 90 us -> 89.7 us (level)
  waiting for transfers between devices: 46.3 us -> 42.8 us
  starting transfers between devices: 21.1 us -> 23.3 us
    ppermute x10 -> x11, waiting for transfers between devices: 45 us -> 40.4 us  [per_device(): lax.ppermute(v, 'blk', [(i, to(i) % n_blk) for i in range(n_blk)])]
    ppermute x10 -> x11, starting transfers between devices: 19.4 us -> 21.6 us  [per_device(): lax.ppermute(v, 'blk', [(i, to(i) % n_blk) for i in range(n_blk)])]
    ppermute x7 -> x8, waiting for transfers between devices: 1.26 us -> 2.4 us  [per_device(): sub_move = lambda v: lax.ppermute(v, 'sub', [(0, 1), (1, 0)])]
    unnamed x6 -> x10, local copies, waits for them, and re-layouts: 2.84 us -> 3.55 us
  transfers between devices with their start and end apart: 17 -> 19, of which waited for: 10 -> 11; matrix products, arithmetic and copies ran while one was open for 0% -> 0% of each run, Pallas kernels for 10% -> 11%
where the time goes in v9:
time: 89.7 us; the launch traced here: 89.4 us
  waiting for transfers between devices  42.8 us (48%)
  starting transfers between devices  23.3 us (26%)
  Pallas kernels  18.3 us (20%)
  local copies, waits for them, and re-layouts  3.55 us (4%)
  between operations  1.4 us (2%)
    ppermute x11, waiting for transfers between devices, per_device(): lax.ppermute(v, 'blk', [(i, to(i) % n_blk) for i in range(n_blk)])  40.4 us
    ppermute x11, starting transfers between devices, per_device(): lax.ppermute(v, 'blk', [(i, to(i) % n_blk) for i in range(n_blk)])  21.6 us
    pallas_call x7, Pallas kernels, vmem_call(): pl.pallas_call(body, out_shape=out_shapes, in_specs=[in_smem] * scalars +...  18.3 us
    unnamed x10, local copies, waits for them, and re-layouts  3.55 us
    ppermute x8, waiting for transfers between devices, per_device(): sub_move = lambda v: lax.ppermute(v, 'sub', [(0, 1), (1, 0)])  2.4 us
  transfers between devices with their start and end apart: 19, of which 11 were waited for; matrix products, arithmetic and copies ran while one was open for 0% of the time, Pallas kernels for 11%

profile of v9, /device:TPU:0, one launch (start us, length us, event | category | flops | bytes accessed | tf_op | source)
XLA Modules:
  0.0 89.4 jit_solution(8249957996208089596)
XLA Ops:
  0.6 5.1 %collective-permute-start.4 = (bf16[512,1024]{1,0:T(8,128)(2,1)}, bf16[512,1024]{1,0:T(8,128)(2,1)S(1)}, u32[]{:S(2)}, u32[]{:S(2)}) collective-permute-start(bf16[512,1024]{1,0:T(8,128)(2,1)} %embeddings.1), channel_id=1, source_target_pairs={{0,12},{2,14},{4,0},{6,2},{8,4},{10,6},{12,8},{14,10},{1,13},{3,15... | collective-permute-start | bytes 3145736 | tf_op jit(solution)/shard_map/ppermute | solution.py:280
  5.7 1.3 %copy-done = bf16[512,1024]{1,0:T(8,128)(2,1)S(1)} copy-done((bf16[512,1024]{1,0:T(8,128)(2,1)S(1)}, bf16[512,1024]{1,0:T(8,128)(2,1)}, u32[]{:S(2)}) %copy-start) | copy-done | bytes 1048600
  7.0 0.9 %copy-done.1 = bf16[512,128]{1,0:T(8,128)(2,1)S(1)} copy-done((bf16[512,128]{1,0:T(8,128)(2,1)S(1)}, bf16[512,128]{1,0:T(8,128)(2,1)}, u32[]{:S(2)}) %copy-start.1) | copy-done | bytes 131096
  7.9 0.7 copy-done.2
  8.6 1.1 %shard_map.59 = (bf16[264,1152]{1,0:T(8,128)(2,1)S(1)}, bf16[256,1152]{1,0:T(8,128)(2,1)S(1)}, bf16[520,128]{1,0:T(8,128)(2,1)}) custom-call(bf16[512,1024]{1,0:T(8,128)(2,1)S(1)} %copy-done, bf16[512,128]{1,0:T(8,128)(2,1)S(1)} %copy-done.1, s32[4,56]{1,0:T(4,128)S(1)} %copy-done.2), custom_call_target="tpu_custom_call" | custom-call | flops 1 | bytes 1 | tf_op jit(solution)/shard_map/pallas_call | solution.py:18
  9.6 0.5 collective-permute-start.2
  10.1 1.5 %collective-permute-start = (bf16[256,1152]{1,0:T(8,128)(2,1)S(1)}, bf16[256,1152]{1,0:T(8,128)(2,1)}, u32[]{:S(2)}, u32[]{:S(2)}) collective-permute-start(bf16[256,1152]{1,0:T(8,128)(2,1)S(1)} %get-tuple-element.21.last), channel_id=1, source_target_pairs={{0,2},{2,0},{4,6},{6,4},{8,10},{10,8},{12,14},{14,12},{1,3},{3,1},... | collective-permute-start | bytes 1769480 | tf_op jit(solution)/shard_map/ppermute | solution.py:280
  12.8 2.1 %shard_map.60.self_image = f32[512,128]{1,0:T(8,128)S(1)} custom-call(f32[1]{0:T(128)S(6)} %copy.6.inverse, s32[1]{0:T(128)} %bitcast.sub, bf16[264,1152]{1,0:T(8,128)(2,1)S(1)} %get-tuple-element.22.first, bf16[256,1152]{1,0:T(8,128)(2,1)S(1)} %get-tuple-element.21.last, bf16[264,1152]{1,0:T(8,128)(2,1)S(1)} %collective-permute-done.1.other_first, ...), custom_call_target="tpu_custom_call" | custom-call | flops 1 | bytes 1 | tf_op jit(solution)/shard_map/pallas_call | solution.py:18
  14.8 10.6 %collective-permute-done = bf16[256,1152]{1,0:T(8,128)(2,1)} collective-permute-done((bf16[256,1152]{1,0:T(8,128)(2,1)S(1)}, bf16[256,1152]{1,0:T(8,128)(2,1)}, u32[]{:S(2)}, u32[]{:S(2)}) %collective-permute-start) | collective-permute-done | bytes 589856 | tf_op jit(solution)/shard_map/ppermute | solution.py:280
  25.5 1.5 %collective-permute-start.3 = (bf16[264,1152]{1,0:T(8,128)(2,1)S(1)}, bf16[264,1152]{1,0:T(8,128)(2,1)S(1)}, u32[]{:S(2)}, u32[]{:S(2)}) collective-permute-start(bf16[264,1152]{1,0:T(8,128)(2,1)S(1)} %get-tuple-element.22.first), channel_id=1, source_target_pairs={{0,2},{2,4},{4,6},{6,8},{8,10},{10,12},{12,14},{14,0},{1,3},{3,5},... | collective-permute-start | bytes 1824776 | tf_op jit(solution)/shard_map/ppermute | solution.py:280
  27.0 1.9 %collective-permute-start.6 = (bf16[256,1152]{1,0:T(8,128)(2,1)}, bf16[256,1152]{1,0:T(8,128)(2,1)S(1)}, u32[]{:S(2)}, u32[]{:S(2)}) collective-permute-start(bf16[256,1152]{1,0:T(8,128)(2,1)} %collective-permute-done), channel_id=1, source_target_pairs={{0,4},{2,2},{4,8},{6,6},{8,12},{10,10},{12,0},{14,14},{1,5},{3,3},... | collective-permute-start | bytes 1769480 | tf_op jit(solution)/shard_map/ppermute | solution.py:280
  28.9 3.6 %collective-permute-done.5.panel = bf16[520,128]{1,0:T(8,128)(2,1)} collective-permute-done((bf16[520,128]{1,0:T(8,128)(2,1)}, bf16[520,128]{1,0:T(8,128)(2,1)}, u32[]{:S(2)}, u32[]{:S(2)}) %collective-permute-start.5) | collective-permute-done | bytes 133152 | tf_op jit(solution)/shard_map/ppermute | solution.py:280
  32.5 3.2 %shard_map.61 = (f32[512,128]{1,0:T(8,128)S(1)}, f32[128,1024]{1,0:T(8,128)S(1)}, f32[512,128]{1,0:T(8,128)S(1)}) custom-call(f32[1]{0:T(128)S(6)} %copy.6.inverse, s32[1]{0:T(128)} %bitcast.sub, bf16[512,1024]{1,0:T(8,128)(2,1)S(1)} %collective-permute-done.4.above, bf16[520,128]{1,0:T(8,128)(2,1)} %collective-permute-done.5.panel, ...), custom_call_target="tpu_custom_call" | custom-call | flops 99999997952 | bytes 1 | tf_op jit(solution)/shard_map/pallas_call | solution.py:18
  35.7 9.3 %collective-permute-done.6.below1 = bf16[256,1152]{1,0:T(8,128)(2,1)S(1)} collective-permute-done((bf16[256,1152]{1,0:T(8,128)(2,1)}, bf16[256,1152]{1,0:T(8,128)(2,1)S(1)}, u32[]{:S(2)}, u32[]{:S(2)}) %collective-permute-start.6) | collective-permute-done | bytes 589856 | tf_op jit(solution)/shard_map/ppermute | solution.py:280
  45.0 1.1 %collective-permute-done.3.below0 = bf16[264,1152]{1,0:T(8,128)(2,1)S(1)} collective-permute-done((bf16[264,1152]{1,0:T(8,128)(2,1)S(1)}, bf16[264,1152]{1,0:T(8,128)(2,1)S(1)}, u32[]{:S(2)}, u32[]{:S(2)}) %collective-permute-start.3) | collective-permute-done | bytes 608288 | tf_op jit(solution)/shard_map/ppermute | solution.py:280
  46.6 3.1 %shard_map.62 = (f32[512,128]{1,0:T(8,128)S(1)}, f32[512,128]{1,0:T(8,128)S(1)}, f32[512,128]{1,0:T(8,128)}) custom-call(f32[1]{0:T(128)S(6)} %copy.6.inverse, s32[1]{0:T(128)} %bitcast.sub, bf16[264,1152]{1,0:T(8,128)(2,1)S(1)} %collective-permute-done.3.below0, bf16[256,1152]{1,0:T(8,128)(2,1)S(1)} %collective-permute-done.6.below1, ...), custom_call_target="tpu_custom_call" | custom-call | flops 99999997952 | bytes 1 | tf_op jit(solution)/shard_map/pallas_call | solution.py:18
  49.7 0.7 copy-done.3
  50.4 3.3 %shard_map.63 = (f32[512,128]{1,0:T(8,128)S(1)}, f32[512,128]{1,0:T(8,128)S(1)}, f32[512,128]{1,0:T(8,128)S(1)}) custom-call(f32[1]{0:T(128)S(6)} %copy.6.inverse, s32[1]{0:T(128)} %bitcast.sub, bf16[512,1024]{1,0:T(8,128)(2,1)S(1)} %collective-permute-done.4.above, bf16[520,128]{1,0:T(8,128)(2,1)} %collective-permute-done.5.panel, ...), custom_call_target="tpu_custom_call" | custom-call | flops 99999997952 | bytes 1 | tf_op jit(solution)/shard_map/pallas_call | solution.py:18
  54.3 1.6 %collective-permute-start.12 = (f32[512,128]{1,0:T(8,128)S(1)}, f32[512,128]{1,0:T(8,128)S(1)}, u32[]{:S(2)}, u32[]{:S(2)}) collective-permute-start(f32[512,128]{1,0:T(8,128)S(1)} %get-tuple-element.35), channel_id=1, source_target_pairs={{0,4},{2,6},{4,8},{6,10},{8,12},{10,14},{12,0},{14,2},{1,5},{3,7},... | collective-permute-start | bytes 786440 | tf_op jit(solution)/shard_map/ppermute | solution.py:280
  56.0 1.6 %collective-permute-start.11 = (f32[512,128]{1,0:T(8,128)S(1)}, f32[512,128]{1,0:T(8,128)S(1)}, u32[]{:S(2)}, u32[]{:S(2)}) collective-permute-start(f32[512,128]{1,0:T(8,128)S(1)} %add.18), channel_id=1, source_target_pairs={{0,14},{2,0},{4,2},{6,4},{8,6},{10,8},{12,10},{14,12},{1,15},{3,1}... | collective-permute-start | bytes 786440 | tf_op jit(solution)/shard_map/ppermute | solution.py:280
  57.5 7.8 %collective-permute-done.12.above = f32[512,128]{1,0:T(8,128)S(1)} collective-permute-done((f32[512,128]{1,0:T(8,128)S(1)}, f32[512,128]{1,0:T(8,128)S(1)}, u32[]{:S(2)}, u32[]{:S(2)}) %collective-permute-start.12) | collective-permute-done | bytes 262176 | tf_op jit(solution)/shard_map/ppermute | solution.py:280
  65.3 2.0 %collective-permute-done.11.below = f32[512,128]{1,0:T(8,128)S(1)} collective-permute-done((f32[512,128]{1,0:T(8,128)S(1)}, f32[512,128]{1,0:T(8,128)S(1)}, u32[]{:S(2)}, u32[]{:S(2)}) %collective-permute-start.11) | collective-permute-done | bytes 262176 | tf_op jit(solution)/shard_map/ppermute | solution.py:280
  67.9 1.2 %collective-permute-done.13 = f32[64,128]{1,0:T(8,128)S(1)} collective-permute-done((f32[64,128]{1,0:T(8,128)S(1)}, f32[64,128]{1,0:T(8,128)S(1)}, u32[]{:S(2)}, u32[]{:S(2)}) %collective-permute-start.13) | collective-permute-done | bytes 32800 | tf_op jit(solution)/shard_map/ppermute | solution.py:279
  69.1 3.6 %collective-permute-start.14 = (f32[64,128]{1,0:T(8,128)S(1)}, f32[64,128]{1,0:T(8,128)S(1)}, u32[]{:S(2)}, u32[]{:S(2)}) collective-permute-start(f32[64,128]{1,0:T(8,128)S(1)} %select_add_fusion), channel_id=1, source_target_pairs={{0,2},{2,0},{4,6},{6,4},{8,10},{10,8},{12,14},{14,12},{1,3},{3,1},... | collective-permute-start | bytes 98312 | tf_op jit(solution)/shard_map/ppermute | solution.py:280
  72.7 1.9 %collective-permute-done.14 = f32[64,128]{1,0:T(8,128)S(1)} collective-permute-done((f32[64,128]{1,0:T(8,128)S(1)}, f32[64,128]{1,0:T(8,128)S(1)}, u32[]{:S(2)}, u32[]{:S(2)}) %collective-permute-start.14) | collective-permute-done | bytes 32800 | tf_op jit(solution)/shard_map/ppermute | solution.py:280
  74.6 1.1 %collective-permute-start.15 = (f32[64,128]{1,0:T(8,128)S(1)}, f32[64,128]{1,0:T(8,128)S(1)}, u32[]{:S(2)}, u32[]{:S(2)}) collective-permute-start(f32[64,128]{1,0:T(8,128)S(1)} %add.20), channel_id=1, source_target_pairs={{0,4},{2,6},{4,0},{6,2},{8,12},{10,14},{12,8},{14,10},{1,5},{3,7},... | collective-permute-start | bytes 98312 | tf_op jit(solution)/shard_map/ppermute | solution.py:280
  75.7 1.6 %collective-permute-start.16 = (f32[64,128]{1,0:T(8,128)S(1)}, f32[64,128]{1,0:T(8,128)S(1)}, u32[]{:S(2)}, u32[]{:S(2)}) collective-permute-start(f32[64,128]{1,0:T(8,128)S(1)} %add.20), channel_id=1, source_target_pairs={{0,8},{2,10},{4,12},{6,14},{8,0},{10,2},{12,4},{14,6},{1,9},{3,11}... | collective-permute-start | bytes 98312 | tf_op jit(solution)/shard_map/ppermute | solution.py:280
  77.3 1.7 %collective-permute-start.17 = (f32[64,128]{1,0:T(8,128)S(1)}, f32[64,128]{1,0:T(8,128)S(1)}, u32[]{:S(2)}, u32[]{:S(2)}) collective-permute-start(f32[64,128]{1,0:T(8,128)S(1)} %add.20), channel_id=1, source_target_pairs={{0,12},{2,14},{4,8},{6,10},{8,4},{10,6},{12,0},{14,2},{1,13},{3,15... | collective-permute-start | bytes 98312 | tf_op jit(solution)/shard_map/ppermute | solution.py:280
  79.0 1.5 %collective-permute-done.16 = f32[64,128]{1,0:T(8,128)S(1)} collective-permute-done((f32[64,128]{1,0:T(8,128)S(1)}, f32[64,128]{1,0:T(8,128)S(1)}, u32[]{:S(2)}, u32[]{:S(2)}) %collective-permute-start.16) | collective-permute-done | bytes 32800 | tf_op jit(solution)/shard_map/ppermute | solution.py:280
  80.5 2.5 %collective-permute-done.17 = f32[64,128]{1,0:T(8,128)S(1)} collective-permute-done((f32[64,128]{1,0:T(8,128)S(1)}, f32[64,128]{1,0:T(8,128)S(1)}, u32[]{:S(2)}, u32[]{:S(2)}) %collective-permute-start.17) | collective-permute-done | bytes 32800 | tf_op jit(solution)/shard_map/ppermute | solution.py:280
  83.1 1.2 %collective-permute-done.18 = f32[64,128]{1,0:T(8,128)S(1)} collective-permute-done((f32[64,128]{1,0:T(8,128)S(1)}, f32[64,128]{1,0:T(8,128)S(1)}, u32[]{:S(2)}, u32[]{:S(2)}) %collective-permute-start.18) | collective-permute-done | bytes 32800 | tf_op jit(solution)/shard_map/ppermute | solution.py:279
  84.3 5.1 %shard_map.65 = (f32[512,128]{1,0:T(8,128)}, f32[128,128]{1,0:T(8,128)}) custom-call(f32[512,128]{1,0:T(8,128)S(1)} %get-tuple-element.36.image, f32[64,128]{1,0:T(8,128)S(1)} %get-tuple-element.39.refs_0_, f32[64,128]{1,0:T(8,128)S(1)} %get-tuple-element.38.refs_1_), custom_call_target="tpu_custom_call" | custom-call | flops 99999997952 | bytes 1 | tf_op jit(solution)/shard_map/pallas_call | solution.py:18
  (29 shorter events, 2.2 us)
Async XLA Ops:
  0.6 31.9 %collective-permute-start.4 = (bf16[512,1024]{1,0:T(8,128)(2,1)}, bf16[512,1024]{1,0:T(8,128)(2,1)S(1)}, u32[]{:S(2)}, u32[]{:S(2)}) collective-permute-start(bf16[512,1024]{1,0:T(8,128)(2,1)} %embeddings.1), channel_id=1, source_target_pairs={{0,12},{2,14},{4,0},{6,2},{8,4},{10,6},{12,8},{14,10},{1,13},{3,15... | collective-permute-start | bytes 3145736 | tf_op jit(solution)/shard_map/ppermute | solution.py:280
  5.7 1.3 %copy-start = (bf16[512,1024]{1,0:T(8,128)(2,1)S(1)}, bf16[512,1024]{1,0:T(8,128)(2,1)}, u32[]{:S(2)}) copy-start(bf16[512,1024]{1,0:T(8,128)(2,1)} %embeddings.1) | copy-start | bytes 3145732
  7.0 0.9 %copy-start.1 = (bf16[512,128]{1,0:T(8,128)(2,1)S(1)}, bf16[512,128]{1,0:T(8,128)(2,1)}, u32[]{:S(2)}) copy-start(bf16[512,128]{1,0:T(8,128)(2,1)} %panel.1) | copy-start | bytes 393220
  7.9 0.7 copy-start.2
  9.6 3.1 %collective-permute-start.1 = (bf16[264,1152]{1,0:T(8,128)(2,1)S(1)}, bf16[264,1152]{1,0:T(8,128)(2,1)S(1)}, u32[]{:S(2)}, u32[]{:S(2)}) collective-permute-start(bf16[264,1152]{1,0:T(8,128)(2,1)S(1)} %get-tuple-element.22.first), channel_id=1, source_target_pairs={{0,1},{1,0},{2,3},{3,2},{4,5},{5,4},{6,7},{7,6},{8,9},{9,8},{10,11... | collective-permute-start | bytes 1824776 | tf_op jit(solution)/shard_map/ppermute | solution.py:279
  9.6 3.1 %collective-permute-start.2 = (bf16[256,1152]{1,0:T(8,128)(2,1)S(1)}, bf16[256,1152]{1,0:T(8,128)(2,1)S(1)}, u32[]{:S(2)}, u32[]{:S(2)}) collective-permute-start(bf16[256,1152]{1,0:T(8,128)(2,1)S(1)} %get-tuple-element.21.last), channel_id=1, source_target_pairs={{0,1},{1,0},{2,3},{3,2},{4,5},{5,4},{6,7},{7,6},{8,9},{9,8},{10,11... | collective-permute-start | bytes 1769480 | tf_op jit(solution)/shard_map/ppermute | solution.py:279
  10.1 15.3 %collective-permute-start = (bf16[256,1152]{1,0:T(8,128)(2,1)S(1)}, bf16[256,1152]{1,0:T(8,128)(2,1)}, u32[]{:S(2)}, u32[]{:S(2)}) collective-permute-start(bf16[256,1152]{1,0:T(8,128)(2,1)S(1)} %get-tuple-element.21.last), channel_id=1, source_target_pairs={{0,2},{2,0},{4,6},{6,4},{8,10},{10,8},{12,14},{14,12},{1,3},{3,1},... | collective-permute-start | bytes 1769480 | tf_op jit(solution)/shard_map/ppermute | solution.py:280
  11.6 20.9 %collective-permute-start.5 = (bf16[520,128]{1,0:T(8,128)(2,1)}, bf16[520,128]{1,0:T(8,128)(2,1)}, u32[]{:S(2)}, u32[]{:S(2)}) collective-permute-start(bf16[520,128]{1,0:T(8,128)(2,1)} %get-tuple-element.23), channel_id=1, source_target_pairs={{0,12},{2,14},{4,0},{6,2},{8,4},{10,6},{12,8},{14,10},{1,13},{3,15... | collective-permute-start | bytes 399368 | tf_op jit(solution)/shard_map/ppermute | solution.py:280
  25.5 20.6 %collective-permute-start.3 = (bf16[264,1152]{1,0:T(8,128)(2,1)S(1)}, bf16[264,1152]{1,0:T(8,128)(2,1)S(1)}, u32[]{:S(2)}, u32[]{:S(2)}) collective-permute-start(bf16[264,1152]{1,0:T(8,128)(2,1)S(1)} %get-tuple-element.22.first), channel_id=1, source_target_pairs={{0,2},{2,4},{4,6},{6,8},{8,10},{10,12},{12,14},{14,0},{1,3},{3,5},... | collective-permute-start | bytes 1824776 | tf_op jit(solution)/shard_map/ppermute | solution.py:280
  27.0 18.0 %collective-permute-start.6 = (bf16[256,1152]{1,0:T(8,128)(2,1)}, bf16[256,1152]{1,0:T(8,128)(2,1)S(1)}, u32[]{:S(2)}, u32[]{:S(2)}) collective-permute-start(bf16[256,1152]{1,0:T(8,128)(2,1)} %collective-permute-done), channel_id=1, source_target_pairs={{0,4},{2,2},{4,8},{6,6},{8,12},{10,10},{12,0},{14,14},{1,5},{3,3},... | collective-permute-start | bytes 1769480 | tf_op jit(solution)/shard_map/ppermute | solution.py:280
  46.1 4.4 %collective-permute-start.8 = (bf16[264,1152]{1,0:T(8,128)(2,1)S(1)}, bf16[264,1152]{1,0:T(8,128)(2,1)S(1)}, u32[]{:S(2)}, u32[]{:S(2)}) collective-permute-start(bf16[264,1152]{1,0:T(8,128)(2,1)S(1)} %collective-permute-done.3.below0), channel_id=1, source_target_pairs={{0,1},{1,0},{2,3},{3,2},{4,5},{5,4},{6,7},{7,6},{8,9},{9,8},{10,11... | collective-permute-start | bytes 1824776 | tf_op jit(solution)/shard_map/ppermute | solution.py:279
  46.1 4.4 %collective-permute-start.9 = (bf16[256,1152]{1,0:T(8,128)(2,1)S(1)}, bf16[256,1152]{1,0:T(8,128)(2,1)S(1)}, u32[]{:S(2)}, u32[]{:S(2)}) collective-permute-start(bf16[256,1152]{1,0:T(8,128)(2,1)S(1)} %collective-permute-done.6.below1), channel_id=1, source_target_pairs={{0,1},{1,0},{2,3},{3,2},{4,5},{5,4},{6,7},{7,6},{8,9},{9,8},{10,11... | collective-permute-start | bytes 1769480 | tf_op jit(solution)/shard_map/ppermute | solution.py:279
  49.7 0.7 copy-start.3
  53.7 2.2 %collective-permute-start.10 = (f32[512,128]{1,0:T(8,128)S(1)}, f32[512,128]{1,0:T(8,128)S(1)}, u32[]{:S(2)}, u32[]{:S(2)}) collective-permute-start(f32[512,128]{1,0:T(8,128)S(1)} %get-tuple-element.34), channel_id=1, source_target_pairs={{0,1},{1,0},{2,3},{3,2},{4,5},{5,4},{6,7},{7,6},{8,9},{9,8},{10,11... | collective-permute-start | bytes 786440 | tf_op jit(solution)/shard_map/ppermute | solution.py:279
  53.8 3.7 %collective-permute-start.7 = (f32[512,128]{1,0:T(8,128)}, f32[512,128]{1,0:T(8,128)S(1)}, u32[]{:S(2)}, u32[]{:S(2)}) collective-permute-start(f32[512,128]{1,0:T(8,128)} %get-tuple-element.30), channel_id=1, source_target_pairs={{0,1},{1,0},{2,3},{3,2},{4,5},{5,4},{6,7},{7,6},{8,9},{9,8},{10,11... | collective-permute-start | bytes 786440 | tf_op jit(solution)/shard_map/ppermute | solution.py:279
  54.3 11.0 %collective-permute-start.12 = (f32[512,128]{1,0:T(8,128)S(1)}, f32[512,128]{1,0:T(8,128)S(1)}, u32[]{:S(2)}, u32[]{:S(2)}) collective-permute-start(f32[512,128]{1,0:T(8,128)S(1)} %get-tuple-element.35), channel_id=1, source_target_pairs={{0,4},{2,6},{4,8},{6,10},{8,12},{10,14},{12,0},{14,2},{1,5},{3,7},... | collective-permute-start | bytes 786440 | tf_op jit(solution)/shard_map/ppermute | solution.py:280
  55.9 11.4 %copy-start.4 = (f32[512,128]{1,0:T(8,128)S(1)}, f32[512,128]{1,0:T(8,128)}, u32[]{:S(2)}) copy-start(f32[512,128]{1,0:T(8,128)} %copy-done.3) | copy-start | bytes 786436
  56.0 11.4 %collective-permute-start.11 = (f32[512,128]{1,0:T(8,128)S(1)}, f32[512,128]{1,0:T(8,128)S(1)}, u32[]{:S(2)}, u32[]{:S(2)}) collective-permute-start(f32[512,128]{1,0:T(8,128)S(1)} %add.18), channel_id=1, source_target_pairs={{0,14},{2,0},{4,2},{6,4},{8,6},{10,8},{12,10},{14,12},{1,15},{3,1}... | collective-permute-start | bytes 786440 | tf_op jit(solution)/shard_map/ppermute | solution.py:280
  67.8 1.3 %collective-permute-start.13 = (f32[64,128]{1,0:T(8,128)S(1)}, f32[64,128]{1,0:T(8,128)S(1)}, u32[]{:S(2)}, u32[]{:S(2)}) collective-permute-start(f32[64,128]{1,0:T(8,128)S(1)} %slice_select_fusion), channel_id=1, source_target_pairs={{0,1},{1,0},{2,3},{3,2},{4,5},{5,4},{6,7},{7,6},{8,9},{9,8},{10,11... | collective-permute-start | bytes 98312 | tf_op jit(solution)/shard_map/ppermute | solution.py:279
  69.1 5.5 %collective-permute-start.14 = (f32[64,128]{1,0:T(8,128)S(1)}, f32[64,128]{1,0:T(8,128)S(1)}, u32[]{:S(2)}, u32[]{:S(2)}) collective-permute-start(f32[64,128]{1,0:T(8,128)S(1)} %select_add_fusion), channel_id=1, source_target_pairs={{0,2},{2,0},{4,6},{6,4},{8,10},{10,8},{12,14},{14,12},{1,3},{3,1},... | collective-permute-start | bytes 98312 | tf_op jit(solution)/shard_map/ppermute | solution.py:280
  74.6 4.4 %collective-permute-start.15 = (f32[64,128]{1,0:T(8,128)S(1)}, f32[64,128]{1,0:T(8,128)S(1)}, u32[]{:S(2)}, u32[]{:S(2)}) collective-permute-start(f32[64,128]{1,0:T(8,128)S(1)} %add.20), channel_id=1, source_target_pairs={{0,4},{2,6},{4,0},{6,2},{8,12},{10,14},{12,8},{14,10},{1,5},{3,7},... | collective-permute-start | bytes 98312 | tf_op jit(solution)/shard_map/ppermute | solution.py:280
  75.7 4.8 %collective-permute-start.16 = (f32[64,128]{1,0:T(8,128)S(1)}, f32[64,128]{1,0:T(8,128)S(1)}, u32[]{:S(2)}, u32[]{:S(2)}) collective-permute-start(f32[64,128]{1,0:T(8,128)S(1)} %add.20), channel_id=1, source_target_pairs={{0,8},{2,10},{4,12},{6,14},{8,0},{10,2},{12,4},{14,6},{1,9},{3,11}... | collective-permute-start | bytes 98312 | tf_op jit(solution)/shard_map/ppermute | solution.py:280
  77.3 5.7 %collective-permute-start.17 = (f32[64,128]{1,0:T(8,128)S(1)}, f32[64,128]{1,0:T(8,128)S(1)}, u32[]{:S(2)}, u32[]{:S(2)}) collective-permute-start(f32[64,128]{1,0:T(8,128)S(1)} %add.20), channel_id=1, source_target_pairs={{0,12},{2,14},{4,8},{6,10},{8,4},{10,6},{12,0},{14,2},{1,13},{3,15... | collective-permute-start | bytes 98312 | tf_op jit(solution)/shard_map/ppermute | solution.py:280
  83.0 1.3 %collective-permute-start.18 = (f32[64,128]{1,0:T(8,128)S(1)}, f32[64,128]{1,0:T(8,128)S(1)}, u32[]{:S(2)}, u32[]{:S(2)}) collective-permute-start(f32[64,128]{1,0:T(8,128)S(1)} %add_add_fusion), channel_id=1, source_target_pairs={{0,1},{1,0},{2,3},{3,2},{4,5},{5,4},{6,7},{7,6},{8,9},{9,8},{10,11... | collective-permute-start | bytes 98312 | tf_op jit(solution)/shard_map/ppermute | solution.py:279

commit v10 on v9

--- a/solution.py
+++ b/solution.py
@@ -179,17 +179,32 @@
     image[...], back[...] = products(inverse[0], rows, columns_sq, columns, jnp.zeros(back.shape, F32))
 
 
-def below_own_body(inverse, sub, below0, below1, first, last, other_first, other_last, self_image, back, image, own_image, cross):
+def below_own_body(inverse, sub, below0, below1, first, last, other_first, other_last, back, image, total):
     half = image.shape[0]
     columns = own_columns(sub[0], marks(below0, half), first, last, other_first, other_last, BELOW)
     rows_sq = [as_column(r) for r in square_rows(below0)]
-    image[...], total = products(inverse[0], pieces(below0, below1), rows_sq, columns, back[...])
-    own_image[...] = self_image[...] + total[:, :half].T
-    cross[...] = total[:, half:].T
+    image[...], total[...] = products(inverse[0], pieces(below0, below1), rows_sq, columns, back[...])
 
 
 def above_below_body(
-    inverse, sub, above, panel, above_sq, below0, below1, other0, other1, above_image, below_image, image, below_out, cross
+    inverse,
+    sub,
+    above,
+    panel,
+    above_sq,
+    below0,
+    below1,
+    other0,
+    other1,
+    above_image,
+    below_image,
+    self_image,
+    back,
+    image,
+    below_out,
+    below_cross,
+    own_out,
+    own_cross,
 ):
     half = image.shape[0]
     size = half // 2
@@ -198,7 +213,9 @@
     products_image, total = products(inverse[0], apart(above, panel), rows_sq, columns, jnp.zeros((TILE, 2 * half), F32))
     image[...] = above_image[...] + products_image
     below_out[...] = below_image[...] + total[:, :half].T
-    cross[...] = total[:, half:].T
+    below_cross[...] = total[:, half:].T
+    own_out[...] = self_image[...] + back[:, :half].T
+    own_cross[...] = back[:, half:].T
 
 
 def gram_body(own, cross, below, above, image, gram):
@@ -266,9 +283,8 @@
     return jnp.where(at_col >= at_row, jnp.concatenate(upper, axis=0), 0.0), jnp.concatenate(inverse, axis=0)
 
 
-def basis_body(image, *refs):
-    *grams, basis, upper = refs
-    upper[...], inverse = factor(jnp.concatenate([g[...] for g in grams], axis=0), 4)
+def basis_body(image, gram, basis, upper):
+    upper[...], inverse = factor(gram[...], 4)
     basis[...] = contract(image[...], inverse, ((1,), (1,)), HIGHEST)
 
 
@@ -307,12 +323,12 @@
     )
     below0, below1 = after(below0, above_image, below1), after(below1, above_image, below0)
     below_other = (sub_move(below0), sub_move(below1))
-    below_image, own_image, own_cross = vmem_call(
-        below_own_body, (image,) * 3, inv_width, sub, below0, below1, *own, self_image, back, scalars=2
-    )
-    above_image, below_image, below_cross = vmem_call(
+    below_image, back = vmem_call(
+        below_own_body, (image, turned), inv_width, sub, below0, below1, *own, back, scalars=2
+    )
+    above_image, below_image, below_cross, own_image, own_cross = vmem_call(
         above_below_body,
-        (image,) * 3,
+        (image,) * 5,
         inv_width,
         sub,
         above,
@@ -323,6 +339,8 @@
         *below_other,
         above_image,
         below_image,
+        self_image,
+        back,
         scalars=2,
     )
     above_image = blk_move(above_image, 2)
@@ -331,23 +349,14 @@
         gram_body, (image, shape(width, width)), own_image, sub_move(own_cross), below_image, above_image
     )
     if n_blk & (n_blk - 1):
-        gram_parts = [lax.psum(gram, ("blk", "sub"))]
+        gram = lax.psum(gram, ("blk", "sub"))
     else:
-        rows = width // 2
-        top, bottom = gram[:rows], gram[rows:]
-        mine = lax.axis_index("sub") == 0
-        part = jnp.where(mine, top, bottom) + sub_move(jnp.where(mine, bottom, top))
-        hops = [1 << k for k in range(n_blk.bit_length() - 1)]
-        part = part + blk_route(part, lambda i: i ^ hops[0])
-        for k in range(1, len(hops), 2):
-            a, *b = hops[k : k + 2]
-            near = part + blk_route(part, lambda i: i ^ a)
-            if b:
-                near = near + (blk_route(part, lambda i: i ^ b[0]) + blk_route(part, lambda i: i ^ a ^ b[0]))
-            part = near
-        moved = sub_move(part)
-        gram_parts = [jnp.where(mine, part, moved), jnp.where(mine, moved, part)]
-    return vmem_call(basis_body, (image, shape(width, width)), image_rows, *gram_parts)
+        gram = gram + sub_move(gram)
+        hop = 1
+        while hop < n_blk:
+            gram = gram + blk_route(gram, lambda i: i ^ hop)
+            hop *= 2
+    return vmem_call(basis_body, (image, shape(width, width)), image_rows, gram)
 
 
 def solution(mesh):

time: 89.7 us -> 89.6 us (level)
  waiting for transfers between devices: 42.8 us -> 46.4 us
  starting transfers between devices: 23.3 us -> 21.1 us
    ppermute x11 -> x10, waiting for transfers between devices: 40.4 us -> 45.1 us  [per_device(): lax.ppermute(v, 'blk', [(i, to(i) % n_blk) for i in range(n_blk)])]
    ppermute x11 -> x10, starting transfers between devices: 21.6 us -> 19.4 us  [per_device(): lax.ppermute(v, 'blk', [(i, to(i) % n_blk) for i in range(n_blk)])]
    ppermute x8 -> x7, waiting for transfers between devices: 2.4 us -> 1.3 us  [per_device(): sub_move = lambda v: lax.ppermute(v, 'sub', [(0, 1), (1, 0)])]
    unnamed x10 -> x6, local copies, waits for them, and re-layouts: 3.55 us -> 2.84 us
  transfers between devices with their start and end apart: 19 -> 17, of which waited for: 11 -> 10; matrix products, arithmetic and copies ran while one was open for 0% -> 0% of each run, Pallas kernels for 11% -> 10%
where the time goes in v10:
time: 89.6 us; the launch traced here: 89.3 us
  waiting for transfers between devices  46.4 us (52%)
  starting transfers between devices  21.1 us (24%)
  Pallas kernels  17.5 us (20%)
  local copies, waits for them, and re-layouts  2.84 us (3%)
  between operations  1.39 us (2%)
    ppermute x10, waiting for transfers between devices, per_device(): lax.ppermute(v, 'blk', [(i, to(i) % n_blk) for i in range(n_blk)])  45.1 us
    ppermute x10, starting transfers between devices, per_device(): lax.ppermute(v, 'blk', [(i, to(i) % n_blk) for i in range(n_blk)])  19.4 us
    pallas_call x7, Pallas kernels, vmem_call(): pl.pallas_call(body, out_shape=out_shapes, in_specs=[in_smem] * scalars +...  17.5 us
    unnamed x6, local copies, waits for them, and re-layouts  2.84 us
  transfers between devices with their start and end apart: 17, of which 10 were waited for; matrix products, arithmetic and copies ran while one was open for 0% of the time, Pallas kernels for 10%

profile of v10, /device:TPU:0, one launch (start us, length us, event | category | flops | bytes accessed | tf_op | source)
XLA Modules:
  0.0 89.3 jit_solution(8869352922408147909)
XLA Ops:
  0.6 5.1 %collective-permute-start = (bf16[512,1024]{1,0:T(8,128)(2,1)}, bf16[512,1024]{1,0:T(8,128)(2,1)S(1)}, u32[]{:S(2)}, u32[]{:S(2)}) collective-permute-start(bf16[512,1024]{1,0:T(8,128)(2,1)} %embeddings.1), channel_id=1, source_target_pairs={{0,12},{2,14},{4,0},{6,2},{8,4},{10,6},{12,8},{14,10},{1,13},{3,15... | collective-permute-start | bytes 3145736 | tf_op jit(solution)/shard_map/ppermute | solution.py:296
  5.7 1.3 %copy-done = bf16[512,1024]{1,0:T(8,128)(2,1)S(1)} copy-done((bf16[512,1024]{1,0:T(8,128)(2,1)S(1)}, bf16[512,1024]{1,0:T(8,128)(2,1)}, u32[]{:S(2)}) %copy-start) | copy-done | bytes 1048600
  7.0 0.9 %copy-done.1 = bf16[512,128]{1,0:T(8,128)(2,1)S(1)} copy-done((bf16[512,128]{1,0:T(8,128)(2,1)S(1)}, bf16[512,128]{1,0:T(8,128)(2,1)}, u32[]{:S(2)}) %copy-start.1) | copy-done | bytes 131096
  7.9 0.7 copy-done.2
  8.6 1.1 %shard_map.59 = (bf16[264,1152]{1,0:T(8,128)(2,1)S(1)}, bf16[256,1152]{1,0:T(8,128)(2,1)S(1)}, bf16[520,128]{1,0:T(8,128)(2,1)}) custom-call(bf16[512,1024]{1,0:T(8,128)(2,1)S(1)} %copy-done, bf16[512,128]{1,0:T(8,128)(2,1)S(1)} %copy-done.1, s32[4,56]{1,0:T(4,128)S(1)} %copy-done.2), custom_call_target="tpu_custom_call" | custom-call | flops 1 | bytes 1 | tf_op jit(solution)/shard_map/pallas_call | solution.py:18
  9.6 0.5 collective-permute-start.3
  10.1 1.5 %collective-permute-start.4 = (bf16[256,1152]{1,0:T(8,128)(2,1)S(1)}, bf16[256,1152]{1,0:T(8,128)(2,1)}, u32[]{:S(2)}, u32[]{:S(2)}) collective-permute-start(bf16[256,1152]{1,0:T(8,128)(2,1)S(1)} %get-tuple-element.23.last), channel_id=1, source_target_pairs={{0,2},{2,0},{4,6},{6,4},{8,10},{10,8},{12,14},{14,12},{1,3},{3,1},... | collective-permute-start | bytes 1769480 | tf_op jit(solution)/shard_map/ppermute | solution.py:296
  11.6 0.4 collective-permute-start.1
  12.8 2.1 %shard_map.61.self_image = f32[512,128]{1,0:T(8,128)S(1)} custom-call(f32[1]{0:T(128)S(6)} %copy.6.inverse, s32[1]{0:T(128)} %bitcast.sub, bf16[264,1152]{1,0:T(8,128)(2,1)S(1)} %get-tuple-element.25.first, bf16[256,1152]{1,0:T(8,128)(2,1)S(1)} %get-tuple-element.23.last, bf16[264,1152]{1,0:T(8,128)(2,1)S(1)} %collective-permute-done.2.other_first, ...), custom_call_target="tpu_custom_call" | custom-call | flops 1 | bytes 1 | tf_op jit(solution)/shard_map/pallas_call | solution.py:18
  14.8 10.6 %collective-permute-done.4 = bf16[256,1152]{1,0:T(8,128)(2,1)} collective-permute-done((bf16[256,1152]{1,0:T(8,128)(2,1)S(1)}, bf16[256,1152]{1,0:T(8,128)(2,1)}, u32[]{:S(2)}, u32[]{:S(2)}) %collective-permute-start.4) | collective-permute-done | bytes 589856 | tf_op jit(solution)/shard_map/ppermute | solution.py:296
  25.5 1.9 %collective-permute-start.6 = (bf16[256,1152]{1,0:T(8,128)(2,1)}, bf16[256,1152]{1,0:T(8,128)(2,1)S(1)}, u32[]{:S(2)}, u32[]{:S(2)}) collective-permute-start(bf16[256,1152]{1,0:T(8,128)(2,1)} %collective-permute-done.4), channel_id=1, source_target_pairs={{0,4},{2,2},{4,8},{6,6},{8,12},{10,10},{12,0},{14,14},{1,5},{3,3},... | collective-permute-start | bytes 1769480 | tf_op jit(solution)/shard_map/ppermute | solution.py:296
  27.4 1.3 %collective-permute-start.5 = (bf16[264,1152]{1,0:T(8,128)(2,1)S(1)}, bf16[264,1152]{1,0:T(8,128)(2,1)S(1)}, u32[]{:S(2)}, u32[]{:S(2)}) collective-permute-start(bf16[264,1152]{1,0:T(8,128)(2,1)S(1)} %get-tuple-element.25.first), channel_id=1, source_target_pairs={{0,2},{2,4},{4,6},{6,8},{8,10},{10,12},{12,14},{14,0},{1,3},{3,5},... | collective-permute-start | bytes 1824776 | tf_op jit(solution)/shard_map/ppermute | solution.py:296
  28.7 3.8 %collective-permute-done.1.panel = bf16[520,128]{1,0:T(8,128)(2,1)} collective-permute-done((bf16[520,128]{1,0:T(8,128)(2,1)}, bf16[520,128]{1,0:T(8,128)(2,1)}, u32[]{:S(2)}, u32[]{:S(2)}) %collective-permute-start.1) | collective-permute-done | bytes 133152 | tf_op jit(solution)/shard_map/ppermute | solution.py:296
  32.5 3.2 %shard_map.60 = (f32[512,128]{1,0:T(8,128)S(1)}, f32[128,1024]{1,0:T(8,128)S(1)}, f32[512,128]{1,0:T(8,128)S(1)}) custom-call(f32[1]{0:T(128)S(6)} %copy.6.inverse, s32[1]{0:T(128)} %bitcast.sub, bf16[512,1024]{1,0:T(8,128)(2,1)S(1)} %collective-permute-done.above, bf16[520,128]{1,0:T(8,128)(2,1)} %collective-permute-done.1.panel, ...), custom_call_target="tpu_custom_call" | custom-call | flops 99999997952 | bytes 1 | tf_op jit(solution)/shard_map/pallas_call | solution.py:18
  35.7 9.1 %collective-permute-done.6.below1 = bf16[256,1152]{1,0:T(8,128)(2,1)S(1)} collective-permute-done((bf16[256,1152]{1,0:T(8,128)(2,1)}, bf16[256,1152]{1,0:T(8,128)(2,1)S(1)}, u32[]{:S(2)}, u32[]{:S(2)}) %collective-permute-start.6) | collective-permute-done | bytes 589856 | tf_op jit(solution)/shard_map/ppermute | solution.py:296
  44.8 1.3 %collective-permute-done.5.below0 = bf16[264,1152]{1,0:T(8,128)(2,1)S(1)} collective-permute-done((bf16[264,1152]{1,0:T(8,128)(2,1)S(1)}, bf16[264,1152]{1,0:T(8,128)(2,1)S(1)}, u32[]{:S(2)}, u32[]{:S(2)}) %collective-permute-start.5) | collective-permute-done | bytes 608288 | tf_op jit(solution)/shard_map/ppermute | solution.py:296
  46.1 0.5 collective-permute-start.7
  46.6 2.3 %shard_map.62 = (f32[512,128]{1,0:T(8,128)S(1)}, f32[128,1024]{1,0:T(8,128)S(1)}) custom-call(f32[1]{0:T(128)S(6)} %copy.6.inverse, s32[1]{0:T(128)} %bitcast.sub, bf16[264,1152]{1,0:T(8,128)(2,1)S(1)} %collective-permute-done.5.below0, bf16[256,1152]{1,0:T(8,128)(2,1)S(1)} %collective-permute-done.6.below1, bf16[264,1152]{1,0:T(8,128)(2,1)S(1)} %get-tuple-element.25.first, ...), custom_call_target="tpu_custom_call" | custom-call | flops 99999997952 | bytes 1 | tf_op jit(solution)/shard_map/pallas_call | solution.py:18
  49.0 3.3 %shard_map.63 = (f32[512,128]{1,0:T(8,128)S(1)}, f32[512,128]{1,0:T(8,128)S(1)}, f32[512,128]{1,0:T(8,128)S(1)}, f32[512,128]{1,0:T(8,128)S(1)}, f32[512,128]{1,0:T(8,128)S(1)}) custom-call(f32[1]{0:T(128)S(6)} %copy.6.inverse, s32[1]{0:T(128)} %bitcast.sub, bf16[512,1024]{1,0:T(8,128)(2,1)S(1)} %collective-permute-done.above, ...), custom_call_target="tpu_custom_call" | custom-call | flops 99999997952 | bytes 1 | tf_op jit(solution)/shard_map/pallas_call | solution.py:18
  52.9 1.6 %collective-permute-start.12 = (f32[512,128]{1,0:T(8,128)S(1)}, f32[512,128]{1,0:T(8,128)S(1)}, u32[]{:S(2)}, u32[]{:S(2)}) collective-permute-start(f32[512,128]{1,0:T(8,128)S(1)} %get-tuple-element.37), channel_id=1, source_target_pairs={{0,4},{2,6},{4,8},{6,10},{8,12},{10,14},{12,0},{14,2},{1,5},{3,7},... | collective-permute-start | bytes 786440 | tf_op jit(solution)/shard_map/ppermute | solution.py:296
  54.5 1.6 %collective-permute-start.11 = (f32[512,128]{1,0:T(8,128)S(1)}, f32[512,128]{1,0:T(8,128)S(1)}, u32[]{:S(2)}, u32[]{:S(2)}) collective-permute-start(f32[512,128]{1,0:T(8,128)S(1)} %add.15), channel_id=1, source_target_pairs={{0,14},{2,0},{4,2},{6,4},{8,6},{10,8},{12,10},{14,12},{1,15},{3,1}... | collective-permute-start | bytes 786440 | tf_op jit(solution)/shard_map/ppermute | solution.py:296
  56.1 7.8 %collective-permute-done.12.above = f32[512,128]{1,0:T(8,128)S(1)} collective-permute-done((f32[512,128]{1,0:T(8,128)S(1)}, f32[512,128]{1,0:T(8,128)S(1)}, u32[]{:S(2)}, u32[]{:S(2)}) %collective-permute-start.12) | collective-permute-done | bytes 262176 | tf_op jit(solution)/shard_map/ppermute | solution.py:296
  63.9 2.1 %collective-permute-done.11.below = f32[512,128]{1,0:T(8,128)S(1)} collective-permute-done((f32[512,128]{1,0:T(8,128)S(1)}, f32[512,128]{1,0:T(8,128)S(1)}, u32[]{:S(2)}, u32[]{:S(2)}) %collective-permute-start.11) | collective-permute-done | bytes 262176 | tf_op jit(solution)/shard_map/ppermute | solution.py:296
  66.0 0.4 shard_map.64
  66.5 1.2 %collective-permute-done.13 = f32[128,128]{1,0:T(8,128)S(1)} collective-permute-done((f32[128,128]{1,0:T(8,128)S(1)}, f32[128,128]{1,0:T(8,128)S(1)}, u32[]{:S(2)}, u32[]{:S(2)}) %collective-permute-start.13) | collective-permute-done | bytes 65568 | tf_op jit(solution)/shard_map/ppermute | solution.py:295
  67.8 3.7 %collective-permute-start.14 = (f32[128,128]{1,0:T(8,128)S(1)}, f32[128,128]{1,0:T(8,128)S(1)}, u32[]{:S(2)}, u32[]{:S(2)}) collective-permute-start(f32[128,128]{1,0:T(8,128)S(1)} %add.16), channel_id=1, source_target_pairs={{0,2},{2,0},{4,6},{6,4},{8,10},{10,8},{12,14},{14,12},{1,3},{3,1},... | collective-permute-start | bytes 196616 | tf_op jit(solution)/shard_map/ppermute | solution.py:296
  71.4 2.4 %collective-permute-done.14 = f32[128,128]{1,0:T(8,128)S(1)} collective-permute-done((f32[128,128]{1,0:T(8,128)S(1)}, f32[128,128]{1,0:T(8,128)S(1)}, u32[]{:S(2)}, u32[]{:S(2)}) %collective-permute-start.14) | collective-permute-done | bytes 65568 | tf_op jit(solution)/shard_map/ppermute | solution.py:296
  73.9 1.1 %collective-permute-start.15 = (f32[128,128]{1,0:T(8,128)S(1)}, f32[128,128]{1,0:T(8,128)S(1)}, u32[]{:S(2)}, u32[]{:S(2)}) collective-permute-start(f32[128,128]{1,0:T(8,128)S(1)} %add.17), channel_id=1, source_target_pairs={{0,4},{2,6},{4,0},{6,2},{8,12},{10,14},{12,8},{14,10},{1,5},{3,7},... | collective-permute-start | bytes 196616 | tf_op jit(solution)/shard_map/ppermute | solution.py:296
  75.0 3.2 %collective-permute-done.15 = f32[128,128]{1,0:T(8,128)S(1)} collective-permute-done((f32[128,128]{1,0:T(8,128)S(1)}, f32[128,128]{1,0:T(8,128)S(1)}, u32[]{:S(2)}, u32[]{:S(2)}) %collective-permute-start.15) | collective-permute-done | bytes 65568 | tf_op jit(solution)/shard_map/ppermute | solution.py:296
  78.2 1.2 %collective-permute-start.16 = (f32[128,128]{1,0:T(8,128)S(1)}, f32[128,128]{1,0:T(8,128)S(1)}, u32[]{:S(2)}, u32[]{:S(2)}) collective-permute-start(f32[128,128]{1,0:T(8,128)S(1)} %add.18), channel_id=1, source_target_pairs={{0,8},{2,10},{4,12},{6,14},{8,0},{10,2},{12,4},{14,6},{1,9},{3,11}... | collective-permute-start | bytes 196616 | tf_op jit(solution)/shard_map/ppermute | solution.py:296
  79.4 4.7 %collective-permute-done.16 = f32[128,128]{1,0:T(8,128)S(1)} collective-permute-done((f32[128,128]{1,0:T(8,128)S(1)}, f32[128,128]{1,0:T(8,128)S(1)}, u32[]{:S(2)}, u32[]{:S(2)}) %collective-permute-start.16) | collective-permute-done | bytes 65568 | tf_op jit(solution)/shard_map/ppermute | solution.py:296
  84.1 5.2 %shard_map.65 = (f32[512,128]{1,0:T(8,128)}, f32[128,128]{1,0:T(8,128)}) custom-call(f32[512,128]{1,0:T(8,128)S(1)} %get-tuple-element.38.image, f32[128,128]{1,0:T(8,128)S(1)} %add.19.gram), custom_call_target="tpu_custom_call" | custom-call | flops 99999997952 | bytes 1 | tf_op jit(solution)/shard_map/pallas_call | solution.py:18
  (20 shorter events, 0.8 us)
Async XLA Ops:
  0.6 31.9 %collective-permute-start = (bf16[512,1024]{1,0:T(8,128)(2,1)}, bf16[512,1024]{1,0:T(8,128)(2,1)S(1)}, u32[]{:S(2)}, u32[]{:S(2)}) collective-permute-start(bf16[512,1024]{1,0:T(8,128)(2,1)} %embeddings.1), channel_id=1, source_target_pairs={{0,12},{2,14},{4,0},{6,2},{8,4},{10,6},{12,8},{14,10},{1,13},{3,15... | collective-permute-start | bytes 3145736 | tf_op jit(solution)/shard_map/ppermute | solution.py:296
  5.7 1.3 %copy-start = (bf16[512,1024]{1,0:T(8,128)(2,1)S(1)}, bf16[512,1024]{1,0:T(8,128)(2,1)}, u32[]{:S(2)}) copy-start(bf16[512,1024]{1,0:T(8,128)(2,1)} %embeddings.1) | copy-start | bytes 3145732
  7.0 0.9 %copy-start.1 = (bf16[512,128]{1,0:T(8,128)(2,1)S(1)}, bf16[512,128]{1,0:T(8,128)(2,1)}, u32[]{:S(2)}) copy-start(bf16[512,128]{1,0:T(8,128)(2,1)} %panel.1) | copy-start | bytes 393220
  7.9 0.7 copy-start.2
  9.6 3.1 %collective-permute-start.2 = (bf16[264,1152]{1,0:T(8,128)(2,1)S(1)}, bf16[264,1152]{1,0:T(8,128)(2,1)S(1)}, u32[]{:S(2)}, u32[]{:S(2)}) collective-permute-start(bf16[264,1152]{1,0:T(8,128)(2,1)S(1)} %get-tuple-element.25.first), channel_id=1, source_target_pairs={{0,1},{1,0},{2,3},{3,2},{4,5},{5,4},{6,7},{7,6},{8,9},{9,8},{10,11... | collective-permute-start | bytes 1824776 | tf_op jit(solution)/shard_map/ppermute | solution.py:295
  9.6 3.1 %collective-permute-start.3 = (bf16[256,1152]{1,0:T(8,128)(2,1)S(1)}, bf16[256,1152]{1,0:T(8,128)(2,1)S(1)}, u32[]{:S(2)}, u32[]{:S(2)}) collective-permute-start(bf16[256,1152]{1,0:T(8,128)(2,1)S(1)} %get-tuple-element.23.last), channel_id=1, source_target_pairs={{0,1},{1,0},{2,3},{3,2},{4,5},{5,4},{6,7},{7,6},{8,9},{9,8},{10,11... | collective-permute-start | bytes 1769480 | tf_op jit(solution)/shard_map/ppermute | solution.py:295
  10.1 15.3 %collective-permute-start.4 = (bf16[256,1152]{1,0:T(8,128)(2,1)S(1)}, bf16[256,1152]{1,0:T(8,128)(2,1)}, u32[]{:S(2)}, u32[]{:S(2)}) collective-permute-start(bf16[256,1152]{1,0:T(8,128)(2,1)S(1)} %get-tuple-element.23.last), channel_id=1, source_target_pairs={{0,2},{2,0},{4,6},{6,4},{8,10},{10,8},{12,14},{14,12},{1,3},{3,1},... | collective-permute-start | bytes 1769480 | tf_op jit(solution)/shard_map/ppermute | solution.py:296
  11.6 20.9 %collective-permute-start.1 = (bf16[520,128]{1,0:T(8,128)(2,1)}, bf16[520,128]{1,0:T(8,128)(2,1)}, u32[]{:S(2)}, u32[]{:S(2)}) collective-permute-start(bf16[520,128]{1,0:T(8,128)(2,1)} %get-tuple-element.21), channel_id=1, source_target_pairs={{0,12},{2,14},{4,0},{6,2},{8,4},{10,6},{12,8},{14,10},{1,13},{3,15... | collective-permute-start | bytes 399368 | tf_op jit(solution)/shard_map/ppermute | solution.py:296
  25.5 19.3 %collective-permute-start.6 = (bf16[256,1152]{1,0:T(8,128)(2,1)}, bf16[256,1152]{1,0:T(8,128)(2,1)S(1)}, u32[]{:S(2)}, u32[]{:S(2)}) collective-permute-start(bf16[256,1152]{1,0:T(8,128)(2,1)} %collective-permute-done.4), channel_id=1, source_target_pairs={{0,4},{2,2},{4,8},{6,6},{8,12},{10,10},{12,0},{14,14},{1,5},{3,3},... | collective-permute-start | bytes 1769480 | tf_op jit(solution)/shard_map/ppermute | solution.py:296
  27.4 18.7 %collective-permute-start.5 = (bf16[264,1152]{1,0:T(8,128)(2,1)S(1)}, bf16[264,1152]{1,0:T(8,128)(2,1)S(1)}, u32[]{:S(2)}, u32[]{:S(2)}) collective-permute-start(bf16[264,1152]{1,0:T(8,128)(2,1)S(1)} %get-tuple-element.25.first), channel_id=1, source_target_pairs={{0,2},{2,4},{4,6},{6,8},{8,10},{10,12},{12,14},{14,0},{1,3},{3,5},... | collective-permute-start | bytes 1824776 | tf_op jit(solution)/shard_map/ppermute | solution.py:296
  46.1 2.8 %collective-permute-start.8 = (bf16[256,1152]{1,0:T(8,128)(2,1)S(1)}, bf16[256,1152]{1,0:T(8,128)(2,1)S(1)}, u32[]{:S(2)}, u32[]{:S(2)}) collective-permute-start(bf16[256,1152]{1,0:T(8,128)(2,1)S(1)} %collective-permute-done.6.below1), channel_id=1, source_target_pairs={{0,1},{1,0},{2,3},{3,2},{4,5},{5,4},{6,7},{7,6},{8,9},{9,8},{10,11... | collective-permute-start | bytes 1769480 | tf_op jit(solution)/shard_map/ppermute | solution.py:295
  46.1 2.9 %collective-permute-start.7 = (bf16[264,1152]{1,0:T(8,128)(2,1)S(1)}, bf16[264,1152]{1,0:T(8,128)(2,1)S(1)}, u32[]{:S(2)}, u32[]{:S(2)}) collective-permute-start(bf16[264,1152]{1,0:T(8,128)(2,1)S(1)} %collective-permute-done.5.below0), channel_id=1, source_target_pairs={{0,1},{1,0},{2,3},{3,2},{4,5},{5,4},{6,7},{7,6},{8,9},{9,8},{10,11... | collective-permute-start | bytes 1824776 | tf_op jit(solution)/shard_map/ppermute | solution.py:295
  52.3 2.2 %collective-permute-start.10 = (f32[512,128]{1,0:T(8,128)S(1)}, f32[512,128]{1,0:T(8,128)S(1)}, u32[]{:S(2)}, u32[]{:S(2)}) collective-permute-start(f32[512,128]{1,0:T(8,128)S(1)} %get-tuple-element.36), channel_id=1, source_target_pairs={{0,1},{1,0},{2,3},{3,2},{4,5},{5,4},{6,7},{7,6},{8,9},{9,8},{10,11... | collective-permute-start | bytes 786440 | tf_op jit(solution)/shard_map/ppermute | solution.py:295
  52.5 3.6 %collective-permute-start.9 = (f32[512,128]{1,0:T(8,128)S(1)}, f32[512,128]{1,0:T(8,128)S(1)}, u32[]{:S(2)}, u32[]{:S(2)}) collective-permute-start(f32[512,128]{1,0:T(8,128)S(1)} %get-tuple-element.34), channel_id=1, source_target_pairs={{0,1},{1,0},{2,3},{3,2},{4,5},{5,4},{6,7},{7,6},{8,9},{9,8},{10,11... | collective-permute-start | bytes 786440 | tf_op jit(solution)/shard_map/ppermute | solution.py:295
  52.9 11.0 %collective-permute-start.12 = (f32[512,128]{1,0:T(8,128)S(1)}, f32[512,128]{1,0:T(8,128)S(1)}, u32[]{:S(2)}, u32[]{:S(2)}) collective-permute-start(f32[512,128]{1,0:T(8,128)S(1)} %get-tuple-element.37), channel_id=1, source_target_pairs={{0,4},{2,6},{4,8},{6,10},{8,12},{10,14},{12,0},{14,2},{1,5},{3,7},... | collective-permute-start | bytes 786440 | tf_op jit(solution)/shard_map/ppermute | solution.py:296
  54.5 11.4 %collective-permute-start.11 = (f32[512,128]{1,0:T(8,128)S(1)}, f32[512,128]{1,0:T(8,128)S(1)}, u32[]{:S(2)}, u32[]{:S(2)}) collective-permute-start(f32[512,128]{1,0:T(8,128)S(1)} %add.15), channel_id=1, source_target_pairs={{0,14},{2,0},{4,2},{6,4},{8,6},{10,8},{12,10},{14,12},{1,15},{3,1}... | collective-permute-start | bytes 786440 | tf_op jit(solution)/shard_map/ppermute | solution.py:296
  66.4 1.3 %collective-permute-start.13 = (f32[128,128]{1,0:T(8,128)S(1)}, f32[128,128]{1,0:T(8,128)S(1)}, u32[]{:S(2)}, u32[]{:S(2)}) collective-permute-start(f32[128,128]{1,0:T(8,128)S(1)} %get-tuple-element.39), channel_id=1, source_target_pairs={{0,1},{1,0},{2,3},{3,2},{4,5},{5,4},{6,7},{7,6},{8,9},{9,8},{10,11... | collective-permute-start | bytes 196616 | tf_op jit(solution)/shard_map/ppermute | solution.py:295
  67.8 6.1 %collective-permute-start.14 = (f32[128,128]{1,0:T(8,128)S(1)}, f32[128,128]{1,0:T(8,128)S(1)}, u32[]{:S(2)}, u32[]{:S(2)}) collective-permute-start(f32[128,128]{1,0:T(8,128)S(1)} %add.16), channel_id=1, source_target_pairs={{0,2},{2,0},{4,6},{6,4},{8,10},{10,8},{12,14},{14,12},{1,3},{3,1},... | collective-permute-start | bytes 196616 | tf_op jit(solution)/shard_map/ppermute | solution.py:296
  73.9 4.3 %collective-permute-start.15 = (f32[128,128]{1,0:T(8,128)S(1)}, f32[128,128]{1,0:T(8,128)S(1)}, u32[]{:S(2)}, u32[]{:S(2)}) collective-permute-start(f32[128,128]{1,0:T(8,128)S(1)} %add.17), channel_id=1, source_target_pairs={{0,4},{2,6},{4,0},{6,2},{8,12},{10,14},{12,8},{14,10},{1,5},{3,7},... | collective-permute-start | bytes 196616 | tf_op jit(solution)/shard_map/ppermute | solution.py:296
  78.2 5.9 %collective-permute-start.16 = (f32[128,128]{1,0:T(8,128)S(1)}, f32[128,128]{1,0:T(8,128)S(1)}, u32[]{:S(2)}, u32[]{:S(2)}) collective-permute-start(f32[128,128]{1,0:T(8,128)S(1)} %add.18), channel_id=1, source_target_pairs={{0,8},{2,10},{4,12},{6,14},{8,0},{10,2},{12,4},{14,6},{1,9},{3,11}... | collective-permute-start | bytes 196616 | tf_op jit(solution)/shard_map/ppermute | solution.py:296

commit v11 on v10

--- a/solution.py
+++ b/solution.py
@@ -98,14 +98,14 @@
     return out
 
 
-def products(inverse, rows, squares_of, columns, back):
+def products(inverse, rows, squares_of, columns, back, first=0):
     panels = jnp.concatenate([panel for _, panel, _, _ in columns], axis=0)
     images = []
     for r, (features, panel) in enumerate(rows):
         size = features.shape[0]
         row_sq = squares_of[r]
         doubled = features * 2
-        tile = r * size // TILE
+        tile = (first + r) * size // TILE
         ahead, behind = [], []
         for other, _, col_sq, mask in columns:
             tiles = mask.shape[0] // 2
@@ -179,43 +179,33 @@
     image[...], back[...] = products(inverse[0], rows, columns_sq, columns, jnp.zeros(back.shape, F32))
 
 
-def below_own_body(inverse, sub, below0, below1, first, last, other_first, other_last, back, image, total):
-    half = image.shape[0]
-    columns = own_columns(sub[0], marks(below0, half), first, last, other_first, other_last, BELOW)
-    rows_sq = [as_column(r) for r in square_rows(below0)]
-    image[...], total[...] = products(inverse[0], pieces(below0, below1), rows_sq, columns, back[...])
-
-
-def above_below_body(
-    inverse,
-    sub,
-    above,
-    panel,
-    above_sq,
-    below0,
-    below1,
-    other0,
-    other1,
-    above_image,
-    below_image,
-    self_image,
-    back,
-    image,
-    below_out,
-    below_cross,
-    own_out,
-    own_cross,
+def below_first_body(inverse, sub, below, first, last, other_first, other_last, back, image, total):
+    half = 2 * last.shape[0]
+    columns = own_columns(sub[0], marks(below, half), first, last, other_first, other_last, BELOW)
+    rows_sq = [as_column(square_rows(below)[0])]
+    image[...], total[...] = products(inverse[0], [pieces(below, last)[0]], rows_sq, columns, back[...])
+
+
+def below_last_body(
+    inverse, sub, marked, below, first, last, other_first, other_last, self_image, back, image, own_image, own_cross
 ):
+    half = 2 * last.shape[0]
+    columns = own_columns(sub[0], marks(marked, half), first, last, other_first, other_last, BELOW)
+    rows_sq = [as_column(square_rows(marked)[1])]
+    image[...], total = products(inverse[0], pieces(below), rows_sq, columns, back[...], 1)
+    own_image[...] = self_image[...] + total[:, :half].T
+    own_cross[...] = total[:, half:].T
+
+
+def above_below_body(inverse, sub, above, panel, above_sq, below0, below1, other0, other1, above_image, image, below_image, cross):
     half = image.shape[0]
     size = half // 2
     columns = own_columns(sub[0], marks(panel, half), below0, below1, other0, other1, ABOVE - BELOW)
     rows_sq = [above_sq[k * size : (k + 1) * size, :1] for k in range(2)]
     products_image, total = products(inverse[0], apart(above, panel), rows_sq, columns, jnp.zeros((TILE, 2 * half), F32))
     image[...] = above_image[...] + products_image
-    below_out[...] = below_image[...] + total[:, :half].T
-    below_cross[...] = total[:, half:].T
-    own_out[...] = self_image[...] + back[:, :half].T
-    own_cross[...] = back[:, half:].T
+    below_image[...] = total[:, :half].T
+    cross[...] = total[:, half:].T
 
 
 def gram_body(own, cross, below, above, image, gram):
@@ -323,12 +313,12 @@
     )
     below0, below1 = after(below0, above_image, below1), after(below1, above_image, below0)
     below_other = (sub_move(below0), sub_move(below1))
-    below_image, back = vmem_call(
-        below_own_body, (image, turned), inv_width, sub, below0, below1, *own, back, scalars=2
-    )
-    above_image, below_image, below_cross, own_image, own_cross = vmem_call(
+    below_image0, back = vmem_call(
+        below_first_body, (shape(size, width), turned), inv_width, sub, below0, *own, back, scalars=2
+    )
+    above_image, below_sum, below_cross = vmem_call(
         above_below_body,
-        (image,) * 5,
+        (image,) * 3,
         inv_width,
         sub,
         above,
@@ -337,14 +327,24 @@
         below0,
         below1,
         *below_other,
-        above_image,
-        below_image,
+        after(above_image, below_image0),
+        scalars=2,
+    )
+    below_image1, own_image, own_cross = vmem_call(
+        below_last_body,
+        (shape(size, width), image, image),
+        inv_width,
+        sub,
+        below0,
+        below1,
+        *own,
         self_image,
-        back,
+        after(back, above_image),
         scalars=2,
     )
     above_image = blk_move(above_image, 2)
-    below_image = blk_move(below_image + sub_move(below_cross), -1)
+    below_image = jnp.concatenate([below_image0, below_image1], axis=0)
+    below_image = blk_move(below_sum + sub_move(below_cross) + below_image, -1)
     image_rows, gram = vmem_call(
         gram_body, (image, shape(width, width)), own_image, sub_move(own_cross), below_image, above_image
     )

time: 89.6 us -> 89.5 us (level)
    ppermute x10, waiting for transfers between devices: 45.1 us -> 44 us  [per_device(): lax.ppermute(v, 'blk', [(i, to(i) % n_blk) for i in range(n_blk)])]
    ppermute x7, waiting for transfers between devices: 1.3 us -> 2.26 us  [per_device(): sub_move = lambda v: lax.ppermute(v, 'sub', [(0, 1), (1, 0)])]
    pallas_call x7 -> x8, Pallas kernels: 17.5 us -> 18 us  [vmem_call(): pl.pallas_call(body, out_shape=out_shapes, in_specs=[in_smem] * scalars +...]
  transfers between devices with their start and end apart: 17 -> 17, of which waited for: 10 -> 12; matrix products, arithmetic and copies ran while one was open for 0% -> 0% of each run, Pallas kernels for 10% -> 10%
where the time goes in v11:
time: 89.5 us; the launch traced here: 89.2 us
  waiting for transfers between devices  46.3 us (52%)
  starting transfers between devices  20.6 us (23%)
  Pallas kernels  18 us (20%)
  local copies, waits for them, and re-layouts  2.84 us (3%)
  between operations  1.39 us (2%)
    ppermute x10, waiting for transfers between devices, per_device(): lax.ppermute(v, 'blk', [(i, to(i) % n_blk) for i in range(n_blk)])  44 us
    ppermute x10, starting transfers between devices, per_device(): lax.ppermute(v, 'blk', [(i, to(i) % n_blk) for i in range(n_blk)])  19 us
    pallas_call x8, Pallas kernels, vmem_call(): pl.pallas_call(body, out_shape=out_shapes, in_specs=[in_smem] * scalars +...  18 us
    unnamed x6, local copies, waits for them, and re-layouts  2.84 us
    ppermute x7, waiting for transfers between devices, per_device(): sub_move = lambda v: lax.ppermute(v, 'sub', [(0, 1), (1, 0)])  2.26 us
  transfers between devices with their start and end apart: 17, of which 12 were waited for; matrix products, arithmetic and copies ran while one was open for 0% of the time, Pallas kernels for 10%

profile of v11, /device:TPU:0, one launch (start us, length us, event | category | flops | bytes accessed | tf_op | source)
XLA Modules:
  0.0 89.2 jit_solution(4246894700765864945)
XLA Ops:
  0.6 5.1 %collective-permute-start.4 = (bf16[512,1024]{1,0:T(8,128)(2,1)}, bf16[512,1024]{1,0:T(8,128)(2,1)S(1)}, u32[]{:S(2)}, u32[]{:S(2)}) collective-permute-start(bf16[512,1024]{1,0:T(8,128)(2,1)} %embeddings.1), channel_id=1, source_target_pairs={{0,12},{2,14},{4,0},{6,2},{8,4},{10,6},{12,8},{14,10},{1,13},{3,15... | collective-permute-start | bytes 3145736 | tf_op jit(solution)/shard_map/ppermute | solution.py:286
  5.7 1.3 %copy-done = bf16[512,1024]{1,0:T(8,128)(2,1)S(1)} copy-done((bf16[512,1024]{1,0:T(8,128)(2,1)S(1)}, bf16[512,1024]{1,0:T(8,128)(2,1)}, u32[]{:S(2)}) %copy-start) | copy-done | bytes 1048600
  7.0 0.9 %copy-done.1 = bf16[512,128]{1,0:T(8,128)(2,1)S(1)} copy-done((bf16[512,128]{1,0:T(8,128)(2,1)S(1)}, bf16[512,128]{1,0:T(8,128)(2,1)}, u32[]{:S(2)}) %copy-start.1) | copy-done | bytes 131096
  7.9 0.7 copy-done.2
  8.6 1.1 %shard_map.59 = (bf16[264,1152]{1,0:T(8,128)(2,1)S(1)}, bf16[256,1152]{1,0:T(8,128)(2,1)S(1)}, bf16[520,128]{1,0:T(8,128)(2,1)}) custom-call(bf16[512,1024]{1,0:T(8,128)(2,1)S(1)} %copy-done, bf16[512,128]{1,0:T(8,128)(2,1)S(1)} %copy-done.1, s32[4,56]{1,0:T(4,128)S(1)} %copy-done.2), custom_call_target="tpu_custom_call" | custom-call | flops 1 | bytes 1 | tf_op jit(solution)/shard_map/pallas_call | solution.py:18
  10.1 1.5 %collective-permute-start = (bf16[256,1152]{1,0:T(8,128)(2,1)S(1)}, bf16[256,1152]{1,0:T(8,128)(2,1)}, u32[]{:S(2)}, u32[]{:S(2)}) collective-permute-start(bf16[256,1152]{1,0:T(8,128)(2,1)S(1)} %get-tuple-element.25.last), channel_id=1, source_target_pairs={{0,2},{2,0},{4,6},{6,4},{8,10},{10,8},{12,14},{14,12},{1,3},{3,1},... | collective-permute-start | bytes 1769480 | tf_op jit(solution)/shard_map/ppermute | solution.py:286
  12.8 2.1 %shard_map.60.self_image = f32[512,128]{1,0:T(8,128)S(1)} custom-call(f32[1]{0:T(128)S(6)} %copy.6.inverse, s32[1]{0:T(128)} %bitcast.sub, bf16[264,1152]{1,0:T(8,128)(2,1)S(1)} %get-tuple-element.26.first, bf16[256,1152]{1,0:T(8,128)(2,1)S(1)} %get-tuple-element.25.last, bf16[264,1152]{1,0:T(8,128)(2,1)S(1)} %collective-permute-done.1.other_first, ...), custom_call_target="tpu_custom_call" | custom-call | flops 1 | bytes 1 | tf_op jit(solution)/shard_map/pallas_call | solution.py:18
  14.8 10.6 %collective-permute-done = bf16[256,1152]{1,0:T(8,128)(2,1)} collective-permute-done((bf16[256,1152]{1,0:T(8,128)(2,1)S(1)}, bf16[256,1152]{1,0:T(8,128)(2,1)}, u32[]{:S(2)}, u32[]{:S(2)}) %collective-permute-start) | collective-permute-done | bytes 589856 | tf_op jit(solution)/shard_map/ppermute | solution.py:286
  25.5 1.9 %collective-permute-start.6 = (bf16[256,1152]{1,0:T(8,128)(2,1)}, bf16[256,1152]{1,0:T(8,128)(2,1)S(1)}, u32[]{:S(2)}, u32[]{:S(2)}) collective-permute-start(bf16[256,1152]{1,0:T(8,128)(2,1)} %collective-permute-done), channel_id=1, source_target_pairs={{0,4},{2,2},{4,8},{6,6},{8,12},{10,10},{12,0},{14,14},{1,5},{3,3},... | collective-permute-start | bytes 1769480 | tf_op jit(solution)/shard_map/ppermute | solution.py:286
  27.4 1.3 %collective-permute-start.3 = (bf16[264,1152]{1,0:T(8,128)(2,1)S(1)}, bf16[264,1152]{1,0:T(8,128)(2,1)S(1)}, u32[]{:S(2)}, u32[]{:S(2)}) collective-permute-start(bf16[264,1152]{1,0:T(8,128)(2,1)S(1)} %get-tuple-element.26.first), channel_id=1, source_target_pairs={{0,2},{2,4},{4,6},{6,8},{8,10},{10,12},{12,14},{14,0},{1,3},{3,5},... | collective-permute-start | bytes 1824776 | tf_op jit(solution)/shard_map/ppermute | solution.py:286
  28.7 3.8 %collective-permute-done.5.panel = bf16[520,128]{1,0:T(8,128)(2,1)} collective-permute-done((bf16[520,128]{1,0:T(8,128)(2,1)}, bf16[520,128]{1,0:T(8,128)(2,1)}, u32[]{:S(2)}, u32[]{:S(2)}) %collective-permute-start.5) | collective-permute-done | bytes 133152 | tf_op jit(solution)/shard_map/ppermute | solution.py:286
  32.5 3.2 %shard_map.61 = (f32[512,128]{1,0:T(8,128)S(1)}, f32[128,1024]{1,0:T(8,128)S(1)}, f32[512,128]{1,0:T(8,128)S(1)}) custom-call(f32[1]{0:T(128)S(6)} %copy.6.inverse, s32[1]{0:T(128)} %bitcast.sub, bf16[512,1024]{1,0:T(8,128)(2,1)S(1)} %collective-permute-done.4.above, bf16[520,128]{1,0:T(8,128)(2,1)} %collective-permute-done.5.panel, ...), custom_call_target="tpu_custom_call" | custom-call | flops 99999997952 | bytes 1 | tf_op jit(solution)/shard_map/pallas_call | solution.py:18
  35.7 9.1 %collective-permute-done.6.below1.below = bf16[256,1152]{1,0:T(8,128)(2,1)S(1)} collective-permute-done((bf16[256,1152]{1,0:T(8,128)(2,1)}, bf16[256,1152]{1,0:T(8,128)(2,1)S(1)}, u32[]{:S(2)}, u32[]{:S(2)}) %collective-permute-start.6) | collective-permute-done | bytes 589856 | tf_op jit(solution)/shard_map/ppermute | solution.py:286
  44.8 1.3 %collective-permute-done.3.below.below0.marked = bf16[264,1152]{1,0:T(8,128)(2,1)S(1)} collective-permute-done((bf16[264,1152]{1,0:T(8,128)(2,1)S(1)}, bf16[264,1152]{1,0:T(8,128)(2,1)S(1)}, u32[]{:S(2)}, u32[]{:S(2)}) %collective-permute-start.3) | collective-permute-done | bytes 608288 | tf_op jit(solution)/shard_map/ppermute | solution.py:286
  46.1 0.5 collective-permute-start.7
  46.6 1.3 %shard_map.62 = (f32[256,128]{1,0:T(8,128)S(1)}, f32[128,1024]{1,0:T(8,128)S(1)}) custom-call(f32[1]{0:T(128)S(6)} %copy.6.inverse, s32[1]{0:T(128)} %bitcast.sub, bf16[264,1152]{1,0:T(8,128)(2,1)S(1)} %collective-permute-done.3.below.below0.marked, bf16[264,1152]{1,0:T(8,128)(2,1)S(1)} %get-tuple-element.26.first, ...), custom_call_target="tpu_custom_call" | custom-call | flops 99999997952 | bytes 1 | tf_op jit(solution)/shard_map/pallas_call | solution.py:18
  48.1 0.9 collective-permute-done.7.other0
  49.0 3.3 %shard_map.63 = (f32[512,128]{1,0:T(8,128)S(1)}, f32[512,128]{1,0:T(8,128)S(1)}, f32[512,128]{1,0:T(8,128)S(1)}) custom-call(f32[1]{0:T(128)S(6)} %copy.6.inverse, s32[1]{0:T(128)} %bitcast.sub, bf16[512,1024]{1,0:T(8,128)(2,1)S(1)} %collective-permute-done.4.above, bf16[520,128]{1,0:T(8,128)(2,1)} %collective-permute-done.5.panel, ...), custom_call_target="tpu_custom_call" | custom-call | flops 99999997952 | bytes 1 | tf_op jit(solution)/shard_map/pallas_call | solution.py:18
  52.2 1.7 %collective-permute-start.12 = (f32[512,128]{1,0:T(8,128)S(1)}, f32[512,128]{1,0:T(8,128)S(1)}, u32[]{:S(2)}, u32[]{:S(2)}) collective-permute-start(f32[512,128]{1,0:T(8,128)S(1)} %get-tuple-element.37), channel_id=1, source_target_pairs={{0,4},{2,6},{4,8},{6,10},{8,12},{10,14},{12,0},{14,2},{1,5},{3,7},... | collective-permute-start | bytes 786440 | tf_op jit(solution)/shard_map/ppermute | solution.py:286
  53.9 1.5 %shard_map.64 = (f32[256,128]{1,0:T(8,128)S(1)}, f32[512,128]{1,0:T(8,128)S(1)}, f32[512,128]{1,0:T(8,128)S(1)}) custom-call(f32[1]{0:T(128)S(6)} %copy.6.inverse, s32[1]{0:T(128)} %bitcast.sub, bf16[264,1152]{1,0:T(8,128)(2,1)S(1)} %collective-permute-done.3.below.below0.marked, bf16[256,1152]{1,0:T(8,128)(2,1)S(1)} %collective-permute-done.6.below1.below, ...), custom_call_target="tpu_custom_call" | custom-call | flops 99999997952 | bytes 1 | tf_op jit(solution)/shard_map/pallas_call | solution.py:18
  55.4 0.6 collective-permute-start.9
  56.0 1.6 %collective-permute-start.11 = (f32[512,128]{1,0:T(8,128)S(1)}, f32[512,128]{1,0:T(8,128)S(1)}, u32[]{:S(2)}, u32[]{:S(2)}) collective-permute-start(f32[512,128]{1,0:T(8,128)S(1)} %maximum_add_fusion), channel_id=1, source_target_pairs={{0,14},{2,0},{4,2},{6,4},{8,6},{10,8},{12,10},{14,12},{1,15},{3,1}... | collective-permute-start | bytes 786440 | tf_op jit(solution)/shard_map/ppermute | solution.py:286
  57.6 5.7 %collective-permute-done.12.above = f32[512,128]{1,0:T(8,128)S(1)} collective-permute-done((f32[512,128]{1,0:T(8,128)S(1)}, f32[512,128]{1,0:T(8,128)S(1)}, u32[]{:S(2)}, u32[]{:S(2)}) %collective-permute-start.12) | collective-permute-done | bytes 262176 | tf_op jit(solution)/shard_map/ppermute | solution.py:286
  63.3 2.1 %collective-permute-done.11.below = f32[512,128]{1,0:T(8,128)S(1)} collective-permute-done((f32[512,128]{1,0:T(8,128)S(1)}, f32[512,128]{1,0:T(8,128)S(1)}, u32[]{:S(2)}, u32[]{:S(2)}) %collective-permute-start.11) | collective-permute-done | bytes 262176 | tf_op jit(solution)/shard_map/ppermute | solution.py:286
  65.9 1.2 %collective-permute-done.13 = f32[128,128]{1,0:T(8,128)S(1)} collective-permute-done((f32[128,128]{1,0:T(8,128)S(1)}, f32[128,128]{1,0:T(8,128)S(1)}, u32[]{:S(2)}, u32[]{:S(2)}) %collective-permute-start.13) | collective-permute-done | bytes 65568 | tf_op jit(solution)/shard_map/ppermute | solution.py:285
  67.2 4.2 %collective-permute-start.14 = (f32[128,128]{1,0:T(8,128)S(1)}, f32[128,128]{1,0:T(8,128)S(1)}, u32[]{:S(2)}, u32[]{:S(2)}) collective-permute-start(f32[128,128]{1,0:T(8,128)S(1)} %add.20), channel_id=1, source_target_pairs={{0,2},{2,0},{4,6},{6,4},{8,10},{10,8},{12,14},{14,12},{1,3},{3,1},... | collective-permute-start | bytes 196616 | tf_op jit(solution)/shard_map/ppermute | solution.py:286
  71.3 2.4 %collective-permute-done.14 = f32[128,128]{1,0:T(8,128)S(1)} collective-permute-done((f32[128,128]{1,0:T(8,128)S(1)}, f32[128,128]{1,0:T(8,128)S(1)}, u32[]{:S(2)}, u32[]{:S(2)}) %collective-permute-start.14) | collective-permute-done | bytes 65568 | tf_op jit(solution)/shard_map/ppermute | solution.py:286
  73.8 0.6 collective-permute-start.15
  74.4 3.7 %collective-permute-done.15 = f32[128,128]{1,0:T(8,128)S(1)} collective-permute-done((f32[128,128]{1,0:T(8,128)S(1)}, f32[128,128]{1,0:T(8,128)S(1)}, u32[]{:S(2)}, u32[]{:S(2)}) %collective-permute-start.15) | collective-permute-done | bytes 65568 | tf_op jit(solution)/shard_map/ppermute | solution.py:286
  78.1 0.7 collective-permute-start.16
  78.8 5.3 %collective-permute-done.16 = f32[128,128]{1,0:T(8,128)S(1)} collective-permute-done((f32[128,128]{1,0:T(8,128)S(1)}, f32[128,128]{1,0:T(8,128)S(1)}, u32[]{:S(2)}, u32[]{:S(2)}) %collective-permute-start.16) | collective-permute-done | bytes 65568 | tf_op jit(solution)/shard_map/ppermute | solution.py:286
  84.1 5.2 %shard_map.66 = (f32[512,128]{1,0:T(8,128)}, f32[128,128]{1,0:T(8,128)}) custom-call(f32[512,128]{1,0:T(8,128)S(1)} %get-tuple-element.44.image, f32[128,128]{1,0:T(8,128)S(1)} %add.23.gram), custom_call_target="tpu_custom_call" | custom-call | flops 99999997952 | bytes 1 | tf_op jit(solution)/shard_map/pallas_call | solution.py:18
  (21 shorter events, 1.7 us)
Async XLA Ops:
  0.6 31.9 %collective-permute-start.4 = (bf16[512,1024]{1,0:T(8,128)(2,1)}, bf16[512,1024]{1,0:T(8,128)(2,1)S(1)}, u32[]{:S(2)}, u32[]{:S(2)}) collective-permute-start(bf16[512,1024]{1,0:T(8,128)(2,1)} %embeddings.1), channel_id=1, source_target_pairs={{0,12},{2,14},{4,0},{6,2},{8,4},{10,6},{12,8},{14,10},{1,13},{3,15... | collective-permute-start | bytes 3145736 | tf_op jit(solution)/shard_map/ppermute | solution.py:286
  5.7 1.3 %copy-start = (bf16[512,1024]{1,0:T(8,128)(2,1)S(1)}, bf16[512,1024]{1,0:T(8,128)(2,1)}, u32[]{:S(2)}) copy-start(bf16[512,1024]{1,0:T(8,128)(2,1)} %embeddings.1) | copy-start | bytes 3145732
  7.0 0.9 %copy-start.1 = (bf16[512,128]{1,0:T(8,128)(2,1)S(1)}, bf16[512,128]{1,0:T(8,128)(2,1)}, u32[]{:S(2)}) copy-start(bf16[512,128]{1,0:T(8,128)(2,1)} %panel.1) | copy-start | bytes 393220
  7.9 0.7 copy-start.2
  9.6 3.1 %collective-permute-start.1 = (bf16[264,1152]{1,0:T(8,128)(2,1)S(1)}, bf16[264,1152]{1,0:T(8,128)(2,1)S(1)}, u32[]{:S(2)}, u32[]{:S(2)}) collective-permute-start(bf16[264,1152]{1,0:T(8,128)(2,1)S(1)} %get-tuple-element.26.first), channel_id=1, source_target_pairs={{0,1},{1,0},{2,3},{3,2},{4,5},{5,4},{6,7},{7,6},{8,9},{9,8},{10,11... | collective-permute-start | bytes 1824776 | tf_op jit(solution)/shard_map/ppermute | solution.py:285
  9.6 3.1 %collective-permute-start.2 = (bf16[256,1152]{1,0:T(8,128)(2,1)S(1)}, bf16[256,1152]{1,0:T(8,128)(2,1)S(1)}, u32[]{:S(2)}, u32[]{:S(2)}) collective-permute-start(bf16[256,1152]{1,0:T(8,128)(2,1)S(1)} %get-tuple-element.25.last), channel_id=1, source_target_pairs={{0,1},{1,0},{2,3},{3,2},{4,5},{5,4},{6,7},{7,6},{8,9},{9,8},{10,11... | collective-permute-start | bytes 1769480 | tf_op jit(solution)/shard_map/ppermute | solution.py:285
  10.1 15.3 %collective-permute-start = (bf16[256,1152]{1,0:T(8,128)(2,1)S(1)}, bf16[256,1152]{1,0:T(8,128)(2,1)}, u32[]{:S(2)}, u32[]{:S(2)}) collective-permute-start(bf16[256,1152]{1,0:T(8,128)(2,1)S(1)} %get-tuple-element.25.last), channel_id=1, source_target_pairs={{0,2},{2,0},{4,6},{6,4},{8,10},{10,8},{12,14},{14,12},{1,3},{3,1},... | collective-permute-start | bytes 1769480 | tf_op jit(solution)/shard_map/ppermute | solution.py:286
  11.6 20.9 %collective-permute-start.5 = (bf16[520,128]{1,0:T(8,128)(2,1)}, bf16[520,128]{1,0:T(8,128)(2,1)}, u32[]{:S(2)}, u32[]{:S(2)}) collective-permute-start(bf16[520,128]{1,0:T(8,128)(2,1)} %get-tuple-element.27), channel_id=1, source_target_pairs={{0,12},{2,14},{4,0},{6,2},{8,4},{10,6},{12,8},{14,10},{1,13},{3,15... | collective-permute-start | bytes 399368 | tf_op jit(solution)/shard_map/ppermute | solution.py:286
  25.5 19.3 %collective-permute-start.6 = (bf16[256,1152]{1,0:T(8,128)(2,1)}, bf16[256,1152]{1,0:T(8,128)(2,1)S(1)}, u32[]{:S(2)}, u32[]{:S(2)}) collective-permute-start(bf16[256,1152]{1,0:T(8,128)(2,1)} %collective-permute-done), channel_id=1, source_target_pairs={{0,4},{2,2},{4,8},{6,6},{8,12},{10,10},{12,0},{14,14},{1,5},{3,3},... | collective-permute-start | bytes 1769480 | tf_op jit(solution)/shard_map/ppermute | solution.py:286
  27.4 18.7 %collective-permute-start.3 = (bf16[264,1152]{1,0:T(8,128)(2,1)S(1)}, bf16[264,1152]{1,0:T(8,128)(2,1)S(1)}, u32[]{:S(2)}, u32[]{:S(2)}) collective-permute-start(bf16[264,1152]{1,0:T(8,128)(2,1)S(1)} %get-tuple-element.26.first), channel_id=1, source_target_pairs={{0,2},{2,4},{4,6},{6,8},{8,10},{10,12},{12,14},{14,0},{1,3},{3,5},... | collective-permute-start | bytes 1824776 | tf_op jit(solution)/shard_map/ppermute | solution.py:286
  46.1 2.0 %collective-permute-start.8 = (bf16[256,1152]{1,0:T(8,128)(2,1)S(1)}, bf16[256,1152]{1,0:T(8,128)(2,1)S(1)}, u32[]{:S(2)}, u32[]{:S(2)}) collective-permute-start(bf16[256,1152]{1,0:T(8,128)(2,1)S(1)} %collective-permute-done.6.below1.below), channel_id=1, source_target_pairs={{0,1},{1,0},{2,3},{3,2},{4,5},{5,4},{6,7},{7,6},{8,9},{9,8},{10,11... | collective-permute-start | bytes 1769480 | tf_op jit(solution)/shard_map/ppermute | solution.py:285
  46.1 2.9 %collective-permute-start.7 = (bf16[264,1152]{1,0:T(8,128)(2,1)S(1)}, bf16[264,1152]{1,0:T(8,128)(2,1)S(1)}, u32[]{:S(2)}, u32[]{:S(2)}) collective-permute-start(bf16[264,1152]{1,0:T(8,128)(2,1)S(1)} %collective-permute-done.3.below.below0.marked), channel_id=1, source_target_pairs={{0,1},{1,0},{2,3},{3,2},{4,5},{5,4},{6,7},{7,6},{8,9},{9,8},{10,11... | collective-permute-start | bytes 1824776 | tf_op jit(solution)/shard_map/ppermute | solution.py:285
  52.2 11.0 %collective-permute-start.12 = (f32[512,128]{1,0:T(8,128)S(1)}, f32[512,128]{1,0:T(8,128)S(1)}, u32[]{:S(2)}, u32[]{:S(2)}) collective-permute-start(f32[512,128]{1,0:T(8,128)S(1)} %get-tuple-element.37), channel_id=1, source_target_pairs={{0,4},{2,6},{4,8},{6,10},{8,12},{10,14},{12,0},{14,2},{1,5},{3,7},... | collective-permute-start | bytes 786440 | tf_op jit(solution)/shard_map/ppermute | solution.py:286
  53.9 2.1 %collective-permute-start.10 = (f32[512,128]{1,0:T(8,128)S(1)}, f32[512,128]{1,0:T(8,128)S(1)}, u32[]{:S(2)}, u32[]{:S(2)}) collective-permute-start(f32[512,128]{1,0:T(8,128)S(1)} %get-tuple-element.42), channel_id=1, source_target_pairs={{0,1},{1,0},{2,3},{3,2},{4,5},{5,4},{6,7},{7,6},{8,9},{9,8},{10,11... | collective-permute-start | bytes 786440 | tf_op jit(solution)/shard_map/ppermute | solution.py:285
  55.4 2.2 %collective-permute-start.9 = (f32[512,128]{1,0:T(8,128)S(1)}, f32[512,128]{1,0:T(8,128)S(1)}, u32[]{:S(2)}, u32[]{:S(2)}) collective-permute-start(f32[512,128]{1,0:T(8,128)S(1)} %get-tuple-element.40), channel_id=1, source_target_pairs={{0,1},{1,0},{2,3},{3,2},{4,5},{5,4},{6,7},{7,6},{8,9},{9,8},{10,11... | collective-permute-start | bytes 786440 | tf_op jit(solution)/shard_map/ppermute | solution.py:285
  56.0 9.4 %collective-permute-start.11 = (f32[512,128]{1,0:T(8,128)S(1)}, f32[512,128]{1,0:T(8,128)S(1)}, u32[]{:S(2)}, u32[]{:S(2)}) collective-permute-start(f32[512,128]{1,0:T(8,128)S(1)} %maximum_add_fusion), channel_id=1, source_target_pairs={{0,14},{2,0},{4,2},{6,4},{8,6},{10,8},{12,10},{14,12},{1,15},{3,1}... | collective-permute-start | bytes 786440 | tf_op jit(solution)/shard_map/ppermute | solution.py:286
  65.8 1.3 %collective-permute-start.13 = (f32[128,128]{1,0:T(8,128)S(1)}, f32[128,128]{1,0:T(8,128)S(1)}, u32[]{:S(2)}, u32[]{:S(2)}) collective-permute-start(f32[128,128]{1,0:T(8,128)S(1)} %get-tuple-element.45), channel_id=1, source_target_pairs={{0,1},{1,0},{2,3},{3,2},{4,5},{5,4},{6,7},{7,6},{8,9},{9,8},{10,11... | collective-permute-start | bytes 196616 | tf_op jit(solution)/shard_map/ppermute | solution.py:285
  67.2 6.6 %collective-permute-start.14 = (f32[128,128]{1,0:T(8,128)S(1)}, f32[128,128]{1,0:T(8,128)S(1)}, u32[]{:S(2)}, u32[]{:S(2)}) collective-permute-start(f32[128,128]{1,0:T(8,128)S(1)} %add.20), channel_id=1, source_target_pairs={{0,2},{2,0},{4,6},{6,4},{8,10},{10,8},{12,14},{14,12},{1,3},{3,1},... | collective-permute-start | bytes 196616 | tf_op jit(solution)/shard_map/ppermute | solution.py:286
  73.8 4.3 %collective-permute-start.15 = (f32[128,128]{1,0:T(8,128)S(1)}, f32[128,128]{1,0:T(8,128)S(1)}, u32[]{:S(2)}, u32[]{:S(2)}) collective-permute-start(f32[128,128]{1,0:T(8,128)S(1)} %add.21), channel_id=1, source_target_pairs={{0,4},{2,6},{4,0},{6,2},{8,12},{10,14},{12,8},{14,10},{1,5},{3,7},... | collective-permute-start | bytes 196616 | tf_op jit(solution)/shard_map/ppermute | solution.py:286
  78.1 5.9 %collective-permute-start.16 = (f32[128,128]{1,0:T(8,128)S(1)}, f32[128,128]{1,0:T(8,128)S(1)}, u32[]{:S(2)}, u32[]{:S(2)}) collective-permute-start(f32[128,128]{1,0:T(8,128)S(1)} %add.22), channel_id=1, source_target_pairs={{0,8},{2,10},{4,12},{6,14},{8,0},{10,2},{12,4},{14,6},{1,9},{3,11}... | collective-permute-start | bytes 196616 | tf_op jit(solution)/shard_map/ppermute | solution.py:286

commit v12 on v11

--- a/solution.py
+++ b/solution.py
@@ -148,17 +148,21 @@
     panel_mark[half:] = mask
 
 
+def place(numbers):
+    return jnp.where(numbers[1] > 0.5, 1, 0)
+
+
 def masks_of(sub, rows, others, offset):
     return [pair_mask(sub, rows, r, offset, h) for h, r in enumerate(others)]
 
 
-def self_body(inverse, sub, first, last, other_first, other_last, image):
+def self_body(numbers, first, last, other_first, other_last, image):
     half = 2 * last.shape[0]
     own, other = pieces(first, last), pieces(other_first, other_last)
     rows = square_rows(first)
     both = [marks(r, half) for r in (first, other_first)]
-    columns = columns_of(own, other, rows + square_rows(other_first), masks_of(sub[0], both[0], both, OWN))
-    image[...], _ = products(inverse[0], own, [as_column(r) for r in rows], columns, None)
+    columns = columns_of(own, other, rows + square_rows(other_first), masks_of(place(numbers), both[0], both, OWN))
+    image[...], _ = products(numbers[0], own, [as_column(r) for r in rows], columns, None)
 
 
 def own_columns(sub, mark, first, last, other_first, other_last, offset):
@@ -168,41 +172,42 @@
     return columns_of(pieces(first, last), pieces(other_first, other_last), rows, masks)
 
 
-def above_own_body(inverse, sub, above, panel, first, last, other_first, other_last, image, back, above_sq):
+def above_own_body(numbers, above, panel, first, last, other_first, other_last, image, back, above_sq, kept_panel):
     half = above.shape[0]
     size = half // 2
-    columns = own_columns(sub[0], marks(panel, half), first, last, other_first, other_last, ABOVE)
+    columns = own_columns(place(numbers), marks(panel, half), first, last, other_first, other_last, ABOVE)
+    kept_panel[...] = panel[...]
     rows = apart(above, panel)
     columns_sq = [squares(features) for features, _ in rows]
     for k, column in enumerate(columns_sq):
         above_sq[k * size : (k + 1) * size] = jnp.broadcast_to(column, (size, TILE))
-    image[...], back[...] = products(inverse[0], rows, columns_sq, columns, jnp.zeros(back.shape, F32))
-
-
-def below_first_body(inverse, sub, below, first, last, other_first, other_last, back, image, total):
+    image[...], back[...] = products(numbers[0], rows, columns_sq, columns, jnp.zeros(back.shape, F32))
+
+
+def below_first_body(numbers, below, first, last, other_first, other_last, back, image, total):
     half = 2 * last.shape[0]
-    columns = own_columns(sub[0], marks(below, half), first, last, other_first, other_last, BELOW)
+    columns = own_columns(place(numbers), marks(below, half), first, last, other_first, other_last, BELOW)
     rows_sq = [as_column(square_rows(below)[0])]
-    image[...], total[...] = products(inverse[0], [pieces(below, last)[0]], rows_sq, columns, back[...])
+    image[...], total[...] = products(numbers[0], [pieces(below, last)[0]], rows_sq, columns, back[...])
 
 
 def below_last_body(
-    inverse, sub, marked, below, first, last, other_first, other_last, self_image, back, image, own_image, own_cross
+    numbers, marked, below, first, last, other_first, other_last, self_image, back, image, own_image, own_cross
 ):
     half = 2 * last.shape[0]
-    columns = own_columns(sub[0], marks(marked, half), first, last, other_first, other_last, BELOW)
+    columns = own_columns(place(numbers), marks(marked, half), first, last, other_first, other_last, BELOW)
     rows_sq = [as_column(square_rows(marked)[1])]
-    image[...], total = products(inverse[0], pieces(below), rows_sq, columns, back[...], 1)
+    image[...], total = products(numbers[0], pieces(below), rows_sq, columns, back[...], 1)
     own_image[...] = self_image[...] + total[:, :half].T
     own_cross[...] = total[:, half:].T
 
 
-def above_below_body(inverse, sub, above, panel, above_sq, below0, below1, other0, other1, above_image, image, below_image, cross):
+def above_below_body(numbers, above, panel, above_sq, below0, below1, other0, other1, above_image, image, below_image, cross):
     half = image.shape[0]
     size = half // 2
-    columns = own_columns(sub[0], marks(panel, half), below0, below1, other0, other1, ABOVE - BELOW)
+    columns = own_columns(place(numbers), marks(panel, half), below0, below1, other0, other1, ABOVE - BELOW)
     rows_sq = [above_sq[k * size : (k + 1) * size, :1] for k in range(2)]
-    products_image, total = products(inverse[0], apart(above, panel), rows_sq, columns, jnp.zeros((TILE, 2 * half), F32))
+    products_image, total = products(numbers[0], apart(above, panel), rows_sq, columns, jnp.zeros((TILE, 2 * half), F32))
     image[...] = above_image[...] + products_image
     below_image[...] = total[:, :half].T
     cross[...] = total[:, half:].T
@@ -287,7 +292,7 @@
     blk_move = lambda v, by: blk_route(v, lambda i: i + by)
 
     after = lambda v, *earlier: lax.optimization_barrier((v, *earlier))[0]
-    sub = lax.axis_index("sub").astype(jnp.int32).reshape(1)
+    numbers = jnp.concatenate([inv_width, lax.axis_index("sub").astype(F32).reshape(1)])
     wide = embeddings.shape[1] + width
     packed = lambda rows, lanes: jax.ShapeDtypeStruct((rows, lanes), BF16)
     above = blk_move(embeddings, -2)
@@ -304,23 +309,28 @@
     above_panel = blk_move(panel_mark, -2)
     own = (first, last, sub_move(first), sub_move(last))
     image, turned = shape(half, width), shape(width, 2 * half)
-    self_image = vmem_call(self_body, image, inv_width, sub, *own, scalars=2, long=False)
+    self_image = vmem_call(self_body, image, numbers, *own, scalars=1, long=False)
     below0 = blk_move(after(first, swapped, self_image), 1)
     swapped = after(swapped, self_image)
     below1 = blk_route(swapped, lambda i: i if i & 1 else i + 2) if relayed else blk_move(swapped, 1)
-    above_image, back, above_sq = vmem_call(
-        above_own_body, (image, turned, image), inv_width, sub, above, above_panel, *own, scalars=2
+    above_image, back, above_sq, above_panel = vmem_call(
+        above_own_body,
+        (image, turned, image, packed(half + MARK, width)),
+        numbers,
+        above,
+        above_panel,
+        *own,
+        scalars=1,
     )
     below0, below1 = after(below0, above_image, below1), after(below1, above_image, below0)
     below_other = (sub_move(below0), sub_move(below1))
     below_image0, back = vmem_call(
-        below_first_body, (shape(size, width), turned), inv_width, sub, below0, *own, back, scalars=2
+        below_first_body, (shape(size, width), turned), numbers, below0, *own, back, scalars=1
     )
     above_image, below_sum, below_cross = vmem_call(
         above_below_body,
         (image,) * 3,
-        inv_width,
-        sub,
+        numbers,
         above,
         above_panel,
         above_sq,
@@ -328,19 +338,18 @@
         below1,
         *below_other,
         after(above_image, below_image0),
-        scalars=2,
+        scalars=1,
     )
     below_image1, own_image, own_cross = vmem_call(
         below_last_body,
         (shape(size, width), image, image),
-        inv_width,
-        sub,
+        numbers,
         below0,
         below1,
         *own,
         self_image,
         after(back, above_image),
-        scalars=2,
+        scalars=1,
     )
     above_image = blk_move(above_image, 2)
     below_image = jnp.concatenate([below_image0, below_image1], axis=0)

time: 89.5 us -> 89.1 us (level)
  waiting for transfers between devices: 46.3 us -> 44.6 us
  Pallas kernels: 18 us -> 19.2 us
    pallas_call x8, Pallas kernels: 18 us -> 19.2 us  [vmem_call(): pl.pallas_call(body, out_shape=out_shapes, in_specs=[in_smem] * scalars +...]
    ppermute x10, waiting for transfers between devices: 44 us -> 42.9 us  [per_device(): lax.ppermute(v, 'blk', [(i, to(i) % n_blk) for i in range(n_blk)])]
  transfers between devices with their start and end apart: 17 -> 17, of which waited for: 12 -> 11; matrix products, arithmetic and copies ran while one was open for 0% -> 0% of each run, Pallas kernels for 10% -> 12%
where the time goes in v12:
time: 89.1 us; the launch traced here: 88.8 us
  waiting for transfers between devices  44.6 us (50%)
  starting transfers between devices  20.6 us (23%)
  Pallas kernels  19.2 us (22%)
  local copies, waits for them, and re-layouts  2.84 us (3%)
  between operations  1.38 us (2%)
    ppermute x10, waiting for transfers between devices, per_device(): lax.ppermute(v, 'blk', [(i, to(i) % n_blk) for i in range(n_blk)])  42.9 us
    pallas_call x8, Pallas kernels, vmem_call(): pl.pallas_call(body, out_shape=out_shapes, in_specs=[in_smem] * scalars +...  19.2 us
    ppermute x10, starting transfers between devices, per_device(): lax.ppermute(v, 'blk', [(i, to(i) % n_blk) for i in range(n_blk)])  18.9 us
    unnamed x6, local copies, waits for them, and re-layouts  2.84 us
  transfers between devices with their start and end apart: 17, of which 11 were waited for; matrix products, arithmetic and copies ran while one was open for 0% of the time, Pallas kernels for 12%

profile of v12, /device:TPU:0, one launch (start us, length us, event | category | flops | bytes accessed | tf_op | source)
XLA Modules:
  0.0 88.8 jit_solution(16624142638971922540)
XLA Ops:
  0.6 5.1 %collective-permute-start.4 = (bf16[512,1024]{1,0:T(8,128)(2,1)}, bf16[512,1024]{1,0:T(8,128)(2,1)S(1)}, u32[]{:S(2)}, u32[]{:S(2)}) collective-permute-start(bf16[512,1024]{1,0:T(8,128)(2,1)} %embeddings.1), channel_id=1, source_target_pairs={{0,12},{2,14},{4,0},{6,2},{8,4},{10,6},{12,8},{14,10},{1,13},{3,15... | collective-permute-start | bytes 3145736 | tf_op jit(solution)/shard_map/ppermute | solution.py:291
  5.7 1.3 %copy-done = bf16[512,1024]{1,0:T(8,128)(2,1)S(1)} copy-done((bf16[512,1024]{1,0:T(8,128)(2,1)S(1)}, bf16[512,1024]{1,0:T(8,128)(2,1)}, u32[]{:S(2)}) %copy-start) | copy-done | bytes 1048600
  7.0 0.9 %copy-done.1 = bf16[512,128]{1,0:T(8,128)(2,1)S(1)} copy-done((bf16[512,128]{1,0:T(8,128)(2,1)S(1)}, bf16[512,128]{1,0:T(8,128)(2,1)}, u32[]{:S(2)}) %copy-start.1) | copy-done | bytes 131096
  7.9 0.7 copy-done.2
  8.6 1.1 %shard_map.59 = (bf16[264,1152]{1,0:T(8,128)(2,1)S(1)}, bf16[256,1152]{1,0:T(8,128)(2,1)S(1)}, bf16[520,128]{1,0:T(8,128)(2,1)}) custom-call(bf16[512,1024]{1,0:T(8,128)(2,1)S(1)} %copy-done, bf16[512,128]{1,0:T(8,128)(2,1)S(1)} %copy-done.1, s32[4,56]{1,0:T(4,128)S(1)} %copy-done.2), custom_call_target="tpu_custom_call" | custom-call | flops 1 | bytes 1 | tf_op jit(solution)/shard_map/pallas_call | solution.py:18
  9.6 0.5 collective-permute-start.2
  10.1 1.5 %collective-permute-start = (bf16[256,1152]{1,0:T(8,128)(2,1)S(1)}, bf16[256,1152]{1,0:T(8,128)(2,1)}, u32[]{:S(2)}, u32[]{:S(2)}) collective-permute-start(bf16[256,1152]{1,0:T(8,128)(2,1)S(1)} %get-tuple-element.26.last), channel_id=1, source_target_pairs={{0,2},{2,0},{4,6},{6,4},{8,10},{10,8},{12,14},{14,12},{1,3},{3,1},... | collective-permute-start | bytes 1769480 | tf_op jit(solution)/shard_map/ppermute | solution.py:291
  12.8 2.6 %shard_map.60.self_image = f32[512,128]{1,0:T(8,128)S(1)} custom-call(f32[2]{0:T(128)S(1)} %pad_maximum_fusion.numbers, bf16[264,1152]{1,0:T(8,128)(2,1)S(1)} %get-tuple-element.27.first, bf16[256,1152]{1,0:T(8,128)(2,1)S(1)} %get-tuple-element.26.last, bf16[264,1152]{1,0:T(8,128)(2,1)S(1)} %collective-permute-done.1.other_first, ...), custom_call_target="tpu_custom_call" | custom-call | flops 1 | bytes 1 | tf_op jit(solution)/shard_map/pallas_call | solution.py:18
  15.4 10.0 %collective-permute-done = bf16[256,1152]{1,0:T(8,128)(2,1)} collective-permute-done((bf16[256,1152]{1,0:T(8,128)(2,1)S(1)}, bf16[256,1152]{1,0:T(8,128)(2,1)}, u32[]{:S(2)}, u32[]{:S(2)}) %collective-permute-start) | collective-permute-done | bytes 589856 | tf_op jit(solution)/shard_map/ppermute | solution.py:291
  25.5 1.9 %collective-permute-start.6 = (bf16[256,1152]{1,0:T(8,128)(2,1)}, bf16[256,1152]{1,0:T(8,128)(2,1)S(1)}, u32[]{:S(2)}, u32[]{:S(2)}) collective-permute-start(bf16[256,1152]{1,0:T(8,128)(2,1)} %collective-permute-done), channel_id=1, source_target_pairs={{0,4},{2,2},{4,8},{6,6},{8,12},{10,10},{12,0},{14,14},{1,5},{3,3},... | collective-permute-start | bytes 1769480 | tf_op jit(solution)/shard_map/ppermute | solution.py:291
  27.4 1.3 %collective-permute-start.3 = (bf16[264,1152]{1,0:T(8,128)(2,1)S(1)}, bf16[264,1152]{1,0:T(8,128)(2,1)S(1)}, u32[]{:S(2)}, u32[]{:S(2)}) collective-permute-start(bf16[264,1152]{1,0:T(8,128)(2,1)S(1)} %get-tuple-element.27.first), channel_id=1, source_target_pairs={{0,2},{2,4},{4,6},{6,8},{8,10},{10,12},{12,14},{14,0},{1,3},{3,5},... | collective-permute-start | bytes 1824776 | tf_op jit(solution)/shard_map/ppermute | solution.py:291
  28.7 3.8 %collective-permute-done.5.panel = bf16[520,128]{1,0:T(8,128)(2,1)} collective-permute-done((bf16[520,128]{1,0:T(8,128)(2,1)}, bf16[520,128]{1,0:T(8,128)(2,1)}, u32[]{:S(2)}, u32[]{:S(2)}) %collective-permute-start.5) | collective-permute-done | bytes 133152 | tf_op jit(solution)/shard_map/ppermute | solution.py:291
  32.5 3.2 %shard_map.61 = (f32[512,128]{1,0:T(8,128)S(1)}, f32[128,1024]{1,0:T(8,128)S(1)}, f32[512,128]{1,0:T(8,128)S(1)}, bf16[520,128]{1,0:T(8,128)(2,1)S(1)}) custom-call(f32[2]{0:T(128)S(1)} %pad_maximum_fusion.numbers, bf16[512,1024]{1,0:T(8,128)(2,1)S(1)} %collective-permute-done.4.above, bf16[520,128]{1,0:T(8,128)(2,1)} %collective-permute-done.5.panel, ...), custom_call_target="tpu_custom_call" | custom-call | flops 99999997952 | bytes 1 | tf_op jit(solution)/shard_map/pallas_call | solution.py:18
  35.7 9.1 %collective-permute-done.6.below1.below = bf16[256,1152]{1,0:T(8,128)(2,1)S(1)} collective-permute-done((bf16[256,1152]{1,0:T(8,128)(2,1)}, bf16[256,1152]{1,0:T(8,128)(2,1)S(1)}, u32[]{:S(2)}, u32[]{:S(2)}) %collective-permute-start.6) | collective-permute-done | bytes 589856 | tf_op jit(solution)/shard_map/ppermute | solution.py:291
  44.8 1.3 %collective-permute-done.3.below.below0.marked = bf16[264,1152]{1,0:T(8,128)(2,1)S(1)} collective-permute-done((bf16[264,1152]{1,0:T(8,128)(2,1)S(1)}, bf16[264,1152]{1,0:T(8,128)(2,1)S(1)}, u32[]{:S(2)}, u32[]{:S(2)}) %collective-permute-start.3) | collective-permute-done | bytes 608288 | tf_op jit(solution)/shard_map/ppermute | solution.py:291
  46.1 0.5 collective-permute-start.7
  46.6 1.9 %shard_map.62 = (f32[256,128]{1,0:T(8,128)S(1)}, f32[128,1024]{1,0:T(8,128)S(1)}) custom-call(f32[2]{0:T(128)S(1)} %pad_maximum_fusion.numbers, bf16[264,1152]{1,0:T(8,128)(2,1)S(1)} %collective-permute-done.3.below.below0.marked, bf16[264,1152]{1,0:T(8,128)(2,1)S(1)} %get-tuple-element.27.first, bf16[256,1152]{1,0:T(8,128)(2,1)S(1)} %get-tuple-element.26.last, ...), custom_call_target="tpu_custom_call" | custom-call | flops 99999997952 | bytes 1 | tf_op jit(solution)/shard_map/pallas_call | solution.py:18
  49.0 2.9 %shard_map.63 = (f32[512,128]{1,0:T(8,128)S(1)}, f32[512,128]{1,0:T(8,128)S(1)}, f32[512,128]{1,0:T(8,128)S(1)}) custom-call(f32[2]{0:T(128)S(1)} %pad_maximum_fusion.numbers, bf16[512,1024]{1,0:T(8,128)(2,1)S(1)} %collective-permute-done.4.above, bf16[520,128]{1,0:T(8,128)(2,1)S(1)} %get-tuple-element.35.panel, f32[512,128]{1,0:T(8,128)S(1)} %get-tuple-element.36.above_sq, ...), custom_call_target="tpu_custom_call" | custom-call | flops 99999997952 | bytes 1 | tf_op jit(solution)/shard_map/pallas_call | solution.py:18
  51.9 1.7 %collective-permute-start.12 = (f32[512,128]{1,0:T(8,128)S(1)}, f32[512,128]{1,0:T(8,128)S(1)}, u32[]{:S(2)}, u32[]{:S(2)}) collective-permute-start(f32[512,128]{1,0:T(8,128)S(1)} %get-tuple-element.39), channel_id=1, source_target_pairs={{0,4},{2,6},{4,8},{6,10},{8,12},{10,14},{12,0},{14,2},{1,5},{3,7},... | collective-permute-start | bytes 786440 | tf_op jit(solution)/shard_map/ppermute | solution.py:291
  53.6 2.0 %shard_map.64 = (f32[256,128]{1,0:T(8,128)S(1)}, f32[512,128]{1,0:T(8,128)S(1)}, f32[512,128]{1,0:T(8,128)S(1)}) custom-call(f32[2]{0:T(128)S(1)} %pad_maximum_fusion.numbers, bf16[264,1152]{1,0:T(8,128)(2,1)S(1)} %collective-permute-done.3.below.below0.marked, bf16[256,1152]{1,0:T(8,128)(2,1)S(1)} %collective-permute-done.6.below1.below, ...), custom_call_target="tpu_custom_call" | custom-call | flops 99999997952 | bytes 1 | tf_op jit(solution)/shard_map/pallas_call | solution.py:18
  55.6 0.6 collective-permute-start.9
  56.2 1.6 %collective-permute-start.11 = (f32[512,128]{1,0:T(8,128)S(1)}, f32[512,128]{1,0:T(8,128)S(1)}, u32[]{:S(2)}, u32[]{:S(2)}) collective-permute-start(f32[512,128]{1,0:T(8,128)S(1)} %maximum_add_fusion), channel_id=1, source_target_pairs={{0,14},{2,0},{4,2},{6,4},{8,6},{10,8},{12,10},{14,12},{1,15},{3,1}... | collective-permute-start | bytes 786440 | tf_op jit(solution)/shard_map/ppermute | solution.py:291
  57.8 5.1 %collective-permute-done.12.above = f32[512,128]{1,0:T(8,128)S(1)} collective-permute-done((f32[512,128]{1,0:T(8,128)S(1)}, f32[512,128]{1,0:T(8,128)S(1)}, u32[]{:S(2)}, u32[]{:S(2)}) %collective-permute-start.12) | collective-permute-done | bytes 262176 | tf_op jit(solution)/shard_map/ppermute | solution.py:291
  62.9 2.2 %collective-permute-done.11.below = f32[512,128]{1,0:T(8,128)S(1)} collective-permute-done((f32[512,128]{1,0:T(8,128)S(1)}, f32[512,128]{1,0:T(8,128)S(1)}, u32[]{:S(2)}, u32[]{:S(2)}) %collective-permute-start.11) | collective-permute-done | bytes 262176 | tf_op jit(solution)/shard_map/ppermute | solution.py:291
  65.5 1.2 %collective-permute-done.13 = f32[128,128]{1,0:T(8,128)S(1)} collective-permute-done((f32[128,128]{1,0:T(8,128)S(1)}, f32[128,128]{1,0:T(8,128)S(1)}, u32[]{:S(2)}, u32[]{:S(2)}) %collective-permute-start.13) | collective-permute-done | bytes 65568 | tf_op jit(solution)/shard_map/ppermute | solution.py:290
  66.8 4.2 %collective-permute-start.14 = (f32[128,128]{1,0:T(8,128)S(1)}, f32[128,128]{1,0:T(8,128)S(1)}, u32[]{:S(2)}, u32[]{:S(2)}) collective-permute-start(f32[128,128]{1,0:T(8,128)S(1)} %add.20), channel_id=1, source_target_pairs={{0,2},{2,0},{4,6},{6,4},{8,10},{10,8},{12,14},{14,12},{1,3},{3,1},... | collective-permute-start | bytes 196616 | tf_op jit(solution)/shard_map/ppermute | solution.py:291
  71.0 2.4 %collective-permute-done.14 = f32[128,128]{1,0:T(8,128)S(1)} collective-permute-done((f32[128,128]{1,0:T(8,128)S(1)}, f32[128,128]{1,0:T(8,128)S(1)}, u32[]{:S(2)}, u32[]{:S(2)}) %collective-permute-start.14) | collective-permute-done | bytes 65568 | tf_op jit(solution)/shard_map/ppermute | solution.py:291
  73.4 0.6 collective-permute-start.15
  74.0 3.7 %collective-permute-done.15 = f32[128,128]{1,0:T(8,128)S(1)} collective-permute-done((f32[128,128]{1,0:T(8,128)S(1)}, f32[128,128]{1,0:T(8,128)S(1)}, u32[]{:S(2)}, u32[]{:S(2)}) %collective-permute-start.15) | collective-permute-done | bytes 65568 | tf_op jit(solution)/shard_map/ppermute | solution.py:291
  77.8 0.6 collective-permute-start.16
  78.4 5.3 %collective-permute-done.16 = f32[128,128]{1,0:T(8,128)S(1)} collective-permute-done((f32[128,128]{1,0:T(8,128)S(1)}, f32[128,128]{1,0:T(8,128)S(1)}, u32[]{:S(2)}, u32[]{:S(2)}) %collective-permute-start.16) | collective-permute-done | bytes 65568 | tf_op jit(solution)/shard_map/ppermute | solution.py:291
  83.7 5.1 %shard_map.66 = (f32[512,128]{1,0:T(8,128)}, f32[128,128]{1,0:T(8,128)}) custom-call(f32[512,128]{1,0:T(8,128)S(1)} %get-tuple-element.46.image, f32[128,128]{1,0:T(8,128)S(1)} %add.23.gram), custom_call_target="tpu_custom_call" | custom-call | flops 99999997952 | bytes 1 | tf_op jit(solution)/shard_map/pallas_call | solution.py:18
  (22 shorter events, 1.6 us)
Async XLA Ops:
  0.6 31.9 %collective-permute-start.4 = (bf16[512,1024]{1,0:T(8,128)(2,1)}, bf16[512,1024]{1,0:T(8,128)(2,1)S(1)}, u32[]{:S(2)}, u32[]{:S(2)}) collective-permute-start(bf16[512,1024]{1,0:T(8,128)(2,1)} %embeddings.1), channel_id=1, source_target_pairs={{0,12},{2,14},{4,0},{6,2},{8,4},{10,6},{12,8},{14,10},{1,13},{3,15... | collective-permute-start | bytes 3145736 | tf_op jit(solution)/shard_map/ppermute | solution.py:291
  5.7 1.3 %copy-start = (bf16[512,1024]{1,0:T(8,128)(2,1)S(1)}, bf16[512,1024]{1,0:T(8,128)(2,1)}, u32[]{:S(2)}) copy-start(bf16[512,1024]{1,0:T(8,128)(2,1)} %embeddings.1) | copy-start | bytes 3145732
  7.0 0.9 %copy-start.1 = (bf16[512,128]{1,0:T(8,128)(2,1)S(1)}, bf16[512,128]{1,0:T(8,128)(2,1)}, u32[]{:S(2)}) copy-start(bf16[512,128]{1,0:T(8,128)(2,1)} %panel.1) | copy-start | bytes 393220
  7.9 0.7 copy-start.2
  9.6 3.2 %collective-permute-start.1 = (bf16[264,1152]{1,0:T(8,128)(2,1)S(1)}, bf16[264,1152]{1,0:T(8,128)(2,1)S(1)}, u32[]{:S(2)}, u32[]{:S(2)}) collective-permute-start(bf16[264,1152]{1,0:T(8,128)(2,1)S(1)} %get-tuple-element.27.first), channel_id=1, source_target_pairs={{0,1},{1,0},{2,3},{3,2},{4,5},{5,4},{6,7},{7,6},{8,9},{9,8},{10,11... | collective-permute-start | bytes 1824776 | tf_op jit(solution)/shard_map/ppermute | solution.py:290
  9.6 3.2 %collective-permute-start.2 = (bf16[256,1152]{1,0:T(8,128)(2,1)S(1)}, bf16[256,1152]{1,0:T(8,128)(2,1)S(1)}, u32[]{:S(2)}, u32[]{:S(2)}) collective-permute-start(bf16[256,1152]{1,0:T(8,128)(2,1)S(1)} %get-tuple-element.26.last), channel_id=1, source_target_pairs={{0,1},{1,0},{2,3},{3,2},{4,5},{5,4},{6,7},{7,6},{8,9},{9,8},{10,11... | collective-permute-start | bytes 1769480 | tf_op jit(solution)/shard_map/ppermute | solution.py:290
  10.1 15.3 %collective-permute-start = (bf16[256,1152]{1,0:T(8,128)(2,1)S(1)}, bf16[256,1152]{1,0:T(8,128)(2,1)}, u32[]{:S(2)}, u32[]{:S(2)}) collective-permute-start(bf16[256,1152]{1,0:T(8,128)(2,1)S(1)} %get-tuple-element.26.last), channel_id=1, source_target_pairs={{0,2},{2,0},{4,6},{6,4},{8,10},{10,8},{12,14},{14,12},{1,3},{3,1},... | collective-permute-start | bytes 1769480 | tf_op jit(solution)/shard_map/ppermute | solution.py:291
  11.6 20.9 %collective-permute-start.5 = (bf16[520,128]{1,0:T(8,128)(2,1)}, bf16[520,128]{1,0:T(8,128)(2,1)}, u32[]{:S(2)}, u32[]{:S(2)}) collective-permute-start(bf16[520,128]{1,0:T(8,128)(2,1)} %get-tuple-element.28), channel_id=1, source_target_pairs={{0,12},{2,14},{4,0},{6,2},{8,4},{10,6},{12,8},{14,10},{1,13},{3,15... | collective-permute-start | bytes 399368 | tf_op jit(solution)/shard_map/ppermute | solution.py:291
  25.5 19.3 %collective-permute-start.6 = (bf16[256,1152]{1,0:T(8,128)(2,1)}, bf16[256,1152]{1,0:T(8,128)(2,1)S(1)}, u32[]{:S(2)}, u32[]{:S(2)}) collective-permute-start(bf16[256,1152]{1,0:T(8,128)(2,1)} %collective-permute-done), channel_id=1, source_target_pairs={{0,4},{2,2},{4,8},{6,6},{8,12},{10,10},{12,0},{14,14},{1,5},{3,3},... | collective-permute-start | bytes 1769480 | tf_op jit(solution)/shard_map/ppermute | solution.py:291
  27.4 18.7 %collective-permute-start.3 = (bf16[264,1152]{1,0:T(8,128)(2,1)S(1)}, bf16[264,1152]{1,0:T(8,128)(2,1)S(1)}, u32[]{:S(2)}, u32[]{:S(2)}) collective-permute-start(bf16[264,1152]{1,0:T(8,128)(2,1)S(1)} %get-tuple-element.27.first), channel_id=1, source_target_pairs={{0,2},{2,4},{4,6},{6,8},{8,10},{10,12},{12,14},{14,0},{1,3},{3,5},... | collective-permute-start | bytes 1824776 | tf_op jit(solution)/shard_map/ppermute | solution.py:291
  46.1 2.4 %collective-permute-start.8 = (bf16[256,1152]{1,0:T(8,128)(2,1)S(1)}, bf16[256,1152]{1,0:T(8,128)(2,1)S(1)}, u32[]{:S(2)}, u32[]{:S(2)}) collective-permute-start(bf16[256,1152]{1,0:T(8,128)(2,1)S(1)} %collective-permute-done.6.below1.below), channel_id=1, source_target_pairs={{0,1},{1,0},{2,3},{3,2},{4,5},{5,4},{6,7},{7,6},{8,9},{9,8},{10,11... | collective-permute-start | bytes 1769480 | tf_op jit(solution)/shard_map/ppermute | solution.py:290
  46.1 2.9 %collective-permute-start.7 = (bf16[264,1152]{1,0:T(8,128)(2,1)S(1)}, bf16[264,1152]{1,0:T(8,128)(2,1)S(1)}, u32[]{:S(2)}, u32[]{:S(2)}) collective-permute-start(bf16[264,1152]{1,0:T(8,128)(2,1)S(1)} %collective-permute-done.3.below.below0.marked), channel_id=1, source_target_pairs={{0,1},{1,0},{2,3},{3,2},{4,5},{5,4},{6,7},{7,6},{8,9},{9,8},{10,11... | collective-permute-start | bytes 1824776 | tf_op jit(solution)/shard_map/ppermute | solution.py:290
  51.9 11.0 %collective-permute-start.12 = (f32[512,128]{1,0:T(8,128)S(1)}, f32[512,128]{1,0:T(8,128)S(1)}, u32[]{:S(2)}, u32[]{:S(2)}) collective-permute-start(f32[512,128]{1,0:T(8,128)S(1)} %get-tuple-element.39), channel_id=1, source_target_pairs={{0,4},{2,6},{4,8},{6,10},{8,12},{10,14},{12,0},{14,2},{1,5},{3,7},... | collective-permute-start | bytes 786440 | tf_op jit(solution)/shard_map/ppermute | solution.py:291
  53.5 2.6 %collective-permute-start.10 = (f32[512,128]{1,0:T(8,128)S(1)}, f32[512,128]{1,0:T(8,128)S(1)}, u32[]{:S(2)}, u32[]{:S(2)}) collective-permute-start(f32[512,128]{1,0:T(8,128)S(1)} %get-tuple-element.44), channel_id=1, source_target_pairs={{0,1},{1,0},{2,3},{3,2},{4,5},{5,4},{6,7},{7,6},{8,9},{9,8},{10,11... | collective-permute-start | bytes 786440 | tf_op jit(solution)/shard_map/ppermute | solution.py:290
  55.6 2.2 %collective-permute-start.9 = (f32[512,128]{1,0:T(8,128)S(1)}, f32[512,128]{1,0:T(8,128)S(1)}, u32[]{:S(2)}, u32[]{:S(2)}) collective-permute-start(f32[512,128]{1,0:T(8,128)S(1)} %get-tuple-element.42), channel_id=1, source_target_pairs={{0,1},{1,0},{2,3},{3,2},{4,5},{5,4},{6,7},{7,6},{8,9},{9,8},{10,11... | collective-permute-start | bytes 786440 | tf_op jit(solution)/shard_map/ppermute | solution.py:290
  56.2 8.8 %collective-permute-start.11 = (f32[512,128]{1,0:T(8,128)S(1)}, f32[512,128]{1,0:T(8,128)S(1)}, u32[]{:S(2)}, u32[]{:S(2)}) collective-permute-start(f32[512,128]{1,0:T(8,128)S(1)} %maximum_add_fusion), channel_id=1, source_target_pairs={{0,14},{2,0},{4,2},{6,4},{8,6},{10,8},{12,10},{14,12},{1,15},{3,1}... | collective-permute-start | bytes 786440 | tf_op jit(solution)/shard_map/ppermute | solution.py:291
  65.5 1.3 %collective-permute-start.13 = (f32[128,128]{1,0:T(8,128)S(1)}, f32[128,128]{1,0:T(8,128)S(1)}, u32[]{:S(2)}, u32[]{:S(2)}) collective-permute-start(f32[128,128]{1,0:T(8,128)S(1)} %get-tuple-element.47), channel_id=1, source_target_pairs={{0,1},{1,0},{2,3},{3,2},{4,5},{5,4},{6,7},{7,6},{8,9},{9,8},{10,11... | collective-permute-start | bytes 196616 | tf_op jit(solution)/shard_map/ppermute | solution.py:290
  66.8 6.6 %collective-permute-start.14 = (f32[128,128]{1,0:T(8,128)S(1)}, f32[128,128]{1,0:T(8,128)S(1)}, u32[]{:S(2)}, u32[]{:S(2)}) collective-permute-start(f32[128,128]{1,0:T(8,128)S(1)} %add.20), channel_id=1, source_target_pairs={{0,2},{2,0},{4,6},{6,4},{8,10},{10,8},{12,14},{14,12},{1,3},{3,1},... | collective-permute-start | bytes 196616 | tf_op jit(solution)/shard_map/ppermute | solution.py:291
  73.4 4.3 %collective-permute-start.15 = (f32[128,128]{1,0:T(8,128)S(1)}, f32[128,128]{1,0:T(8,128)S(1)}, u32[]{:S(2)}, u32[]{:S(2)}) collective-permute-start(f32[128,128]{1,0:T(8,128)S(1)} %add.21), channel_id=1, source_target_pairs={{0,4},{2,6},{4,0},{6,2},{8,12},{10,14},{12,8},{14,10},{1,5},{3,7},... | collective-permute-start | bytes 196616 | tf_op jit(solution)/shard_map/ppermute | solution.py:291
  77.8 5.9 %collective-permute-start.16 = (f32[128,128]{1,0:T(8,128)S(1)}, f32[128,128]{1,0:T(8,128)S(1)}, u32[]{:S(2)}, u32[]{:S(2)}) collective-permute-start(f32[128,128]{1,0:T(8,128)S(1)} %add.22), channel_id=1, source_target_pairs={{0,8},{2,10},{4,12},{6,14},{8,0},{10,2},{12,4},{14,6},{1,9},{3,11}... | collective-permute-start | bytes 196616 | tf_op jit(solution)/shard_map/ppermute | solution.py:291

commit v13 on v12

--- a/solution.py
+++ b/solution.py
@@ -12,13 +12,12 @@
 HIGHEST = lax.Precision.HIGHEST
 
 
-def vmem_call(body, out_shapes, *operands, scalars=0, long=True):
+def vmem_call(body, out_shapes, *operands, long=True):
     in_vmem = pl.BlockSpec(memory_space=pltpu.VMEM)
-    in_smem = pl.BlockSpec(memory_space=pltpu.SMEM)
     return pl.pallas_call(
         body,
         out_shape=out_shapes,
-        in_specs=[in_smem] * scalars + [in_vmem] * (len(operands) - scalars),
+        in_specs=[in_vmem] * len(operands),
         out_specs=jax.tree.map(lambda _: in_vmem, out_shapes),
         compiler_params=pltpu.CompilerParams(vmem_limit_bytes=24 << 20),
         cost_estimate=pl.CostEstimate(flops=10**11 if long else 1, transcendentals=0, bytes_accessed=1),
@@ -148,8 +147,12 @@
     panel_mark[half:] = mask
 
 
+def width_of(numbers):
+    return numbers[0:1, 0:1]
+
+
 def place(numbers):
-    return jnp.where(numbers[1] > 0.5, 1, 0)
+    return jnp.where(numbers[1:2, 0:1] > 0.5, 1, 0)
 
 
 def masks_of(sub, rows, others, offset):
@@ -162,7 +165,7 @@
     rows = square_rows(first)
     both = [marks(r, half) for r in (first, other_first)]
     columns = columns_of(own, other, rows + square_rows(other_first), masks_of(place(numbers), both[0], both, OWN))
-    image[...], _ = products(numbers[0], own, [as_column(r) for r in rows], columns, None)
+    image[...], _ = products(width_of(numbers), own, [as_column(r) for r in rows], columns, None)
 
 
 def own_columns(sub, mark, first, last, other_first, other_last, offset):
@@ -181,14 +184,14 @@
     columns_sq = [squares(features) for features, _ in rows]
     for k, column in enumerate(columns_sq):
         above_sq[k * size : (k + 1) * size] = jnp.broadcast_to(column, (size, TILE))
-    image[...], back[...] = products(numbers[0], rows, columns_sq, columns, jnp.zeros(back.shape, F32))
+    image[...], back[...] = products(width_of(numbers), rows, columns_sq, columns, jnp.zeros(back.shape, F32))
 
 
 def below_first_body(numbers, below, first, last, other_first, other_last, back, image, total):
     half = 2 * last.shape[0]
     columns = own_columns(place(numbers), marks(below, half), first, last, other_first, other_last, BELOW)
     rows_sq = [as_column(square_rows(below)[0])]
-    image[...], total[...] = products(numbers[0], [pieces(below, last)[0]], rows_sq, columns, back[...])
+    image[...], total[...] = products(width_of(numbers), [pieces(below, last)[0]], rows_sq, columns, back[...])
 
 
 def below_last_body(
@@ -197,7 +200,7 @@
     half = 2 * last.shape[0]
     columns = own_columns(place(numbers), marks(marked, half), first, last, other_first, other_last, BELOW)
     rows_sq = [as_column(square_rows(marked)[1])]
-    image[...], total = products(numbers[0], pieces(below), rows_sq, columns, back[...], 1)
+    image[...], total = products(width_of(numbers), pieces(below), rows_sq, columns, back[...], 1)
     own_image[...] = self_image[...] + total[:, :half].T
     own_cross[...] = total[:, half:].T
 
@@ -207,7 +210,7 @@
     size = half // 2
     columns = own_columns(place(numbers), marks(panel, half), below0, below1, other0, other1, ABOVE - BELOW)
     rows_sq = [above_sq[k * size : (k + 1) * size, :1] for k in range(2)]
-    products_image, total = products(numbers[0], apart(above, panel), rows_sq, columns, jnp.zeros((TILE, 2 * half), F32))
+    products_image, total = products(width_of(numbers), apart(above, panel), rows_sq, columns, jnp.zeros((TILE, 2 * half), F32))
     image[...] = above_image[...] + products_image
     below_image[...] = total[:, :half].T
     cross[...] = total[:, half:].T
@@ -293,6 +296,7 @@
 
     after = lambda v, *earlier: lax.optimization_barrier((v, *earlier))[0]
     numbers = jnp.concatenate([inv_width, lax.axis_index("sub").astype(F32).reshape(1)])
+    numbers = jnp.broadcast_to(numbers[:, None], (2, TILE))
     wide = embeddings.shape[1] + width
     packed = lambda rows, lanes: jax.ShapeDtypeStruct((rows, lanes), BF16)
     above = blk_move(embeddings, -2)
@@ -309,7 +313,7 @@
     above_panel = blk_move(panel_mark, -2)
     own = (first, last, sub_move(first), sub_move(last))
     image, turned = shape(half, width), shape(width, 2 * half)
-    self_image = vmem_call(self_body, image, numbers, *own, scalars=1, long=False)
+    self_image = vmem_call(self_body, image, numbers, *own, long=False)
     below0 = blk_move(after(first, swapped, self_image), 1)
     swapped = after(swapped, self_image)
     below1 = blk_route(swapped, lambda i: i if i & 1 else i + 2) if relayed else blk_move(swapped, 1)
@@ -320,12 +324,11 @@
         above,
         above_panel,
         *own,
-        scalars=1,
     )
     below0, below1 = after(below0, above_image, below1), after(below1, above_image, below0)
     below_other = (sub_move(below0), sub_move(below1))
     below_image0, back = vmem_call(
-        below_first_body, (shape(size, width), turned), numbers, below0, *own, back, scalars=1
+        below_first_body, (shape(size, width), turned), numbers, below0, *own, back
     )
     above_image, below_sum, below_cross = vmem_call(
         above_below_body,
@@ -338,7 +341,6 @@
         below1,
         *below_other,
         after(above_image, below_image0),
-        scalars=1,
     )
     below_image1, own_image, own_cross = vmem_call(
         below_last_body,
@@ -349,7 +351,6 @@
         *own,
         self_image,
         after(back, above_image),
-        scalars=1,
     )
     above_image = blk_move(above_image, 2)
     below_image = jnp.concatenate([below_image0, below_image1], axis=0)

time: 89.1 us -> 88.6 us (level)
  Pallas kernels: 19.2 us -> 17.3 us
  waiting for transfers between devices: 44.6 us -> 46 us
    pallas_call x8, Pallas kernels: 19.2 us -> 17.3 us  [vmem_call(): pl.pallas_call(body, out_shape=out_shapes, in_specs=[in_vmem] * len(opera...]
  transfers between devices with their start and end apart: 17 -> 17, of which waited for: 11 -> 12; matrix products, arithmetic and copies ran while one was open for 0% -> 0% of each run, Pallas kernels for 12% -> 10%
where the time goes in v13:
time: 88.6 us; the launch traced here: 88.3 us
  waiting for transfers between devices  46 us (52%)
  starting transfers between devices  20.6 us (23%)
  Pallas kernels  17.3 us (20%)
  local copies, waits for them, and re-layouts  2.91 us (3%)
  between operations  1.38 us (2%)
    ppermute x10, waiting for transfers between devices, per_device(): lax.ppermute(v, 'blk', [(i, to(i) % n_blk) for i in range(n_blk)])  43.8 us
    ppermute x10, starting transfers between devices, per_device(): lax.ppermute(v, 'blk', [(i, to(i) % n_blk) for i in range(n_blk)])  19 us
    pallas_call x8, Pallas kernels, vmem_call(): pl.pallas_call(body, out_shape=out_shapes, in_specs=[in_vmem] * len(opera...  17.3 us
    unnamed x6, local copies, waits for them, and re-layouts  2.84 us
    ppermute x7, waiting for transfers between devices, per_device(): sub_move = lambda v: lax.ppermute(v, 'sub', [(0, 1), (1, 0)])  2.22 us
  transfers between devices with their start and end apart: 17, of which 12 were waited for; matrix products, arithmetic and copies ran while one was open for 0% of the time, Pallas kernels for 10%

profile of v13, /device:TPU:0, one launch (start us, length us, event | category | flops | bytes accessed | tf_op | source)
XLA Modules:
  0.0 88.3 jit_solution(10078723559578156521)
XLA Ops:
  0.6 5.1 %collective-permute-start.4 = (bf16[512,1024]{1,0:T(8,128)(2,1)}, bf16[512,1024]{1,0:T(8,128)(2,1)S(1)}, u32[]{:S(2)}, u32[]{:S(2)}) collective-permute-start(bf16[512,1024]{1,0:T(8,128)(2,1)} %embeddings.1), channel_id=1, source_target_pairs={{0,12},{2,14},{4,0},{6,2},{8,4},{10,6},{12,8},{14,10},{1,13},{3,15... | collective-permute-start | bytes 3145736 | tf_op jit(solution)/shard_map/ppermute | solution.py:294
  5.7 1.3 %copy-done = bf16[512,1024]{1,0:T(8,128)(2,1)S(1)} copy-done((bf16[512,1024]{1,0:T(8,128)(2,1)S(1)}, bf16[512,1024]{1,0:T(8,128)(2,1)}, u32[]{:S(2)}) %copy-start) | copy-done | bytes 1048600
  7.0 0.9 %copy-done.1 = bf16[512,128]{1,0:T(8,128)(2,1)S(1)} copy-done((bf16[512,128]{1,0:T(8,128)(2,1)S(1)}, bf16[512,128]{1,0:T(8,128)(2,1)}, u32[]{:S(2)}) %copy-start.1) | copy-done | bytes 131096
  7.9 0.7 copy-done.2
  8.6 1.1 %shard_map.59 = (bf16[264,1152]{1,0:T(8,128)(2,1)S(1)}, bf16[256,1152]{1,0:T(8,128)(2,1)S(1)}, bf16[520,128]{1,0:T(8,128)(2,1)}) custom-call(bf16[512,1024]{1,0:T(8,128)(2,1)S(1)} %copy-done, bf16[512,128]{1,0:T(8,128)(2,1)S(1)} %copy-done.1, s32[4,56]{1,0:T(4,128)S(1)} %copy-done.2), custom_call_target="tpu_custom_call" | custom-call | flops 1 | bytes 1 | tf_op jit(solution)/shard_map/pallas_call | solution.py:17
  9.6 0.5 collective-permute-start.2
  10.1 1.5 %collective-permute-start = (bf16[256,1152]{1,0:T(8,128)(2,1)S(1)}, bf16[256,1152]{1,0:T(8,128)(2,1)}, u32[]{:S(2)}, u32[]{:S(2)}) collective-permute-start(bf16[256,1152]{1,0:T(8,128)(2,1)S(1)} %get-tuple-element.26.last), channel_id=1, source_target_pairs={{0,2},{2,0},{4,6},{6,4},{8,10},{10,8},{12,14},{14,12},{1,3},{3,1},... | collective-permute-start | bytes 1769480 | tf_op jit(solution)/shard_map/ppermute | solution.py:294
  12.9 2.1 %shard_map.60.self_image = f32[512,128]{1,0:T(8,128)S(1)} custom-call(f32[2,128]{1,0:T(2,128)S(1)} %broadcast_in_dim.2.numbers, bf16[264,1152]{1,0:T(8,128)(2,1)S(1)} %get-tuple-element.27.first, bf16[256,1152]{1,0:T(8,128)(2,1)S(1)} %get-tuple-element.26.last, bf16[264,1152]{1,0:T(8,128)(2,1)S(1)} %collective-permute-done.1.other_first, ...), custom_call_target="tpu_custom_call" | custom-call | flops 1 | bytes 1 | tf_op jit(solution)/shard_map/pallas_call | solution.py:17
  15.0 10.5 %collective-permute-done = bf16[256,1152]{1,0:T(8,128)(2,1)} collective-permute-done((bf16[256,1152]{1,0:T(8,128)(2,1)S(1)}, bf16[256,1152]{1,0:T(8,128)(2,1)}, u32[]{:S(2)}, u32[]{:S(2)}) %collective-permute-start) | collective-permute-done | bytes 589856 | tf_op jit(solution)/shard_map/ppermute | solution.py:294
  25.5 1.9 %collective-permute-start.6 = (bf16[256,1152]{1,0:T(8,128)(2,1)}, bf16[256,1152]{1,0:T(8,128)(2,1)S(1)}, u32[]{:S(2)}, u32[]{:S(2)}) collective-permute-start(bf16[256,1152]{1,0:T(8,128)(2,1)} %collective-permute-done), channel_id=1, source_target_pairs={{0,4},{2,2},{4,8},{6,6},{8,12},{10,10},{12,0},{14,14},{1,5},{3,3},... | collective-permute-start | bytes 1769480 | tf_op jit(solution)/shard_map/ppermute | solution.py:294
  27.4 1.3 %collective-permute-start.3 = (bf16[264,1152]{1,0:T(8,128)(2,1)S(1)}, bf16[264,1152]{1,0:T(8,128)(2,1)S(1)}, u32[]{:S(2)}, u32[]{:S(2)}) collective-permute-start(bf16[264,1152]{1,0:T(8,128)(2,1)S(1)} %get-tuple-element.27.first), channel_id=1, source_target_pairs={{0,2},{2,4},{4,6},{6,8},{8,10},{10,12},{12,14},{14,0},{1,3},{3,5},... | collective-permute-start | bytes 1824776 | tf_op jit(solution)/shard_map/ppermute | solution.py:294
  28.7 3.8 %collective-permute-done.5.panel = bf16[520,128]{1,0:T(8,128)(2,1)} collective-permute-done((bf16[520,128]{1,0:T(8,128)(2,1)}, bf16[520,128]{1,0:T(8,128)(2,1)}, u32[]{:S(2)}, u32[]{:S(2)}) %collective-permute-start.5) | collective-permute-done | bytes 133152 | tf_op jit(solution)/shard_map/ppermute | solution.py:294
  32.5 3.2 %shard_map.61 = (f32[512,128]{1,0:T(8,128)S(1)}, f32[128,1024]{1,0:T(8,128)S(1)}, f32[512,128]{1,0:T(8,128)S(1)}, bf16[520,128]{1,0:T(8,128)(2,1)S(1)}) custom-call(f32[2,128]{1,0:T(2,128)S(1)} %broadcast_in_dim.2.numbers, bf16[512,1024]{1,0:T(8,128)(2,1)S(1)} %collective-permute-done.4.above, bf16[520,128]{1,0:T(8,128)(2,1)} %collective-permute-done.5.panel, ...), custom_call_target="tpu_custom_call" | custom-call | flops 99999997952 | bytes 1 | tf_op jit(solution)/shard_map/pallas_call | solution.py:17
  35.7 9.0 %collective-permute-done.6.below1.below = bf16[256,1152]{1,0:T(8,128)(2,1)S(1)} collective-permute-done((bf16[256,1152]{1,0:T(8,128)(2,1)}, bf16[256,1152]{1,0:T(8,128)(2,1)S(1)}, u32[]{:S(2)}, u32[]{:S(2)}) %collective-permute-start.6) | collective-permute-done | bytes 589856 | tf_op jit(solution)/shard_map/ppermute | solution.py:294
  44.8 1.3 %collective-permute-done.3.below.below0.marked = bf16[264,1152]{1,0:T(8,128)(2,1)S(1)} collective-permute-done((bf16[264,1152]{1,0:T(8,128)(2,1)S(1)}, bf16[264,1152]{1,0:T(8,128)(2,1)S(1)}, u32[]{:S(2)}, u32[]{:S(2)}) %collective-permute-start.3) | collective-permute-done | bytes 608288 | tf_op jit(solution)/shard_map/ppermute | solution.py:294
  46.6 1.4 %shard_map.62 = (f32[256,128]{1,0:T(8,128)S(1)}, f32[128,1024]{1,0:T(8,128)S(1)}) custom-call(f32[2,128]{1,0:T(2,128)S(1)} %broadcast_in_dim.2.numbers, bf16[264,1152]{1,0:T(8,128)(2,1)S(1)} %collective-permute-done.3.below.below0.marked, bf16[264,1152]{1,0:T(8,128)(2,1)S(1)} %get-tuple-element.27.first, bf16[256,1152]{1,0:T(8,128)(2,1)S(1)} %get-tuple-element.26.last, ...), custom_call_target="tpu_custom_call" | custom-call | flops 99999997952 | bytes 1 | tf_op jit(solution)/shard_map/pallas_call | solution.py:17
  48.1 0.9 collective-permute-done.7.other0
  49.0 2.4 %shard_map.63 = (f32[512,128]{1,0:T(8,128)S(1)}, f32[512,128]{1,0:T(8,128)S(1)}, f32[512,128]{1,0:T(8,128)S(1)}) custom-call(f32[2,128]{1,0:T(2,128)S(1)} %broadcast_in_dim.2.numbers, bf16[512,1024]{1,0:T(8,128)(2,1)S(1)} %collective-permute-done.4.above, bf16[520,128]{1,0:T(8,128)(2,1)S(1)} %get-tuple-element.35.panel, ...), custom_call_target="tpu_custom_call" | custom-call | flops 99999997952 | bytes 1 | tf_op jit(solution)/shard_map/pallas_call | solution.py:17
  51.4 1.7 %collective-permute-start.12 = (f32[512,128]{1,0:T(8,128)S(1)}, f32[512,128]{1,0:T(8,128)S(1)}, u32[]{:S(2)}, u32[]{:S(2)}) collective-permute-start(f32[512,128]{1,0:T(8,128)S(1)} %get-tuple-element.39), channel_id=1, source_target_pairs={{0,4},{2,6},{4,8},{6,10},{8,12},{10,14},{12,0},{14,2},{1,5},{3,7},... | collective-permute-start | bytes 786440 | tf_op jit(solution)/shard_map/ppermute | solution.py:294
  53.1 1.5 %shard_map.64 = (f32[256,128]{1,0:T(8,128)S(1)}, f32[512,128]{1,0:T(8,128)S(1)}, f32[512,128]{1,0:T(8,128)S(1)}) custom-call(f32[2,128]{1,0:T(2,128)S(1)} %broadcast_in_dim.2.numbers, bf16[264,1152]{1,0:T(8,128)(2,1)S(1)} %collective-permute-done.3.below.below0.marked, bf16[256,1152]{1,0:T(8,128)(2,1)S(1)} %collective-permute-done.6.below1.below, ...), custom_call_target="tpu_custom_call" | custom-call | flops 99999997952 | bytes 1 | tf_op jit(solution)/shard_map/pallas_call | solution.py:17
  54.6 0.6 collective-permute-start.9
  55.2 1.6 %collective-permute-start.11 = (f32[512,128]{1,0:T(8,128)S(1)}, f32[512,128]{1,0:T(8,128)S(1)}, u32[]{:S(2)}, u32[]{:S(2)}) collective-permute-start(f32[512,128]{1,0:T(8,128)S(1)} %maximum_add_fusion), channel_id=1, source_target_pairs={{0,14},{2,0},{4,2},{6,4},{8,6},{10,8},{12,10},{14,12},{1,15},{3,1}... | collective-permute-start | bytes 786440 | tf_op jit(solution)/shard_map/ppermute | solution.py:294
  56.8 5.6 %collective-permute-done.12.above = f32[512,128]{1,0:T(8,128)S(1)} collective-permute-done((f32[512,128]{1,0:T(8,128)S(1)}, f32[512,128]{1,0:T(8,128)S(1)}, u32[]{:S(2)}, u32[]{:S(2)}) %collective-permute-start.12) | collective-permute-done | bytes 262176 | tf_op jit(solution)/shard_map/ppermute | solution.py:294
  62.4 2.1 %collective-permute-done.11.below = f32[512,128]{1,0:T(8,128)S(1)} collective-permute-done((f32[512,128]{1,0:T(8,128)S(1)}, f32[512,128]{1,0:T(8,128)S(1)}, u32[]{:S(2)}, u32[]{:S(2)}) %collective-permute-start.11) | collective-permute-done | bytes 262176 | tf_op jit(solution)/shard_map/ppermute | solution.py:294
  65.0 1.2 %collective-permute-done.13 = f32[128,128]{1,0:T(8,128)S(1)} collective-permute-done((f32[128,128]{1,0:T(8,128)S(1)}, f32[128,128]{1,0:T(8,128)S(1)}, u32[]{:S(2)}, u32[]{:S(2)}) %collective-permute-start.13) | collective-permute-done | bytes 65568 | tf_op jit(solution)/shard_map/ppermute | solution.py:293
  66.3 4.2 %collective-permute-start.14 = (f32[128,128]{1,0:T(8,128)S(1)}, f32[128,128]{1,0:T(8,128)S(1)}, u32[]{:S(2)}, u32[]{:S(2)}) collective-permute-start(f32[128,128]{1,0:T(8,128)S(1)} %add.20), channel_id=1, source_target_pairs={{0,2},{2,0},{4,6},{6,4},{8,10},{10,8},{12,14},{14,12},{1,3},{3,1},... | collective-permute-start | bytes 196616 | tf_op jit(solution)/shard_map/ppermute | solution.py:294
  70.5 2.4 %collective-permute-done.14 = f32[128,128]{1,0:T(8,128)S(1)} collective-permute-done((f32[128,128]{1,0:T(8,128)S(1)}, f32[128,128]{1,0:T(8,128)S(1)}, u32[]{:S(2)}, u32[]{:S(2)}) %collective-permute-start.14) | collective-permute-done | bytes 65568 | tf_op jit(solution)/shard_map/ppermute | solution.py:294
  72.9 0.6 collective-permute-start.15
  73.5 3.7 %collective-permute-done.15 = f32[128,128]{1,0:T(8,128)S(1)} collective-permute-done((f32[128,128]{1,0:T(8,128)S(1)}, f32[128,128]{1,0:T(8,128)S(1)}, u32[]{:S(2)}, u32[]{:S(2)}) %collective-permute-start.15) | collective-permute-done | bytes 65568 | tf_op jit(solution)/shard_map/ppermute | solution.py:294
  77.3 0.7 collective-permute-start.16
  77.9 5.3 %collective-permute-done.16 = f32[128,128]{1,0:T(8,128)S(1)} collective-permute-done((f32[128,128]{1,0:T(8,128)S(1)}, f32[128,128]{1,0:T(8,128)S(1)}, u32[]{:S(2)}, u32[]{:S(2)}) %collective-permute-start.16) | collective-permute-done | bytes 65568 | tf_op jit(solution)/shard_map/ppermute | solution.py:294
  83.2 5.2 %shard_map.66 = (f32[512,128]{1,0:T(8,128)}, f32[128,128]{1,0:T(8,128)}) custom-call(f32[512,128]{1,0:T(8,128)S(1)} %get-tuple-element.46.image, f32[128,128]{1,0:T(8,128)S(1)} %add.23.gram), custom_call_target="tpu_custom_call" | custom-call | flops 99999997952 | bytes 1 | tf_op jit(solution)/shard_map/pallas_call | solution.py:17
  (23 shorter events, 1.8 us)
Async XLA Ops:
  0.6 31.9 %collective-permute-start.4 = (bf16[512,1024]{1,0:T(8,128)(2,1)}, bf16[512,1024]{1,0:T(8,128)(2,1)S(1)}, u32[]{:S(2)}, u32[]{:S(2)}) collective-permute-start(bf16[512,1024]{1,0:T(8,128)(2,1)} %embeddings.1), channel_id=1, source_target_pairs={{0,12},{2,14},{4,0},{6,2},{8,4},{10,6},{12,8},{14,10},{1,13},{3,15... | collective-permute-start | bytes 3145736 | tf_op jit(solution)/shard_map/ppermute | solution.py:294
  5.7 1.3 %copy-start = (bf16[512,1024]{1,0:T(8,128)(2,1)S(1)}, bf16[512,1024]{1,0:T(8,128)(2,1)}, u32[]{:S(2)}) copy-start(bf16[512,1024]{1,0:T(8,128)(2,1)} %embeddings.1) | copy-start | bytes 3145732
  7.0 0.9 %copy-start.1 = (bf16[512,128]{1,0:T(8,128)(2,1)S(1)}, bf16[512,128]{1,0:T(8,128)(2,1)}, u32[]{:S(2)}) copy-start(bf16[512,128]{1,0:T(8,128)(2,1)} %panel.1) | copy-start | bytes 393220
  7.9 0.7 copy-start.2
  9.6 3.2 %collective-permute-start.1 = (bf16[264,1152]{1,0:T(8,128)(2,1)S(1)}, bf16[264,1152]{1,0:T(8,128)(2,1)S(1)}, u32[]{:S(2)}, u32[]{:S(2)}) collective-permute-start(bf16[264,1152]{1,0:T(8,128)(2,1)S(1)} %get-tuple-element.27.first), channel_id=1, source_target_pairs={{0,1},{1,0},{2,3},{3,2},{4,5},{5,4},{6,7},{7,6},{8,9},{9,8},{10,11... | collective-permute-start | bytes 1824776 | tf_op jit(solution)/shard_map/ppermute | solution.py:293
  9.6 3.2 %collective-permute-start.2 = (bf16[256,1152]{1,0:T(8,128)(2,1)S(1)}, bf16[256,1152]{1,0:T(8,128)(2,1)S(1)}, u32[]{:S(2)}, u32[]{:S(2)}) collective-permute-start(bf16[256,1152]{1,0:T(8,128)(2,1)S(1)} %get-tuple-element.26.last), channel_id=1, source_target_pairs={{0,1},{1,0},{2,3},{3,2},{4,5},{5,4},{6,7},{7,6},{8,9},{9,8},{10,11... | collective-permute-start | bytes 1769480 | tf_op jit(solution)/shard_map/ppermute | solution.py:293
  10.1 15.3 %collective-permute-start = (bf16[256,1152]{1,0:T(8,128)(2,1)S(1)}, bf16[256,1152]{1,0:T(8,128)(2,1)}, u32[]{:S(2)}, u32[]{:S(2)}) collective-permute-start(bf16[256,1152]{1,0:T(8,128)(2,1)S(1)} %get-tuple-element.26.last), channel_id=1, source_target_pairs={{0,2},{2,0},{4,6},{6,4},{8,10},{10,8},{12,14},{14,12},{1,3},{3,1},... | collective-permute-start | bytes 1769480 | tf_op jit(solution)/shard_map/ppermute | solution.py:294
  11.6 20.9 %collective-permute-start.5 = (bf16[520,128]{1,0:T(8,128)(2,1)}, bf16[520,128]{1,0:T(8,128)(2,1)}, u32[]{:S(2)}, u32[]{:S(2)}) collective-permute-start(bf16[520,128]{1,0:T(8,128)(2,1)} %get-tuple-element.28), channel_id=1, source_target_pairs={{0,12},{2,14},{4,0},{6,2},{8,4},{10,6},{12,8},{14,10},{1,13},{3,15... | collective-permute-start | bytes 399368 | tf_op jit(solution)/shard_map/ppermute | solution.py:294
  25.5 19.3 %collective-permute-start.6 = (bf16[256,1152]{1,0:T(8,128)(2,1)}, bf16[256,1152]{1,0:T(8,128)(2,1)S(1)}, u32[]{:S(2)}, u32[]{:S(2)}) collective-permute-start(bf16[256,1152]{1,0:T(8,128)(2,1)} %collective-permute-done), channel_id=1, source_target_pairs={{0,4},{2,2},{4,8},{6,6},{8,12},{10,10},{12,0},{14,14},{1,5},{3,3},... | collective-permute-start | bytes 1769480 | tf_op jit(solution)/shard_map/ppermute | solution.py:294
  27.4 18.7 %collective-permute-start.3 = (bf16[264,1152]{1,0:T(8,128)(2,1)S(1)}, bf16[264,1152]{1,0:T(8,128)(2,1)S(1)}, u32[]{:S(2)}, u32[]{:S(2)}) collective-permute-start(bf16[264,1152]{1,0:T(8,128)(2,1)S(1)} %get-tuple-element.27.first), channel_id=1, source_target_pairs={{0,2},{2,4},{4,6},{6,8},{8,10},{10,12},{12,14},{14,0},{1,3},{3,5},... | collective-permute-start | bytes 1824776 | tf_op jit(solution)/shard_map/ppermute | solution.py:294
  46.1 2.0 %collective-permute-start.8 = (bf16[256,1152]{1,0:T(8,128)(2,1)S(1)}, bf16[256,1152]{1,0:T(8,128)(2,1)S(1)}, u32[]{:S(2)}, u32[]{:S(2)}) collective-permute-start(bf16[256,1152]{1,0:T(8,128)(2,1)S(1)} %collective-permute-done.6.below1.below), channel_id=1, source_target_pairs={{0,1},{1,0},{2,3},{3,2},{4,5},{5,4},{6,7},{7,6},{8,9},{9,8},{10,11... | collective-permute-start | bytes 1769480 | tf_op jit(solution)/shard_map/ppermute | solution.py:293
  46.1 2.9 %collective-permute-start.7 = (bf16[264,1152]{1,0:T(8,128)(2,1)S(1)}, bf16[264,1152]{1,0:T(8,128)(2,1)S(1)}, u32[]{:S(2)}, u32[]{:S(2)}) collective-permute-start(bf16[264,1152]{1,0:T(8,128)(2,1)S(1)} %collective-permute-done.3.below.below0.marked), channel_id=1, source_target_pairs={{0,1},{1,0},{2,3},{3,2},{4,5},{5,4},{6,7},{7,6},{8,9},{9,8},{10,11... | collective-permute-start | bytes 1824776 | tf_op jit(solution)/shard_map/ppermute | solution.py:293
  51.4 11.0 %collective-permute-start.12 = (f32[512,128]{1,0:T(8,128)S(1)}, f32[512,128]{1,0:T(8,128)S(1)}, u32[]{:S(2)}, u32[]{:S(2)}) collective-permute-start(f32[512,128]{1,0:T(8,128)S(1)} %get-tuple-element.39), channel_id=1, source_target_pairs={{0,4},{2,6},{4,8},{6,10},{8,12},{10,14},{12,0},{14,2},{1,5},{3,7},... | collective-permute-start | bytes 786440 | tf_op jit(solution)/shard_map/ppermute | solution.py:294
  53.0 2.1 %collective-permute-start.10 = (f32[512,128]{1,0:T(8,128)S(1)}, f32[512,128]{1,0:T(8,128)S(1)}, u32[]{:S(2)}, u32[]{:S(2)}) collective-permute-start(f32[512,128]{1,0:T(8,128)S(1)} %get-tuple-element.44), channel_id=1, source_target_pairs={{0,1},{1,0},{2,3},{3,2},{4,5},{5,4},{6,7},{7,6},{8,9},{9,8},{10,11... | collective-permute-start | bytes 786440 | tf_op jit(solution)/shard_map/ppermute | solution.py:293
  54.6 2.2 %collective-permute-start.9 = (f32[512,128]{1,0:T(8,128)S(1)}, f32[512,128]{1,0:T(8,128)S(1)}, u32[]{:S(2)}, u32[]{:S(2)}) collective-permute-start(f32[512,128]{1,0:T(8,128)S(1)} %get-tuple-element.42), channel_id=1, source_target_pairs={{0,1},{1,0},{2,3},{3,2},{4,5},{5,4},{6,7},{7,6},{8,9},{9,8},{10,11... | collective-permute-start | bytes 786440 | tf_op jit(solution)/shard_map/ppermute | solution.py:293
  55.2 9.3 %collective-permute-start.11 = (f32[512,128]{1,0:T(8,128)S(1)}, f32[512,128]{1,0:T(8,128)S(1)}, u32[]{:S(2)}, u32[]{:S(2)}) collective-permute-start(f32[512,128]{1,0:T(8,128)S(1)} %maximum_add_fusion), channel_id=1, source_target_pairs={{0,14},{2,0},{4,2},{6,4},{8,6},{10,8},{12,10},{14,12},{1,15},{3,1}... | collective-permute-start | bytes 786440 | tf_op jit(solution)/shard_map/ppermute | solution.py:294
  65.0 1.3 %collective-permute-start.13 = (f32[128,128]{1,0:T(8,128)S(1)}, f32[128,128]{1,0:T(8,128)S(1)}, u32[]{:S(2)}, u32[]{:S(2)}) collective-permute-start(f32[128,128]{1,0:T(8,128)S(1)} %get-tuple-element.47), channel_id=1, source_target_pairs={{0,1},{1,0},{2,3},{3,2},{4,5},{5,4},{6,7},{7,6},{8,9},{9,8},{10,11... | collective-permute-start | bytes 196616 | tf_op jit(solution)/shard_map/ppermute | solution.py:293
  66.3 6.6 %collective-permute-start.14 = (f32[128,128]{1,0:T(8,128)S(1)}, f32[128,128]{1,0:T(8,128)S(1)}, u32[]{:S(2)}, u32[]{:S(2)}) collective-permute-start(f32[128,128]{1,0:T(8,128)S(1)} %add.20), channel_id=1, source_target_pairs={{0,2},{2,0},{4,6},{6,4},{8,10},{10,8},{12,14},{14,12},{1,3},{3,1},... | collective-permute-start | bytes 196616 | tf_op jit(solution)/shard_map/ppermute | solution.py:294
  72.9 4.3 %collective-permute-start.15 = (f32[128,128]{1,0:T(8,128)S(1)}, f32[128,128]{1,0:T(8,128)S(1)}, u32[]{:S(2)}, u32[]{:S(2)}) collective-permute-start(f32[128,128]{1,0:T(8,128)S(1)} %add.21), channel_id=1, source_target_pairs={{0,4},{2,6},{4,0},{6,2},{8,12},{10,14},{12,8},{14,10},{1,5},{3,7},... | collective-permute-start | bytes 196616 | tf_op jit(solution)/shard_map/ppermute | solution.py:294
  77.3 5.9 %collective-permute-start.16 = (f32[128,128]{1,0:T(8,128)S(1)}, f32[128,128]{1,0:T(8,128)S(1)}, u32[]{:S(2)}, u32[]{:S(2)}) collective-permute-start(f32[128,128]{1,0:T(8,128)S(1)} %add.22), channel_id=1, source_target_pairs={{0,8},{2,10},{4,12},{6,14},{8,0},{10,2},{12,4},{14,6},{1,9},{3,11}... | collective-permute-start | bytes 196616 | tf_op jit(solution)/shard_map/ppermute | solution.py:294

commit v14 on v13

--- a/solution.py
+++ b/solution.py
@@ -216,8 +216,11 @@
     cross[...] = total[:, half:].T
 
 
-def gram_body(own, cross, below, above, image, gram):
-    total = own[...] + cross[...] + below[...] + above[...]
+def gram_body(own, cross, below, *refs):
+    *above, image, gram = refs
+    total = own[...] + cross[...] + below[...]
+    for part in above:
+        total = total + part[...]
     image[...] = total
     gram[...] = contract(total, total, ((0,), (0,)), HIGHEST)
 
@@ -352,11 +355,19 @@
         self_image,
         after(back, above_image),
     )
-    above_image = blk_move(above_image, 2)
+    if relayed:
+        pair_route = lambda v, pairs: lax.ppermute(v, ("blk", "sub"), [((a[0] % n_blk) * 2 + a[1], (b[0] % n_blk) * 2 + b[1]) for a, b in pairs])
+        aside = [i for i in range(n_blk) if not i & 1]
+        straight = [((i, s), (i + 2, s)) for i in range(n_blk) for s in range(2) if i & 1 or s == 0]
+        turned_aside = pair_route(above_image, [((i, 1), (i + 1, 1)) for i in aside])
+        turned_aside = pair_route(turned_aside, [((i + 1, 1), (i + 2, 1)) for i in aside])
+        above_parts = (pair_route(above_image, straight), turned_aside)
+    else:
+        above_parts = (blk_move(above_image, 2),)
     below_image = jnp.concatenate([below_image0, below_image1], axis=0)
     below_image = blk_move(below_sum + sub_move(below_cross) + below_image, -1)
     image_rows, gram = vmem_call(
-        gram_body, (image, shape(width, width)), own_image, sub_move(own_cross), below_image, above_image
+        gram_body, (image, shape(width, width)), own_image, sub_move(own_cross), below_image, *above_parts
     )
     if n_blk & (n_blk - 1):
         gram = lax.psum(gram, ("blk", "sub"))

time: 88.6 us -> 90.1 us (1.017)
  starting transfers between devices: 20.6 us -> 25.8 us
  waiting for transfers between devices: 46 us -> 42.2 us
    ppermute x10 -> x9, waiting for transfers between devices: 43.8 us -> 37.2 us  [per_device(): lax.ppermute(v, 'blk', [(i, to(i) % n_blk) for i in range(n_blk)])]
    ppermute x0 -> x3, starting transfers between devices: none -> 5.05 us  [per_device(): lax.ppermute(v, ('blk', 'sub'), [(a[0] % n_blk * 2 + a[1], b[0] % n_blk *...]
    ppermute x7, starting transfers between devices: 1.68 us -> 4.8 us  [per_device(): sub_move = lambda v: lax.ppermute(v, 'sub', [(0, 1), (1, 0)])]
    ppermute x0 -> x3, waiting for transfers between devices: none -> 3.12 us  [per_device(): lax.ppermute(v, ('blk', 'sub'), [(a[0] % n_blk * 2 + a[1], b[0] % n_blk *...]
    ppermute x10 -> x9, starting transfers between devices: 19 us -> 16 us  [per_device(): lax.ppermute(v, 'blk', [(i, to(i) % n_blk) for i in range(n_blk)])]
  transfers between devices with their start and end apart: 17 -> 19, of which waited for: 12 -> 12; matrix products, arithmetic and copies ran while one was open for 0% -> 0% of each run, Pallas kernels for 10% -> 10%
where the time goes in v14:
time: 90.1 us; the launch traced here: 89.8 us
  waiting for transfers between devices  42.2 us (47%)
  starting transfers between devices  25.8 us (29%)
  Pallas kernels  17.3 us (19%)
  local copies, waits for them, and re-layouts  2.91 us (3%)
  between operations  1.41 us (2%)
    ppermute x9, waiting for transfers between devices, per_device(): lax.ppermute(v, 'blk', [(i, to(i) % n_blk) for i in range(n_blk)])  37.2 us
    pallas_call x8, Pallas kernels, vmem_call(): pl.pallas_call(body, out_shape=out_shapes, in_specs=[in_vmem] * len(opera...  17.3 us
    ppermute x9, starting transfers between devices, per_device(): lax.ppermute(v, 'blk', [(i, to(i) % n_blk) for i in range(n_blk)])  16 us
    ppermute x3, starting transfers between devices, per_device(): lax.ppermute(v, ('blk', 'sub'), [(a[0] % n_blk * 2 + a[1], b[0] % n_blk *...  5.05 us
    ppermute x7, starting transfers between devices, per_device(): sub_move = lambda v: lax.ppermute(v, 'sub', [(0, 1), (1, 0)])  4.8 us
    ppermute x3, waiting for transfers between devices, per_device(): lax.ppermute(v, ('blk', 'sub'), [(a[0] % n_blk * 2 + a[1], b[0] % n_blk *...  3.12 us
    unnamed x6, local copies, waits for them, and re-layouts  2.84 us
    ppermute x7, waiting for transfers between devices, per_device(): sub_move = lambda v: lax.ppermute(v, 'sub', [(0, 1), (1, 0)])  1.88 us
  transfers between devices with their start and end apart: 19, of which 12 were waited for; matrix products, arithmetic and copies ran while one was open for 0% of the time, Pallas kernels for 10%

profile of v14, /device:TPU:0, one launch (start us, length us, event | category | flops | bytes accessed | tf_op | source)
XLA Modules:
  0.0 89.8 jit_solution(14605757244963623784)
XLA Ops:
  0.6 5.1 %collective-permute-start.4 = (bf16[512,1024]{1,0:T(8,128)(2,1)}, bf16[512,1024]{1,0:T(8,128)(2,1)S(1)}, u32[]{:S(2)}, u32[]{:S(2)}) collective-permute-start(bf16[512,1024]{1,0:T(8,128)(2,1)} %embeddings.1), channel_id=1, source_target_pairs={{0,12},{2,14},{4,0},{6,2},{8,4},{10,6},{12,8},{14,10},{1,13},{3,15... | collective-permute-start | bytes 3145736 | tf_op jit(solution)/shard_map/ppermute | solution.py:297
  5.7 1.3 %copy-done = bf16[512,1024]{1,0:T(8,128)(2,1)S(1)} copy-done((bf16[512,1024]{1,0:T(8,128)(2,1)S(1)}, bf16[512,1024]{1,0:T(8,128)(2,1)}, u32[]{:S(2)}) %copy-start) | copy-done | bytes 1048600
  7.0 0.9 %copy-done.1 = bf16[512,128]{1,0:T(8,128)(2,1)S(1)} copy-done((bf16[512,128]{1,0:T(8,128)(2,1)S(1)}, bf16[512,128]{1,0:T(8,128)(2,1)}, u32[]{:S(2)}) %copy-start.1) | copy-done | bytes 131096
  7.9 0.7 copy-done.2
  8.6 1.1 %shard_map.59 = (bf16[264,1152]{1,0:T(8,128)(2,1)S(1)}, bf16[256,1152]{1,0:T(8,128)(2,1)S(1)}, bf16[520,128]{1,0:T(8,128)(2,1)}) custom-call(bf16[512,1024]{1,0:T(8,128)(2,1)S(1)} %copy-done, bf16[512,128]{1,0:T(8,128)(2,1)S(1)} %copy-done.1, s32[4,56]{1,0:T(4,128)S(1)} %copy-done.2), custom_call_target="tpu_custom_call" | custom-call | flops 1 | bytes 1 | tf_op jit(solution)/shard_map/pallas_call | solution.py:17
  10.1 1.5 %collective-permute-start = (bf16[256,1152]{1,0:T(8,128)(2,1)S(1)}, bf16[256,1152]{1,0:T(8,128)(2,1)}, u32[]{:S(2)}, u32[]{:S(2)}) collective-permute-start(bf16[256,1152]{1,0:T(8,128)(2,1)S(1)} %get-tuple-element.26.last), channel_id=1, source_target_pairs={{0,2},{2,0},{4,6},{6,4},{8,10},{10,8},{12,14},{14,12},{1,3},{3,1},... | collective-permute-start | bytes 1769480 | tf_op jit(solution)/shard_map/ppermute | solution.py:297
  12.9 2.1 %shard_map.60.self_image = f32[512,128]{1,0:T(8,128)S(1)} custom-call(f32[2,128]{1,0:T(2,128)S(1)} %broadcast_in_dim.2.numbers, bf16[264,1152]{1,0:T(8,128)(2,1)S(1)} %get-tuple-element.27.first, bf16[256,1152]{1,0:T(8,128)(2,1)S(1)} %get-tuple-element.26.last, bf16[264,1152]{1,0:T(8,128)(2,1)S(1)} %collective-permute-done.1.other_first, ...), custom_call_target="tpu_custom_call" | custom-call | flops 1 | bytes 1 | tf_op jit(solution)/shard_map/pallas_call | solution.py:17
  15.0 10.5 %collective-permute-done = bf16[256,1152]{1,0:T(8,128)(2,1)} collective-permute-done((bf16[256,1152]{1,0:T(8,128)(2,1)S(1)}, bf16[256,1152]{1,0:T(8,128)(2,1)}, u32[]{:S(2)}, u32[]{:S(2)}) %collective-permute-start) | collective-permute-done | bytes 589856 | tf_op jit(solution)/shard_map/ppermute | solution.py:297
  25.5 1.9 %collective-permute-start.6 = (bf16[256,1152]{1,0:T(8,128)(2,1)}, bf16[256,1152]{1,0:T(8,128)(2,1)S(1)}, u32[]{:S(2)}, u32[]{:S(2)}) collective-permute-start(bf16[256,1152]{1,0:T(8,128)(2,1)} %collective-permute-done), channel_id=1, source_target_pairs={{0,4},{2,2},{4,8},{6,6},{8,12},{10,10},{12,0},{14,14},{1,5},{3,3},... | collective-permute-start | bytes 1769480 | tf_op jit(solution)/shard_map/ppermute | solution.py:297
  27.4 1.3 %collective-permute-start.3 = (bf16[264,1152]{1,0:T(8,128)(2,1)S(1)}, bf16[264,1152]{1,0:T(8,128)(2,1)S(1)}, u32[]{:S(2)}, u32[]{:S(2)}) collective-permute-start(bf16[264,1152]{1,0:T(8,128)(2,1)S(1)} %get-tuple-element.27.first), channel_id=1, source_target_pairs={{0,2},{2,4},{4,6},{6,8},{8,10},{10,12},{12,14},{14,0},{1,3},{3,5},... | collective-permute-start | bytes 1824776 | tf_op jit(solution)/shard_map/ppermute | solution.py:297
  28.7 3.8 %collective-permute-done.5.panel = bf16[520,128]{1,0:T(8,128)(2,1)} collective-permute-done((bf16[520,128]{1,0:T(8,128)(2,1)}, bf16[520,128]{1,0:T(8,128)(2,1)}, u32[]{:S(2)}, u32[]{:S(2)}) %collective-permute-start.5) | collective-permute-done | bytes 133152 | tf_op jit(solution)/shard_map/ppermute | solution.py:297
  32.5 3.2 %shard_map.61 = (f32[512,128]{1,0:T(8,128)S(1)}, f32[128,1024]{1,0:T(8,128)S(1)}, f32[512,128]{1,0:T(8,128)S(1)}, bf16[520,128]{1,0:T(8,128)(2,1)S(1)}) custom-call(f32[2,128]{1,0:T(2,128)S(1)} %broadcast_in_dim.2.numbers, bf16[512,1024]{1,0:T(8,128)(2,1)S(1)} %collective-permute-done.4.above, bf16[520,128]{1,0:T(8,128)(2,1)} %collective-permute-done.5.panel, ...), custom_call_target="tpu_custom_call" | custom-call | flops 99999997952 | bytes 1 | tf_op jit(solution)/shard_map/pallas_call | solution.py:17
  35.7 9.0 %collective-permute-done.6.below1.below = bf16[256,1152]{1,0:T(8,128)(2,1)S(1)} collective-permute-done((bf16[256,1152]{1,0:T(8,128)(2,1)}, bf16[256,1152]{1,0:T(8,128)(2,1)S(1)}, u32[]{:S(2)}, u32[]{:S(2)}) %collective-permute-start.6) | collective-permute-done | bytes 589856 | tf_op jit(solution)/shard_map/ppermute | solution.py:297
  44.8 1.3 %collective-permute-done.3.below.below0.marked = bf16[264,1152]{1,0:T(8,128)(2,1)S(1)} collective-permute-done((bf16[264,1152]{1,0:T(8,128)(2,1)S(1)}, bf16[264,1152]{1,0:T(8,128)(2,1)S(1)}, u32[]{:S(2)}, u32[]{:S(2)}) %collective-permute-start.3) | collective-permute-done | bytes 608288 | tf_op jit(solution)/shard_map/ppermute | solution.py:297
  46.6 1.4 %shard_map.62 = (f32[256,128]{1,0:T(8,128)S(1)}, f32[128,1024]{1,0:T(8,128)S(1)}) custom-call(f32[2,128]{1,0:T(2,128)S(1)} %broadcast_in_dim.2.numbers, bf16[264,1152]{1,0:T(8,128)(2,1)S(1)} %collective-permute-done.3.below.below0.marked, bf16[264,1152]{1,0:T(8,128)(2,1)S(1)} %get-tuple-element.27.first, bf16[256,1152]{1,0:T(8,128)(2,1)S(1)} %get-tuple-element.26.last, ...), custom_call_target="tpu_custom_call" | custom-call | flops 99999997952 | bytes 1 | tf_op jit(solution)/shard_map/pallas_call | solution.py:17
  48.1 0.9 collective-permute-done.7.other0
  49.0 2.4 %shard_map.63 = (f32[512,128]{1,0:T(8,128)S(1)}, f32[512,128]{1,0:T(8,128)S(1)}, f32[512,128]{1,0:T(8,128)S(1)}) custom-call(f32[2,128]{1,0:T(2,128)S(1)} %broadcast_in_dim.2.numbers, bf16[512,1024]{1,0:T(8,128)(2,1)S(1)} %collective-permute-done.4.above, bf16[520,128]{1,0:T(8,128)(2,1)S(1)} %get-tuple-element.35.panel, ...), custom_call_target="tpu_custom_call" | custom-call | flops 99999997952 | bytes 1 | tf_op jit(solution)/shard_map/pallas_call | solution.py:17
  51.4 0.7 collective-permute-start.13
  52.1 3.5 %collective-permute-start.12 = (f32[512,128]{1,0:T(8,128)S(1)}, f32[512,128]{1,0:T(8,128)S(1)}, u32[]{:S(2)}, u32[]{:S(2)}) collective-permute-start(f32[512,128]{1,0:T(8,128)S(1)} %get-tuple-element.39), channel_id=1, source_target_pairs={{0,4},{2,6},{3,7},{4,8},{6,10},{7,11},{8,12},{10,14},{11,15},{12,0... | collective-permute-start | bytes 786440 | tf_op jit(solution)/shard_map/ppermute | solution.py:359
  55.7 1.5 %shard_map.64 = (f32[256,128]{1,0:T(8,128)S(1)}, f32[512,128]{1,0:T(8,128)S(1)}, f32[512,128]{1,0:T(8,128)S(1)}) custom-call(f32[2,128]{1,0:T(2,128)S(1)} %broadcast_in_dim.2.numbers, bf16[264,1152]{1,0:T(8,128)(2,1)S(1)} %collective-permute-done.3.below.below0.marked, bf16[256,1152]{1,0:T(8,128)(2,1)S(1)} %collective-permute-done.6.below1.below, ...), custom_call_target="tpu_custom_call" | custom-call | flops 99999997952 | bytes 1 | tf_op jit(solution)/shard_map/pallas_call | solution.py:17
  57.8 1.4 %collective-permute-start.11 = (f32[512,128]{1,0:T(8,128)S(1)}, f32[512,128]{1,0:T(8,128)S(1)}, u32[]{:S(2)}, u32[]{:S(2)}) collective-permute-start(f32[512,128]{1,0:T(8,128)S(1)} %maximum_add_fusion), channel_id=1, source_target_pairs={{0,14},{2,0},{4,2},{6,4},{8,6},{10,8},{12,10},{14,12},{1,15},{3,1}... | collective-permute-start | bytes 786440 | tf_op jit(solution)/shard_map/ppermute | solution.py:297
  59.2 0.8 collective-permute-start.14
  60.1 3.1 %collective-permute-done.12.refs_0_ = f32[512,128]{1,0:T(8,128)S(1)} collective-permute-done((f32[512,128]{1,0:T(8,128)S(1)}, f32[512,128]{1,0:T(8,128)S(1)}, u32[]{:S(2)}, u32[]{:S(2)}) %collective-permute-start.12) | collective-permute-done | bytes 262176 | tf_op jit(solution)/shard_map/ppermute | solution.py:359
  63.2 2.9 %collective-permute-done.11.below = f32[512,128]{1,0:T(8,128)S(1)} collective-permute-done((f32[512,128]{1,0:T(8,128)S(1)}, f32[512,128]{1,0:T(8,128)S(1)}, u32[]{:S(2)}, u32[]{:S(2)}) %collective-permute-start.11) | collective-permute-done | bytes 262176 | tf_op jit(solution)/shard_map/ppermute | solution.py:297
  66.6 3.2 %collective-permute-start.15 = (f32[128,128]{1,0:T(8,128)S(1)}, f32[128,128]{1,0:T(8,128)S(1)}, u32[]{:S(2)}, u32[]{:S(2)}) collective-permute-start(f32[128,128]{1,0:T(8,128)S(1)} %get-tuple-element.47), channel_id=1, source_target_pairs={{0,1},{1,0},{2,3},{3,2},{4,5},{5,4},{6,7},{7,6},{8,9},{9,8},{10,11... | collective-permute-start | bytes 196616 | tf_op jit(solution)/shard_map/ppermute | solution.py:296
  69.7 0.9 %collective-permute-done.15 = f32[128,128]{1,0:T(8,128)S(1)} collective-permute-done((f32[128,128]{1,0:T(8,128)S(1)}, f32[128,128]{1,0:T(8,128)S(1)}, u32[]{:S(2)}, u32[]{:S(2)}) %collective-permute-start.15) | collective-permute-done | bytes 65568 | tf_op jit(solution)/shard_map/ppermute | solution.py:296
  71.0 4.0 %collective-permute-done.16 = f32[128,128]{1,0:T(8,128)S(1)} collective-permute-done((f32[128,128]{1,0:T(8,128)S(1)}, f32[128,128]{1,0:T(8,128)S(1)}, u32[]{:S(2)}, u32[]{:S(2)}) %collective-permute-start.16) | collective-permute-done | bytes 65568 | tf_op jit(solution)/shard_map/ppermute | solution.py:297
  75.1 1.5 %collective-permute-start.17 = (f32[128,128]{1,0:T(8,128)S(1)}, f32[128,128]{1,0:T(8,128)S(1)}, u32[]{:S(2)}, u32[]{:S(2)}) collective-permute-start(f32[128,128]{1,0:T(8,128)S(1)} %add.21), channel_id=1, source_target_pairs={{0,4},{2,6},{4,0},{6,2},{8,12},{10,14},{12,8},{14,10},{1,5},{3,7},... | collective-permute-start | bytes 196616 | tf_op jit(solution)/shard_map/ppermute | solution.py:297
  76.5 2.9 %collective-permute-done.17 = f32[128,128]{1,0:T(8,128)S(1)} collective-permute-done((f32[128,128]{1,0:T(8,128)S(1)}, f32[128,128]{1,0:T(8,128)S(1)}, u32[]{:S(2)}, u32[]{:S(2)}) %collective-permute-start.17) | collective-permute-done | bytes 65568 | tf_op jit(solution)/shard_map/ppermute | solution.py:297
  79.4 2.5 %collective-permute-start.18 = (f32[128,128]{1,0:T(8,128)S(1)}, f32[128,128]{1,0:T(8,128)S(1)}, u32[]{:S(2)}, u32[]{:S(2)}) collective-permute-start(f32[128,128]{1,0:T(8,128)S(1)} %add.22), channel_id=1, source_target_pairs={{0,8},{2,10},{4,12},{6,14},{8,0},{10,2},{12,4},{14,6},{1,9},{3,11}... | collective-permute-start | bytes 196616 | tf_op jit(solution)/shard_map/ppermute | solution.py:297
  81.9 2.8 %collective-permute-done.18 = f32[128,128]{1,0:T(8,128)S(1)} collective-permute-done((f32[128,128]{1,0:T(8,128)S(1)}, f32[128,128]{1,0:T(8,128)S(1)}, u32[]{:S(2)}, u32[]{:S(2)}) %collective-permute-start.18) | collective-permute-done | bytes 65568 | tf_op jit(solution)/shard_map/ppermute | solution.py:297
  84.6 5.2 %shard_map.66 = (f32[512,128]{1,0:T(8,128)}, f32[128,128]{1,0:T(8,128)}) custom-call(f32[512,128]{1,0:T(8,128)S(1)} %get-tuple-element.46.image, f32[128,128]{1,0:T(8,128)S(1)} %add.23.gram), custom_call_target="tpu_custom_call" | custom-call | flops 99999997952 | bytes 1 | tf_op jit(solution)/shard_map/pallas_call | solution.py:17
  (27 shorter events, 3.3 us)
Async XLA Ops:
  0.6 31.9 %collective-permute-start.4 = (bf16[512,1024]{1,0:T(8,128)(2,1)}, bf16[512,1024]{1,0:T(8,128)(2,1)S(1)}, u32[]{:S(2)}, u32[]{:S(2)}) collective-permute-start(bf16[512,1024]{1,0:T(8,128)(2,1)} %embeddings.1), channel_id=1, source_target_pairs={{0,12},{2,14},{4,0},{6,2},{8,4},{10,6},{12,8},{14,10},{1,13},{3,15... | collective-permute-start | bytes 3145736 | tf_op jit(solution)/shard_map/ppermute | solution.py:297
  5.7 1.3 %copy-start = (bf16[512,1024]{1,0:T(8,128)(2,1)S(1)}, bf16[512,1024]{1,0:T(8,128)(2,1)}, u32[]{:S(2)}) copy-start(bf16[512,1024]{1,0:T(8,128)(2,1)} %embeddings.1) | copy-start | bytes 3145732
  7.0 0.9 %copy-start.1 = (bf16[512,128]{1,0:T(8,128)(2,1)S(1)}, bf16[512,128]{1,0:T(8,128)(2,1)}, u32[]{:S(2)}) copy-start(bf16[512,128]{1,0:T(8,128)(2,1)} %panel.1) | copy-start | bytes 393220
  7.9 0.7 copy-start.2
  9.6 3.2 %collective-permute-start.1 = (bf16[264,1152]{1,0:T(8,128)(2,1)S(1)}, bf16[264,1152]{1,0:T(8,128)(2,1)S(1)}, u32[]{:S(2)}, u32[]{:S(2)}) collective-permute-start(bf16[264,1152]{1,0:T(8,128)(2,1)S(1)} %get-tuple-element.27.first), channel_id=1, source_target_pairs={{0,1},{1,0},{2,3},{3,2},{4,5},{5,4},{6,7},{7,6},{8,9},{9,8},{10,11... | collective-permute-start | bytes 1824776 | tf_op jit(solution)/shard_map/ppermute | solution.py:296
  9.6 3.2 %collective-permute-start.2 = (bf16[256,1152]{1,0:T(8,128)(2,1)S(1)}, bf16[256,1152]{1,0:T(8,128)(2,1)S(1)}, u32[]{:S(2)}, u32[]{:S(2)}) collective-permute-start(bf16[256,1152]{1,0:T(8,128)(2,1)S(1)} %get-tuple-element.26.last), channel_id=1, source_target_pairs={{0,1},{1,0},{2,3},{3,2},{4,5},{5,4},{6,7},{7,6},{8,9},{9,8},{10,11... | collective-permute-start | bytes 1769480 | tf_op jit(solution)/shard_map/ppermute | solution.py:296
  10.1 15.3 %collective-permute-start = (bf16[256,1152]{1,0:T(8,128)(2,1)S(1)}, bf16[256,1152]{1,0:T(8,128)(2,1)}, u32[]{:S(2)}, u32[]{:S(2)}) collective-permute-start(bf16[256,1152]{1,0:T(8,128)(2,1)S(1)} %get-tuple-element.26.last), channel_id=1, source_target_pairs={{0,2},{2,0},{4,6},{6,4},{8,10},{10,8},{12,14},{14,12},{1,3},{3,1},... | collective-permute-start | bytes 1769480 | tf_op jit(solution)/shard_map/ppermute | solution.py:297
  11.6 20.9 %collective-permute-start.5 = (bf16[520,128]{1,0:T(8,128)(2,1)}, bf16[520,128]{1,0:T(8,128)(2,1)}, u32[]{:S(2)}, u32[]{:S(2)}) collective-permute-start(bf16[520,128]{1,0:T(8,128)(2,1)} %get-tuple-element.28), channel_id=1, source_target_pairs={{0,12},{2,14},{4,0},{6,2},{8,4},{10,6},{12,8},{14,10},{1,13},{3,15... | collective-permute-start | bytes 399368 | tf_op jit(solution)/shard_map/ppermute | solution.py:297
  25.5 19.3 %collective-permute-start.6 = (bf16[256,1152]{1,0:T(8,128)(2,1)}, bf16[256,1152]{1,0:T(8,128)(2,1)S(1)}, u32[]{:S(2)}, u32[]{:S(2)}) collective-permute-start(bf16[256,1152]{1,0:T(8,128)(2,1)} %collective-permute-done), channel_id=1, source_target_pairs={{0,4},{2,2},{4,8},{6,6},{8,12},{10,10},{12,0},{14,14},{1,5},{3,3},... | collective-permute-start | bytes 1769480 | tf_op jit(solution)/shard_map/ppermute | solution.py:297
  27.4 18.7 %collective-permute-start.3 = (bf16[264,1152]{1,0:T(8,128)(2,1)S(1)}, bf16[264,1152]{1,0:T(8,128)(2,1)S(1)}, u32[]{:S(2)}, u32[]{:S(2)}) collective-permute-start(bf16[264,1152]{1,0:T(8,128)(2,1)S(1)} %get-tuple-element.27.first), channel_id=1, source_target_pairs={{0,2},{2,4},{4,6},{6,8},{8,10},{10,12},{12,14},{14,0},{1,3},{3,5},... | collective-permute-start | bytes 1824776 | tf_op jit(solution)/shard_map/ppermute | solution.py:297
  46.1 2.0 %collective-permute-start.8 = (bf16[256,1152]{1,0:T(8,128)(2,1)S(1)}, bf16[256,1152]{1,0:T(8,128)(2,1)S(1)}, u32[]{:S(2)}, u32[]{:S(2)}) collective-permute-start(bf16[256,1152]{1,0:T(8,128)(2,1)S(1)} %collective-permute-done.6.below1.below), channel_id=1, source_target_pairs={{0,1},{1,0},{2,3},{3,2},{4,5},{5,4},{6,7},{7,6},{8,9},{9,8},{10,11... | collective-permute-start | bytes 1769480 | tf_op jit(solution)/shard_map/ppermute | solution.py:296
  46.1 2.9 %collective-permute-start.7 = (bf16[264,1152]{1,0:T(8,128)(2,1)S(1)}, bf16[264,1152]{1,0:T(8,128)(2,1)S(1)}, u32[]{:S(2)}, u32[]{:S(2)}) collective-permute-start(bf16[264,1152]{1,0:T(8,128)(2,1)S(1)} %collective-permute-done.3.below.below0.marked), channel_id=1, source_target_pairs={{0,1},{1,0},{2,3},{3,2},{4,5},{5,4},{6,7},{7,6},{8,9},{9,8},{10,11... | collective-permute-start | bytes 1824776 | tf_op jit(solution)/shard_map/ppermute | solution.py:296
  51.4 7.8 %collective-permute-start.13 = (f32[512,128]{1,0:T(8,128)S(1)}, f32[512,128]{1,0:T(8,128)S(1)}, u32[]{:S(2)}, u32[]{:S(2)}) collective-permute-start(f32[512,128]{1,0:T(8,128)S(1)} %get-tuple-element.39), channel_id=1, source_target_pairs={{1,3},{5,7},{9,11},{13,15},{17,19},{21,23},{25,27},{29,31}} | collective-permute-start | bytes 786440 | tf_op jit(solution)/shard_map/ppermute | solution.py:359
  52.1 11.1 %collective-permute-start.12 = (f32[512,128]{1,0:T(8,128)S(1)}, f32[512,128]{1,0:T(8,128)S(1)}, u32[]{:S(2)}, u32[]{:S(2)}) collective-permute-start(f32[512,128]{1,0:T(8,128)S(1)} %get-tuple-element.39), channel_id=1, source_target_pairs={{0,4},{2,6},{3,7},{4,8},{6,10},{7,11},{8,12},{10,14},{11,15},{12,0... | collective-permute-start | bytes 786440 | tf_op jit(solution)/shard_map/ppermute | solution.py:359
  55.6 2.2 %collective-permute-start.10 = (f32[512,128]{1,0:T(8,128)S(1)}, f32[512,128]{1,0:T(8,128)S(1)}, u32[]{:S(2)}, u32[]{:S(2)}) collective-permute-start(f32[512,128]{1,0:T(8,128)S(1)} %get-tuple-element.44), channel_id=1, source_target_pairs={{0,1},{1,0},{2,3},{3,2},{4,5},{5,4},{6,7},{7,6},{8,9},{9,8},{10,11... | collective-permute-start | bytes 786440 | tf_op jit(solution)/shard_map/ppermute | solution.py:296
  57.2 2.8 %collective-permute-start.9 = (f32[512,128]{1,0:T(8,128)S(1)}, f32[512,128]{1,0:T(8,128)S(1)}, u32[]{:S(2)}, u32[]{:S(2)}) collective-permute-start(f32[512,128]{1,0:T(8,128)S(1)} %get-tuple-element.42), channel_id=1, source_target_pairs={{0,1},{1,0},{2,3},{3,2},{4,5},{5,4},{6,7},{7,6},{8,9},{9,8},{10,11... | collective-permute-start | bytes 786440 | tf_op jit(solution)/shard_map/ppermute | solution.py:296
  57.8 8.3 %collective-permute-start.11 = (f32[512,128]{1,0:T(8,128)S(1)}, f32[512,128]{1,0:T(8,128)S(1)}, u32[]{:S(2)}, u32[]{:S(2)}) collective-permute-start(f32[512,128]{1,0:T(8,128)S(1)} %maximum_add_fusion), channel_id=1, source_target_pairs={{0,14},{2,0},{4,2},{6,4},{8,6},{10,8},{12,10},{14,12},{1,15},{3,1}... | collective-permute-start | bytes 786440 | tf_op jit(solution)/shard_map/ppermute | solution.py:297
  59.2 6.9 %collective-permute-start.14 = (f32[512,128]{1,0:T(8,128)S(1)}, f32[512,128]{1,0:T(8,128)S(1)}, u32[]{:S(2)}, u32[]{:S(2)}) collective-permute-start(f32[512,128]{1,0:T(8,128)S(1)} %collective-permute-done.13), channel_id=1, source_target_pairs={{3,5},{7,9},{11,13},{15,1},{19,21},{23,25},{27,29},{31,17}} | collective-permute-start | bytes 786440 | tf_op jit(solution)/shard_map/ppermute | solution.py:359
  66.6 4.1 %collective-permute-start.15 = (f32[128,128]{1,0:T(8,128)S(1)}, f32[128,128]{1,0:T(8,128)S(1)}, u32[]{:S(2)}, u32[]{:S(2)}) collective-permute-start(f32[128,128]{1,0:T(8,128)S(1)} %get-tuple-element.47), channel_id=1, source_target_pairs={{0,1},{1,0},{2,3},{3,2},{4,5},{5,4},{6,7},{7,6},{8,9},{9,8},{10,11... | collective-permute-start | bytes 196616 | tf_op jit(solution)/shard_map/ppermute | solution.py:296
  70.6 4.4 %collective-permute-start.16 = (f32[128,128]{1,0:T(8,128)S(1)}, f32[128,128]{1,0:T(8,128)S(1)}, u32[]{:S(2)}, u32[]{:S(2)}) collective-permute-start(f32[128,128]{1,0:T(8,128)S(1)} %add.20), channel_id=1, source_target_pairs={{0,2},{2,0},{4,6},{6,4},{8,10},{10,8},{12,14},{14,12},{1,3},{3,1},... | collective-permute-start | bytes 196616 | tf_op jit(solution)/shard_map/ppermute | solution.py:297
  75.1 4.3 %collective-permute-start.17 = (f32[128,128]{1,0:T(8,128)S(1)}, f32[128,128]{1,0:T(8,128)S(1)}, u32[]{:S(2)}, u32[]{:S(2)}) collective-permute-start(f32[128,128]{1,0:T(8,128)S(1)} %add.21), channel_id=1, source_target_pairs={{0,4},{2,6},{4,0},{6,2},{8,12},{10,14},{12,8},{14,10},{1,5},{3,7},... | collective-permute-start | bytes 196616 | tf_op jit(solution)/shard_map/ppermute | solution.py:297
  79.4 5.2 %collective-permute-start.18 = (f32[128,128]{1,0:T(8,128)S(1)}, f32[128,128]{1,0:T(8,128)S(1)}, u32[]{:S(2)}, u32[]{:S(2)}) collective-permute-start(f32[128,128]{1,0:T(8,128)S(1)} %add.22), channel_id=1, source_target_pairs={{0,8},{2,10},{4,12},{6,14},{8,0},{10,2},{12,4},{14,6},{1,9},{3,11}... | collective-permute-start | bytes 196616 | tf_op jit(solution)/shard_map/ppermute | solution.py:297

commit v15 on v13

--- a/solution.py
+++ b/solution.py
@@ -141,8 +141,8 @@
         carried.append(row.astype(BF16).astype(F32))
         row = row - carried[-1]
     carried = jnp.concatenate(carried + [jnp.zeros((MARK - SPLIT, half), F32)], axis=0).astype(BF16)
-    first[size:, :features] = jnp.concatenate([carried, jnp.zeros((MARK, features - half), BF16)], axis=1)
-    first[size:, features:] = mask
+    last[size:, :features] = jnp.concatenate([carried, jnp.zeros((MARK, features - half), BF16)], axis=1)
+    last[size:, features:] = mask
     panel_mark[:half] = panel[...]
     panel_mark[half:] = mask
 
@@ -160,18 +160,18 @@
 
 
 def self_body(numbers, first, last, other_first, other_last, image):
-    half = 2 * last.shape[0]
+    half = 2 * first.shape[0]
     own, other = pieces(first, last), pieces(other_first, other_last)
-    rows = square_rows(first)
-    both = [marks(r, half) for r in (first, other_first)]
-    columns = columns_of(own, other, rows + square_rows(other_first), masks_of(place(numbers), both[0], both, OWN))
+    rows = square_rows(last)
+    both = [marks(r, half) for r in (last, other_last)]
+    columns = columns_of(own, other, rows + square_rows(other_last), masks_of(place(numbers), both[0], both, OWN))
     image[...], _ = products(width_of(numbers), own, [as_column(r) for r in rows], columns, None)
 
 
-def own_columns(sub, mark, first, last, other_first, other_last, offset):
-    half = 2 * last.shape[0]
-    masks = masks_of(sub, mark, [marks(r, half) for r in (first, other_first)], offset)
-    rows = square_rows(first) + square_rows(other_first)
+def own_columns(place_here, mark, first, last, other_first, other_last, offset):
+    half = 2 * first.shape[0]
+    masks = masks_of(place_here, mark, [marks(r, half) for r in (last, other_last)], offset)
+    rows = square_rows(last) + square_rows(other_last)
     return columns_of(pieces(first, last), pieces(other_first, other_last), rows, masks)
 
 
@@ -187,33 +187,44 @@
     image[...], back[...] = products(width_of(numbers), rows, columns_sq, columns, jnp.zeros(back.shape, F32))
 
 
-def below_first_body(numbers, below, first, last, other_first, other_last, back, image, total):
-    half = 2 * last.shape[0]
+def below_last_body(numbers, below, first, last, other_first, other_last, back, image, total):
+    half = 2 * first.shape[0]
     columns = own_columns(place(numbers), marks(below, half), first, last, other_first, other_last, BELOW)
-    rows_sq = [as_column(square_rows(below)[0])]
-    image[...], total[...] = products(width_of(numbers), [pieces(below, last)[0]], rows_sq, columns, back[...])
-
-
-def below_last_body(
+    rows_sq = [as_column(square_rows(below)[1])]
+    image[...], total[...] = products(width_of(numbers), [pieces(below, first)[0]], rows_sq, columns, back[...], 1)
+
+
+def below_first_body(
     numbers, marked, below, first, last, other_first, other_last, self_image, back, image, own_image, own_cross
 ):
-    half = 2 * last.shape[0]
+    half = 2 * first.shape[0]
     columns = own_columns(place(numbers), marks(marked, half), first, last, other_first, other_last, BELOW)
-    rows_sq = [as_column(square_rows(marked)[1])]
-    image[...], total = products(width_of(numbers), pieces(below), rows_sq, columns, back[...], 1)
+    rows_sq = [as_column(square_rows(marked)[0])]
+    image[...], total = products(width_of(numbers), pieces(below), rows_sq, columns, back[...])
     own_image[...] = self_image[...] + total[:, :half].T
     own_cross[...] = total[:, half:].T
 
 
-def above_below_body(numbers, above, panel, above_sq, below0, below1, other0, other1, above_image, image, below_image, cross):
+def above_below(part, numbers, above, panel, above_sq, marked, other_marked, below, other, above_image, image, below_image, cross):
     half = image.shape[0]
     size = half // 2
-    columns = own_columns(place(numbers), marks(panel, half), below0, below1, other0, other1, ABOVE - BELOW)
+    masks = masks_of(place(numbers), marks(panel, half), [marks(r, half) for r in (marked, other_marked)], ABOVE - BELOW)
+    masks = [mask[:, part * size : (part + 1) * size] for mask in masks]
+    columns_sq = [square_rows(r)[part] for r in (marked, other_marked)]
+    columns = columns_of([(below[:size, :-TILE], below[:size, -TILE:])], [(other[:size, :-TILE], other[:size, -TILE:])], columns_sq, masks)
     rows_sq = [above_sq[k * size : (k + 1) * size, :1] for k in range(2)]
-    products_image, total = products(width_of(numbers), apart(above, panel), rows_sq, columns, jnp.zeros((TILE, 2 * half), F32))
+    products_image, total = products(width_of(numbers), apart(above, panel), rows_sq, columns, jnp.zeros((TILE, half), F32))
     image[...] = above_image[...] + products_image
-    below_image[...] = total[:, :half].T
-    cross[...] = total[:, half:].T
+    below_image[...] = total[:, :size].T
+    cross[...] = total[:, size:].T
+
+
+def above_below_last_body(numbers, above, panel, above_sq, below, other, above_image, *outs):
+    above_below(1, numbers, above, panel, above_sq, below, other, below, other, above_image, *outs)
+
+
+def above_below_first_body(numbers, above, panel, above_sq, marked, other_marked, below, other, above_image, *outs):
+    above_below(0, numbers, above, panel, above_sq, marked, other_marked, below, other, above_image, *outs)
 
 
 def gram_body(own, cross, below, above, image, gram):
@@ -302,7 +313,7 @@
     above = blk_move(embeddings, -2)
     first, last, panel_mark = vmem_call(
         pack_body,
-        (packed(size + MARK, wide), packed(size, wide), packed(half + MARK, width)),
+        (packed(size, wide), packed(size + MARK, wide), packed(half + MARK, width)),
         embeddings,
         start_panel,
         tile_mask,
@@ -325,36 +336,27 @@
         above_panel,
         *own,
     )
-    below0, below1 = after(below0, above_image, below1), after(below1, above_image, below0)
-    below_other = (sub_move(below0), sub_move(below1))
-    below_image0, back = vmem_call(
-        below_first_body, (shape(size, width), turned), numbers, below0, *own, back
-    )
-    above_image, below_sum, below_cross = vmem_call(
-        above_below_body,
-        (image,) * 3,
-        numbers,
-        above,
-        above_panel,
-        above_sq,
-        below0,
-        below1,
-        *below_other,
-        after(above_image, below_image0),
-    )
-    below_image1, own_image, own_cross = vmem_call(
-        below_last_body,
-        (shape(size, width), image, image),
-        numbers,
-        below0,
-        below1,
-        *own,
-        self_image,
-        after(back, above_image),
+    piece = shape(size, width)
+    below1 = after(below1, above_image)
+    other1 = sub_move(below1)
+    below_image1, back = vmem_call(below_last_body, (piece, turned), numbers, below1, *own, back)
+    below0 = after(below0, below_image1)
+    other0 = sub_move(below0)
+    here = (numbers, above, above_panel, above_sq)
+    above_image, below_sum1, below_cross1 = vmem_call(
+        above_below_last_body, (image, piece, piece), *here, below1, other1, after(above_image, below0)
+    )
+    above_image, below_sum0, below_cross0 = vmem_call(
+        above_below_first_body, (image, piece, piece), *here, below1, other1, below0, other0, above_image
+    )
+    below_image0, own_image, own_cross = vmem_call(
+        below_first_body, (piece, image, image), numbers, below1, below0, *own, self_image, after(back, above_image)
     )
     above_image = blk_move(above_image, 2)
-    below_image = jnp.concatenate([below_image0, below_image1], axis=0)
-    below_image = blk_move(below_sum + sub_move(below_cross) + below_image, -1)
+    join = lambda *parts: jnp.concatenate(parts, axis=0)
+    below_cross = sub_move(join(below_cross0, below_cross1))
+    below_image = join(below_sum0, below_sum1) + below_cross + join(below_image0, below_image1)
+    below_image = blk_move(below_image, -1)
     image_rows, gram = vmem_call(
         gram_body, (image, shape(width, width)), own_image, sub_move(own_cross), below_image, above_image
     )

time: 88.6 us -> 91.6 us (1.034)
  Pallas kernels: 17.3 us -> 22.5 us
  starting transfers between devices: 20.6 us -> 19 us
    pallas_call x8 -> x9, Pallas kernels: 17.3 us -> 22.5 us  [vmem_call(): pl.pallas_call(body, out_shape=out_shapes, in_specs=[in_vmem] * len(opera...]
    ppermute x10, waiting for transfers between devices: 43.8 us -> 41.8 us  [per_device(): lax.ppermute(v, 'blk', [(i, to(i) % n_blk) for i in range(n_blk)])]
    ppermute x10, starting transfers between devices: 19 us -> 17.5 us  [per_device(): lax.ppermute(v, 'blk', [(i, to(i) % n_blk) for i in range(n_blk)])]
    ppermute x7, waiting for transfers between devices: 2.22 us -> 3.26 us  [per_device(): sub_move = lambda v: lax.ppermute(v, 'sub', [(0, 1), (1, 0)])]
  transfers between devices with their start and end apart: 17 -> 17, of which waited for: 12 -> 12; matrix products, arithmetic and copies ran while one was open for 0% -> 0% of each run, Pallas kernels for 10% -> 16%
where the time goes in v15:
time: 91.6 us; the launch traced here: 91.1 us
  waiting for transfers between devices  45.1 us (49%)
  Pallas kernels  22.5 us (25%)
  starting transfers between devices  19 us (21%)
  local copies, waits for them, and re-layouts  2.91 us (3%)
  between operations  1.4 us (2%)
    ppermute x10, waiting for transfers between devices, per_device(): lax.ppermute(v, 'blk', [(i, to(i) % n_blk) for i in range(n_blk)])  41.8 us
    pallas_call x9, Pallas kernels, vmem_call(): pl.pallas_call(body, out_shape=out_shapes, in_specs=[in_vmem] * len(opera...  22.5 us
    ppermute x10, starting transfers between devices, per_device(): lax.ppermute(v, 'blk', [(i, to(i) % n_blk) for i in range(n_blk)])  17.5 us
    ppermute x7, waiting for transfers between devices, per_device(): sub_move = lambda v: lax.ppermute(v, 'sub', [(0, 1), (1, 0)])  3.26 us
    unnamed x6, local copies, waits for them, and re-layouts  2.84 us
  transfers between devices with their start and end apart: 17, of which 12 were waited for; matrix products, arithmetic and copies ran while one was open for 0% of the time, Pallas kernels for 16%

profile of v15, /device:TPU:0, one launch (start us, length us, event | category | flops | bytes accessed | tf_op | source)
XLA Modules:
  0.0 91.1 jit_solution(4062691243008131036)
XLA Ops:
  0.6 5.1 %collective-permute-start.4 = (bf16[512,1024]{1,0:T(8,128)(2,1)}, bf16[512,1024]{1,0:T(8,128)(2,1)S(1)}, u32[]{:S(2)}, u32[]{:S(2)}) collective-permute-start(bf16[512,1024]{1,0:T(8,128)(2,1)} %embeddings.1), channel_id=1, source_target_pairs={{0,12},{2,14},{4,0},{6,2},{8,4},{10,6},{12,8},{14,10},{1,13},{3,15... | collective-permute-start | bytes 3145736 | tf_op jit(solution)/shard_map/ppermute | solution.py:305
  5.7 1.3 %copy-done = bf16[512,1024]{1,0:T(8,128)(2,1)S(1)} copy-done((bf16[512,1024]{1,0:T(8,128)(2,1)S(1)}, bf16[512,1024]{1,0:T(8,128)(2,1)}, u32[]{:S(2)}) %copy-start) | copy-done | bytes 1048600
  7.0 0.9 copy-done.1
  7.9 0.7 copy-done.2
  8.6 1.2 %shard_map.59 = (bf16[256,1152]{1,0:T(8,128)(2,1)}, bf16[264,1152]{1,0:T(8,128)(2,1)S(1)}, bf16[520,128]{1,0:T(8,128)(2,1)S(1)}) custom-call(bf16[512,1024]{1,0:T(8,128)(2,1)S(1)} %copy-done, bf16[512,128]{1,0:T(8,128)(2,1)S(1)} %copy-done.1, s32[4,56]{1,0:T(4,128)S(1)} %copy-done.2), custom_call_target="tpu_custom_call" | custom-call | flops 1 | bytes 1 | tf_op jit(solution)/shard_map/pallas_call | solution.py:17
  9.8 1.5 %collective-permute-start = (bf16[264,1152]{1,0:T(8,128)(2,1)S(1)}, bf16[264,1152]{1,0:T(8,128)(2,1)}, u32[]{:S(2)}, u32[]{:S(2)}) collective-permute-start(bf16[264,1152]{1,0:T(8,128)(2,1)S(1)} %get-tuple-element.28.last), channel_id=1, source_target_pairs={{0,2},{2,0},{4,6},{6,4},{8,10},{10,8},{12,14},{14,12},{1,3},{3,1},... | collective-permute-start | bytes 1824776 | tf_op jit(solution)/shard_map/ppermute | solution.py:305
  11.5 0.4 collective-permute-start.5
  12.7 0.8 collective-permute-done.1.other_first
  13.6 3.2 %shard_map.60.self_image = f32[512,128]{1,0:T(8,128)S(1)} custom-call(f32[2,128]{1,0:T(2,128)S(1)} %broadcast_in_dim.2.numbers, bf16[256,1152]{1,0:T(8,128)(2,1)} %get-tuple-element.34.first, bf16[264,1152]{1,0:T(8,128)(2,1)S(1)} %get-tuple-element.28.last, bf16[256,1152]{1,0:T(8,128)(2,1)S(1)} %collective-permute-done.1.other_first, ...), custom_call_target="tpu_custom_call" | custom-call | flops 1 | bytes 1 | tf_op jit(solution)/shard_map/pallas_call | solution.py:17
  16.7 9.3 %collective-permute-done = bf16[264,1152]{1,0:T(8,128)(2,1)} collective-permute-done((bf16[264,1152]{1,0:T(8,128)(2,1)S(1)}, bf16[264,1152]{1,0:T(8,128)(2,1)}, u32[]{:S(2)}, u32[]{:S(2)}) %collective-permute-start) | collective-permute-done | bytes 608288 | tf_op jit(solution)/shard_map/ppermute | solution.py:305
  26.0 1.5 %collective-permute-start.6 = (bf16[256,1152]{1,0:T(8,128)(2,1)}, bf16[256,1152]{1,0:T(8,128)(2,1)}, u32[]{:S(2)}, u32[]{:S(2)}) collective-permute-start(bf16[256,1152]{1,0:T(8,128)(2,1)} %get-tuple-element.34.first), channel_id=1, source_target_pairs={{0,2},{2,4},{4,6},{6,8},{8,10},{10,12},{12,14},{14,0},{1,3},{3,5},... | collective-permute-start | bytes 1769480 | tf_op jit(solution)/shard_map/ppermute | solution.py:305
  27.5 1.9 %collective-permute-start.3 = (bf16[264,1152]{1,0:T(8,128)(2,1)}, bf16[264,1152]{1,0:T(8,128)(2,1)S(1)}, u32[]{:S(2)}, u32[]{:S(2)}) collective-permute-start(bf16[264,1152]{1,0:T(8,128)(2,1)} %collective-permute-done), channel_id=1, source_target_pairs={{0,4},{2,2},{4,8},{6,6},{8,12},{10,10},{12,0},{14,14},{1,5},{3,3},... | collective-permute-start | bytes 1824776 | tf_op jit(solution)/shard_map/ppermute | solution.py:305
  29.5 3.0 %collective-permute-done.5.panel = bf16[520,128]{1,0:T(8,128)(2,1)S(1)} collective-permute-done((bf16[520,128]{1,0:T(8,128)(2,1)S(1)}, bf16[520,128]{1,0:T(8,128)(2,1)S(1)}, u32[]{:S(2)}, u32[]{:S(2)}) %collective-permute-start.5) | collective-permute-done | bytes 133152 | tf_op jit(solution)/shard_map/ppermute | solution.py:305
  32.4 3.3 %shard_map.61 = (f32[512,128]{1,0:T(8,128)S(1)}, f32[128,1024]{1,0:T(8,128)S(1)}, f32[512,128]{1,0:T(8,128)S(1)}, bf16[520,128]{1,0:T(8,128)(2,1)S(1)}) custom-call(f32[2,128]{1,0:T(2,128)S(1)} %broadcast_in_dim.2.numbers, bf16[512,1024]{1,0:T(8,128)(2,1)S(1)} %collective-permute-done.4.above, bf16[520,128]{1,0:T(8,128)(2,1)S(1)} %collective-permute-done.5.panel, ...), custom_call_target="tpu_custom_call" | custom-call | flops 99999997952 | bytes 1 | tf_op jit(solution)/shard_map/pallas_call | solution.py:17
  35.8 10.7 %collective-permute-done.3.below.marked = bf16[264,1152]{1,0:T(8,128)(2,1)S(1)} collective-permute-done((bf16[264,1152]{1,0:T(8,128)(2,1)}, bf16[264,1152]{1,0:T(8,128)(2,1)S(1)}, u32[]{:S(2)}, u32[]{:S(2)}) %collective-permute-start.3) | collective-permute-done | bytes 608288 | tf_op jit(solution)/shard_map/ppermute | solution.py:305
  46.5 2.5 %shard_map.62 = (f32[256,128]{1,0:T(8,128)S(1)}, f32[128,1024]{1,0:T(8,128)S(1)}) custom-call(f32[2,128]{1,0:T(2,128)S(1)} %broadcast_in_dim.2.numbers, bf16[264,1152]{1,0:T(8,128)(2,1)S(1)} %collective-permute-done.3.below.marked, bf16[256,1152]{1,0:T(8,128)(2,1)} %get-tuple-element.34.first, bf16[264,1152]{1,0:T(8,128)(2,1)S(1)} %get-tuple-element.28.last, ...), custom_call_target="tpu_custom_call" | custom-call | flops 99999997952 | bytes 1 | tf_op jit(solution)/shard_map/pallas_call | solution.py:17
  49.0 0.5 collective-permute-start.8
  49.5 1.5 %shard_map.63 = (f32[512,128]{1,0:T(8,128)S(1)}, f32[256,128]{1,0:T(8,128)S(1)}, f32[256,128]{1,0:T(8,128)S(1)}) custom-call(f32[2,128]{1,0:T(2,128)S(1)} %broadcast_in_dim.2.numbers, bf16[512,1024]{1,0:T(8,128)(2,1)S(1)} %collective-permute-done.4.above, bf16[520,128]{1,0:T(8,128)(2,1)S(1)} %get-tuple-element.39.panel, ...), custom_call_target="tpu_custom_call" | custom-call | flops 99999997952 | bytes 1 | tf_op jit(solution)/shard_map/pallas_call | solution.py:17
  51.4 2.5 %shard_map.64 = (f32[512,128]{1,0:T(8,128)S(1)}, f32[256,128]{1,0:T(8,128)S(1)}, f32[256,128]{1,0:T(8,128)S(1)}) custom-call(f32[2,128]{1,0:T(2,128)S(1)} %broadcast_in_dim.2.numbers, bf16[512,1024]{1,0:T(8,128)(2,1)S(1)} %collective-permute-done.4.above, bf16[520,128]{1,0:T(8,128)(2,1)S(1)} %get-tuple-element.39.panel, ...), custom_call_target="tpu_custom_call" | custom-call | flops 99999997952 | bytes 1 | tf_op jit(solution)/shard_map/pallas_call | solution.py:17
  54.5 2.8 %shard_map.65 = (f32[256,128]{1,0:T(8,128)S(1)}, f32[512,128]{1,0:T(8,128)S(1)}, f32[512,128]{1,0:T(8,128)S(1)}) custom-call(f32[2,128]{1,0:T(2,128)S(1)} %broadcast_in_dim.2.numbers, bf16[264,1152]{1,0:T(8,128)(2,1)S(1)} %collective-permute-done.3.below.marked, bf16[256,1152]{1,0:T(8,128)(2,1)} %collective-permute-done.6.below, ...), custom_call_target="tpu_custom_call" | custom-call | flops 99999997952 | bytes 1 | tf_op jit(solution)/shard_map/pallas_call | solution.py:17
  57.2 0.5 collective-permute-start.9
  58.0 0.9 collective-permute-done.9.cross
  58.9 6.1 %collective-permute-done.12.above = f32[512,128]{1,0:T(8,128)S(1)} collective-permute-done((f32[512,128]{1,0:T(8,128)S(1)}, f32[512,128]{1,0:T(8,128)S(1)}, u32[]{:S(2)}, u32[]{:S(2)}) %collective-permute-start.12) | collective-permute-done | bytes 262176 | tf_op jit(solution)/shard_map/ppermute | solution.py:305
  65.0 1.3 %collective-permute-done.11.below = f32[512,128]{1,0:T(8,128)S(1)} collective-permute-done((f32[512,128]{1,0:T(8,128)S(1)}, f32[512,128]{1,0:T(8,128)S(1)}, u32[]{:S(2)}, u32[]{:S(2)}) %collective-permute-start.11) | collective-permute-done | bytes 262176 | tf_op jit(solution)/shard_map/ppermute | solution.py:305
  66.8 1.2 %collective-permute-done.13 = f32[128,128]{1,0:T(8,128)S(1)} collective-permute-done((f32[128,128]{1,0:T(8,128)S(1)}, f32[128,128]{1,0:T(8,128)S(1)}, u32[]{:S(2)}, u32[]{:S(2)}) %collective-permute-start.13) | collective-permute-done | bytes 65568 | tf_op jit(solution)/shard_map/ppermute | solution.py:304
  68.1 5.2 %collective-permute-start.14 = (f32[128,128]{1,0:T(8,128)S(1)}, f32[128,128]{1,0:T(8,128)S(1)}, u32[]{:S(2)}, u32[]{:S(2)}) collective-permute-start(f32[128,128]{1,0:T(8,128)S(1)} %add.20), channel_id=1, source_target_pairs={{0,2},{2,0},{4,6},{6,4},{8,10},{10,8},{12,14},{14,12},{1,3},{3,1},... | collective-permute-start | bytes 196616 | tf_op jit(solution)/shard_map/ppermute | solution.py:305
  73.3 2.4 %collective-permute-done.14 = f32[128,128]{1,0:T(8,128)S(1)} collective-permute-done((f32[128,128]{1,0:T(8,128)S(1)}, f32[128,128]{1,0:T(8,128)S(1)}, u32[]{:S(2)}, u32[]{:S(2)}) %collective-permute-start.14) | collective-permute-done | bytes 65568 | tf_op jit(solution)/shard_map/ppermute | solution.py:305
  75.7 0.6 collective-permute-start.15
  76.3 3.7 %collective-permute-done.15 = f32[128,128]{1,0:T(8,128)S(1)} collective-permute-done((f32[128,128]{1,0:T(8,128)S(1)}, f32[128,128]{1,0:T(8,128)S(1)}, u32[]{:S(2)}, u32[]{:S(2)}) %collective-permute-start.15) | collective-permute-done | bytes 65568 | tf_op jit(solution)/shard_map/ppermute | solution.py:305
  80.0 0.7 collective-permute-start.16
  80.7 5.3 %collective-permute-done.16 = f32[128,128]{1,0:T(8,128)S(1)} collective-permute-done((f32[128,128]{1,0:T(8,128)S(1)}, f32[128,128]{1,0:T(8,128)S(1)}, u32[]{:S(2)}, u32[]{:S(2)}) %collective-permute-start.16) | collective-permute-done | bytes 65568 | tf_op jit(solution)/shard_map/ppermute | solution.py:305
  86.0 5.2 %shard_map.67 = (f32[512,128]{1,0:T(8,128)}, f32[128,128]{1,0:T(8,128)}) custom-call(f32[512,128]{1,0:T(8,128)S(1)} %get-tuple-element.52.image, f32[128,128]{1,0:T(8,128)S(1)} %add.23.gram), custom_call_target="tpu_custom_call" | custom-call | flops 99999997952 | bytes 1 | tf_op jit(solution)/shard_map/pallas_call | solution.py:17
  (25 shorter events, 2.1 us)
Async XLA Ops:
  0.6 31.8 %collective-permute-start.4 = (bf16[512,1024]{1,0:T(8,128)(2,1)}, bf16[512,1024]{1,0:T(8,128)(2,1)S(1)}, u32[]{:S(2)}, u32[]{:S(2)}) collective-permute-start(bf16[512,1024]{1,0:T(8,128)(2,1)} %embeddings.1), channel_id=1, source_target_pairs={{0,12},{2,14},{4,0},{6,2},{8,4},{10,6},{12,8},{14,10},{1,13},{3,15... | collective-permute-start | bytes 3145736 | tf_op jit(solution)/shard_map/ppermute | solution.py:305
  5.7 1.3 %copy-start = (bf16[512,1024]{1,0:T(8,128)(2,1)S(1)}, bf16[512,1024]{1,0:T(8,128)(2,1)}, u32[]{:S(2)}) copy-start(bf16[512,1024]{1,0:T(8,128)(2,1)} %embeddings.1) | copy-start | bytes 3145732
  7.0 0.9 copy-start.1
  7.9 0.7 copy-start.2
  9.8 3.7 %collective-permute-start.2 = (bf16[264,1152]{1,0:T(8,128)(2,1)S(1)}, bf16[264,1152]{1,0:T(8,128)(2,1)S(1)}, u32[]{:S(2)}, u32[]{:S(2)}) collective-permute-start(bf16[264,1152]{1,0:T(8,128)(2,1)S(1)} %get-tuple-element.28.last), channel_id=1, source_target_pairs={{0,1},{1,0},{2,3},{3,2},{4,5},{5,4},{6,7},{7,6},{8,9},{9,8},{10,11... | collective-permute-start | bytes 1824776 | tf_op jit(solution)/shard_map/ppermute | solution.py:304
  9.8 16.2 %collective-permute-start = (bf16[264,1152]{1,0:T(8,128)(2,1)S(1)}, bf16[264,1152]{1,0:T(8,128)(2,1)}, u32[]{:S(2)}, u32[]{:S(2)}) collective-permute-start(bf16[264,1152]{1,0:T(8,128)(2,1)S(1)} %get-tuple-element.28.last), channel_id=1, source_target_pairs={{0,2},{2,0},{4,6},{6,4},{8,10},{10,8},{12,14},{14,12},{1,3},{3,1},... | collective-permute-start | bytes 1824776 | tf_op jit(solution)/shard_map/ppermute | solution.py:305
  11.3 2.2 %collective-permute-start.1 = (bf16[256,1152]{1,0:T(8,128)(2,1)}, bf16[256,1152]{1,0:T(8,128)(2,1)S(1)}, u32[]{:S(2)}, u32[]{:S(2)}) collective-permute-start(bf16[256,1152]{1,0:T(8,128)(2,1)} %get-tuple-element.34.first), channel_id=1, source_target_pairs={{0,1},{1,0},{2,3},{3,2},{4,5},{5,4},{6,7},{7,6},{8,9},{9,8},{10,11... | collective-permute-start | bytes 1769480 | tf_op jit(solution)/shard_map/ppermute | solution.py:304
  11.5 20.9 %collective-permute-start.5 = (bf16[520,128]{1,0:T(8,128)(2,1)S(1)}, bf16[520,128]{1,0:T(8,128)(2,1)S(1)}, u32[]{:S(2)}, u32[]{:S(2)}) collective-permute-start(bf16[520,128]{1,0:T(8,128)(2,1)S(1)} %get-tuple-element.31), channel_id=1, source_target_pairs={{0,12},{2,14},{4,0},{6,2},{8,4},{10,6},{12,8},{14,10},{1,13},{3,15... | collective-permute-start | bytes 399368 | tf_op jit(solution)/shard_map/ppermute | solution.py:305
  26.0 22.9 %collective-permute-start.6 = (bf16[256,1152]{1,0:T(8,128)(2,1)}, bf16[256,1152]{1,0:T(8,128)(2,1)}, u32[]{:S(2)}, u32[]{:S(2)}) collective-permute-start(bf16[256,1152]{1,0:T(8,128)(2,1)} %get-tuple-element.34.first), channel_id=1, source_target_pairs={{0,2},{2,4},{4,6},{6,8},{8,10},{10,12},{12,14},{14,0},{1,3},{3,5},... | collective-permute-start | bytes 1769480 | tf_op jit(solution)/shard_map/ppermute | solution.py:305
  27.5 19.0 %collective-permute-start.3 = (bf16[264,1152]{1,0:T(8,128)(2,1)}, bf16[264,1152]{1,0:T(8,128)(2,1)S(1)}, u32[]{:S(2)}, u32[]{:S(2)}) collective-permute-start(bf16[264,1152]{1,0:T(8,128)(2,1)} %collective-permute-done), channel_id=1, source_target_pairs={{0,4},{2,2},{4,8},{6,6},{8,12},{10,10},{12,0},{14,14},{1,5},{3,3},... | collective-permute-start | bytes 1824776 | tf_op jit(solution)/shard_map/ppermute | solution.py:305
  46.5 3.0 %collective-permute-start.7 = (bf16[264,1152]{1,0:T(8,128)(2,1)S(1)}, bf16[264,1152]{1,0:T(8,128)(2,1)S(1)}, u32[]{:S(2)}, u32[]{:S(2)}) collective-permute-start(bf16[264,1152]{1,0:T(8,128)(2,1)S(1)} %collective-permute-done.3.below.marked), channel_id=1, source_target_pairs={{0,1},{1,0},{2,3},{3,2},{4,5},{5,4},{6,7},{7,6},{8,9},{9,8},{10,11... | collective-permute-start | bytes 1824776 | tf_op jit(solution)/shard_map/ppermute | solution.py:304
  49.0 2.4 %collective-permute-start.8 = (bf16[256,1152]{1,0:T(8,128)(2,1)}, bf16[256,1152]{1,0:T(8,128)(2,1)S(1)}, u32[]{:S(2)}, u32[]{:S(2)}) collective-permute-start(bf16[256,1152]{1,0:T(8,128)(2,1)} %collective-permute-done.6.below), channel_id=1, source_target_pairs={{0,1},{1,0},{2,3},{3,2},{4,5},{5,4},{6,7},{7,6},{8,9},{9,8},{10,11... | collective-permute-start | bytes 1769480 | tf_op jit(solution)/shard_map/ppermute | solution.py:304
  53.9 11.0 %collective-permute-start.12 = (f32[512,128]{1,0:T(8,128)S(1)}, f32[512,128]{1,0:T(8,128)S(1)}, u32[]{:S(2)}, u32[]{:S(2)}) collective-permute-start(f32[512,128]{1,0:T(8,128)S(1)} %get-tuple-element.43), channel_id=1, source_target_pairs={{0,4},{2,6},{4,8},{6,10},{8,12},{10,14},{12,0},{14,2},{1,5},{3,7},... | collective-permute-start | bytes 786440 | tf_op jit(solution)/shard_map/ppermute | solution.py:305
  54.3 3.4 %collective-permute-start.10 = (f32[512,128]{1,0:T(8,128)S(1)}, f32[512,128]{1,0:T(8,128)S(1)}, u32[]{:S(2)}, u32[]{:S(2)}) collective-permute-start(f32[512,128]{1,0:T(8,128)S(1)} %pad_maximum_fusion), channel_id=1, source_target_pairs={{0,1},{1,0},{2,3},{3,2},{4,5},{5,4},{6,7},{7,6},{8,9},{9,8},{10,11... | collective-permute-start | bytes 786440 | tf_op jit(solution)/shard_map/ppermute | solution.py:304
  57.2 1.6 %collective-permute-start.9 = (f32[512,128]{1,0:T(8,128)S(1)}, f32[512,128]{1,0:T(8,128)S(1)}, u32[]{:S(2)}, u32[]{:S(2)}) collective-permute-start(f32[512,128]{1,0:T(8,128)S(1)} %get-tuple-element.46), channel_id=1, source_target_pairs={{0,1},{1,0},{2,3},{3,2},{4,5},{5,4},{6,7},{7,6},{8,9},{9,8},{10,11... | collective-permute-start | bytes 786440 | tf_op jit(solution)/shard_map/ppermute | solution.py:304
  57.7 8.6 %collective-permute-start.11 = (f32[512,128]{1,0:T(8,128)S(1)}, f32[512,128]{1,0:T(8,128)S(1)}, u32[]{:S(2)}, u32[]{:S(2)}) collective-permute-start(f32[512,128]{1,0:T(8,128)S(1)} %fusion), channel_id=1, source_target_pairs={{0,14},{2,0},{4,2},{6,4},{8,6},{10,8},{12,10},{14,12},{1,15},{3,1}... | collective-permute-start | bytes 786440 | tf_op jit(solution)/shard_map/ppermute | solution.py:305
  66.7 1.3 %collective-permute-start.13 = (f32[128,128]{1,0:T(8,128)S(1)}, f32[128,128]{1,0:T(8,128)S(1)}, u32[]{:S(2)}, u32[]{:S(2)}) collective-permute-start(f32[128,128]{1,0:T(8,128)S(1)} %get-tuple-element.53), channel_id=1, source_target_pairs={{0,1},{1,0},{2,3},{3,2},{4,5},{5,4},{6,7},{7,6},{8,9},{9,8},{10,11... | collective-permute-start | bytes 196616 | tf_op jit(solution)/shard_map/ppermute | solution.py:304
  68.1 7.6 %collective-permute-start.14 = (f32[128,128]{1,0:T(8,128)S(1)}, f32[128,128]{1,0:T(8,128)S(1)}, u32[]{:S(2)}, u32[]{:S(2)}) collective-permute-start(f32[128,128]{1,0:T(8,128)S(1)} %add.20), channel_id=1, source_target_pairs={{0,2},{2,0},{4,6},{6,4},{8,10},{10,8},{12,14},{14,12},{1,3},{3,1},... | collective-permute-start | bytes 196616 | tf_op jit(solution)/shard_map/ppermute | solution.py:305
  75.7 4.3 %collective-permute-start.15 = (f32[128,128]{1,0:T(8,128)S(1)}, f32[128,128]{1,0:T(8,128)S(1)}, u32[]{:S(2)}, u32[]{:S(2)}) collective-permute-start(f32[128,128]{1,0:T(8,128)S(1)} %add.21), channel_id=1, source_target_pairs={{0,4},{2,6},{4,0},{6,2},{8,12},{10,14},{12,8},{14,10},{1,5},{3,7},... | collective-permute-start | bytes 196616 | tf_op jit(solution)/shard_map/ppermute | solution.py:305
  80.0 5.9 %collective-permute-start.16 = (f32[128,128]{1,0:T(8,128)S(1)}, f32[128,128]{1,0:T(8,128)S(1)}, u32[]{:S(2)}, u32[]{:S(2)}) collective-permute-start(f32[128,128]{1,0:T(8,128)S(1)} %add.22), channel_id=1, source_target_pairs={{0,8},{2,10},{4,12},{6,14},{8,0},{10,2},{12,4},{14,6},{1,9},{3,11}... | collective-permute-start | bytes 196616 | tf_op jit(solution)/shard_map/ppermute | solution.py:305

commit v16 on v13

--- a/solution.py
+++ b/solution.py
@@ -168,9 +168,9 @@
     image[...], _ = products(width_of(numbers), own, [as_column(r) for r in rows], columns, None)
 
 
-def own_columns(sub, mark, first, last, other_first, other_last, offset):
+def own_columns(place_here, mark, first, last, other_first, other_last, offset):
     half = 2 * last.shape[0]
-    masks = masks_of(sub, mark, [marks(r, half) for r in (first, other_first)], offset)
+    masks = masks_of(place_here, mark, [marks(r, half) for r in (first, other_first)], offset)
     rows = square_rows(first) + square_rows(other_first)
     return columns_of(pieces(first, last), pieces(other_first, other_last), rows, masks)
 
@@ -205,15 +205,26 @@
     own_cross[...] = total[:, half:].T
 
 
-def above_below_body(numbers, above, panel, above_sq, below0, below1, other0, other1, above_image, image, below_image, cross):
+def above_below(part, numbers, above, panel, above_sq, marked, other_marked, below, other, above_image, image, below_image, cross):
     half = image.shape[0]
     size = half // 2
-    columns = own_columns(place(numbers), marks(panel, half), below0, below1, other0, other1, ABOVE - BELOW)
+    masks = masks_of(place(numbers), marks(panel, half), [marks(r, half) for r in (marked, other_marked)], ABOVE - BELOW)
+    masks = [mask[:, part * size : (part + 1) * size] for mask in masks]
+    columns_sq = [square_rows(r)[part] for r in (marked, other_marked)]
+    columns = columns_of([(below[:size, :-TILE], below[:size, -TILE:])], [(other[:size, :-TILE], other[:size, -TILE:])], columns_sq, masks)
     rows_sq = [above_sq[k * size : (k + 1) * size, :1] for k in range(2)]
-    products_image, total = products(width_of(numbers), apart(above, panel), rows_sq, columns, jnp.zeros((TILE, 2 * half), F32))
+    products_image, total = products(width_of(numbers), apart(above, panel), rows_sq, columns, jnp.zeros((TILE, half), F32))
     image[...] = above_image[...] + products_image
-    below_image[...] = total[:, :half].T
-    cross[...] = total[:, half:].T
+    below_image[...] = total[:, :size].T
+    cross[...] = total[:, size:].T
+
+
+def above_below_first_body(numbers, above, panel, above_sq, below, other, above_image, *outs):
+    above_below(0, numbers, above, panel, above_sq, below, other, below, other, above_image, *outs)
+
+
+def above_below_last_body(numbers, above, panel, above_sq, marked, other_marked, below, other, above_image, *outs):
+    above_below(1, numbers, above, panel, above_sq, marked, other_marked, below, other, above_image, *outs)
 
 
 def gram_body(own, cross, below, above, image, gram):
@@ -325,36 +336,27 @@
         above_panel,
         *own,
     )
-    below0, below1 = after(below0, above_image, below1), after(below1, above_image, below0)
-    below_other = (sub_move(below0), sub_move(below1))
-    below_image0, back = vmem_call(
-        below_first_body, (shape(size, width), turned), numbers, below0, *own, back
-    )
-    above_image, below_sum, below_cross = vmem_call(
-        above_below_body,
-        (image,) * 3,
-        numbers,
-        above,
-        above_panel,
-        above_sq,
-        below0,
-        below1,
-        *below_other,
-        after(above_image, below_image0),
+    piece = shape(size, width)
+    below0 = after(below0, above_image)
+    other0 = sub_move(below0)
+    below_image0, back = vmem_call(below_first_body, (piece, turned), numbers, below0, *own, back)
+    below1 = after(below1, below_image0)
+    other1 = sub_move(below1)
+    here = (numbers, above, above_panel, above_sq)
+    above_image, below_sum0, below_cross0 = vmem_call(
+        above_below_first_body, (image, piece, piece), *here, below0, other0, after(above_image, below1)
+    )
+    above_image, below_sum1, below_cross1 = vmem_call(
+        above_below_last_body, (image, piece, piece), *here, below0, other0, below1, other1, above_image
     )
     below_image1, own_image, own_cross = vmem_call(
-        below_last_body,
-        (shape(size, width), image, image),
-        numbers,
-        below0,
-        below1,
-        *own,
-        self_image,
-        after(back, above_image),
+        below_last_body, (piece, image, image), numbers, below0, below1, *own, self_image, after(back, above_image)
     )
     above_image = blk_move(above_image, 2)
-    below_image = jnp.concatenate([below_image0, below_image1], axis=0)
-    below_image = blk_move(below_sum + sub_move(below_cross) + below_image, -1)
+    join = lambda *parts: jnp.concatenate(parts, axis=0)
+    below_cross = sub_move(join(below_cross0, below_cross1))
+    below_image = join(below_sum0, below_sum1) + below_cross + join(below_image0, below_image1)
+    below_image = blk_move(below_image, -1)
     image_rows, gram = vmem_call(
         gram_body, (image, shape(width, width)), own_image, sub_move(own_cross), below_image, above_image
     )

time: 88.6 us -> 90.2 us (1.018)
  waiting for transfers between devices: 46 us -> 38.7 us
  starting transfers between devices: 20.6 us -> 26.5 us
  Pallas kernels: 17.3 us -> 19.9 us
    ppermute x10, waiting for transfers between devices: 43.8 us -> 37.1 us  [per_device(): lax.ppermute(v, 'blk', [(i, to(i) % n_blk) for i in range(n_blk)])]
    ppermute x10, starting transfers between devices: 19 us -> 24.7 us  [per_device(): lax.ppermute(v, 'blk', [(i, to(i) % n_blk) for i in range(n_blk)])]
    pallas_call x8 -> x9, Pallas kernels: 17.3 us -> 19.9 us  [vmem_call(): pl.pallas_call(body, out_shape=out_shapes, in_specs=[in_vmem] * len(opera...]
  transfers between devices with their start and end apart: 17 -> 17, of which waited for: 12 -> 10; matrix products, arithmetic and copies ran while one was open for 0% -> 0% of each run, Pallas kernels for 10% -> 13%
where the time goes in v16:
time: 90.2 us; the launch traced here: 89.6 us
  waiting for transfers between devices  38.7 us (43%)
  starting transfers between devices  26.5 us (29%)
  Pallas kernels  19.9 us (22%)
  local copies, waits for them, and re-layouts  2.91 us (3%)
  between operations  1.39 us (2%)
    ppermute x10, waiting for transfers between devices, per_device(): lax.ppermute(v, 'blk', [(i, to(i) % n_blk) for i in range(n_blk)])  37.1 us
    ppermute x10, starting transfers between devices, per_device(): lax.ppermute(v, 'blk', [(i, to(i) % n_blk) for i in range(n_blk)])  24.7 us
    pallas_call x9, Pallas kernels, vmem_call(): pl.pallas_call(body, out_shape=out_shapes, in_specs=[in_vmem] * len(opera...  19.9 us
    unnamed x6, local copies, waits for them, and re-layouts  2.84 us
  transfers between devices with their start and end apart: 17, of which 10 were waited for; matrix products, arithmetic and copies ran while one was open for 0% of the time, Pallas kernels for 13%

profile of v16, /device:TPU:0, one launch (start us, length us, event | category | flops | bytes accessed | tf_op | source)
XLA Modules:
  0.0 89.6 jit_solution(4573724445366003793)
XLA Ops:
  0.6 5.1 %collective-permute-start.4 = (bf16[512,1024]{1,0:T(8,128)(2,1)}, bf16[512,1024]{1,0:T(8,128)(2,1)S(1)}, u32[]{:S(2)}, u32[]{:S(2)}) collective-permute-start(bf16[512,1024]{1,0:T(8,128)(2,1)} %embeddings.1), channel_id=1, source_target_pairs={{0,12},{2,14},{4,0},{6,2},{8,4},{10,6},{12,8},{14,10},{1,13},{3,15... | collective-permute-start | bytes 3145736 | tf_op jit(solution)/shard_map/ppermute | solution.py:305
  5.7 1.3 %copy-done = bf16[512,1024]{1,0:T(8,128)(2,1)S(1)} copy-done((bf16[512,1024]{1,0:T(8,128)(2,1)S(1)}, bf16[512,1024]{1,0:T(8,128)(2,1)}, u32[]{:S(2)}) %copy-start) | copy-done | bytes 1048600
  7.0 0.9 %copy-done.1 = bf16[512,128]{1,0:T(8,128)(2,1)S(1)} copy-done((bf16[512,128]{1,0:T(8,128)(2,1)S(1)}, bf16[512,128]{1,0:T(8,128)(2,1)}, u32[]{:S(2)}) %copy-start.1) | copy-done | bytes 131096
  7.9 0.7 copy-done.2
  8.6 1.1 %shard_map.59 = (bf16[264,1152]{1,0:T(8,128)(2,1)S(1)}, bf16[256,1152]{1,0:T(8,128)(2,1)S(1)}, bf16[520,128]{1,0:T(8,128)(2,1)}) custom-call(bf16[512,1024]{1,0:T(8,128)(2,1)S(1)} %copy-done, bf16[512,128]{1,0:T(8,128)(2,1)S(1)} %copy-done.1, s32[4,56]{1,0:T(4,128)S(1)} %copy-done.2), custom_call_target="tpu_custom_call" | custom-call | flops 1 | bytes 1 | tf_op jit(solution)/shard_map/pallas_call | solution.py:17
  9.6 0.5 collective-permute-start.2
  10.1 1.5 %collective-permute-start = (bf16[256,1152]{1,0:T(8,128)(2,1)S(1)}, bf16[256,1152]{1,0:T(8,128)(2,1)}, u32[]{:S(2)}, u32[]{:S(2)}) collective-permute-start(bf16[256,1152]{1,0:T(8,128)(2,1)S(1)} %get-tuple-element.29.last), channel_id=1, source_target_pairs={{0,2},{2,0},{4,6},{6,4},{8,10},{10,8},{12,14},{14,12},{1,3},{3,1},... | collective-permute-start | bytes 1769480 | tf_op jit(solution)/shard_map/ppermute | solution.py:305
  11.6 0.4 collective-permute-start.5
  12.9 2.1 %shard_map.60.self_image = f32[512,128]{1,0:T(8,128)S(1)} custom-call(f32[2,128]{1,0:T(2,128)S(1)} %broadcast_in_dim.2.numbers, bf16[264,1152]{1,0:T(8,128)(2,1)S(1)} %get-tuple-element.30.first, bf16[256,1152]{1,0:T(8,128)(2,1)S(1)} %get-tuple-element.29.last, bf16[264,1152]{1,0:T(8,128)(2,1)S(1)} %collective-permute-done.1.other_first, ...), custom_call_target="tpu_custom_call" | custom-call | flops 1 | bytes 1 | tf_op jit(solution)/shard_map/pallas_call | solution.py:17
  15.0 10.5 %collective-permute-done = bf16[256,1152]{1,0:T(8,128)(2,1)} collective-permute-done((bf16[256,1152]{1,0:T(8,128)(2,1)S(1)}, bf16[256,1152]{1,0:T(8,128)(2,1)}, u32[]{:S(2)}, u32[]{:S(2)}) %collective-permute-start) | collective-permute-done | bytes 589856 | tf_op jit(solution)/shard_map/ppermute | solution.py:305
  25.5 1.9 %collective-permute-start.6 = (bf16[256,1152]{1,0:T(8,128)(2,1)}, bf16[256,1152]{1,0:T(8,128)(2,1)}, u32[]{:S(2)}, u32[]{:S(2)}) collective-permute-start(bf16[256,1152]{1,0:T(8,128)(2,1)} %collective-permute-done), channel_id=1, source_target_pairs={{0,4},{2,2},{4,8},{6,6},{8,12},{10,10},{12,0},{14,14},{1,5},{3,3},... | collective-permute-start | bytes 1769480 | tf_op jit(solution)/shard_map/ppermute | solution.py:305
  27.4 5.5 %collective-permute-start.3 = (bf16[264,1152]{1,0:T(8,128)(2,1)S(1)}, bf16[264,1152]{1,0:T(8,128)(2,1)S(1)}, u32[]{:S(2)}, u32[]{:S(2)}) collective-permute-start(bf16[264,1152]{1,0:T(8,128)(2,1)S(1)} %get-tuple-element.30.first), channel_id=1, source_target_pairs={{0,2},{2,4},{4,6},{6,8},{8,10},{10,12},{12,14},{14,0},{1,3},{3,5},... | collective-permute-start | bytes 1824776 | tf_op jit(solution)/shard_map/ppermute | solution.py:305
  32.9 3.2 %shard_map.61 = (f32[512,128]{1,0:T(8,128)S(1)}, f32[128,1024]{1,0:T(8,128)S(1)}, f32[512,128]{1,0:T(8,128)S(1)}, bf16[520,128]{1,0:T(8,128)(2,1)S(1)}) custom-call(f32[2,128]{1,0:T(2,128)S(1)} %broadcast_in_dim.2.numbers, bf16[512,1024]{1,0:T(8,128)(2,1)S(1)} %collective-permute-done.4.above, bf16[520,128]{1,0:T(8,128)(2,1)} %collective-permute-done.5.panel, ...), custom_call_target="tpu_custom_call" | custom-call | flops 99999997952 | bytes 1 | tf_op jit(solution)/shard_map/pallas_call | solution.py:17
  36.2 9.9 %collective-permute-done.3.below.marked = bf16[264,1152]{1,0:T(8,128)(2,1)S(1)} collective-permute-done((bf16[264,1152]{1,0:T(8,128)(2,1)S(1)}, bf16[264,1152]{1,0:T(8,128)(2,1)S(1)}, u32[]{:S(2)}, u32[]{:S(2)}) %collective-permute-start.3) | collective-permute-done | bytes 608288 | tf_op jit(solution)/shard_map/ppermute | solution.py:305
  46.1 1.4 %shard_map.62 = (f32[256,128]{1,0:T(8,128)S(1)}, f32[128,1024]{1,0:T(8,128)S(1)}) custom-call(f32[2,128]{1,0:T(2,128)S(1)} %broadcast_in_dim.2.numbers, bf16[264,1152]{1,0:T(8,128)(2,1)S(1)} %collective-permute-done.3.below.marked, bf16[264,1152]{1,0:T(8,128)(2,1)S(1)} %get-tuple-element.30.first, bf16[256,1152]{1,0:T(8,128)(2,1)S(1)} %get-tuple-element.29.last, ...), custom_call_target="tpu_custom_call" | custom-call | flops 99999997952 | bytes 1 | tf_op jit(solution)/shard_map/pallas_call | solution.py:17
  47.5 0.6 collective-permute-start.8
  48.1 1.5 %shard_map.63 = (f32[512,128]{1,0:T(8,128)S(1)}, f32[256,128]{1,0:T(8,128)S(1)}, f32[256,128]{1,0:T(8,128)S(1)}) custom-call(f32[2,128]{1,0:T(2,128)S(1)} %broadcast_in_dim.2.numbers, bf16[512,1024]{1,0:T(8,128)(2,1)S(1)} %collective-permute-done.4.above, bf16[520,128]{1,0:T(8,128)(2,1)S(1)} %get-tuple-element.39.panel, ...), custom_call_target="tpu_custom_call" | custom-call | flops 99999997952 | bytes 1 | tf_op jit(solution)/shard_map/pallas_call | solution.py:17
  49.9 2.5 %shard_map.64 = (f32[512,128]{1,0:T(8,128)S(1)}, f32[256,128]{1,0:T(8,128)S(1)}, f32[256,128]{1,0:T(8,128)S(1)}) custom-call(f32[2,128]{1,0:T(2,128)S(1)} %broadcast_in_dim.2.numbers, bf16[512,1024]{1,0:T(8,128)(2,1)S(1)} %collective-permute-done.4.above, bf16[520,128]{1,0:T(8,128)(2,1)S(1)} %get-tuple-element.39.panel, ...), custom_call_target="tpu_custom_call" | custom-call | flops 99999997952 | bytes 1 | tf_op jit(solution)/shard_map/pallas_call | solution.py:17
  52.4 1.7 %collective-permute-start.12 = (f32[512,128]{1,0:T(8,128)S(1)}, f32[512,128]{1,0:T(8,128)S(1)}, u32[]{:S(2)}, u32[]{:S(2)}) collective-permute-start(f32[512,128]{1,0:T(8,128)S(1)} %get-tuple-element.43), channel_id=1, source_target_pairs={{0,4},{2,6},{4,8},{6,10},{8,12},{10,14},{12,0},{14,2},{1,5},{3,7},... | collective-permute-start | bytes 786440 | tf_op jit(solution)/shard_map/ppermute | solution.py:305
  54.3 2.6 %shard_map.65 = (f32[256,128]{1,0:T(8,128)S(1)}, f32[512,128]{1,0:T(8,128)S(1)}, f32[512,128]{1,0:T(8,128)S(1)}) custom-call(f32[2,128]{1,0:T(2,128)S(1)} %broadcast_in_dim.2.numbers, bf16[264,1152]{1,0:T(8,128)(2,1)S(1)} %collective-permute-done.3.below.marked, bf16[256,1152]{1,0:T(8,128)(2,1)} %collective-permute-done.6.below, ...), custom_call_target="tpu_custom_call" | custom-call | flops 99999997952 | bytes 1 | tf_op jit(solution)/shard_map/pallas_call | solution.py:17
  56.9 0.5 collective-permute-start.9
  57.4 3.5 %collective-permute-start.11 = (f32[512,128]{1,0:T(8,128)S(1)}, f32[512,128]{1,0:T(8,128)S(1)}, u32[]{:S(2)}, u32[]{:S(2)}) collective-permute-start(f32[512,128]{1,0:T(8,128)S(1)} %fusion), channel_id=1, source_target_pairs={{0,14},{2,0},{4,2},{6,4},{8,6},{10,8},{12,10},{14,12},{1,15},{3,1}... | collective-permute-start | bytes 786440 | tf_op jit(solution)/shard_map/ppermute | solution.py:305
  60.9 2.5 %collective-permute-done.12.above = f32[512,128]{1,0:T(8,128)S(1)} collective-permute-done((f32[512,128]{1,0:T(8,128)S(1)}, f32[512,128]{1,0:T(8,128)S(1)}, u32[]{:S(2)}, u32[]{:S(2)}) %collective-permute-start.12) | collective-permute-done | bytes 262176 | tf_op jit(solution)/shard_map/ppermute | solution.py:305
  63.4 3.3 %collective-permute-done.11.below = f32[512,128]{1,0:T(8,128)S(1)} collective-permute-done((f32[512,128]{1,0:T(8,128)S(1)}, f32[512,128]{1,0:T(8,128)S(1)}, u32[]{:S(2)}, u32[]{:S(2)}) %collective-permute-start.11) | collective-permute-done | bytes 262176 | tf_op jit(solution)/shard_map/ppermute | solution.py:305
  67.2 1.2 %collective-permute-done.13 = f32[128,128]{1,0:T(8,128)S(1)} collective-permute-done((f32[128,128]{1,0:T(8,128)S(1)}, f32[128,128]{1,0:T(8,128)S(1)}, u32[]{:S(2)}, u32[]{:S(2)}) %collective-permute-start.13) | collective-permute-done | bytes 65568 | tf_op jit(solution)/shard_map/ppermute | solution.py:304
  68.5 3.3 %collective-permute-start.14 = (f32[128,128]{1,0:T(8,128)S(1)}, f32[128,128]{1,0:T(8,128)S(1)}, u32[]{:S(2)}, u32[]{:S(2)}) collective-permute-start(f32[128,128]{1,0:T(8,128)S(1)} %add.20), channel_id=1, source_target_pairs={{0,2},{2,0},{4,6},{6,4},{8,10},{10,8},{12,14},{14,12},{1,3},{3,1},... | collective-permute-start | bytes 196616 | tf_op jit(solution)/shard_map/ppermute | solution.py:305
  71.8 2.4 %collective-permute-done.14 = f32[128,128]{1,0:T(8,128)S(1)} collective-permute-done((f32[128,128]{1,0:T(8,128)S(1)}, f32[128,128]{1,0:T(8,128)S(1)}, u32[]{:S(2)}, u32[]{:S(2)}) %collective-permute-start.14) | collective-permute-done | bytes 65568 | tf_op jit(solution)/shard_map/ppermute | solution.py:305
  74.2 0.6 collective-permute-start.15
  74.8 3.7 %collective-permute-done.15 = f32[128,128]{1,0:T(8,128)S(1)} collective-permute-done((f32[128,128]{1,0:T(8,128)S(1)}, f32[128,128]{1,0:T(8,128)S(1)}, u32[]{:S(2)}, u32[]{:S(2)}) %collective-permute-start.15) | collective-permute-done | bytes 65568 | tf_op jit(solution)/shard_map/ppermute | solution.py:305
  78.6 1.1 %collective-permute-start.16 = (f32[128,128]{1,0:T(8,128)S(1)}, f32[128,128]{1,0:T(8,128)S(1)}, u32[]{:S(2)}, u32[]{:S(2)}) collective-permute-start(f32[128,128]{1,0:T(8,128)S(1)} %add.22), channel_id=1, source_target_pairs={{0,8},{2,10},{4,12},{6,14},{8,0},{10,2},{12,4},{14,6},{1,9},{3,11}... | collective-permute-start | bytes 196616 | tf_op jit(solution)/shard_map/ppermute | solution.py:305
  79.7 4.8 %collective-permute-done.16 = f32[128,128]{1,0:T(8,128)S(1)} collective-permute-done((f32[128,128]{1,0:T(8,128)S(1)}, f32[128,128]{1,0:T(8,128)S(1)}, u32[]{:S(2)}, u32[]{:S(2)}) %collective-permute-start.16) | collective-permute-done | bytes 65568 | tf_op jit(solution)/shard_map/ppermute | solution.py:305
  84.5 5.1 %shard_map.67 = (f32[512,128]{1,0:T(8,128)}, f32[128,128]{1,0:T(8,128)}) custom-call(f32[512,128]{1,0:T(8,128)S(1)} %get-tuple-element.52.image, f32[128,128]{1,0:T(8,128)S(1)} %add.23.gram), custom_call_target="tpu_custom_call" | custom-call | flops 99999997952 | bytes 1 | tf_op jit(solution)/shard_map/pallas_call | solution.py:17
  (25 shorter events, 1.2 us)
Async XLA Ops:
  0.6 32.3 %collective-permute-start.4 = (bf16[512,1024]{1,0:T(8,128)(2,1)}, bf16[512,1024]{1,0:T(8,128)(2,1)S(1)}, u32[]{:S(2)}, u32[]{:S(2)}) collective-permute-start(bf16[512,1024]{1,0:T(8,128)(2,1)} %embeddings.1), channel_id=1, source_target_pairs={{0,12},{2,14},{4,0},{6,2},{8,4},{10,6},{12,8},{14,10},{1,13},{3,15... | collective-permute-start | bytes 3145736 | tf_op jit(solution)/shard_map/ppermute | solution.py:305
  5.7 1.3 %copy-start = (bf16[512,1024]{1,0:T(8,128)(2,1)S(1)}, bf16[512,1024]{1,0:T(8,128)(2,1)}, u32[]{:S(2)}) copy-start(bf16[512,1024]{1,0:T(8,128)(2,1)} %embeddings.1) | copy-start | bytes 3145732
  7.0 0.9 %copy-start.1 = (bf16[512,128]{1,0:T(8,128)(2,1)S(1)}, bf16[512,128]{1,0:T(8,128)(2,1)}, u32[]{:S(2)}) copy-start(bf16[512,128]{1,0:T(8,128)(2,1)} %panel.1) | copy-start | bytes 393220
  7.9 0.7 copy-start.2
  9.6 3.2 %collective-permute-start.1 = (bf16[264,1152]{1,0:T(8,128)(2,1)S(1)}, bf16[264,1152]{1,0:T(8,128)(2,1)S(1)}, u32[]{:S(2)}, u32[]{:S(2)}) collective-permute-start(bf16[264,1152]{1,0:T(8,128)(2,1)S(1)} %get-tuple-element.30.first), channel_id=1, source_target_pairs={{0,1},{1,0},{2,3},{3,2},{4,5},{5,4},{6,7},{7,6},{8,9},{9,8},{10,11... | collective-permute-start | bytes 1824776 | tf_op jit(solution)/shard_map/ppermute | solution.py:304
  9.6 3.2 %collective-permute-start.2 = (bf16[256,1152]{1,0:T(8,128)(2,1)S(1)}, bf16[256,1152]{1,0:T(8,128)(2,1)S(1)}, u32[]{:S(2)}, u32[]{:S(2)}) collective-permute-start(bf16[256,1152]{1,0:T(8,128)(2,1)S(1)} %get-tuple-element.29.last), channel_id=1, source_target_pairs={{0,1},{1,0},{2,3},{3,2},{4,5},{5,4},{6,7},{7,6},{8,9},{9,8},{10,11... | collective-permute-start | bytes 1769480 | tf_op jit(solution)/shard_map/ppermute | solution.py:304
  10.1 15.3 %collective-permute-start = (bf16[256,1152]{1,0:T(8,128)(2,1)S(1)}, bf16[256,1152]{1,0:T(8,128)(2,1)}, u32[]{:S(2)}, u32[]{:S(2)}) collective-permute-start(bf16[256,1152]{1,0:T(8,128)(2,1)S(1)} %get-tuple-element.29.last), channel_id=1, source_target_pairs={{0,2},{2,0},{4,6},{6,4},{8,10},{10,8},{12,14},{14,12},{1,3},{3,1},... | collective-permute-start | bytes 1769480 | tf_op jit(solution)/shard_map/ppermute | solution.py:305
  11.6 21.3 %collective-permute-start.5 = (bf16[520,128]{1,0:T(8,128)(2,1)}, bf16[520,128]{1,0:T(8,128)(2,1)}, u32[]{:S(2)}, u32[]{:S(2)}) collective-permute-start(bf16[520,128]{1,0:T(8,128)(2,1)} %get-tuple-element.31), channel_id=1, source_target_pairs={{0,12},{2,14},{4,0},{6,2},{8,4},{10,6},{12,8},{14,10},{1,13},{3,15... | collective-permute-start | bytes 399368 | tf_op jit(solution)/shard_map/ppermute | solution.py:305
  25.5 22.0 %collective-permute-start.6 = (bf16[256,1152]{1,0:T(8,128)(2,1)}, bf16[256,1152]{1,0:T(8,128)(2,1)}, u32[]{:S(2)}, u32[]{:S(2)}) collective-permute-start(bf16[256,1152]{1,0:T(8,128)(2,1)} %collective-permute-done), channel_id=1, source_target_pairs={{0,4},{2,2},{4,8},{6,6},{8,12},{10,10},{12,0},{14,14},{1,5},{3,3},... | collective-permute-start | bytes 1769480 | tf_op jit(solution)/shard_map/ppermute | solution.py:305
  27.4 18.7 %collective-permute-start.3 = (bf16[264,1152]{1,0:T(8,128)(2,1)S(1)}, bf16[264,1152]{1,0:T(8,128)(2,1)S(1)}, u32[]{:S(2)}, u32[]{:S(2)}) collective-permute-start(bf16[264,1152]{1,0:T(8,128)(2,1)S(1)} %get-tuple-element.30.first), channel_id=1, source_target_pairs={{0,2},{2,4},{4,6},{6,8},{8,10},{10,12},{12,14},{14,0},{1,3},{3,5},... | collective-permute-start | bytes 1824776 | tf_op jit(solution)/shard_map/ppermute | solution.py:305
  46.1 2.0 %collective-permute-start.7 = (bf16[264,1152]{1,0:T(8,128)(2,1)S(1)}, bf16[264,1152]{1,0:T(8,128)(2,1)S(1)}, u32[]{:S(2)}, u32[]{:S(2)}) collective-permute-start(bf16[264,1152]{1,0:T(8,128)(2,1)S(1)} %collective-permute-done.3.below.marked), channel_id=1, source_target_pairs={{0,1},{1,0},{2,3},{3,2},{4,5},{5,4},{6,7},{7,6},{8,9},{9,8},{10,11... | collective-permute-start | bytes 1824776 | tf_op jit(solution)/shard_map/ppermute | solution.py:304
  47.5 2.4 %collective-permute-start.8 = (bf16[256,1152]{1,0:T(8,128)(2,1)}, bf16[256,1152]{1,0:T(8,128)(2,1)S(1)}, u32[]{:S(2)}, u32[]{:S(2)}) collective-permute-start(bf16[256,1152]{1,0:T(8,128)(2,1)} %collective-permute-done.6.below), channel_id=1, source_target_pairs={{0,1},{1,0},{2,3},{3,2},{4,5},{5,4},{6,7},{7,6},{8,9},{9,8},{10,11... | collective-permute-start | bytes 1769480 | tf_op jit(solution)/shard_map/ppermute | solution.py:304
  52.4 11.0 %collective-permute-start.12 = (f32[512,128]{1,0:T(8,128)S(1)}, f32[512,128]{1,0:T(8,128)S(1)}, u32[]{:S(2)}, u32[]{:S(2)}) collective-permute-start(f32[512,128]{1,0:T(8,128)S(1)} %get-tuple-element.43), channel_id=1, source_target_pairs={{0,4},{2,6},{4,8},{6,10},{8,12},{10,14},{12,0},{14,2},{1,5},{3,7},... | collective-permute-start | bytes 786440 | tf_op jit(solution)/shard_map/ppermute | solution.py:305
  54.1 3.2 %collective-permute-start.10 = (f32[512,128]{1,0:T(8,128)S(1)}, f32[512,128]{1,0:T(8,128)S(1)}, u32[]{:S(2)}, u32[]{:S(2)}) collective-permute-start(f32[512,128]{1,0:T(8,128)S(1)} %pad_maximum_fusion), channel_id=1, source_target_pairs={{0,1},{1,0},{2,3},{3,2},{4,5},{5,4},{6,7},{7,6},{8,9},{9,8},{10,11... | collective-permute-start | bytes 786440 | tf_op jit(solution)/shard_map/ppermute | solution.py:304
  56.9 4.1 %collective-permute-start.9 = (f32[512,128]{1,0:T(8,128)S(1)}, f32[512,128]{1,0:T(8,128)S(1)}, u32[]{:S(2)}, u32[]{:S(2)}) collective-permute-start(f32[512,128]{1,0:T(8,128)S(1)} %get-tuple-element.46), channel_id=1, source_target_pairs={{0,1},{1,0},{2,3},{3,2},{4,5},{5,4},{6,7},{7,6},{8,9},{9,8},{10,11... | collective-permute-start | bytes 786440 | tf_op jit(solution)/shard_map/ppermute | solution.py:304
  57.4 9.3 %collective-permute-start.11 = (f32[512,128]{1,0:T(8,128)S(1)}, f32[512,128]{1,0:T(8,128)S(1)}, u32[]{:S(2)}, u32[]{:S(2)}) collective-permute-start(f32[512,128]{1,0:T(8,128)S(1)} %fusion), channel_id=1, source_target_pairs={{0,14},{2,0},{4,2},{6,4},{8,6},{10,8},{12,10},{14,12},{1,15},{3,1}... | collective-permute-start | bytes 786440 | tf_op jit(solution)/shard_map/ppermute | solution.py:305
  67.2 1.3 %collective-permute-start.13 = (f32[128,128]{1,0:T(8,128)S(1)}, f32[128,128]{1,0:T(8,128)S(1)}, u32[]{:S(2)}, u32[]{:S(2)}) collective-permute-start(f32[128,128]{1,0:T(8,128)S(1)} %get-tuple-element.53), channel_id=1, source_target_pairs={{0,1},{1,0},{2,3},{3,2},{4,5},{5,4},{6,7},{7,6},{8,9},{9,8},{10,11... | collective-permute-start | bytes 196616 | tf_op jit(solution)/shard_map/ppermute | solution.py:304
  68.5 5.7 %collective-permute-start.14 = (f32[128,128]{1,0:T(8,128)S(1)}, f32[128,128]{1,0:T(8,128)S(1)}, u32[]{:S(2)}, u32[]{:S(2)}) collective-permute-start(f32[128,128]{1,0:T(8,128)S(1)} %add.20), channel_id=1, source_target_pairs={{0,2},{2,0},{4,6},{6,4},{8,10},{10,8},{12,14},{14,12},{1,3},{3,1},... | collective-permute-start | bytes 196616 | tf_op jit(solution)/shard_map/ppermute | solution.py:305
  74.2 4.3 %collective-permute-start.15 = (f32[128,128]{1,0:T(8,128)S(1)}, f32[128,128]{1,0:T(8,128)S(1)}, u32[]{:S(2)}, u32[]{:S(2)}) collective-permute-start(f32[128,128]{1,0:T(8,128)S(1)} %add.21), channel_id=1, source_target_pairs={{0,4},{2,6},{4,0},{6,2},{8,12},{10,14},{12,8},{14,10},{1,5},{3,7},... | collective-permute-start | bytes 196616 | tf_op jit(solution)/shard_map/ppermute | solution.py:305
  78.6 5.9 %collective-permute-start.16 = (f32[128,128]{1,0:T(8,128)S(1)}, f32[128,128]{1,0:T(8,128)S(1)}, u32[]{:S(2)}, u32[]{:S(2)}) collective-permute-start(f32[128,128]{1,0:T(8,128)S(1)} %add.22), channel_id=1, source_target_pairs={{0,8},{2,10},{4,12},{6,14},{8,0},{10,2},{12,4},{14,6},{1,9},{3,11}... | collective-permute-start | bytes 196616 | tf_op jit(solution)/shard_map/ppermute | solution.py:305

commit v17 on v16

--- a/solution.py
+++ b/solution.py
@@ -20,7 +20,7 @@
         in_specs=[in_vmem] * len(operands),
         out_specs=jax.tree.map(lambda _: in_vmem, out_shapes),
         compiler_params=pltpu.CompilerParams(vmem_limit_bytes=24 << 20),
-        cost_estimate=pl.CostEstimate(flops=10**11 if long else 1, transcendentals=0, bytes_accessed=1),
+        cost_estimate=pl.CostEstimate(flops=2 * 10**10 if long else 1, transcendentals=0, bytes_accessed=1),
     )(*operands)
 
 

time: 90.2 us -> 88.6 us (0.982)
  waiting for transfers between devices: 38.7 us -> 45.3 us
  starting transfers between devices: 26.5 us -> 20.8 us
  Pallas kernels: 19.9 us -> 17.8 us
    ppermute x10, waiting for transfers between devices: 37.1 us -> 43.9 us  [per_device(): lax.ppermute(v, 'blk', [(i, to(i) % n_blk) for i in range(n_blk)])]
    ppermute x10, starting transfers between devices: 24.7 us -> 19 us  [per_device(): lax.ppermute(v, 'blk', [(i, to(i) % n_blk) for i in range(n_blk)])]
    pallas_call x9, Pallas kernels: 19.9 us -> 17.8 us  [vmem_call(): pl.pallas_call(body, out_shape=out_shapes, in_specs=[in_vmem] * len(opera...]
  transfers between devices with their start and end apart: 17 -> 17, of which waited for: 10 -> 11; matrix products, arithmetic and copies ran while one was open for 0% -> 0% of each run, Pallas kernels for 13% -> 12%
where the time goes in v17:
time: 88.6 us; the launch traced here: 88.4 us
  waiting for transfers between devices  45.3 us (51%)
  starting transfers between devices  20.8 us (23%)
  Pallas kernels  17.8 us (20%)
  local copies, waits for them, and re-layouts  2.91 us (3%)
  between operations  1.4 us (2%)
    ppermute x10, waiting for transfers between devices, per_device(): lax.ppermute(v, 'blk', [(i, to(i) % n_blk) for i in range(n_blk)])  43.9 us
    ppermute x10, starting transfers between devices, per_device(): lax.ppermute(v, 'blk', [(i, to(i) % n_blk) for i in range(n_blk)])  19 us
    pallas_call x9, Pallas kernels, vmem_call(): pl.pallas_call(body, out_shape=out_shapes, in_specs=[in_vmem] * len(opera...  17.8 us
    unnamed x6, local copies, waits for them, and re-layouts  2.84 us
    ppermute x7, starting transfers between devices, per_device(): sub_move = lambda v: lax.ppermute(v, 'sub', [(0, 1), (1, 0)])  1.78 us
  transfers between devices with their start and end apart: 17, of which 11 were waited for; matrix products, arithmetic and copies ran while one was open for 0% of the time, Pallas kernels for 12%

profile of v17, /device:TPU:0, one launch (start us, length us, event | category | flops | bytes accessed | tf_op | source)
XLA Modules:
  0.0 88.4 jit_solution(11891550017491379232)
XLA Ops:
  0.6 5.1 %collective-permute-start.4 = (bf16[512,1024]{1,0:T(8,128)(2,1)}, bf16[512,1024]{1,0:T(8,128)(2,1)S(1)}, u32[]{:S(2)}, u32[]{:S(2)}) collective-permute-start(bf16[512,1024]{1,0:T(8,128)(2,1)} %embeddings.1), channel_id=1, source_target_pairs={{0,12},{2,14},{4,0},{6,2},{8,4},{10,6},{12,8},{14,10},{1,13},{3,15... | collective-permute-start | bytes 3145736 | tf_op jit(solution)/shard_map/ppermute | solution.py:305
  5.7 1.3 %copy-done = bf16[512,1024]{1,0:T(8,128)(2,1)S(1)} copy-done((bf16[512,1024]{1,0:T(8,128)(2,1)S(1)}, bf16[512,1024]{1,0:T(8,128)(2,1)}, u32[]{:S(2)}) %copy-start) | copy-done | bytes 1048600
  7.0 0.9 %copy-done.1 = bf16[512,128]{1,0:T(8,128)(2,1)S(1)} copy-done((bf16[512,128]{1,0:T(8,128)(2,1)S(1)}, bf16[512,128]{1,0:T(8,128)(2,1)}, u32[]{:S(2)}) %copy-start.1) | copy-done | bytes 131096
  7.9 0.7 copy-done.2
  8.6 1.1 %shard_map.59 = (bf16[264,1152]{1,0:T(8,128)(2,1)S(1)}, bf16[256,1152]{1,0:T(8,128)(2,1)S(1)}, bf16[520,128]{1,0:T(8,128)(2,1)}) custom-call(bf16[512,1024]{1,0:T(8,128)(2,1)S(1)} %copy-done, bf16[512,128]{1,0:T(8,128)(2,1)S(1)} %copy-done.1, s32[4,56]{1,0:T(4,128)S(1)} %copy-done.2), custom_call_target="tpu_custom_call" | custom-call | flops 1 | bytes 1 | tf_op jit(solution)/shard_map/pallas_call | solution.py:17
  9.6 0.5 collective-permute-start.2
  10.1 1.5 %collective-permute-start = (bf16[256,1152]{1,0:T(8,128)(2,1)S(1)}, bf16[256,1152]{1,0:T(8,128)(2,1)}, u32[]{:S(2)}, u32[]{:S(2)}) collective-permute-start(bf16[256,1152]{1,0:T(8,128)(2,1)S(1)} %get-tuple-element.29.last), channel_id=1, source_target_pairs={{0,2},{2,0},{4,6},{6,4},{8,10},{10,8},{12,14},{14,12},{1,3},{3,1},... | collective-permute-start | bytes 1769480 | tf_op jit(solution)/shard_map/ppermute | solution.py:305
  12.9 2.1 %shard_map.60.self_image = f32[512,128]{1,0:T(8,128)S(1)} custom-call(f32[2,128]{1,0:T(2,128)S(1)} %broadcast_in_dim.2.numbers, bf16[264,1152]{1,0:T(8,128)(2,1)S(1)} %get-tuple-element.30.first, bf16[256,1152]{1,0:T(8,128)(2,1)S(1)} %get-tuple-element.29.last, bf16[264,1152]{1,0:T(8,128)(2,1)S(1)} %collective-permute-done.1.other_first, ...), custom_call_target="tpu_custom_call" | custom-call | flops 1 | bytes 1 | tf_op jit(solution)/shard_map/pallas_call | solution.py:17
  15.0 10.5 %collective-permute-done = bf16[256,1152]{1,0:T(8,128)(2,1)} collective-permute-done((bf16[256,1152]{1,0:T(8,128)(2,1)S(1)}, bf16[256,1152]{1,0:T(8,128)(2,1)}, u32[]{:S(2)}, u32[]{:S(2)}) %collective-permute-start) | collective-permute-done | bytes 589856 | tf_op jit(solution)/shard_map/ppermute | solution.py:305
  25.5 1.9 %collective-permute-start.6 = (bf16[256,1152]{1,0:T(8,128)(2,1)}, bf16[256,1152]{1,0:T(8,128)(2,1)S(1)}, u32[]{:S(2)}, u32[]{:S(2)}) collective-permute-start(bf16[256,1152]{1,0:T(8,128)(2,1)} %collective-permute-done), channel_id=1, source_target_pairs={{0,4},{2,2},{4,8},{6,6},{8,12},{10,10},{12,0},{14,14},{1,5},{3,3},... | collective-permute-start | bytes 1769480 | tf_op jit(solution)/shard_map/ppermute | solution.py:305
  27.4 1.3 %collective-permute-start.3 = (bf16[264,1152]{1,0:T(8,128)(2,1)S(1)}, bf16[264,1152]{1,0:T(8,128)(2,1)S(1)}, u32[]{:S(2)}, u32[]{:S(2)}) collective-permute-start(bf16[264,1152]{1,0:T(8,128)(2,1)S(1)} %get-tuple-element.30.first), channel_id=1, source_target_pairs={{0,2},{2,4},{4,6},{6,8},{8,10},{10,12},{12,14},{14,0},{1,3},{3,5},... | collective-permute-start | bytes 1824776 | tf_op jit(solution)/shard_map/ppermute | solution.py:305
  28.7 3.8 %collective-permute-done.5.panel = bf16[520,128]{1,0:T(8,128)(2,1)} collective-permute-done((bf16[520,128]{1,0:T(8,128)(2,1)}, bf16[520,128]{1,0:T(8,128)(2,1)}, u32[]{:S(2)}, u32[]{:S(2)}) %collective-permute-start.5) | collective-permute-done | bytes 133152 | tf_op jit(solution)/shard_map/ppermute | solution.py:305
  32.5 3.2 %shard_map.61 = (f32[512,128]{1,0:T(8,128)S(1)}, f32[128,1024]{1,0:T(8,128)S(1)}, f32[512,128]{1,0:T(8,128)S(1)}, bf16[520,128]{1,0:T(8,128)(2,1)S(1)}) custom-call(f32[2,128]{1,0:T(2,128)S(1)} %broadcast_in_dim.2.numbers, bf16[512,1024]{1,0:T(8,128)(2,1)S(1)} %collective-permute-done.4.above, bf16[520,128]{1,0:T(8,128)(2,1)} %collective-permute-done.5.panel, ...), custom_call_target="tpu_custom_call" | custom-call | flops 20000000000 | bytes 1 | tf_op jit(solution)/shard_map/pallas_call | solution.py:17
  35.7 10.3 %collective-permute-done.3.below.marked = bf16[264,1152]{1,0:T(8,128)(2,1)S(1)} collective-permute-done((bf16[264,1152]{1,0:T(8,128)(2,1)S(1)}, bf16[264,1152]{1,0:T(8,128)(2,1)S(1)}, u32[]{:S(2)}, u32[]{:S(2)}) %collective-permute-start.3) | collective-permute-done | bytes 608288 | tf_op jit(solution)/shard_map/ppermute | solution.py:305
  46.1 1.4 %shard_map.62 = (f32[256,128]{1,0:T(8,128)S(1)}, f32[128,1024]{1,0:T(8,128)S(1)}) custom-call(f32[2,128]{1,0:T(2,128)S(1)} %broadcast_in_dim.2.numbers, bf16[264,1152]{1,0:T(8,128)(2,1)S(1)} %collective-permute-done.3.below.marked, bf16[264,1152]{1,0:T(8,128)(2,1)S(1)} %get-tuple-element.30.first, bf16[256,1152]{1,0:T(8,128)(2,1)S(1)} %get-tuple-element.29.last, ...), custom_call_target="tpu_custom_call" | custom-call | flops 20000000000 | bytes 1 | tf_op jit(solution)/shard_map/pallas_call | solution.py:17
  47.5 0.6 collective-permute-start.8
  48.1 1.5 %shard_map.63 = (f32[512,128]{1,0:T(8,128)S(1)}, f32[256,128]{1,0:T(8,128)S(1)}, f32[256,128]{1,0:T(8,128)S(1)}) custom-call(f32[2,128]{1,0:T(2,128)S(1)} %broadcast_in_dim.2.numbers, bf16[512,1024]{1,0:T(8,128)(2,1)S(1)} %collective-permute-done.4.above, bf16[520,128]{1,0:T(8,128)(2,1)S(1)} %get-tuple-element.39.panel, ...), custom_call_target="tpu_custom_call" | custom-call | flops 20000000000 | bytes 1 | tf_op jit(solution)/shard_map/pallas_call | solution.py:17
  49.7 1.5 %shard_map.64 = (f32[512,128]{1,0:T(8,128)S(1)}, f32[256,128]{1,0:T(8,128)S(1)}, f32[256,128]{1,0:T(8,128)S(1)}) custom-call(f32[2,128]{1,0:T(2,128)S(1)} %broadcast_in_dim.2.numbers, bf16[512,1024]{1,0:T(8,128)(2,1)S(1)} %collective-permute-done.4.above, bf16[520,128]{1,0:T(8,128)(2,1)S(1)} %get-tuple-element.39.panel, ...), custom_call_target="tpu_custom_call" | custom-call | flops 20000000000 | bytes 1 | tf_op jit(solution)/shard_map/pallas_call | solution.py:17
  51.2 1.7 %collective-permute-start.12 = (f32[512,128]{1,0:T(8,128)S(1)}, f32[512,128]{1,0:T(8,128)S(1)}, u32[]{:S(2)}, u32[]{:S(2)}) collective-permute-start(f32[512,128]{1,0:T(8,128)S(1)} %get-tuple-element.43), channel_id=1, source_target_pairs={{0,4},{2,6},{4,8},{6,10},{8,12},{10,14},{12,0},{14,2},{1,5},{3,7},... | collective-permute-start | bytes 786440 | tf_op jit(solution)/shard_map/ppermute | solution.py:305
  53.0 1.5 %shard_map.65 = (f32[256,128]{1,0:T(8,128)S(1)}, f32[512,128]{1,0:T(8,128)S(1)}, f32[512,128]{1,0:T(8,128)S(1)}) custom-call(f32[2,128]{1,0:T(2,128)S(1)} %broadcast_in_dim.2.numbers, bf16[264,1152]{1,0:T(8,128)(2,1)S(1)} %collective-permute-done.3.below.marked, bf16[256,1152]{1,0:T(8,128)(2,1)S(1)} %collective-permute-done.6.below, ...), custom_call_target="tpu_custom_call" | custom-call | flops 20000000000 | bytes 1 | tf_op jit(solution)/shard_map/pallas_call | solution.py:17
  54.6 0.5 collective-permute-start.9
  55.1 1.6 %collective-permute-start.11 = (f32[512,128]{1,0:T(8,128)S(1)}, f32[512,128]{1,0:T(8,128)S(1)}, u32[]{:S(2)}, u32[]{:S(2)}) collective-permute-start(f32[512,128]{1,0:T(8,128)S(1)} %fusion), channel_id=1, source_target_pairs={{0,14},{2,0},{4,2},{6,4},{8,6},{10,8},{12,10},{14,12},{1,15},{3,1}... | collective-permute-start | bytes 786440 | tf_op jit(solution)/shard_map/ppermute | solution.py:305
  56.7 5.5 %collective-permute-done.12.above = f32[512,128]{1,0:T(8,128)S(1)} collective-permute-done((f32[512,128]{1,0:T(8,128)S(1)}, f32[512,128]{1,0:T(8,128)S(1)}, u32[]{:S(2)}, u32[]{:S(2)}) %collective-permute-start.12) | collective-permute-done | bytes 262176 | tf_op jit(solution)/shard_map/ppermute | solution.py:305
  62.2 2.4 %collective-permute-done.11.below = f32[512,128]{1,0:T(8,128)S(1)} collective-permute-done((f32[512,128]{1,0:T(8,128)S(1)}, f32[512,128]{1,0:T(8,128)S(1)}, u32[]{:S(2)}, u32[]{:S(2)}) %collective-permute-start.11) | collective-permute-done | bytes 262176 | tf_op jit(solution)/shard_map/ppermute | solution.py:305
  65.1 1.2 %collective-permute-done.13 = f32[128,128]{1,0:T(8,128)S(1)} collective-permute-done((f32[128,128]{1,0:T(8,128)S(1)}, f32[128,128]{1,0:T(8,128)S(1)}, u32[]{:S(2)}, u32[]{:S(2)}) %collective-permute-start.13) | collective-permute-done | bytes 65568 | tf_op jit(solution)/shard_map/ppermute | solution.py:304
  66.3 4.2 %collective-permute-start.14 = (f32[128,128]{1,0:T(8,128)S(1)}, f32[128,128]{1,0:T(8,128)S(1)}, u32[]{:S(2)}, u32[]{:S(2)}) collective-permute-start(f32[128,128]{1,0:T(8,128)S(1)} %add.20), channel_id=1, source_target_pairs={{0,2},{2,0},{4,6},{6,4},{8,10},{10,8},{12,14},{14,12},{1,3},{3,1},... | collective-permute-start | bytes 196616 | tf_op jit(solution)/shard_map/ppermute | solution.py:305
  70.5 2.4 %collective-permute-done.14 = f32[128,128]{1,0:T(8,128)S(1)} collective-permute-done((f32[128,128]{1,0:T(8,128)S(1)}, f32[128,128]{1,0:T(8,128)S(1)}, u32[]{:S(2)}, u32[]{:S(2)}) %collective-permute-start.14) | collective-permute-done | bytes 65568 | tf_op jit(solution)/shard_map/ppermute | solution.py:305
  72.9 0.6 collective-permute-start.15
  73.6 3.7 %collective-permute-done.15 = f32[128,128]{1,0:T(8,128)S(1)} collective-permute-done((f32[128,128]{1,0:T(8,128)S(1)}, f32[128,128]{1,0:T(8,128)S(1)}, u32[]{:S(2)}, u32[]{:S(2)}) %collective-permute-start.15) | collective-permute-done | bytes 65568 | tf_op jit(solution)/shard_map/ppermute | solution.py:305
  77.3 0.7 collective-permute-start.16
  78.0 5.3 %collective-permute-done.16 = f32[128,128]{1,0:T(8,128)S(1)} collective-permute-done((f32[128,128]{1,0:T(8,128)S(1)}, f32[128,128]{1,0:T(8,128)S(1)}, u32[]{:S(2)}, u32[]{:S(2)}) %collective-permute-start.16) | collective-permute-done | bytes 65568 | tf_op jit(solution)/shard_map/ppermute | solution.py:305
  83.2 5.2 %shard_map.67 = (f32[512,128]{1,0:T(8,128)}, f32[128,128]{1,0:T(8,128)}) custom-call(f32[512,128]{1,0:T(8,128)S(1)} %get-tuple-element.52.image, f32[128,128]{1,0:T(8,128)S(1)} %add.23.gram), custom_call_target="tpu_custom_call" | custom-call | flops 20000000000 | bytes 1 | tf_op jit(solution)/shard_map/pallas_call | solution.py:17
  (25 shorter events, 1.5 us)
Async XLA Ops:
  0.6 31.9 %collective-permute-start.4 = (bf16[512,1024]{1,0:T(8,128)(2,1)}, bf16[512,1024]{1,0:T(8,128)(2,1)S(1)}, u32[]{:S(2)}, u32[]{:S(2)}) collective-permute-start(bf16[512,1024]{1,0:T(8,128)(2,1)} %embeddings.1), channel_id=1, source_target_pairs={{0,12},{2,14},{4,0},{6,2},{8,4},{10,6},{12,8},{14,10},{1,13},{3,15... | collective-permute-start | bytes 3145736 | tf_op jit(solution)/shard_map/ppermute | solution.py:305
  5.7 1.3 %copy-start = (bf16[512,1024]{1,0:T(8,128)(2,1)S(1)}, bf16[512,1024]{1,0:T(8,128)(2,1)}, u32[]{:S(2)}) copy-start(bf16[512,1024]{1,0:T(8,128)(2,1)} %embeddings.1) | copy-start | bytes 3145732
  7.0 0.9 %copy-start.1 = (bf16[512,128]{1,0:T(8,128)(2,1)S(1)}, bf16[512,128]{1,0:T(8,128)(2,1)}, u32[]{:S(2)}) copy-start(bf16[512,128]{1,0:T(8,128)(2,1)} %panel.1) | copy-start | bytes 393220
  7.9 0.7 copy-start.2
  9.6 3.2 %collective-permute-start.1 = (bf16[264,1152]{1,0:T(8,128)(2,1)S(1)}, bf16[264,1152]{1,0:T(8,128)(2,1)S(1)}, u32[]{:S(2)}, u32[]{:S(2)}) collective-permute-start(bf16[264,1152]{1,0:T(8,128)(2,1)S(1)} %get-tuple-element.30.first), channel_id=1, source_target_pairs={{0,1},{1,0},{2,3},{3,2},{4,5},{5,4},{6,7},{7,6},{8,9},{9,8},{10,11... | collective-permute-start | bytes 1824776 | tf_op jit(solution)/shard_map/ppermute | solution.py:304
  9.6 3.2 %collective-permute-start.2 = (bf16[256,1152]{1,0:T(8,128)(2,1)S(1)}, bf16[256,1152]{1,0:T(8,128)(2,1)S(1)}, u32[]{:S(2)}, u32[]{:S(2)}) collective-permute-start(bf16[256,1152]{1,0:T(8,128)(2,1)S(1)} %get-tuple-element.29.last), channel_id=1, source_target_pairs={{0,1},{1,0},{2,3},{3,2},{4,5},{5,4},{6,7},{7,6},{8,9},{9,8},{10,11... | collective-permute-start | bytes 1769480 | tf_op jit(solution)/shard_map/ppermute | solution.py:304
  10.1 15.3 %collective-permute-start = (bf16[256,1152]{1,0:T(8,128)(2,1)S(1)}, bf16[256,1152]{1,0:T(8,128)(2,1)}, u32[]{:S(2)}, u32[]{:S(2)}) collective-permute-start(bf16[256,1152]{1,0:T(8,128)(2,1)S(1)} %get-tuple-element.29.last), channel_id=1, source_target_pairs={{0,2},{2,0},{4,6},{6,4},{8,10},{10,8},{12,14},{14,12},{1,3},{3,1},... | collective-permute-start | bytes 1769480 | tf_op jit(solution)/shard_map/ppermute | solution.py:305
  11.6 20.9 %collective-permute-start.5 = (bf16[520,128]{1,0:T(8,128)(2,1)}, bf16[520,128]{1,0:T(8,128)(2,1)}, u32[]{:S(2)}, u32[]{:S(2)}) collective-permute-start(bf16[520,128]{1,0:T(8,128)(2,1)} %get-tuple-element.31), channel_id=1, source_target_pairs={{0,12},{2,14},{4,0},{6,2},{8,4},{10,6},{12,8},{14,10},{1,13},{3,15... | collective-permute-start | bytes 399368 | tf_op jit(solution)/shard_map/ppermute | solution.py:305
  25.5 22.0 %collective-permute-start.6 = (bf16[256,1152]{1,0:T(8,128)(2,1)}, bf16[256,1152]{1,0:T(8,128)(2,1)S(1)}, u32[]{:S(2)}, u32[]{:S(2)}) collective-permute-start(bf16[256,1152]{1,0:T(8,128)(2,1)} %collective-permute-done), channel_id=1, source_target_pairs={{0,4},{2,2},{4,8},{6,6},{8,12},{10,10},{12,0},{14,14},{1,5},{3,3},... | collective-permute-start | bytes 1769480 | tf_op jit(solution)/shard_map/ppermute | solution.py:305
  27.4 18.7 %collective-permute-start.3 = (bf16[264,1152]{1,0:T(8,128)(2,1)S(1)}, bf16[264,1152]{1,0:T(8,128)(2,1)S(1)}, u32[]{:S(2)}, u32[]{:S(2)}) collective-permute-start(bf16[264,1152]{1,0:T(8,128)(2,1)S(1)} %get-tuple-element.30.first), channel_id=1, source_target_pairs={{0,2},{2,4},{4,6},{6,8},{8,10},{10,12},{12,14},{14,0},{1,3},{3,5},... | collective-permute-start | bytes 1824776 | tf_op jit(solution)/shard_map/ppermute | solution.py:305
  46.1 2.0 %collective-permute-start.7 = (bf16[264,1152]{1,0:T(8,128)(2,1)S(1)}, bf16[264,1152]{1,0:T(8,128)(2,1)S(1)}, u32[]{:S(2)}, u32[]{:S(2)}) collective-permute-start(bf16[264,1152]{1,0:T(8,128)(2,1)S(1)} %collective-permute-done.3.below.marked), channel_id=1, source_target_pairs={{0,1},{1,0},{2,3},{3,2},{4,5},{5,4},{6,7},{7,6},{8,9},{9,8},{10,11... | collective-permute-start | bytes 1824776 | tf_op jit(solution)/shard_map/ppermute | solution.py:304
  47.5 2.2 %collective-permute-start.8 = (bf16[256,1152]{1,0:T(8,128)(2,1)S(1)}, bf16[256,1152]{1,0:T(8,128)(2,1)S(1)}, u32[]{:S(2)}, u32[]{:S(2)}) collective-permute-start(bf16[256,1152]{1,0:T(8,128)(2,1)S(1)} %collective-permute-done.6.below), channel_id=1, source_target_pairs={{0,1},{1,0},{2,3},{3,2},{4,5},{5,4},{6,7},{7,6},{8,9},{9,8},{10,11... | collective-permute-start | bytes 1769480 | tf_op jit(solution)/shard_map/ppermute | solution.py:304
  51.2 11.0 %collective-permute-start.12 = (f32[512,128]{1,0:T(8,128)S(1)}, f32[512,128]{1,0:T(8,128)S(1)}, u32[]{:S(2)}, u32[]{:S(2)}) collective-permute-start(f32[512,128]{1,0:T(8,128)S(1)} %get-tuple-element.43), channel_id=1, source_target_pairs={{0,4},{2,6},{4,8},{6,10},{8,12},{10,14},{12,0},{14,2},{1,5},{3,7},... | collective-permute-start | bytes 786440 | tf_op jit(solution)/shard_map/ppermute | solution.py:305
  52.9 2.2 %collective-permute-start.10 = (f32[512,128]{1,0:T(8,128)S(1)}, f32[512,128]{1,0:T(8,128)S(1)}, u32[]{:S(2)}, u32[]{:S(2)}) collective-permute-start(f32[512,128]{1,0:T(8,128)S(1)} %pad_maximum_fusion), channel_id=1, source_target_pairs={{0,1},{1,0},{2,3},{3,2},{4,5},{5,4},{6,7},{7,6},{8,9},{9,8},{10,11... | collective-permute-start | bytes 786440 | tf_op jit(solution)/shard_map/ppermute | solution.py:304
  54.6 2.1 %collective-permute-start.9 = (f32[512,128]{1,0:T(8,128)S(1)}, f32[512,128]{1,0:T(8,128)S(1)}, u32[]{:S(2)}, u32[]{:S(2)}) collective-permute-start(f32[512,128]{1,0:T(8,128)S(1)} %get-tuple-element.46), channel_id=1, source_target_pairs={{0,1},{1,0},{2,3},{3,2},{4,5},{5,4},{6,7},{7,6},{8,9},{9,8},{10,11... | collective-permute-start | bytes 786440 | tf_op jit(solution)/shard_map/ppermute | solution.py:304
  55.1 9.5 %collective-permute-start.11 = (f32[512,128]{1,0:T(8,128)S(1)}, f32[512,128]{1,0:T(8,128)S(1)}, u32[]{:S(2)}, u32[]{:S(2)}) collective-permute-start(f32[512,128]{1,0:T(8,128)S(1)} %fusion), channel_id=1, source_target_pairs={{0,14},{2,0},{4,2},{6,4},{8,6},{10,8},{12,10},{14,12},{1,15},{3,1}... | collective-permute-start | bytes 786440 | tf_op jit(solution)/shard_map/ppermute | solution.py:305
  65.0 1.3 %collective-permute-start.13 = (f32[128,128]{1,0:T(8,128)S(1)}, f32[128,128]{1,0:T(8,128)S(1)}, u32[]{:S(2)}, u32[]{:S(2)}) collective-permute-start(f32[128,128]{1,0:T(8,128)S(1)} %get-tuple-element.53), channel_id=1, source_target_pairs={{0,1},{1,0},{2,3},{3,2},{4,5},{5,4},{6,7},{7,6},{8,9},{9,8},{10,11... | collective-permute-start | bytes 196616 | tf_op jit(solution)/shard_map/ppermute | solution.py:304
  66.3 6.6 %collective-permute-start.14 = (f32[128,128]{1,0:T(8,128)S(1)}, f32[128,128]{1,0:T(8,128)S(1)}, u32[]{:S(2)}, u32[]{:S(2)}) collective-permute-start(f32[128,128]{1,0:T(8,128)S(1)} %add.20), channel_id=1, source_target_pairs={{0,2},{2,0},{4,6},{6,4},{8,10},{10,8},{12,14},{14,12},{1,3},{3,1},... | collective-permute-start | bytes 196616 | tf_op jit(solution)/shard_map/ppermute | solution.py:305
  72.9 4.3 %collective-permute-start.15 = (f32[128,128]{1,0:T(8,128)S(1)}, f32[128,128]{1,0:T(8,128)S(1)}, u32[]{:S(2)}, u32[]{:S(2)}) collective-permute-start(f32[128,128]{1,0:T(8,128)S(1)} %add.21), channel_id=1, source_target_pairs={{0,4},{2,6},{4,0},{6,2},{8,12},{10,14},{12,8},{14,10},{1,5},{3,7},... | collective-permute-start | bytes 196616 | tf_op jit(solution)/shard_map/ppermute | solution.py:305
  77.3 5.9 %collective-permute-start.16 = (f32[128,128]{1,0:T(8,128)S(1)}, f32[128,128]{1,0:T(8,128)S(1)}, u32[]{:S(2)}, u32[]{:S(2)}) collective-permute-start(f32[128,128]{1,0:T(8,128)S(1)} %add.22), channel_id=1, source_target_pairs={{0,8},{2,10},{4,12},{6,14},{8,0},{10,2},{12,4},{14,6},{1,9},{3,11}... | collective-permute-start | bytes 196616 | tf_op jit(solution)/shard_map/ppermute | solution.py:305

commit v18 on v15

--- a/solution.py
+++ b/solution.py
@@ -20,7 +20,7 @@
         in_specs=[in_vmem] * len(operands),
         out_specs=jax.tree.map(lambda _: in_vmem, out_shapes),
         compiler_params=pltpu.CompilerParams(vmem_limit_bytes=24 << 20),
-        cost_estimate=pl.CostEstimate(flops=10**11 if long else 1, transcendentals=0, bytes_accessed=1),
+        cost_estimate=pl.CostEstimate(flops=2 * 10**10 if long else 1, transcendentals=0, bytes_accessed=1),
     )(*operands)
 
 

time: 91.6 us -> 88.9 us (0.971)
  Pallas kernels: 22.5 us -> 17.8 us
  waiting for transfers between devices: 45.1 us -> 46.7 us
    pallas_call x9, Pallas kernels: 22.5 us -> 17.8 us  [vmem_call(): pl.pallas_call(body, out_shape=out_shapes, in_specs=[in_vmem] * len(opera...]
    ppermute x10, waiting for transfers between devices: 41.8 us -> 44.1 us  [per_device(): lax.ppermute(v, 'blk', [(i, to(i) % n_blk) for i in range(n_blk)])]
  transfers between devices with their start and end apart: 17 -> 17, of which waited for: 12 -> 13; matrix products, arithmetic and copies ran while one was open for 0% -> 0% of each run, Pallas kernels for 16% -> 12%
where the time goes in v18:
time: 88.9 us; the launch traced here: 88.6 us
  waiting for transfers between devices  46.7 us (53%)
  starting transfers between devices  19.6 us (22%)
  Pallas kernels  17.8 us (20%)
  local copies, waits for them, and re-layouts  2.91 us (3%)
  between operations  1.4 us (2%)
    ppermute x10, waiting for transfers between devices, per_device(): lax.ppermute(v, 'blk', [(i, to(i) % n_blk) for i in range(n_blk)])  44.1 us
    ppermute x10, starting transfers between devices, per_device(): lax.ppermute(v, 'blk', [(i, to(i) % n_blk) for i in range(n_blk)])  18.1 us
    pallas_call x9, Pallas kernels, vmem_call(): pl.pallas_call(body, out_shape=out_shapes, in_specs=[in_vmem] * len(opera...  17.8 us
    unnamed x6, local copies, waits for them, and re-layouts  2.84 us
    ppermute x7, waiting for transfers between devices, per_device(): sub_move = lambda v: lax.ppermute(v, 'sub', [(0, 1), (1, 0)])  2.58 us
  transfers between devices with their start and end apart: 17, of which 13 were waited for; matrix products, arithmetic and copies ran while one was open for 0% of the time, Pallas kernels for 12%

profile of v18, /device:TPU:0, one launch (start us, length us, event | category | flops | bytes accessed | tf_op | source)
XLA Modules:
  0.0 88.6 jit_solution(3614961795913614805)
XLA Ops:
  0.6 5.1 %collective-permute-start.4 = (bf16[512,1024]{1,0:T(8,128)(2,1)}, bf16[512,1024]{1,0:T(8,128)(2,1)S(1)}, u32[]{:S(2)}, u32[]{:S(2)}) collective-permute-start(bf16[512,1024]{1,0:T(8,128)(2,1)} %embeddings.1), channel_id=1, source_target_pairs={{0,12},{2,14},{4,0},{6,2},{8,4},{10,6},{12,8},{14,10},{1,13},{3,15... | collective-permute-start | bytes 3145736 | tf_op jit(solution)/shard_map/ppermute | solution.py:305
  5.7 1.3 %copy-done = bf16[512,1024]{1,0:T(8,128)(2,1)S(1)} copy-done((bf16[512,1024]{1,0:T(8,128)(2,1)S(1)}, bf16[512,1024]{1,0:T(8,128)(2,1)}, u32[]{:S(2)}) %copy-start) | copy-done | bytes 1048600
  7.0 0.9 %copy-done.1 = bf16[512,128]{1,0:T(8,128)(2,1)S(1)} copy-done((bf16[512,128]{1,0:T(8,128)(2,1)S(1)}, bf16[512,128]{1,0:T(8,128)(2,1)}, u32[]{:S(2)}) %copy-start.1) | copy-done | bytes 131096
  7.9 0.7 copy-done.2
  8.6 1.1 %shard_map.59 = (bf16[256,1152]{1,0:T(8,128)(2,1)S(1)}, bf16[264,1152]{1,0:T(8,128)(2,1)S(1)}, bf16[520,128]{1,0:T(8,128)(2,1)}) custom-call(bf16[512,1024]{1,0:T(8,128)(2,1)S(1)} %copy-done, bf16[512,128]{1,0:T(8,128)(2,1)S(1)} %copy-done.1, s32[4,56]{1,0:T(4,128)S(1)} %copy-done.2), custom_call_target="tpu_custom_call" | custom-call | flops 1 | bytes 1 | tf_op jit(solution)/shard_map/pallas_call | solution.py:17
  9.6 1.5 %collective-permute-start = (bf16[264,1152]{1,0:T(8,128)(2,1)S(1)}, bf16[264,1152]{1,0:T(8,128)(2,1)}, u32[]{:S(2)}, u32[]{:S(2)}) collective-permute-start(bf16[264,1152]{1,0:T(8,128)(2,1)S(1)} %get-tuple-element.28.last), channel_id=1, source_target_pairs={{0,2},{2,0},{4,6},{6,4},{8,10},{10,8},{12,14},{14,12},{1,3},{3,1},... | collective-permute-start | bytes 1824776 | tf_op jit(solution)/shard_map/ppermute | solution.py:305
  12.5 0.6 collective-permute-done.1.other_first
  13.2 2.1 %shard_map.60.self_image = f32[512,128]{1,0:T(8,128)S(1)} custom-call(f32[2,128]{1,0:T(2,128)S(1)} %broadcast_in_dim.2.numbers, bf16[256,1152]{1,0:T(8,128)(2,1)S(1)} %get-tuple-element.34.first, bf16[264,1152]{1,0:T(8,128)(2,1)S(1)} %get-tuple-element.28.last, bf16[256,1152]{1,0:T(8,128)(2,1)S(1)} %collective-permute-done.1.other_first, ...), custom_call_target="tpu_custom_call" | custom-call | flops 1 | bytes 1 | tf_op jit(solution)/shard_map/pallas_call | solution.py:17
  15.3 10.6 %collective-permute-done = bf16[264,1152]{1,0:T(8,128)(2,1)} collective-permute-done((bf16[264,1152]{1,0:T(8,128)(2,1)S(1)}, bf16[264,1152]{1,0:T(8,128)(2,1)}, u32[]{:S(2)}, u32[]{:S(2)}) %collective-permute-start) | collective-permute-done | bytes 608288 | tf_op jit(solution)/shard_map/ppermute | solution.py:305
  25.9 1.5 %collective-permute-start.6 = (bf16[256,1152]{1,0:T(8,128)(2,1)S(1)}, bf16[256,1152]{1,0:T(8,128)(2,1)S(1)}, u32[]{:S(2)}, u32[]{:S(2)}) collective-permute-start(bf16[256,1152]{1,0:T(8,128)(2,1)S(1)} %get-tuple-element.34.first), channel_id=1, source_target_pairs={{0,2},{2,4},{4,6},{6,8},{8,10},{10,12},{12,14},{14,0},{1,3},{3,5},... | collective-permute-start | bytes 1769480 | tf_op jit(solution)/shard_map/ppermute | solution.py:305
  27.4 1.9 %collective-permute-start.3 = (bf16[264,1152]{1,0:T(8,128)(2,1)}, bf16[264,1152]{1,0:T(8,128)(2,1)S(1)}, u32[]{:S(2)}, u32[]{:S(2)}) collective-permute-start(bf16[264,1152]{1,0:T(8,128)(2,1)} %collective-permute-done), channel_id=1, source_target_pairs={{0,4},{2,2},{4,8},{6,6},{8,12},{10,10},{12,0},{14,14},{1,5},{3,3},... | collective-permute-start | bytes 1824776 | tf_op jit(solution)/shard_map/ppermute | solution.py:305
  29.3 3.2 %collective-permute-done.5.panel = bf16[520,128]{1,0:T(8,128)(2,1)} collective-permute-done((bf16[520,128]{1,0:T(8,128)(2,1)}, bf16[520,128]{1,0:T(8,128)(2,1)}, u32[]{:S(2)}, u32[]{:S(2)}) %collective-permute-start.5) | collective-permute-done | bytes 133152 | tf_op jit(solution)/shard_map/ppermute | solution.py:305
  32.5 3.2 %shard_map.61 = (f32[512,128]{1,0:T(8,128)S(1)}, f32[128,1024]{1,0:T(8,128)S(1)}, f32[512,128]{1,0:T(8,128)S(1)}, bf16[520,128]{1,0:T(8,128)(2,1)S(1)}) custom-call(f32[2,128]{1,0:T(2,128)S(1)} %broadcast_in_dim.2.numbers, bf16[512,1024]{1,0:T(8,128)(2,1)S(1)} %collective-permute-done.4.above, bf16[520,128]{1,0:T(8,128)(2,1)} %collective-permute-done.5.panel, ...), custom_call_target="tpu_custom_call" | custom-call | flops 20000000000 | bytes 1 | tf_op jit(solution)/shard_map/pallas_call | solution.py:17
  35.7 10.6 %collective-permute-done.3.below.marked = bf16[264,1152]{1,0:T(8,128)(2,1)S(1)} collective-permute-done((bf16[264,1152]{1,0:T(8,128)(2,1)}, bf16[264,1152]{1,0:T(8,128)(2,1)S(1)}, u32[]{:S(2)}, u32[]{:S(2)}) %collective-permute-start.3) | collective-permute-done | bytes 608288 | tf_op jit(solution)/shard_map/ppermute | solution.py:305
  46.3 1.4 %shard_map.62 = (f32[256,128]{1,0:T(8,128)S(1)}, f32[128,1024]{1,0:T(8,128)S(1)}) custom-call(f32[2,128]{1,0:T(2,128)S(1)} %broadcast_in_dim.2.numbers, bf16[264,1152]{1,0:T(8,128)(2,1)S(1)} %collective-permute-done.3.below.marked, bf16[256,1152]{1,0:T(8,128)(2,1)S(1)} %get-tuple-element.34.first, bf16[264,1152]{1,0:T(8,128)(2,1)S(1)} %get-tuple-element.28.last, ...), custom_call_target="tpu_custom_call" | custom-call | flops 20000000000 | bytes 1 | tf_op jit(solution)/shard_map/pallas_call | solution.py:17
  47.7 0.6 collective-permute-start.8
  48.4 1.5 %shard_map.63 = (f32[512,128]{1,0:T(8,128)S(1)}, f32[256,128]{1,0:T(8,128)S(1)}, f32[256,128]{1,0:T(8,128)S(1)}) custom-call(f32[2,128]{1,0:T(2,128)S(1)} %broadcast_in_dim.2.numbers, bf16[512,1024]{1,0:T(8,128)(2,1)S(1)} %collective-permute-done.4.above, bf16[520,128]{1,0:T(8,128)(2,1)S(1)} %get-tuple-element.39.panel, ...), custom_call_target="tpu_custom_call" | custom-call | flops 20000000000 | bytes 1 | tf_op jit(solution)/shard_map/pallas_call | solution.py:17
  49.9 1.5 %shard_map.64 = (f32[512,128]{1,0:T(8,128)S(1)}, f32[256,128]{1,0:T(8,128)S(1)}, f32[256,128]{1,0:T(8,128)S(1)}) custom-call(f32[2,128]{1,0:T(2,128)S(1)} %broadcast_in_dim.2.numbers, bf16[512,1024]{1,0:T(8,128)(2,1)S(1)} %collective-permute-done.4.above, bf16[520,128]{1,0:T(8,128)(2,1)S(1)} %get-tuple-element.39.panel, ...), custom_call_target="tpu_custom_call" | custom-call | flops 20000000000 | bytes 1 | tf_op jit(solution)/shard_map/pallas_call | solution.py:17
  51.4 0.5 collective-permute-start.12
  52.1 1.5 %shard_map.65 = (f32[256,128]{1,0:T(8,128)S(1)}, f32[512,128]{1,0:T(8,128)S(1)}, f32[512,128]{1,0:T(8,128)S(1)}) custom-call(f32[2,128]{1,0:T(2,128)S(1)} %broadcast_in_dim.2.numbers, bf16[264,1152]{1,0:T(8,128)(2,1)S(1)} %collective-permute-done.3.below.marked, bf16[256,1152]{1,0:T(8,128)(2,1)S(1)} %collective-permute-done.6.below, ...), custom_call_target="tpu_custom_call" | custom-call | flops 20000000000 | bytes 1 | tf_op jit(solution)/shard_map/pallas_call | solution.py:17
  54.2 0.5 collective-permute-start.11
  54.7 0.6 collective-permute-done.9.cross
  55.3 7.2 %collective-permute-done.12.above = f32[512,128]{1,0:T(8,128)S(1)} collective-permute-done((f32[512,128]{1,0:T(8,128)S(1)}, f32[512,128]{1,0:T(8,128)S(1)}, u32[]{:S(2)}, u32[]{:S(2)}) %collective-permute-start.12) | collective-permute-done | bytes 262176 | tf_op jit(solution)/shard_map/ppermute | solution.py:305
  62.4 1.2 %collective-permute-done.11.below = f32[512,128]{1,0:T(8,128)S(1)} collective-permute-done((f32[512,128]{1,0:T(8,128)S(1)}, f32[512,128]{1,0:T(8,128)S(1)}, u32[]{:S(2)}, u32[]{:S(2)}) %collective-permute-start.11) | collective-permute-done | bytes 262176 | tf_op jit(solution)/shard_map/ppermute | solution.py:305
  64.1 1.2 %collective-permute-done.13 = f32[128,128]{1,0:T(8,128)S(1)} collective-permute-done((f32[128,128]{1,0:T(8,128)S(1)}, f32[128,128]{1,0:T(8,128)S(1)}, u32[]{:S(2)}, u32[]{:S(2)}) %collective-permute-start.13) | collective-permute-done | bytes 65568 | tf_op jit(solution)/shard_map/ppermute | solution.py:304
  65.4 5.4 %collective-permute-start.14 = (f32[128,128]{1,0:T(8,128)S(1)}, f32[128,128]{1,0:T(8,128)S(1)}, u32[]{:S(2)}, u32[]{:S(2)}) collective-permute-start(f32[128,128]{1,0:T(8,128)S(1)} %add.20), channel_id=1, source_target_pairs={{0,2},{2,0},{4,6},{6,4},{8,10},{10,8},{12,14},{14,12},{1,3},{3,1},... | collective-permute-start | bytes 196616 | tf_op jit(solution)/shard_map/ppermute | solution.py:305
  70.8 2.4 %collective-permute-done.14 = f32[128,128]{1,0:T(8,128)S(1)} collective-permute-done((f32[128,128]{1,0:T(8,128)S(1)}, f32[128,128]{1,0:T(8,128)S(1)}, u32[]{:S(2)}, u32[]{:S(2)}) %collective-permute-start.14) | collective-permute-done | bytes 65568 | tf_op jit(solution)/shard_map/ppermute | solution.py:305
  73.2 0.6 collective-permute-start.15
  73.8 3.7 %collective-permute-done.15 = f32[128,128]{1,0:T(8,128)S(1)} collective-permute-done((f32[128,128]{1,0:T(8,128)S(1)}, f32[128,128]{1,0:T(8,128)S(1)}, u32[]{:S(2)}, u32[]{:S(2)}) %collective-permute-start.15) | collective-permute-done | bytes 65568 | tf_op jit(solution)/shard_map/ppermute | solution.py:305
  77.5 0.7 collective-permute-start.16
  78.2 5.3 %collective-permute-done.16 = f32[128,128]{1,0:T(8,128)S(1)} collective-permute-done((f32[128,128]{1,0:T(8,128)S(1)}, f32[128,128]{1,0:T(8,128)S(1)}, u32[]{:S(2)}, u32[]{:S(2)}) %collective-permute-start.16) | collective-permute-done | bytes 65568 | tf_op jit(solution)/shard_map/ppermute | solution.py:305
  83.5 5.2 %shard_map.67 = (f32[512,128]{1,0:T(8,128)}, f32[128,128]{1,0:T(8,128)}) custom-call(f32[512,128]{1,0:T(8,128)S(1)} %get-tuple-element.52.image, f32[128,128]{1,0:T(8,128)S(1)} %add.23.gram), custom_call_target="tpu_custom_call" | custom-call | flops 20000000000 | bytes 1 | tf_op jit(solution)/shard_map/pallas_call | solution.py:17
  (25 shorter events, 2.2 us)
Async XLA Ops:
  0.6 31.9 %collective-permute-start.4 = (bf16[512,1024]{1,0:T(8,128)(2,1)}, bf16[512,1024]{1,0:T(8,128)(2,1)S(1)}, u32[]{:S(2)}, u32[]{:S(2)}) collective-permute-start(bf16[512,1024]{1,0:T(8,128)(2,1)} %embeddings.1), channel_id=1, source_target_pairs={{0,12},{2,14},{4,0},{6,2},{8,4},{10,6},{12,8},{14,10},{1,13},{3,15... | collective-permute-start | bytes 3145736 | tf_op jit(solution)/shard_map/ppermute | solution.py:305
  5.7 1.3 %copy-start = (bf16[512,1024]{1,0:T(8,128)(2,1)S(1)}, bf16[512,1024]{1,0:T(8,128)(2,1)}, u32[]{:S(2)}) copy-start(bf16[512,1024]{1,0:T(8,128)(2,1)} %embeddings.1) | copy-start | bytes 3145732
  7.0 0.9 %copy-start.1 = (bf16[512,128]{1,0:T(8,128)(2,1)S(1)}, bf16[512,128]{1,0:T(8,128)(2,1)}, u32[]{:S(2)}) copy-start(bf16[512,128]{1,0:T(8,128)(2,1)} %panel.1) | copy-start | bytes 393220
  7.9 0.7 copy-start.2
  9.6 3.5 %collective-permute-start.2 = (bf16[264,1152]{1,0:T(8,128)(2,1)S(1)}, bf16[264,1152]{1,0:T(8,128)(2,1)S(1)}, u32[]{:S(2)}, u32[]{:S(2)}) collective-permute-start(bf16[264,1152]{1,0:T(8,128)(2,1)S(1)} %get-tuple-element.28.last), channel_id=1, source_target_pairs={{0,1},{1,0},{2,3},{3,2},{4,5},{5,4},{6,7},{7,6},{8,9},{9,8},{10,11... | collective-permute-start | bytes 1824776 | tf_op jit(solution)/shard_map/ppermute | solution.py:304
  9.6 16.2 %collective-permute-start = (bf16[264,1152]{1,0:T(8,128)(2,1)S(1)}, bf16[264,1152]{1,0:T(8,128)(2,1)}, u32[]{:S(2)}, u32[]{:S(2)}) collective-permute-start(bf16[264,1152]{1,0:T(8,128)(2,1)S(1)} %get-tuple-element.28.last), channel_id=1, source_target_pairs={{0,2},{2,0},{4,6},{6,4},{8,10},{10,8},{12,14},{14,12},{1,3},{3,1},... | collective-permute-start | bytes 1824776 | tf_op jit(solution)/shard_map/ppermute | solution.py:305
  11.1 2.0 %collective-permute-start.1 = (bf16[256,1152]{1,0:T(8,128)(2,1)S(1)}, bf16[256,1152]{1,0:T(8,128)(2,1)S(1)}, u32[]{:S(2)}, u32[]{:S(2)}) collective-permute-start(bf16[256,1152]{1,0:T(8,128)(2,1)S(1)} %get-tuple-element.34.first), channel_id=1, source_target_pairs={{0,1},{1,0},{2,3},{3,2},{4,5},{5,4},{6,7},{7,6},{8,9},{9,8},{10,11... | collective-permute-start | bytes 1769480 | tf_op jit(solution)/shard_map/ppermute | solution.py:304
  11.4 21.2 %collective-permute-start.5 = (bf16[520,128]{1,0:T(8,128)(2,1)}, bf16[520,128]{1,0:T(8,128)(2,1)}, u32[]{:S(2)}, u32[]{:S(2)}) collective-permute-start(bf16[520,128]{1,0:T(8,128)(2,1)} %get-tuple-element.31), channel_id=1, source_target_pairs={{0,12},{2,14},{4,0},{6,2},{8,4},{10,6},{12,8},{14,10},{1,13},{3,15... | collective-permute-start | bytes 399368 | tf_op jit(solution)/shard_map/ppermute | solution.py:305
  25.9 21.9 %collective-permute-start.6 = (bf16[256,1152]{1,0:T(8,128)(2,1)S(1)}, bf16[256,1152]{1,0:T(8,128)(2,1)S(1)}, u32[]{:S(2)}, u32[]{:S(2)}) collective-permute-start(bf16[256,1152]{1,0:T(8,128)(2,1)S(1)} %get-tuple-element.34.first), channel_id=1, source_target_pairs={{0,2},{2,4},{4,6},{6,8},{8,10},{10,12},{12,14},{14,0},{1,3},{3,5},... | collective-permute-start | bytes 1769480 | tf_op jit(solution)/shard_map/ppermute | solution.py:305
  27.4 19.0 %collective-permute-start.3 = (bf16[264,1152]{1,0:T(8,128)(2,1)}, bf16[264,1152]{1,0:T(8,128)(2,1)S(1)}, u32[]{:S(2)}, u32[]{:S(2)}) collective-permute-start(bf16[264,1152]{1,0:T(8,128)(2,1)} %collective-permute-done), channel_id=1, source_target_pairs={{0,4},{2,2},{4,8},{6,6},{8,12},{10,10},{12,0},{14,14},{1,5},{3,3},... | collective-permute-start | bytes 1824776 | tf_op jit(solution)/shard_map/ppermute | solution.py:305
  46.3 2.0 %collective-permute-start.7 = (bf16[264,1152]{1,0:T(8,128)(2,1)S(1)}, bf16[264,1152]{1,0:T(8,128)(2,1)S(1)}, u32[]{:S(2)}, u32[]{:S(2)}) collective-permute-start(bf16[264,1152]{1,0:T(8,128)(2,1)S(1)} %collective-permute-done.3.below.marked), channel_id=1, source_target_pairs={{0,1},{1,0},{2,3},{3,2},{4,5},{5,4},{6,7},{7,6},{8,9},{9,8},{10,11... | collective-permute-start | bytes 1824776 | tf_op jit(solution)/shard_map/ppermute | solution.py:304
  47.7 2.2 %collective-permute-start.8 = (bf16[256,1152]{1,0:T(8,128)(2,1)S(1)}, bf16[256,1152]{1,0:T(8,128)(2,1)S(1)}, u32[]{:S(2)}, u32[]{:S(2)}) collective-permute-start(bf16[256,1152]{1,0:T(8,128)(2,1)S(1)} %collective-permute-done.6.below), channel_id=1, source_target_pairs={{0,1},{1,0},{2,3},{3,2},{4,5},{5,4},{6,7},{7,6},{8,9},{9,8},{10,11... | collective-permute-start | bytes 1769480 | tf_op jit(solution)/shard_map/ppermute | solution.py:304
  51.4 11.0 %collective-permute-start.12 = (f32[512,128]{1,0:T(8,128)S(1)}, f32[512,128]{1,0:T(8,128)S(1)}, u32[]{:S(2)}, u32[]{:S(2)}) collective-permute-start(f32[512,128]{1,0:T(8,128)S(1)} %get-tuple-element.43), channel_id=1, source_target_pairs={{0,4},{2,6},{4,8},{6,10},{8,12},{10,14},{12,0},{14,2},{1,5},{3,7},... | collective-permute-start | bytes 786440 | tf_op jit(solution)/shard_map/ppermute | solution.py:305
  51.9 2.2 %collective-permute-start.10 = (f32[512,128]{1,0:T(8,128)S(1)}, f32[512,128]{1,0:T(8,128)S(1)}, u32[]{:S(2)}, u32[]{:S(2)}) collective-permute-start(f32[512,128]{1,0:T(8,128)S(1)} %pad_maximum_fusion), channel_id=1, source_target_pairs={{0,1},{1,0},{2,3},{3,2},{4,5},{5,4},{6,7},{7,6},{8,9},{9,8},{10,11... | collective-permute-start | bytes 786440 | tf_op jit(solution)/shard_map/ppermute | solution.py:304
  53.6 1.6 %collective-permute-start.9 = (f32[512,128]{1,0:T(8,128)S(1)}, f32[512,128]{1,0:T(8,128)S(1)}, u32[]{:S(2)}, u32[]{:S(2)}) collective-permute-start(f32[512,128]{1,0:T(8,128)S(1)} %get-tuple-element.46), channel_id=1, source_target_pairs={{0,1},{1,0},{2,3},{3,2},{4,5},{5,4},{6,7},{7,6},{8,9},{9,8},{10,11... | collective-permute-start | bytes 786440 | tf_op jit(solution)/shard_map/ppermute | solution.py:304
  54.2 9.5 %collective-permute-start.11 = (f32[512,128]{1,0:T(8,128)S(1)}, f32[512,128]{1,0:T(8,128)S(1)}, u32[]{:S(2)}, u32[]{:S(2)}) collective-permute-start(f32[512,128]{1,0:T(8,128)S(1)} %fusion), channel_id=1, source_target_pairs={{0,14},{2,0},{4,2},{6,4},{8,6},{10,8},{12,10},{14,12},{1,15},{3,1}... | collective-permute-start | bytes 786440 | tf_op jit(solution)/shard_map/ppermute | solution.py:305
  64.1 1.3 %collective-permute-start.13 = (f32[128,128]{1,0:T(8,128)S(1)}, f32[128,128]{1,0:T(8,128)S(1)}, u32[]{:S(2)}, u32[]{:S(2)}) collective-permute-start(f32[128,128]{1,0:T(8,128)S(1)} %get-tuple-element.53), channel_id=1, source_target_pairs={{0,1},{1,0},{2,3},{3,2},{4,5},{5,4},{6,7},{7,6},{8,9},{9,8},{10,11... | collective-permute-start | bytes 196616 | tf_op jit(solution)/shard_map/ppermute | solution.py:304
  65.4 7.8 %collective-permute-start.14 = (f32[128,128]{1,0:T(8,128)S(1)}, f32[128,128]{1,0:T(8,128)S(1)}, u32[]{:S(2)}, u32[]{:S(2)}) collective-permute-start(f32[128,128]{1,0:T(8,128)S(1)} %add.20), channel_id=1, source_target_pairs={{0,2},{2,0},{4,6},{6,4},{8,10},{10,8},{12,14},{14,12},{1,3},{3,1},... | collective-permute-start | bytes 196616 | tf_op jit(solution)/shard_map/ppermute | solution.py:305
  73.2 4.3 %collective-permute-start.15 = (f32[128,128]{1,0:T(8,128)S(1)}, f32[128,128]{1,0:T(8,128)S(1)}, u32[]{:S(2)}, u32[]{:S(2)}) collective-permute-start(f32[128,128]{1,0:T(8,128)S(1)} %add.21), channel_id=1, source_target_pairs={{0,4},{2,6},{4,0},{6,2},{8,12},{10,14},{12,8},{14,10},{1,5},{3,7},... | collective-permute-start | bytes 196616 | tf_op jit(solution)/shard_map/ppermute | solution.py:305
  77.5 5.9 %collective-permute-start.16 = (f32[128,128]{1,0:T(8,128)S(1)}, f32[128,128]{1,0:T(8,128)S(1)}, u32[]{:S(2)}, u32[]{:S(2)}) collective-permute-start(f32[128,128]{1,0:T(8,128)S(1)} %add.22), channel_id=1, source_target_pairs={{0,8},{2,10},{4,12},{6,14},{8,0},{10,2},{12,4},{14,6},{1,9},{3,11}... | collective-permute-start | bytes 196616 | tf_op jit(solution)/shard_map/ppermute | solution.py:305

commit v19 on v17

--- a/solution.py
+++ b/solution.py
@@ -195,14 +195,18 @@
 
 
 def below_last_body(
-    numbers, marked, below, first, last, other_first, other_last, self_image, back, image, own_image, own_cross
+    numbers, marked, below, first, last, other_first, other_last, back, image, total
 ):
     half = 2 * last.shape[0]
     columns = own_columns(place(numbers), marks(marked, half), first, last, other_first, other_last, BELOW)
     rows_sq = [as_column(square_rows(marked)[1])]
-    image[...], total = products(width_of(numbers), pieces(below), rows_sq, columns, back[...], 1)
-    own_image[...] = self_image[...] + total[:, :half].T
-    own_cross[...] = total[:, half:].T
+    image[...], total[...] = products(width_of(numbers), pieces(below), rows_sq, columns, back[...], 1)
+
+
+def own_body(self_image, back, image, cross):
+    half = image.shape[0]
+    image[...] = self_image[...] + back[:, :half].T
+    cross[...] = back[:, half:].T
 
 
 def above_below(part, numbers, above, panel, above_sq, marked, other_marked, below, other, above_image, image, below_image, cross):
@@ -349,13 +353,14 @@
     above_image, below_sum1, below_cross1 = vmem_call(
         above_below_last_body, (image, piece, piece), *here, below0, other0, below1, other1, above_image
     )
-    below_image1, own_image, own_cross = vmem_call(
-        below_last_body, (piece, image, image), numbers, below0, below1, *own, self_image, after(back, above_image)
+    below_image1, back = vmem_call(
+        below_last_body, (piece, turned), numbers, below0, below1, *own, after(back, above_image)
     )
     above_image = blk_move(above_image, 2)
     join = lambda *parts: jnp.concatenate(parts, axis=0)
     below_cross = sub_move(join(below_cross0, below_cross1))
     below_image = join(below_sum0, below_sum1) + below_cross + join(below_image0, below_image1)
+    own_image, own_cross = vmem_call(own_body, (image, image), self_image, after(back, above_image))
     below_image = blk_move(below_image, -1)
     image_rows, gram = vmem_call(
         gram_body, (image, shape(width, width)), own_image, sub_move(own_cross), below_image, above_image

time: 88.6 us -> 88.6 us (level)
    pallas_call x9 -> x10, Pallas kernels: 17.8 us -> 17.9 us  [vmem_call(): pl.pallas_call(body, out_shape=out_shapes, in_specs=[in_vmem] * len(opera...]
where the time goes in v19:
time: 88.6 us; the launch traced here: 88.4 us
  waiting for transfers between devices  45.6 us (51%)
  starting transfers between devices  20.3 us (23%)
  Pallas kernels  17.9 us (20%)
  local copies, waits for them, and re-layouts  2.91 us (3%)
  between operations  1.41 us (2%)
    ppermute x10, waiting for transfers between devices, per_device(): lax.ppermute(v, 'blk', [(i, to(i) % n_blk) for i in range(n_blk)])  44.2 us
    ppermute x10, starting transfers between devices, per_device(): lax.ppermute(v, 'blk', [(i, to(i) % n_blk) for i in range(n_blk)])  19 us
    pallas_call x10, Pallas kernels, vmem_call(): pl.pallas_call(body, out_shape=out_shapes, in_specs=[in_vmem] * len(opera...  17.9 us
    unnamed x6, local copies, waits for them, and re-layouts  2.84 us
  transfers between devices with their start and end apart: 17, of which 11 were waited for; matrix products, arithmetic and copies ran while one was open for 0% of the time, Pallas kernels for 12%

profile of v19, /device:TPU:0, one launch (start us, length us, event | category | flops | bytes accessed | tf_op | source)
XLA Modules:
  0.0 88.4 jit_solution(11514330229468780336)
XLA Ops:
  0.6 5.1 %collective-permute-start.4 = (bf16[512,1024]{1,0:T(8,128)(2,1)}, bf16[512,1024]{1,0:T(8,128)(2,1)S(1)}, u32[]{:S(2)}, u32[]{:S(2)}) collective-permute-start(bf16[512,1024]{1,0:T(8,128)(2,1)} %embeddings.1), channel_id=1, source_target_pairs={{0,12},{2,14},{4,0},{6,2},{8,4},{10,6},{12,8},{14,10},{1,13},{3,15... | collective-permute-start | bytes 3145736 | tf_op jit(solution)/shard_map/ppermute | solution.py:309
  5.7 1.3 %copy-done = bf16[512,1024]{1,0:T(8,128)(2,1)S(1)} copy-done((bf16[512,1024]{1,0:T(8,128)(2,1)S(1)}, bf16[512,1024]{1,0:T(8,128)(2,1)}, u32[]{:S(2)}) %copy-start) | copy-done | bytes 1048600
  7.0 0.9 %copy-done.1 = bf16[512,128]{1,0:T(8,128)(2,1)S(1)} copy-done((bf16[512,128]{1,0:T(8,128)(2,1)S(1)}, bf16[512,128]{1,0:T(8,128)(2,1)}, u32[]{:S(2)}) %copy-start.1) | copy-done | bytes 131096
  7.9 0.7 copy-done.2
  8.6 1.1 %shard_map.59 = (bf16[264,1152]{1,0:T(8,128)(2,1)S(1)}, bf16[256,1152]{1,0:T(8,128)(2,1)S(1)}, bf16[520,128]{1,0:T(8,128)(2,1)}) custom-call(bf16[512,1024]{1,0:T(8,128)(2,1)S(1)} %copy-done, bf16[512,128]{1,0:T(8,128)(2,1)S(1)} %copy-done.1, s32[4,56]{1,0:T(4,128)S(1)} %copy-done.2), custom_call_target="tpu_custom_call" | custom-call | flops 1 | bytes 1 | tf_op jit(solution)/shard_map/pallas_call | solution.py:17
  9.6 0.5 collective-permute-start.1
  10.1 1.5 %collective-permute-start.2 = (bf16[256,1152]{1,0:T(8,128)(2,1)S(1)}, bf16[256,1152]{1,0:T(8,128)(2,1)}, u32[]{:S(2)}, u32[]{:S(2)}) collective-permute-start(bf16[256,1152]{1,0:T(8,128)(2,1)S(1)} %get-tuple-element.31.last), channel_id=1, source_target_pairs={{0,2},{2,0},{4,6},{6,4},{8,10},{10,8},{12,14},{14,12},{1,3},{3,1},... | collective-permute-start | bytes 1769480 | tf_op jit(solution)/shard_map/ppermute | solution.py:309
  11.6 0.4 collective-permute-start.5
  12.9 2.1 %shard_map.60.self_image = f32[512,128]{1,0:T(8,128)S(1)} custom-call(f32[2,128]{1,0:T(2,128)S(1)} %broadcast_in_dim.2.numbers, bf16[264,1152]{1,0:T(8,128)(2,1)S(1)} %get-tuple-element.32.first, bf16[256,1152]{1,0:T(8,128)(2,1)S(1)} %get-tuple-element.31.last, bf16[264,1152]{1,0:T(8,128)(2,1)S(1)} %collective-permute-done.other_first, ...), custom_call_target="tpu_custom_call" | custom-call | flops 1 | bytes 1 | tf_op jit(solution)/shard_map/pallas_call | solution.py:17
  15.0 10.5 %collective-permute-done.2 = bf16[256,1152]{1,0:T(8,128)(2,1)} collective-permute-done((bf16[256,1152]{1,0:T(8,128)(2,1)S(1)}, bf16[256,1152]{1,0:T(8,128)(2,1)}, u32[]{:S(2)}, u32[]{:S(2)}) %collective-permute-start.2) | collective-permute-done | bytes 589856 | tf_op jit(solution)/shard_map/ppermute | solution.py:309
  25.5 1.9 %collective-permute-start.6 = (bf16[256,1152]{1,0:T(8,128)(2,1)}, bf16[256,1152]{1,0:T(8,128)(2,1)S(1)}, u32[]{:S(2)}, u32[]{:S(2)}) collective-permute-start(bf16[256,1152]{1,0:T(8,128)(2,1)} %collective-permute-done.2), channel_id=1, source_target_pairs={{0,4},{2,2},{4,8},{6,6},{8,12},{10,10},{12,0},{14,14},{1,5},{3,3},... | collective-permute-start | bytes 1769480 | tf_op jit(solution)/shard_map/ppermute | solution.py:309
  27.4 1.3 %collective-permute-start.3 = (bf16[264,1152]{1,0:T(8,128)(2,1)S(1)}, bf16[264,1152]{1,0:T(8,128)(2,1)S(1)}, u32[]{:S(2)}, u32[]{:S(2)}) collective-permute-start(bf16[264,1152]{1,0:T(8,128)(2,1)S(1)} %get-tuple-element.32.first), channel_id=1, source_target_pairs={{0,2},{2,4},{4,6},{6,8},{8,10},{10,12},{12,14},{14,0},{1,3},{3,5},... | collective-permute-start | bytes 1824776 | tf_op jit(solution)/shard_map/ppermute | solution.py:309
  28.7 3.8 %collective-permute-done.5.panel = bf16[520,128]{1,0:T(8,128)(2,1)} collective-permute-done((bf16[520,128]{1,0:T(8,128)(2,1)}, bf16[520,128]{1,0:T(8,128)(2,1)}, u32[]{:S(2)}, u32[]{:S(2)}) %collective-permute-start.5) | collective-permute-done | bytes 133152 | tf_op jit(solution)/shard_map/ppermute | solution.py:309
  32.5 3.2 %shard_map.61 = (f32[512,128]{1,0:T(8,128)S(1)}, f32[128,1024]{1,0:T(8,128)S(1)}, f32[512,128]{1,0:T(8,128)S(1)}, bf16[520,128]{1,0:T(8,128)(2,1)S(1)}) custom-call(f32[2,128]{1,0:T(2,128)S(1)} %broadcast_in_dim.2.numbers, bf16[512,1024]{1,0:T(8,128)(2,1)S(1)} %collective-permute-done.4.above, bf16[520,128]{1,0:T(8,128)(2,1)} %collective-permute-done.5.panel, ...), custom_call_target="tpu_custom_call" | custom-call | flops 20000000000 | bytes 1 | tf_op jit(solution)/shard_map/pallas_call | solution.py:17
  35.7 10.3 %collective-permute-done.3.below.marked = bf16[264,1152]{1,0:T(8,128)(2,1)S(1)} collective-permute-done((bf16[264,1152]{1,0:T(8,128)(2,1)S(1)}, bf16[264,1152]{1,0:T(8,128)(2,1)S(1)}, u32[]{:S(2)}, u32[]{:S(2)}) %collective-permute-start.3) | collective-permute-done | bytes 608288 | tf_op jit(solution)/shard_map/ppermute | solution.py:309
  46.1 1.4 %shard_map.62 = (f32[256,128]{1,0:T(8,128)S(1)}, f32[128,1024]{1,0:T(8,128)S(1)}) custom-call(f32[2,128]{1,0:T(2,128)S(1)} %broadcast_in_dim.2.numbers, bf16[264,1152]{1,0:T(8,128)(2,1)S(1)} %collective-permute-done.3.below.marked, bf16[264,1152]{1,0:T(8,128)(2,1)S(1)} %get-tuple-element.32.first, bf16[256,1152]{1,0:T(8,128)(2,1)S(1)} %get-tuple-element.31.last, ...), custom_call_target="tpu_custom_call" | custom-call | flops 20000000000 | bytes 1 | tf_op jit(solution)/shard_map/pallas_call | solution.py:17
  47.5 0.6 collective-permute-start.8
  48.1 1.5 %shard_map.63 = (f32[512,128]{1,0:T(8,128)S(1)}, f32[256,128]{1,0:T(8,128)S(1)}, f32[256,128]{1,0:T(8,128)S(1)}) custom-call(f32[2,128]{1,0:T(2,128)S(1)} %broadcast_in_dim.2.numbers, bf16[512,1024]{1,0:T(8,128)(2,1)S(1)} %collective-permute-done.4.above, bf16[520,128]{1,0:T(8,128)(2,1)S(1)} %get-tuple-element.41.panel, ...), custom_call_target="tpu_custom_call" | custom-call | flops 20000000000 | bytes 1 | tf_op jit(solution)/shard_map/pallas_call | solution.py:17
  49.7 1.5 %shard_map.64 = (f32[512,128]{1,0:T(8,128)S(1)}, f32[256,128]{1,0:T(8,128)S(1)}, f32[256,128]{1,0:T(8,128)S(1)}) custom-call(f32[2,128]{1,0:T(2,128)S(1)} %broadcast_in_dim.2.numbers, bf16[512,1024]{1,0:T(8,128)(2,1)S(1)} %collective-permute-done.4.above, bf16[520,128]{1,0:T(8,128)(2,1)S(1)} %get-tuple-element.41.panel, ...), custom_call_target="tpu_custom_call" | custom-call | flops 20000000000 | bytes 1 | tf_op jit(solution)/shard_map/pallas_call | solution.py:17
  51.2 1.7 %collective-permute-start.9 = (f32[512,128]{1,0:T(8,128)S(1)}, f32[512,128]{1,0:T(8,128)S(1)}, u32[]{:S(2)}, u32[]{:S(2)}) collective-permute-start(f32[512,128]{1,0:T(8,128)S(1)} %get-tuple-element.45), channel_id=1, source_target_pairs={{0,4},{2,6},{4,8},{6,10},{8,12},{10,14},{12,0},{14,2},{1,5},{3,7},... | collective-permute-start | bytes 786440 | tf_op jit(solution)/shard_map/ppermute | solution.py:309
  53.0 1.4 %shard_map.65 = (f32[256,128]{1,0:T(8,128)S(1)}, f32[128,1024]{1,0:T(8,128)S(1)}) custom-call(f32[2,128]{1,0:T(2,128)S(1)} %broadcast_in_dim.2.numbers, bf16[264,1152]{1,0:T(8,128)(2,1)S(1)} %collective-permute-done.3.below.marked, bf16[256,1152]{1,0:T(8,128)(2,1)S(1)} %collective-permute-done.6.below, bf16[264,1152]{1,0:T(8,128)(2,1)S(1)} %get-tuple-element.32.first, ...), custom_call_target="tpu_custom_call" | custom-call | flops 20000000000 | bytes 1 | tf_op jit(solution)/shard_map/pallas_call | solution.py:17
  54.5 1.6 %collective-permute-start.12 = (f32[512,128]{1,0:T(8,128)S(1)}, f32[512,128]{1,0:T(8,128)S(1)}, u32[]{:S(2)}, u32[]{:S(2)}) collective-permute-start(f32[512,128]{1,0:T(8,128)S(1)} %fusion), channel_id=1, source_target_pairs={{0,14},{2,0},{4,2},{6,4},{8,6},{10,8},{12,10},{14,12},{1,15},{3,1}... | collective-permute-start | bytes 786440 | tf_op jit(solution)/shard_map/ppermute | solution.py:309
  56.1 6.1 %collective-permute-done.9.above = f32[512,128]{1,0:T(8,128)S(1)} collective-permute-done((f32[512,128]{1,0:T(8,128)S(1)}, f32[512,128]{1,0:T(8,128)S(1)}, u32[]{:S(2)}, u32[]{:S(2)}) %collective-permute-start.9) | collective-permute-done | bytes 262176 | tf_op jit(solution)/shard_map/ppermute | solution.py:309
  62.5 2.1 %collective-permute-done.12.below = f32[512,128]{1,0:T(8,128)S(1)} collective-permute-done((f32[512,128]{1,0:T(8,128)S(1)}, f32[512,128]{1,0:T(8,128)S(1)}, u32[]{:S(2)}, u32[]{:S(2)}) %collective-permute-start.12) | collective-permute-done | bytes 262176 | tf_op jit(solution)/shard_map/ppermute | solution.py:309
  65.1 1.2 %collective-permute-done.13 = f32[128,128]{1,0:T(8,128)S(1)} collective-permute-done((f32[128,128]{1,0:T(8,128)S(1)}, f32[128,128]{1,0:T(8,128)S(1)}, u32[]{:S(2)}, u32[]{:S(2)}) %collective-permute-start.13) | collective-permute-done | bytes 65568 | tf_op jit(solution)/shard_map/ppermute | solution.py:308
  66.3 4.2 %collective-permute-start.14 = (f32[128,128]{1,0:T(8,128)S(1)}, f32[128,128]{1,0:T(8,128)S(1)}, u32[]{:S(2)}, u32[]{:S(2)}) collective-permute-start(f32[128,128]{1,0:T(8,128)S(1)} %add.20), channel_id=1, source_target_pairs={{0,2},{2,0},{4,6},{6,4},{8,10},{10,8},{12,14},{14,12},{1,3},{3,1},... | collective-permute-start | bytes 196616 | tf_op jit(solution)/shard_map/ppermute | solution.py:309
  70.5 2.4 %collective-permute-done.14 = f32[128,128]{1,0:T(8,128)S(1)} collective-permute-done((f32[128,128]{1,0:T(8,128)S(1)}, f32[128,128]{1,0:T(8,128)S(1)}, u32[]{:S(2)}, u32[]{:S(2)}) %collective-permute-start.14) | collective-permute-done | bytes 65568 | tf_op jit(solution)/shard_map/ppermute | solution.py:309
  72.9 0.6 collective-permute-start.15
  73.6 3.7 %collective-permute-done.15 = f32[128,128]{1,0:T(8,128)S(1)} collective-permute-done((f32[128,128]{1,0:T(8,128)S(1)}, f32[128,128]{1,0:T(8,128)S(1)}, u32[]{:S(2)}, u32[]{:S(2)}) %collective-permute-start.15) | collective-permute-done | bytes 65568 | tf_op jit(solution)/shard_map/ppermute | solution.py:309
  77.3 0.7 collective-permute-start.16
  78.0 5.3 %collective-permute-done.16 = f32[128,128]{1,0:T(8,128)S(1)} collective-permute-done((f32[128,128]{1,0:T(8,128)S(1)}, f32[128,128]{1,0:T(8,128)S(1)}, u32[]{:S(2)}, u32[]{:S(2)}) %collective-permute-start.16) | collective-permute-done | bytes 65568 | tf_op jit(solution)/shard_map/ppermute | solution.py:309
  83.2 5.1 %shard_map.68 = (f32[512,128]{1,0:T(8,128)}, f32[128,128]{1,0:T(8,128)}) custom-call(f32[512,128]{1,0:T(8,128)S(1)} %get-tuple-element.56.image, f32[128,128]{1,0:T(8,128)S(1)} %add.23.gram), custom_call_target="tpu_custom_call" | custom-call | flops 20000000000 | bytes 1 | tf_op jit(solution)/shard_map/pallas_call | solution.py:17
  (26 shorter events, 1.3 us)
Async XLA Ops:
  0.6 31.9 %collective-permute-start.4 = (bf16[512,1024]{1,0:T(8,128)(2,1)}, bf16[512,1024]{1,0:T(8,128)(2,1)S(1)}, u32[]{:S(2)}, u32[]{:S(2)}) collective-permute-start(bf16[512,1024]{1,0:T(8,128)(2,1)} %embeddings.1), channel_id=1, source_target_pairs={{0,12},{2,14},{4,0},{6,2},{8,4},{10,6},{12,8},{14,10},{1,13},{3,15... | collective-permute-start | bytes 3145736 | tf_op jit(solution)/shard_map/ppermute | solution.py:309
  5.7 1.3 %copy-start = (bf16[512,1024]{1,0:T(8,128)(2,1)S(1)}, bf16[512,1024]{1,0:T(8,128)(2,1)}, u32[]{:S(2)}) copy-start(bf16[512,1024]{1,0:T(8,128)(2,1)} %embeddings.1) | copy-start | bytes 3145732
  7.0 0.9 %copy-start.1 = (bf16[512,128]{1,0:T(8,128)(2,1)S(1)}, bf16[512,128]{1,0:T(8,128)(2,1)}, u32[]{:S(2)}) copy-start(bf16[512,128]{1,0:T(8,128)(2,1)} %panel.1) | copy-start | bytes 393220
  7.9 0.7 copy-start.2
  9.6 3.2 %collective-permute-start = (bf16[264,1152]{1,0:T(8,128)(2,1)S(1)}, bf16[264,1152]{1,0:T(8,128)(2,1)S(1)}, u32[]{:S(2)}, u32[]{:S(2)}) collective-permute-start(bf16[264,1152]{1,0:T(8,128)(2,1)S(1)} %get-tuple-element.32.first), channel_id=1, source_target_pairs={{0,1},{1,0},{2,3},{3,2},{4,5},{5,4},{6,7},{7,6},{8,9},{9,8},{10,11... | collective-permute-start | bytes 1824776 | tf_op jit(solution)/shard_map/ppermute | solution.py:308
  9.6 3.2 %collective-permute-start.1 = (bf16[256,1152]{1,0:T(8,128)(2,1)S(1)}, bf16[256,1152]{1,0:T(8,128)(2,1)S(1)}, u32[]{:S(2)}, u32[]{:S(2)}) collective-permute-start(bf16[256,1152]{1,0:T(8,128)(2,1)S(1)} %get-tuple-element.31.last), channel_id=1, source_target_pairs={{0,1},{1,0},{2,3},{3,2},{4,5},{5,4},{6,7},{7,6},{8,9},{9,8},{10,11... | collective-permute-start | bytes 1769480 | tf_op jit(solution)/shard_map/ppermute | solution.py:308
  10.1 15.3 %collective-permute-start.2 = (bf16[256,1152]{1,0:T(8,128)(2,1)S(1)}, bf16[256,1152]{1,0:T(8,128)(2,1)}, u32[]{:S(2)}, u32[]{:S(2)}) collective-permute-start(bf16[256,1152]{1,0:T(8,128)(2,1)S(1)} %get-tuple-element.31.last), channel_id=1, source_target_pairs={{0,2},{2,0},{4,6},{6,4},{8,10},{10,8},{12,14},{14,12},{1,3},{3,1},... | collective-permute-start | bytes 1769480 | tf_op jit(solution)/shard_map/ppermute | solution.py:309
  11.6 20.9 %collective-permute-start.5 = (bf16[520,128]{1,0:T(8,128)(2,1)}, bf16[520,128]{1,0:T(8,128)(2,1)}, u32[]{:S(2)}, u32[]{:S(2)}) collective-permute-start(bf16[520,128]{1,0:T(8,128)(2,1)} %get-tuple-element.33), channel_id=1, source_target_pairs={{0,12},{2,14},{4,0},{6,2},{8,4},{10,6},{12,8},{14,10},{1,13},{3,15... | collective-permute-start | bytes 399368 | tf_op jit(solution)/shard_map/ppermute | solution.py:309
  25.5 22.0 %collective-permute-start.6 = (bf16[256,1152]{1,0:T(8,128)(2,1)}, bf16[256,1152]{1,0:T(8,128)(2,1)S(1)}, u32[]{:S(2)}, u32[]{:S(2)}) collective-permute-start(bf16[256,1152]{1,0:T(8,128)(2,1)} %collective-permute-done.2), channel_id=1, source_target_pairs={{0,4},{2,2},{4,8},{6,6},{8,12},{10,10},{12,0},{14,14},{1,5},{3,3},... | collective-permute-start | bytes 1769480 | tf_op jit(solution)/shard_map/ppermute | solution.py:309
  27.4 18.7 %collective-permute-start.3 = (bf16[264,1152]{1,0:T(8,128)(2,1)S(1)}, bf16[264,1152]{1,0:T(8,128)(2,1)S(1)}, u32[]{:S(2)}, u32[]{:S(2)}) collective-permute-start(bf16[264,1152]{1,0:T(8,128)(2,1)S(1)} %get-tuple-element.32.first), channel_id=1, source_target_pairs={{0,2},{2,4},{4,6},{6,8},{8,10},{10,12},{12,14},{14,0},{1,3},{3,5},... | collective-permute-start | bytes 1824776 | tf_op jit(solution)/shard_map/ppermute | solution.py:309
  46.1 2.0 %collective-permute-start.7 = (bf16[264,1152]{1,0:T(8,128)(2,1)S(1)}, bf16[264,1152]{1,0:T(8,128)(2,1)S(1)}, u32[]{:S(2)}, u32[]{:S(2)}) collective-permute-start(bf16[264,1152]{1,0:T(8,128)(2,1)S(1)} %collective-permute-done.3.below.marked), channel_id=1, source_target_pairs={{0,1},{1,0},{2,3},{3,2},{4,5},{5,4},{6,7},{7,6},{8,9},{9,8},{10,11... | collective-permute-start | bytes 1824776 | tf_op jit(solution)/shard_map/ppermute | solution.py:308
  47.5 2.2 %collective-permute-start.8 = (bf16[256,1152]{1,0:T(8,128)(2,1)S(1)}, bf16[256,1152]{1,0:T(8,128)(2,1)S(1)}, u32[]{:S(2)}, u32[]{:S(2)}) collective-permute-start(bf16[256,1152]{1,0:T(8,128)(2,1)S(1)} %collective-permute-done.6.below), channel_id=1, source_target_pairs={{0,1},{1,0},{2,3},{3,2},{4,5},{5,4},{6,7},{7,6},{8,9},{9,8},{10,11... | collective-permute-start | bytes 1769480 | tf_op jit(solution)/shard_map/ppermute | solution.py:308
  51.2 11.0 %collective-permute-start.9 = (f32[512,128]{1,0:T(8,128)S(1)}, f32[512,128]{1,0:T(8,128)S(1)}, u32[]{:S(2)}, u32[]{:S(2)}) collective-permute-start(f32[512,128]{1,0:T(8,128)S(1)} %get-tuple-element.45), channel_id=1, source_target_pairs={{0,4},{2,6},{4,8},{6,10},{8,12},{10,14},{12,0},{14,2},{1,5},{3,7},... | collective-permute-start | bytes 786440 | tf_op jit(solution)/shard_map/ppermute | solution.py:309
  52.9 1.6 %collective-permute-start.11 = (f32[512,128]{1,0:T(8,128)S(1)}, f32[512,128]{1,0:T(8,128)S(1)}, u32[]{:S(2)}, u32[]{:S(2)}) collective-permute-start(f32[512,128]{1,0:T(8,128)S(1)} %pad_maximum_fusion), channel_id=1, source_target_pairs={{0,1},{1,0},{2,3},{3,2},{4,5},{5,4},{6,7},{7,6},{8,9},{9,8},{10,11... | collective-permute-start | bytes 786440 | tf_op jit(solution)/shard_map/ppermute | solution.py:308
  54.5 10.0 %collective-permute-start.12 = (f32[512,128]{1,0:T(8,128)S(1)}, f32[512,128]{1,0:T(8,128)S(1)}, u32[]{:S(2)}, u32[]{:S(2)}) collective-permute-start(f32[512,128]{1,0:T(8,128)S(1)} %fusion), channel_id=1, source_target_pairs={{0,14},{2,0},{4,2},{6,4},{8,6},{10,8},{12,10},{14,12},{1,15},{3,1}... | collective-permute-start | bytes 786440 | tf_op jit(solution)/shard_map/ppermute | solution.py:309
  62.4 2.2 %collective-permute-start.10 = (f32[512,128]{1,0:T(8,128)S(1)}, f32[512,128]{1,0:T(8,128)S(1)}, u32[]{:S(2)}, u32[]{:S(2)}) collective-permute-start(f32[512,128]{1,0:T(8,128)S(1)} %get-tuple-element.50), channel_id=1, source_target_pairs={{0,1},{1,0},{2,3},{3,2},{4,5},{5,4},{6,7},{7,6},{8,9},{9,8},{10,11... | collective-permute-start | bytes 786440 | tf_op jit(solution)/shard_map/ppermute | solution.py:308
  65.0 1.3 %collective-permute-start.13 = (f32[128,128]{1,0:T(8,128)S(1)}, f32[128,128]{1,0:T(8,128)S(1)}, u32[]{:S(2)}, u32[]{:S(2)}) collective-permute-start(f32[128,128]{1,0:T(8,128)S(1)} %get-tuple-element.57), channel_id=1, source_target_pairs={{0,1},{1,0},{2,3},{3,2},{4,5},{5,4},{6,7},{7,6},{8,9},{9,8},{10,11... | collective-permute-start | bytes 196616 | tf_op jit(solution)/shard_map/ppermute | solution.py:308
  66.3 6.6 %collective-permute-start.14 = (f32[128,128]{1,0:T(8,128)S(1)}, f32[128,128]{1,0:T(8,128)S(1)}, u32[]{:S(2)}, u32[]{:S(2)}) collective-permute-start(f32[128,128]{1,0:T(8,128)S(1)} %add.20), channel_id=1, source_target_pairs={{0,2},{2,0},{4,6},{6,4},{8,10},{10,8},{12,14},{14,12},{1,3},{3,1},... | collective-permute-start | bytes 196616 | tf_op jit(solution)/shard_map/ppermute | solution.py:309
  72.9 4.3 %collective-permute-start.15 = (f32[128,128]{1,0:T(8,128)S(1)}, f32[128,128]{1,0:T(8,128)S(1)}, u32[]{:S(2)}, u32[]{:S(2)}) collective-permute-start(f32[128,128]{1,0:T(8,128)S(1)} %add.21), channel_id=1, source_target_pairs={{0,4},{2,6},{4,0},{6,2},{8,12},{10,14},{12,8},{14,10},{1,5},{3,7},... | collective-permute-start | bytes 196616 | tf_op jit(solution)/shard_map/ppermute | solution.py:309
  77.3 5.9 %collective-permute-start.16 = (f32[128,128]{1,0:T(8,128)S(1)}, f32[128,128]{1,0:T(8,128)S(1)}, u32[]{:S(2)}, u32[]{:S(2)}) collective-permute-start(f32[128,128]{1,0:T(8,128)S(1)} %add.22), channel_id=1, source_target_pairs={{0,8},{2,10},{4,12},{6,14},{8,0},{10,2},{12,4},{14,6},{1,9},{3,11}... | collective-permute-start | bytes 196616 | tf_op jit(solution)/shard_map/ppermute | solution.py:309

commit v20 on v17

--- a/solution.py
+++ b/solution.py
@@ -293,7 +293,7 @@
 
 
 def basis_body(image, gram, basis, upper):
-    upper[...], inverse = factor(gram[...], 4)
+    upper[...], inverse = factor(gram[...], 8)
     basis[...] = contract(image[...], inverse, ((1,), (1,)), HIGHEST)
 
 

time: 88.6 us -> 88.5 us (level)
  no operation moved by 1% of the time
where the time goes in v20:
time: 88.5 us; the launch traced here: 88.3 us
  waiting for transfers between devices  45.3 us (51%)
  starting transfers between devices  20.8 us (24%)
  Pallas kernels  17.7 us (20%)
  local copies, waits for them, and re-layouts  2.91 us (3%)
  between operations  1.4 us (2%)
    ppermute x10, waiting for transfers between devices, per_device(): lax.ppermute(v, 'blk', [(i, to(i) % n_blk) for i in range(n_blk)])  43.9 us
    ppermute x10, starting transfers between devices, per_device(): lax.ppermute(v, 'blk', [(i, to(i) % n_blk) for i in range(n_blk)])  19 us
    pallas_call x9, Pallas kernels, vmem_call(): pl.pallas_call(body, out_shape=out_shapes, in_specs=[in_vmem] * len(opera...  17.7 us
    unnamed x6, local copies, waits for them, and re-layouts  2.84 us
    ppermute x7, starting transfers between devices, per_device(): sub_move = lambda v: lax.ppermute(v, 'sub', [(0, 1), (1, 0)])  1.78 us
  transfers between devices with their start and end apart: 17, of which 11 were waited for; matrix products, arithmetic and copies ran while one was open for 0% of the time, Pallas kernels for 12%

profile of v20, /device:TPU:0, one launch (start us, length us, event | category | flops | bytes accessed | tf_op | source)
XLA Modules:
  0.0 88.3 jit_solution(17239352934345493112)
XLA Ops:
  0.6 5.1 %collective-permute-start.4 = (bf16[512,1024]{1,0:T(8,128)(2,1)}, bf16[512,1024]{1,0:T(8,128)(2,1)S(1)}, u32[]{:S(2)}, u32[]{:S(2)}) collective-permute-start(bf16[512,1024]{1,0:T(8,128)(2,1)} %embeddings.1), channel_id=1, source_target_pairs={{0,12},{2,14},{4,0},{6,2},{8,4},{10,6},{12,8},{14,10},{1,13},{3,15... | collective-permute-start | bytes 3145736 | tf_op jit(solution)/shard_map/ppermute | solution.py:305
  5.7 1.3 %copy-done = bf16[512,1024]{1,0:T(8,128)(2,1)S(1)} copy-done((bf16[512,1024]{1,0:T(8,128)(2,1)S(1)}, bf16[512,1024]{1,0:T(8,128)(2,1)}, u32[]{:S(2)}) %copy-start) | copy-done | bytes 1048600
  7.0 0.9 %copy-done.1 = bf16[512,128]{1,0:T(8,128)(2,1)S(1)} copy-done((bf16[512,128]{1,0:T(8,128)(2,1)S(1)}, bf16[512,128]{1,0:T(8,128)(2,1)}, u32[]{:S(2)}) %copy-start.1) | copy-done | bytes 131096
  7.9 0.7 copy-done.2
  8.6 1.1 %shard_map.59 = (bf16[264,1152]{1,0:T(8,128)(2,1)S(1)}, bf16[256,1152]{1,0:T(8,128)(2,1)S(1)}, bf16[520,128]{1,0:T(8,128)(2,1)}) custom-call(bf16[512,1024]{1,0:T(8,128)(2,1)S(1)} %copy-done, bf16[512,128]{1,0:T(8,128)(2,1)S(1)} %copy-done.1, s32[4,56]{1,0:T(4,128)S(1)} %copy-done.2), custom_call_target="tpu_custom_call" | custom-call | flops 1 | bytes 1 | tf_op jit(solution)/shard_map/pallas_call | solution.py:17
  9.6 0.5 collective-permute-start.2
  10.1 1.5 %collective-permute-start = (bf16[256,1152]{1,0:T(8,128)(2,1)S(1)}, bf16[256,1152]{1,0:T(8,128)(2,1)}, u32[]{:S(2)}, u32[]{:S(2)}) collective-permute-start(bf16[256,1152]{1,0:T(8,128)(2,1)S(1)} %get-tuple-element.29.last), channel_id=1, source_target_pairs={{0,2},{2,0},{4,6},{6,4},{8,10},{10,8},{12,14},{14,12},{1,3},{3,1},... | collective-permute-start | bytes 1769480 | tf_op jit(solution)/shard_map/ppermute | solution.py:305
  12.9 2.1 %shard_map.60.self_image = f32[512,128]{1,0:T(8,128)S(1)} custom-call(f32[2,128]{1,0:T(2,128)S(1)} %broadcast_in_dim.2.numbers, bf16[264,1152]{1,0:T(8,128)(2,1)S(1)} %get-tuple-element.30.first, bf16[256,1152]{1,0:T(8,128)(2,1)S(1)} %get-tuple-element.29.last, bf16[264,1152]{1,0:T(8,128)(2,1)S(1)} %collective-permute-done.1.other_first, ...), custom_call_target="tpu_custom_call" | custom-call | flops 1 | bytes 1 | tf_op jit(solution)/shard_map/pallas_call | solution.py:17
  15.0 10.5 %collective-permute-done = bf16[256,1152]{1,0:T(8,128)(2,1)} collective-permute-done((bf16[256,1152]{1,0:T(8,128)(2,1)S(1)}, bf16[256,1152]{1,0:T(8,128)(2,1)}, u32[]{:S(2)}, u32[]{:S(2)}) %collective-permute-start) | collective-permute-done | bytes 589856 | tf_op jit(solution)/shard_map/ppermute | solution.py:305
  25.5 1.9 %collective-permute-start.6 = (bf16[256,1152]{1,0:T(8,128)(2,1)}, bf16[256,1152]{1,0:T(8,128)(2,1)S(1)}, u32[]{:S(2)}, u32[]{:S(2)}) collective-permute-start(bf16[256,1152]{1,0:T(8,128)(2,1)} %collective-permute-done), channel_id=1, source_target_pairs={{0,4},{2,2},{4,8},{6,6},{8,12},{10,10},{12,0},{14,14},{1,5},{3,3},... | collective-permute-start | bytes 1769480 | tf_op jit(solution)/shard_map/ppermute | solution.py:305
  27.4 1.3 %collective-permute-start.3 = (bf16[264,1152]{1,0:T(8,128)(2,1)S(1)}, bf16[264,1152]{1,0:T(8,128)(2,1)S(1)}, u32[]{:S(2)}, u32[]{:S(2)}) collective-permute-start(bf16[264,1152]{1,0:T(8,128)(2,1)S(1)} %get-tuple-element.30.first), channel_id=1, source_target_pairs={{0,2},{2,4},{4,6},{6,8},{8,10},{10,12},{12,14},{14,0},{1,3},{3,5},... | collective-permute-start | bytes 1824776 | tf_op jit(solution)/shard_map/ppermute | solution.py:305
  28.7 3.8 %collective-permute-done.5.panel = bf16[520,128]{1,0:T(8,128)(2,1)} collective-permute-done((bf16[520,128]{1,0:T(8,128)(2,1)}, bf16[520,128]{1,0:T(8,128)(2,1)}, u32[]{:S(2)}, u32[]{:S(2)}) %collective-permute-start.5) | collective-permute-done | bytes 133152 | tf_op jit(solution)/shard_map/ppermute | solution.py:305
  32.5 3.2 %shard_map.61 = (f32[512,128]{1,0:T(8,128)S(1)}, f32[128,1024]{1,0:T(8,128)S(1)}, f32[512,128]{1,0:T(8,128)S(1)}, bf16[520,128]{1,0:T(8,128)(2,1)S(1)}) custom-call(f32[2,128]{1,0:T(2,128)S(1)} %broadcast_in_dim.2.numbers, bf16[512,1024]{1,0:T(8,128)(2,1)S(1)} %collective-permute-done.4.above, bf16[520,128]{1,0:T(8,128)(2,1)} %collective-permute-done.5.panel, ...), custom_call_target="tpu_custom_call" | custom-call | flops 20000000000 | bytes 1 | tf_op jit(solution)/shard_map/pallas_call | solution.py:17
  35.7 10.3 %collective-permute-done.3.below.marked = bf16[264,1152]{1,0:T(8,128)(2,1)S(1)} collective-permute-done((bf16[264,1152]{1,0:T(8,128)(2,1)S(1)}, bf16[264,1152]{1,0:T(8,128)(2,1)S(1)}, u32[]{:S(2)}, u32[]{:S(2)}) %collective-permute-start.3) | collective-permute-done | bytes 608288 | tf_op jit(solution)/shard_map/ppermute | solution.py:305
  46.1 1.4 %shard_map.62 = (f32[256,128]{1,0:T(8,128)S(1)}, f32[128,1024]{1,0:T(8,128)S(1)}) custom-call(f32[2,128]{1,0:T(2,128)S(1)} %broadcast_in_dim.2.numbers, bf16[264,1152]{1,0:T(8,128)(2,1)S(1)} %collective-permute-done.3.below.marked, bf16[264,1152]{1,0:T(8,128)(2,1)S(1)} %get-tuple-element.30.first, bf16[256,1152]{1,0:T(8,128)(2,1)S(1)} %get-tuple-element.29.last, ...), custom_call_target="tpu_custom_call" | custom-call | flops 20000000000 | bytes 1 | tf_op jit(solution)/shard_map/pallas_call | solution.py:17
  47.5 0.6 collective-permute-start.8
  48.1 1.5 %shard_map.63 = (f32[512,128]{1,0:T(8,128)S(1)}, f32[256,128]{1,0:T(8,128)S(1)}, f32[256,128]{1,0:T(8,128)S(1)}) custom-call(f32[2,128]{1,0:T(2,128)S(1)} %broadcast_in_dim.2.numbers, bf16[512,1024]{1,0:T(8,128)(2,1)S(1)} %collective-permute-done.4.above, bf16[520,128]{1,0:T(8,128)(2,1)S(1)} %get-tuple-element.39.panel, ...), custom_call_target="tpu_custom_call" | custom-call | flops 20000000000 | bytes 1 | tf_op jit(solution)/shard_map/pallas_call | solution.py:17
  49.7 1.5 %shard_map.64 = (f32[512,128]{1,0:T(8,128)S(1)}, f32[256,128]{1,0:T(8,128)S(1)}, f32[256,128]{1,0:T(8,128)S(1)}) custom-call(f32[2,128]{1,0:T(2,128)S(1)} %broadcast_in_dim.2.numbers, bf16[512,1024]{1,0:T(8,128)(2,1)S(1)} %collective-permute-done.4.above, bf16[520,128]{1,0:T(8,128)(2,1)S(1)} %get-tuple-element.39.panel, ...), custom_call_target="tpu_custom_call" | custom-call | flops 20000000000 | bytes 1 | tf_op jit(solution)/shard_map/pallas_call | solution.py:17
  51.2 1.7 %collective-permute-start.12 = (f32[512,128]{1,0:T(8,128)S(1)}, f32[512,128]{1,0:T(8,128)S(1)}, u32[]{:S(2)}, u32[]{:S(2)}) collective-permute-start(f32[512,128]{1,0:T(8,128)S(1)} %get-tuple-element.43), channel_id=1, source_target_pairs={{0,4},{2,6},{4,8},{6,10},{8,12},{10,14},{12,0},{14,2},{1,5},{3,7},... | collective-permute-start | bytes 786440 | tf_op jit(solution)/shard_map/ppermute | solution.py:305
  53.0 1.5 %shard_map.65 = (f32[256,128]{1,0:T(8,128)S(1)}, f32[512,128]{1,0:T(8,128)S(1)}, f32[512,128]{1,0:T(8,128)S(1)}) custom-call(f32[2,128]{1,0:T(2,128)S(1)} %broadcast_in_dim.2.numbers, bf16[264,1152]{1,0:T(8,128)(2,1)S(1)} %collective-permute-done.3.below.marked, bf16[256,1152]{1,0:T(8,128)(2,1)S(1)} %collective-permute-done.6.below, ...), custom_call_target="tpu_custom_call" | custom-call | flops 20000000000 | bytes 1 | tf_op jit(solution)/shard_map/pallas_call | solution.py:17
  54.6 0.5 collective-permute-start.9
  55.1 1.6 %collective-permute-start.11 = (f32[512,128]{1,0:T(8,128)S(1)}, f32[512,128]{1,0:T(8,128)S(1)}, u32[]{:S(2)}, u32[]{:S(2)}) collective-permute-start(f32[512,128]{1,0:T(8,128)S(1)} %fusion), channel_id=1, source_target_pairs={{0,14},{2,0},{4,2},{6,4},{8,6},{10,8},{12,10},{14,12},{1,15},{3,1}... | collective-permute-start | bytes 786440 | tf_op jit(solution)/shard_map/ppermute | solution.py:305
  56.7 5.5 %collective-permute-done.12.above = f32[512,128]{1,0:T(8,128)S(1)} collective-permute-done((f32[512,128]{1,0:T(8,128)S(1)}, f32[512,128]{1,0:T(8,128)S(1)}, u32[]{:S(2)}, u32[]{:S(2)}) %collective-permute-start.12) | collective-permute-done | bytes 262176 | tf_op jit(solution)/shard_map/ppermute | solution.py:305
  62.2 2.4 %collective-permute-done.11.below = f32[512,128]{1,0:T(8,128)S(1)} collective-permute-done((f32[512,128]{1,0:T(8,128)S(1)}, f32[512,128]{1,0:T(8,128)S(1)}, u32[]{:S(2)}, u32[]{:S(2)}) %collective-permute-start.11) | collective-permute-done | bytes 262176 | tf_op jit(solution)/shard_map/ppermute | solution.py:305
  65.1 1.2 %collective-permute-done.13 = f32[128,128]{1,0:T(8,128)S(1)} collective-permute-done((f32[128,128]{1,0:T(8,128)S(1)}, f32[128,128]{1,0:T(8,128)S(1)}, u32[]{:S(2)}, u32[]{:S(2)}) %collective-permute-start.13) | collective-permute-done | bytes 65568 | tf_op jit(solution)/shard_map/ppermute | solution.py:304
  66.3 4.2 %collective-permute-start.14 = (f32[128,128]{1,0:T(8,128)S(1)}, f32[128,128]{1,0:T(8,128)S(1)}, u32[]{:S(2)}, u32[]{:S(2)}) collective-permute-start(f32[128,128]{1,0:T(8,128)S(1)} %add.20), channel_id=1, source_target_pairs={{0,2},{2,0},{4,6},{6,4},{8,10},{10,8},{12,14},{14,12},{1,3},{3,1},... | collective-permute-start | bytes 196616 | tf_op jit(solution)/shard_map/ppermute | solution.py:305
  70.5 2.4 %collective-permute-done.14 = f32[128,128]{1,0:T(8,128)S(1)} collective-permute-done((f32[128,128]{1,0:T(8,128)S(1)}, f32[128,128]{1,0:T(8,128)S(1)}, u32[]{:S(2)}, u32[]{:S(2)}) %collective-permute-start.14) | collective-permute-done | bytes 65568 | tf_op jit(solution)/shard_map/ppermute | solution.py:305
  72.9 0.6 collective-permute-start.15
  73.6 3.7 %collective-permute-done.15 = f32[128,128]{1,0:T(8,128)S(1)} collective-permute-done((f32[128,128]{1,0:T(8,128)S(1)}, f32[128,128]{1,0:T(8,128)S(1)}, u32[]{:S(2)}, u32[]{:S(2)}) %collective-permute-start.15) | collective-permute-done | bytes 65568 | tf_op jit(solution)/shard_map/ppermute | solution.py:305
  77.3 0.7 collective-permute-start.16
  78.0 5.3 %collective-permute-done.16 = f32[128,128]{1,0:T(8,128)S(1)} collective-permute-done((f32[128,128]{1,0:T(8,128)S(1)}, f32[128,128]{1,0:T(8,128)S(1)}, u32[]{:S(2)}, u32[]{:S(2)}) %collective-permute-start.16) | collective-permute-done | bytes 65568 | tf_op jit(solution)/shard_map/ppermute | solution.py:305
  83.2 5.0 %shard_map.67 = (f32[512,128]{1,0:T(8,128)}, f32[128,128]{1,0:T(8,128)}) custom-call(f32[512,128]{1,0:T(8,128)S(1)} %get-tuple-element.52.image, f32[128,128]{1,0:T(8,128)S(1)} %add.23.gram), custom_call_target="tpu_custom_call" | custom-call | flops 20000000000 | bytes 1 | tf_op jit(solution)/shard_map/pallas_call | solution.py:17
  (25 shorter events, 1.5 us)
Async XLA Ops:
  0.6 31.9 %collective-permute-start.4 = (bf16[512,1024]{1,0:T(8,128)(2,1)}, bf16[512,1024]{1,0:T(8,128)(2,1)S(1)}, u32[]{:S(2)}, u32[]{:S(2)}) collective-permute-start(bf16[512,1024]{1,0:T(8,128)(2,1)} %embeddings.1), channel_id=1, source_target_pairs={{0,12},{2,14},{4,0},{6,2},{8,4},{10,6},{12,8},{14,10},{1,13},{3,15... | collective-permute-start | bytes 3145736 | tf_op jit(solution)/shard_map/ppermute | solution.py:305
  5.7 1.3 %copy-start = (bf16[512,1024]{1,0:T(8,128)(2,1)S(1)}, bf16[512,1024]{1,0:T(8,128)(2,1)}, u32[]{:S(2)}) copy-start(bf16[512,1024]{1,0:T(8,128)(2,1)} %embeddings.1) | copy-start | bytes 3145732
  7.0 0.9 %copy-start.1 = (bf16[512,128]{1,0:T(8,128)(2,1)S(1)}, bf16[512,128]{1,0:T(8,128)(2,1)}, u32[]{:S(2)}) copy-start(bf16[512,128]{1,0:T(8,128)(2,1)} %panel.1) | copy-start | bytes 393220
  7.9 0.7 copy-start.2
  9.6 3.2 %collective-permute-start.1 = (bf16[264,1152]{1,0:T(8,128)(2,1)S(1)}, bf16[264,1152]{1,0:T(8,128)(2,1)S(1)}, u32[]{:S(2)}, u32[]{:S(2)}) collective-permute-start(bf16[264,1152]{1,0:T(8,128)(2,1)S(1)} %get-tuple-element.30.first), channel_id=1, source_target_pairs={{0,1},{1,0},{2,3},{3,2},{4,5},{5,4},{6,7},{7,6},{8,9},{9,8},{10,11... | collective-permute-start | bytes 1824776 | tf_op jit(solution)/shard_map/ppermute | solution.py:304
  9.6 3.2 %collective-permute-start.2 = (bf16[256,1152]{1,0:T(8,128)(2,1)S(1)}, bf16[256,1152]{1,0:T(8,128)(2,1)S(1)}, u32[]{:S(2)}, u32[]{:S(2)}) collective-permute-start(bf16[256,1152]{1,0:T(8,128)(2,1)S(1)} %get-tuple-element.29.last), channel_id=1, source_target_pairs={{0,1},{1,0},{2,3},{3,2},{4,5},{5,4},{6,7},{7,6},{8,9},{9,8},{10,11... | collective-permute-start | bytes 1769480 | tf_op jit(solution)/shard_map/ppermute | solution.py:304
  10.1 15.3 %collective-permute-start = (bf16[256,1152]{1,0:T(8,128)(2,1)S(1)}, bf16[256,1152]{1,0:T(8,128)(2,1)}, u32[]{:S(2)}, u32[]{:S(2)}) collective-permute-start(bf16[256,1152]{1,0:T(8,128)(2,1)S(1)} %get-tuple-element.29.last), channel_id=1, source_target_pairs={{0,2},{2,0},{4,6},{6,4},{8,10},{10,8},{12,14},{14,12},{1,3},{3,1},... | collective-permute-start | bytes 1769480 | tf_op jit(solution)/shard_map/ppermute | solution.py:305
  11.6 20.9 %collective-permute-start.5 = (bf16[520,128]{1,0:T(8,128)(2,1)}, bf16[520,128]{1,0:T(8,128)(2,1)}, u32[]{:S(2)}, u32[]{:S(2)}) collective-permute-start(bf16[520,128]{1,0:T(8,128)(2,1)} %get-tuple-element.31), channel_id=1, source_target_pairs={{0,12},{2,14},{4,0},{6,2},{8,4},{10,6},{12,8},{14,10},{1,13},{3,15... | collective-permute-start | bytes 399368 | tf_op jit(solution)/shard_map/ppermute | solution.py:305
  25.5 22.0 %collective-permute-start.6 = (bf16[256,1152]{1,0:T(8,128)(2,1)}, bf16[256,1152]{1,0:T(8,128)(2,1)S(1)}, u32[]{:S(2)}, u32[]{:S(2)}) collective-permute-start(bf16[256,1152]{1,0:T(8,128)(2,1)} %collective-permute-done), channel_id=1, source_target_pairs={{0,4},{2,2},{4,8},{6,6},{8,12},{10,10},{12,0},{14,14},{1,5},{3,3},... | collective-permute-start | bytes 1769480 | tf_op jit(solution)/shard_map/ppermute | solution.py:305
  27.4 18.7 %collective-permute-start.3 = (bf16[264,1152]{1,0:T(8,128)(2,1)S(1)}, bf16[264,1152]{1,0:T(8,128)(2,1)S(1)}, u32[]{:S(2)}, u32[]{:S(2)}) collective-permute-start(bf16[264,1152]{1,0:T(8,128)(2,1)S(1)} %get-tuple-element.30.first), channel_id=1, source_target_pairs={{0,2},{2,4},{4,6},{6,8},{8,10},{10,12},{12,14},{14,0},{1,3},{3,5},... | collective-permute-start | bytes 1824776 | tf_op jit(solution)/shard_map/ppermute | solution.py:305
  46.1 2.0 %collective-permute-start.7 = (bf16[264,1152]{1,0:T(8,128)(2,1)S(1)}, bf16[264,1152]{1,0:T(8,128)(2,1)S(1)}, u32[]{:S(2)}, u32[]{:S(2)}) collective-permute-start(bf16[264,1152]{1,0:T(8,128)(2,1)S(1)} %collective-permute-done.3.below.marked), channel_id=1, source_target_pairs={{0,1},{1,0},{2,3},{3,2},{4,5},{5,4},{6,7},{7,6},{8,9},{9,8},{10,11... | collective-permute-start | bytes 1824776 | tf_op jit(solution)/shard_map/ppermute | solution.py:304
  47.5 2.2 %collective-permute-start.8 = (bf16[256,1152]{1,0:T(8,128)(2,1)S(1)}, bf16[256,1152]{1,0:T(8,128)(2,1)S(1)}, u32[]{:S(2)}, u32[]{:S(2)}) collective-permute-start(bf16[256,1152]{1,0:T(8,128)(2,1)S(1)} %collective-permute-done.6.below), channel_id=1, source_target_pairs={{0,1},{1,0},{2,3},{3,2},{4,5},{5,4},{6,7},{7,6},{8,9},{9,8},{10,11... | collective-permute-start | bytes 1769480 | tf_op jit(solution)/shard_map/ppermute | solution.py:304
  51.2 11.0 %collective-permute-start.12 = (f32[512,128]{1,0:T(8,128)S(1)}, f32[512,128]{1,0:T(8,128)S(1)}, u32[]{:S(2)}, u32[]{:S(2)}) collective-permute-start(f32[512,128]{1,0:T(8,128)S(1)} %get-tuple-element.43), channel_id=1, source_target_pairs={{0,4},{2,6},{4,8},{6,10},{8,12},{10,14},{12,0},{14,2},{1,5},{3,7},... | collective-permute-start | bytes 786440 | tf_op jit(solution)/shard_map/ppermute | solution.py:305
  52.9 2.2 %collective-permute-start.10 = (f32[512,128]{1,0:T(8,128)S(1)}, f32[512,128]{1,0:T(8,128)S(1)}, u32[]{:S(2)}, u32[]{:S(2)}) collective-permute-start(f32[512,128]{1,0:T(8,128)S(1)} %pad_maximum_fusion), channel_id=1, source_target_pairs={{0,1},{1,0},{2,3},{3,2},{4,5},{5,4},{6,7},{7,6},{8,9},{9,8},{10,11... | collective-permute-start | bytes 786440 | tf_op jit(solution)/shard_map/ppermute | solution.py:304
  54.6 2.1 %collective-permute-start.9 = (f32[512,128]{1,0:T(8,128)S(1)}, f32[512,128]{1,0:T(8,128)S(1)}, u32[]{:S(2)}, u32[]{:S(2)}) collective-permute-start(f32[512,128]{1,0:T(8,128)S(1)} %get-tuple-element.46), channel_id=1, source_target_pairs={{0,1},{1,0},{2,3},{3,2},{4,5},{5,4},{6,7},{7,6},{8,9},{9,8},{10,11... | collective-permute-start | bytes 786440 | tf_op jit(solution)/shard_map/ppermute | solution.py:304
  55.1 9.5 %collective-permute-start.11 = (f32[512,128]{1,0:T(8,128)S(1)}, f32[512,128]{1,0:T(8,128)S(1)}, u32[]{:S(2)}, u32[]{:S(2)}) collective-permute-start(f32[512,128]{1,0:T(8,128)S(1)} %fusion), channel_id=1, source_target_pairs={{0,14},{2,0},{4,2},{6,4},{8,6},{10,8},{12,10},{14,12},{1,15},{3,1}... | collective-permute-start | bytes 786440 | tf_op jit(solution)/shard_map/ppermute | solution.py:305
  65.0 1.3 %collective-permute-start.13 = (f32[128,128]{1,0:T(8,128)S(1)}, f32[128,128]{1,0:T(8,128)S(1)}, u32[]{:S(2)}, u32[]{:S(2)}) collective-permute-start(f32[128,128]{1,0:T(8,128)S(1)} %get-tuple-element.53), channel_id=1, source_target_pairs={{0,1},{1,0},{2,3},{3,2},{4,5},{5,4},{6,7},{7,6},{8,9},{9,8},{10,11... | collective-permute-start | bytes 196616 | tf_op jit(solution)/shard_map/ppermute | solution.py:304
  66.3 6.6 %collective-permute-start.14 = (f32[128,128]{1,0:T(8,128)S(1)}, f32[128,128]{1,0:T(8,128)S(1)}, u32[]{:S(2)}, u32[]{:S(2)}) collective-permute-start(f32[128,128]{1,0:T(8,128)S(1)} %add.20), channel_id=1, source_target_pairs={{0,2},{2,0},{4,6},{6,4},{8,10},{10,8},{12,14},{14,12},{1,3},{3,1},... | collective-permute-start | bytes 196616 | tf_op jit(solution)/shard_map/ppermute | solution.py:305
  72.9 4.3 %collective-permute-start.15 = (f32[128,128]{1,0:T(8,128)S(1)}, f32[128,128]{1,0:T(8,128)S(1)}, u32[]{:S(2)}, u32[]{:S(2)}) collective-permute-start(f32[128,128]{1,0:T(8,128)S(1)} %add.21), channel_id=1, source_target_pairs={{0,4},{2,6},{4,0},{6,2},{8,12},{10,14},{12,8},{14,10},{1,5},{3,7},... | collective-permute-start | bytes 196616 | tf_op jit(solution)/shard_map/ppermute | solution.py:305
  77.3 5.9 %collective-permute-start.16 = (f32[128,128]{1,0:T(8,128)S(1)}, f32[128,128]{1,0:T(8,128)S(1)}, u32[]{:S(2)}, u32[]{:S(2)}) collective-permute-start(f32[128,128]{1,0:T(8,128)S(1)} %add.22), channel_id=1, source_target_pairs={{0,8},{2,10},{4,12},{6,14},{8,0},{10,2},{12,4},{14,6},{1,9},{3,11}... | collective-permute-start | bytes 196616 | tf_op jit(solution)/shard_map/ppermute | solution.py:305
